TPU v7x, 256 devices: a whole 4x4x8 slice. The times are simulated.
256 devices in a mesh: grp: 8 (over y, core), shard: 32 (over z, x).
Axes of the slice: x: 4, y: 4, z: 8, core: 2. Of those that a mesh axis runs over, the one named last changes fastest.
Arguments:
- table: float32 [131072, 256], P('shard'), may hold values from -6 to 6
- accum: float32 [131072], P('shard'), may hold values from 0.05 to 2
- pooled_grad: bfloat16 [8, 32, 512, 256], P('grp', 'shard'), may hold values from -6 to 6
- row_ids: int32 [8, 32, 4096], P('grp', 'shard'), may hold values from 0 to 131071, as said below
- bag_ids: int32 [8, 32, 4096], P('grp', 'shard'), may hold values from 0 to 511, never falling along the last dimension, each value on 1 to 16 neighbouring positions
- touched: int32 [32, 1024], P('shard'), may hold values from 0 to 4095, as said below
Outputs:
- new_table: float32 [131072, 256], P('shard')
- new_accum: float32 [131072], P('shard')
Inputs may be any that keep to these rules, and one draw needn't show every extreme that they name: `row_ids`: every id is s * 4096 + touched[s, k] for some shard s and some k: it lies in a listed row. At most 512 lookups of one device fall on one shard s (ids in s * 4096 to (s + 1) * 4096 - 1); in every draw some device sends exactly 512 to some shard, and in each replica one shard receives 512 from every device of that replica. Each row of touched holds 1024 distinct row numbers in increasing order.
All inputs are finite; a program needn't handle non-finite values.
Results may differ from a plain program's by a relative error of at most 0.0003.
Values may be sent and summed in bfloat16 or wider, within the bound.
No kernel may reach another device: no remote copies, remote signals or barrier semaphores. Data moves between devices by JAX's collectives and lax.ppermute only.
A program may use at most 128 MiB of HBM per device.

v0:
```python
import jax
import jax.numpy as jnp
from jax import lax
from jax.sharding import PartitionSpec as P


def expand(listed, slot_rows, slot_grads):
    count = listed.shape[0]
    block = min(128, count)
    blocks = listed.reshape(count // block, block)

    def one_block(block_rows):
        hits = (block_rows[:, None] == slot_rows[None, :]).astype(jnp.bfloat16)
        return jnp.dot(hits, slot_grads, preferred_element_type=jnp.float32)

    return lax.map(one_block, blocks).reshape(count, slot_grads.shape[1])


def adagrad(rows_now, accum_now, grads):
    accum_next = accum_now + jnp.mean(grads * grads, axis=1)
    rows_next = rows_now - 0.5 * grads / (jnp.sqrt(accum_next)[:, None] + 1e-08)
    return (rows_next, accum_next)


def body(table, accum, pooled_grad, row_ids, bag_ids, touched):
    shards = lax.axis_size("shard")
    rows_dev = table.shape[0]
    width = table.shape[1]
    samples = pooled_grad.shape[2]
    grads = pooled_grad.reshape(samples, width)
    ids = row_ids.reshape(-1)
    bags = bag_ids.reshape(-1)
    looks = ids.shape[0]
    slots_each = looks // 8
    listed = touched.reshape(-1)
    owner = ids // rows_dev
    onehot_owner = (owner[:, None] == jnp.arange(shards, dtype=jnp.int32)[None, :]).astype(
        jnp.int32
    )
    ranks = jnp.sum((jnp.cumsum(onehot_owner, axis=0) - 1) * onehot_owner, axis=1)
    slot = owner * slots_each + ranks
    lookup_rows = jnp.take(grads, bags, axis=0)
    send_grads = jnp.zeros((shards * slots_each, width), jnp.bfloat16).at[slot].set(lookup_rows)
    send_rows = jnp.full((shards * slots_each,), -1, jnp.int32).at[slot].set(ids % rows_dev)
    send_grads = send_grads.reshape(shards, slots_each, width)
    send_rows = send_rows.reshape(shards, slots_each)
    got_grads, got_rows = (
        lax.all_to_all(send_grads, "shard", split_axis=0, concat_axis=0, tiled=True),
        lax.all_to_all(send_rows, "shard", split_axis=0, concat_axis=0, tiled=True),
    )
    grad_rows = expand(listed, got_rows.reshape(-1), got_grads.reshape(-1, width))
    summed = lax.psum(grad_rows, "grp")
    rows_next, accum_next = adagrad(
        jnp.take(table, listed, axis=0), jnp.take(accum, listed), summed
    )
    new_table = table.at[listed].set(rows_next)
    new_accum = accum.at[listed].set(accum_next)
    return (new_table, new_accum)


def solution(mesh):
    return jax.shard_map(
        body,
        mesh=mesh,
        in_specs=(
            P("shard", None),
            P("shard"),
            P("grp", "shard", None, None),
            P("grp", "shard", None),
            P("grp", "shard", None),
            P("shard", None),
        ),
        out_specs=(P("shard", None), P("shard")),
        check_vma=False,
    )
```

profile of v0, /device:TPU:1, one launch (start us, length us, event | category | flops | bytes accessed | tf_op | source)
XLA Modules:
  0.0 426.8 jit_solution(2835037826303349041)
XLA Ops:
  7.2 0.8 copy.30
  7.9 4.5 %copy.29 = f32[4096,256]{1,0:T(8,128)} copy(f32[4096,256]{1,0:T(8,128)} %param.8) | data formatting | bytes 8388608
  12.5 9.2 %reduce-window.6 = s32[32,32,128]{2,1,0:T(8,128)S(1)} reduce-window(s32[32,32,128]{2,1,0:T(8,128)S(1)} %fusion.27, s32[]{:T(128)} %copy.31), window={size=1x1x128 pad=0_0x0_0x127_0}, to_apply=%region_0.1 | reduce-window | flops 16646144 | bytes 1048580 | tf_op jit(solution)/shard_map/reduce-window
  21.7 0.8 slice_reduce_fusion
  23.0 0.3 fusion.22
  23.4 16.1 %scatter_custom_fusion = s32[16384]{0:T(1024)} fusion(s32[4096]{0:T(1024)S(1)} %bitcast.80, s32[4096]{0:T(1024)S(1)} %get-tuple-element.43, s32[]{:T(128)} %constant.92.clone.1), kind=kCustom, calls=%fused_computation.46 | custom fusion | bytes 65540 | tf_op jit(solution)/shard_map/scatter | solution.py:44
  39.5 11.9 %all-to-all-start = ((s32[32,1,512]{2,1,0:T(1,128)}), s32[32,1,512]{2,1,0:T(1,128)S(1)}, u32[]{:S(2)}, u32[]{:S(2)}) async-start(s32[32,1,512]{2,1,0:T(1,128)} %bitcast.12), calls=%async_computation | async-start | bytes 131072 | tf_op jit(solution)/shard_map/all_to_all | solution.py:49
  51.4 37.7 %scatter_custom_fusion.1 = bf16[16384,256]{1,0:T(8,128)(2,1)} fusion(s32[4096]{0:T(1024)S(1)} %bitcast.81, bf16[]{:T(256)} %constant.97.clone.1, pred[4096]{0:T(1024)(128)(4,1)S(1)} %compare_and_fusion, bf16[]{:T(256)} %constant.99.clone.1, bf16[512,256]{1,0:T(8,128)(2,1)S(1)} %bitcast.64, s32[4096]{0:T(1024)S(1)} %broadcast_clamp_fusion), kind=kCustom, calls=%fused_computation.15 | custom fusion | flops 1048576 | bytes 8671236 | tf_op jit(solution)/shard_map/scatter | solution.py:43
  89.2 9.7 %all-to-all-start.1 = ((bf16[32,512,256]{2,1,0:T(8,128)(2,1)}), bf16[32,512,256]{2,1,0:T(8,128)(2,1)}, u32[]{:S(2)}, u32[]{:S(2)}) async-start(bf16[32,512,256]{2,1,0:T(8,128)(2,1)} %bitcast.65), calls=%async_computation.1 | async-start | bytes 16777216 | tf_op jit(solution)/shard_map/all_to_all | solution.py:48
  98.9 191.0 %all-to-all-done.1 = bf16[32,512,256]{2,1,0:T(8,128)(2,1)} async-done(((bf16[32,512,256]{2,1,0:T(8,128)(2,1)}), bf16[32,512,256]{2,1,0:T(8,128)(2,1)}, u32[]{:S(2)}, u32[]{:S(2)}) %all-to-all-start.1) | async-done | bytes 8388640 | tf_op jit(solution)/shard_map/all_to_all | solution.py:48
  289.9 42.9 %while.10 = (s32[]{:T(128)}, f32[8,128,256]{2,1,0:T(8,128)}, s32[8,128]{1,0:T(8,128)S(1)}, s32[32,512]{1,0:T(8,128)S(1)}, bf16[16384,256]{1,0:T(8,128)(2,1)}, /*index=5*/s32[]{:T(128)}) while((s32[]{:T(128)}, f32[8,128,256]{2,1,0:T(8,128)}, s32[8,128]{1,0:T(8,128)S(1)}, s32[32,512]{1,0:T(8,128)S(1)}, bf16[16384,256]{1,0:T(8,128)(2,1)}, ...), condition=%wide.region_6.7_spmd, body=%wide.region_5.6_spmd.sunk | while | flops 1075838976 | bytes 8718409 | solution.py:16
  289.9 5.3 %fusion.44 = f32[8,128,256]{2,1,0:T(8,128)} fusion(f32[8,128,256]{2,1,0:T(8,128)} %get-tuple-element.83, s32[]{:T(128)} %get-tuple-element.82, bf16[16384,256]{1,0:T(8,128)(2,1)} %get-tuple-element.92, s32[16384]{0:T(1024)S(1)} %bitcast.69, s32[128]{0:T(128)S(1)} %fusion.43), kind=kOutput, calls=%fused_computation.12.clone.1 | convolution fusion | flops 1075838976 | bytes 8586240 | tf_op jit(solution)/shard_map/while/body/eval_jaxpr/dot_general | solution.py:14
  295.2 5.3 %fusion.44 = f32[8,128,256]{2,1,0:T(8,128)} fusion(f32[8,128,256]{2,1,0:T(8,128)} %get-tuple-element.83, s32[]{:T(128)} %get-tuple-element.82, bf16[16384,256]{1,0:T(8,128)(2,1)} %get-tuple-element.92, s32[16384]{0:T(1024)S(1)} %bitcast.69, s32[128]{0:T(128)S(1)} %fusion.43), kind=kOutput, calls=%fused_computation.12.clone.1 | convolution fusion | flops 1075838976 | bytes 8586240 | tf_op jit(solution)/shard_map/while/body/eval_jaxpr/dot_general | solution.py:14
  300.6 5.4 %fusion.44 = f32[8,128,256]{2,1,0:T(8,128)} fusion(f32[8,128,256]{2,1,0:T(8,128)} %get-tuple-element.83, s32[]{:T(128)} %get-tuple-element.82, bf16[16384,256]{1,0:T(8,128)(2,1)} %get-tuple-element.92, s32[16384]{0:T(1024)S(1)} %bitcast.69, s32[128]{0:T(128)S(1)} %fusion.43), kind=kOutput, calls=%fused_computation.12.clone.1 | convolution fusion | flops 1075838976 | bytes 8586240 | tf_op jit(solution)/shard_map/while/body/eval_jaxpr/dot_general | solution.py:14
  306.0 5.3 %fusion.44 = f32[8,128,256]{2,1,0:T(8,128)} fusion(f32[8,128,256]{2,1,0:T(8,128)} %get-tuple-element.83, s32[]{:T(128)} %get-tuple-element.82, bf16[16384,256]{1,0:T(8,128)(2,1)} %get-tuple-element.92, s32[16384]{0:T(1024)S(1)} %bitcast.69, s32[128]{0:T(128)S(1)} %fusion.43), kind=kOutput, calls=%fused_computation.12.clone.1 | convolution fusion | flops 1075838976 | bytes 8586240 | tf_op jit(solution)/shard_map/while/body/eval_jaxpr/dot_general | solution.py:14
  311.3 5.3 %fusion.44 = f32[8,128,256]{2,1,0:T(8,128)} fusion(f32[8,128,256]{2,1,0:T(8,128)} %get-tuple-element.83, s32[]{:T(128)} %get-tuple-element.82, bf16[16384,256]{1,0:T(8,128)(2,1)} %get-tuple-element.92, s32[16384]{0:T(1024)S(1)} %bitcast.69, s32[128]{0:T(128)S(1)} %fusion.43), kind=kOutput, calls=%fused_computation.12.clone.1 | convolution fusion | flops 1075838976 | bytes 8586240 | tf_op jit(solution)/shard_map/while/body/eval_jaxpr/dot_general | solution.py:14
  316.7 5.3 %fusion.44 = f32[8,128,256]{2,1,0:T(8,128)} fusion(f32[8,128,256]{2,1,0:T(8,128)} %get-tuple-element.83, s32[]{:T(128)} %get-tuple-element.82, bf16[16384,256]{1,0:T(8,128)(2,1)} %get-tuple-element.92, s32[16384]{0:T(1024)S(1)} %bitcast.69, s32[128]{0:T(128)S(1)} %fusion.43), kind=kOutput, calls=%fused_computation.12.clone.1 | convolution fusion | flops 1075838976 | bytes 8586240 | tf_op jit(solution)/shard_map/while/body/eval_jaxpr/dot_general | solution.py:14
  322.1 5.3 %fusion.44 = f32[8,128,256]{2,1,0:T(8,128)} fusion(f32[8,128,256]{2,1,0:T(8,128)} %get-tuple-element.83, s32[]{:T(128)} %get-tuple-element.82, bf16[16384,256]{1,0:T(8,128)(2,1)} %get-tuple-element.92, s32[16384]{0:T(1024)S(1)} %bitcast.69, s32[128]{0:T(128)S(1)} %fusion.43), kind=kOutput, calls=%fused_computation.12.clone.1 | convolution fusion | flops 1075838976 | bytes 8586240 | tf_op jit(solution)/shard_map/while/body/eval_jaxpr/dot_general | solution.py:14
  327.4 5.3 %fusion.44 = f32[8,128,256]{2,1,0:T(8,128)} fusion(f32[8,128,256]{2,1,0:T(8,128)} %get-tuple-element.83, s32[]{:T(128)} %get-tuple-element.82, bf16[16384,256]{1,0:T(8,128)(2,1)} %get-tuple-element.92, s32[16384]{0:T(1024)S(1)} %bitcast.69, s32[128]{0:T(128)S(1)} %fusion.43), kind=kOutput, calls=%fused_computation.12.clone.1 | convolution fusion | flops 1075838976 | bytes 8586240 | tf_op jit(solution)/shard_map/while/body/eval_jaxpr/dot_general | solution.py:14
  332.8 6.2 %gather_fusion = f32[1024]{0:T(1024)S(1)} fusion(f32[4096]{0:T(1024)S(1)} %copy.30, s32[1024]{0:T(1024)S(1)} %broadcast_clamp_fusion.1), kind=kCustom, calls=%fused_computation.2 | custom fusion | bytes 12288 | tf_op jit(solution)/shard_map/jit(_take)/gather | solution.py:54
  339.0 59.2 %all-reduce.2.cloned.1.call-done = f32[1024,256]{1,0:T(8,128)} async-done(((f32[1024,256]{1,0:T(8,128)}), f32[1024,256]{1,0:T(8,128)}) %all-reduce.2.cloned.1.call-update) | async-done | bytes 1048592 | tf_op jit(solution)/shard_map/psum | solution.py:52
  398.2 1.4 multiply_reduce_fusion
  399.7 4.3 %scatter_fusion = f32[4096]{0:T(1024)S(1)} fusion(f32[4096]{0:T(1024)S(1)} %copy.30, s32[1024]{0:T(1024)S(1)} %bitcast.78, f32[1024]{0:T(1024)S(1)} %get-tuple-element.41), kind=kCustom, calls=%fused_computation.6 | custom fusion | bytes 16384 | tf_op jit(solution)/shard_map/scatter | solution.py:57
  404.1 15.9 %scatter_custom_fusion.2 = f32[4096,256]{1,0:T(8,128)} fusion(f32[4096,256]{1,0:T(8,128)} %copy.29, s32[1024]{0:T(1024)S(1)} %bitcast.79, f32[1024,256]{1,0:T(8,128)S(1)} %copy-done.2, f32[1024]{0:T(1024)S(1)} %get-tuple-element.40, f32[]{:T(128)} %constant.100.clone.1, f32[]{:T(128)} %constant.90.clone.1, pred[1024]{0:T(1024)(128)(4,1)S(1)} %get-tuple-element.42, ...), kind=kCustom, calls=%fused_computation.19 | custom fusion | flops 1048576 | bytes 9446408 | tf_op jit(solution)/shard_map/scatter | solution.py:56
  (45 shorter events, 0.9 us)
Async XLA Ops:
  7.2 44.3 %copy-start = (bf16[1,1,512,256]{3,2,1,0:T(8,128)(2,1)S(1)}, bf16[1,1,512,256]{3,2,1,0:T(8,128)(2,1)}, u32[]{:S(2)}) copy-start(bf16[1,1,512,256]{3,2,1,0:T(8,128)(2,1)} %param.10) | copy-start | bytes 786436
  7.9 4.5 %copy-start.3 = (s32[1,1,4096]{2,1,0:T(1,128)S(1)}, s32[1,1,4096]{2,1,0:T(1,128)}, u32[]{:S(2)}) copy-start(s32[1,1,4096]{2,1,0:T(1,128)} %param.11) | copy-start | bytes 49156
  7.9 43.4 %copy-start.4 = (s32[1,1,4096]{2,1,0:T(1,128)S(1)}, s32[1,1,4096]{2,1,0:T(1,128)}, u32[]{:S(2)}) copy-start(s32[1,1,4096]{2,1,0:T(1,128)} %param.12) | copy-start | bytes 49156
  39.5 49.6 %all-to-all-start = ((s32[32,1,512]{2,1,0:T(1,128)}), s32[32,1,512]{2,1,0:T(1,128)S(1)}, u32[]{:S(2)}, u32[]{:S(2)}) async-start(s32[32,1,512]{2,1,0:T(1,128)} %bitcast.12), calls=%async_computation | async-start | bytes 131072 | tf_op jit(solution)/shard_map/all_to_all | solution.py:49
  89.1 200.7 %copy-start.5 = (s32[1,1024]{1,0:T(1,128)S(1)}, s32[1,1024]{1,0:T(1,128)}, u32[]{:S(2)}) copy-start(s32[1,1024]{1,0:T(1,128)} %param.13) | copy-start | bytes 12292
  89.2 200.7 %all-to-all-start.1 = ((bf16[32,512,256]{2,1,0:T(8,128)(2,1)}), bf16[32,512,256]{2,1,0:T(8,128)(2,1)}, u32[]{:S(2)}, u32[]{:S(2)}) async-start(bf16[32,512,256]{2,1,0:T(8,128)(2,1)} %bitcast.65), calls=%async_computation.1 | async-start | bytes 16777216 | tf_op jit(solution)/shard_map/all_to_all | solution.py:48
  98.8 299.4 %all-reduce.2.cloned.1.call-start = ((), (), s32[]{:S(2)}) async-start(), calls=%async_computation.2 | async-start | bytes 2097152 | tf_op jit(solution)/shard_map/psum | solution.py:52
  399.7 4.4 %copy-start.2 = (f32[1024,256]{1,0:T(8,128)S(1)}, f32[1024,256]{1,0:T(8,128)}, u32[]{:S(2)}) copy-start(f32[1024,256]{1,0:T(8,128)} %all-reduce.2.cloned.1.call-done) | copy-start | bytes 3145732
  404.1 15.9 %copy-start.1 = (f32[4096]{0:T(1024)}, f32[4096]{0:T(1024)S(1)}, u32[]{:S(2)}) copy-start(f32[4096]{0:T(1024)S(1)} %scatter_fusion) | copy-start | bytes 49156
Sparse Core Ops, SparseCore 0:
  332.9 65.2 all-reduce.1
where the time goes:
time: 429 us; the launch traced here: 427 us
  waiting for transfers between devices  250 us (58%)
  other arithmetic  65.2 us (15%)
  matrix products  42.7 us (10%)
  local copies, waits for them, and re-layouts  32.9 us (8%)
  starting transfers between devices  21.6 us (5%)
  between operations  14.2 us (3%)
    all_to_all x1, waiting for transfers between devices, body(): lax.all_to_all(send_grads, 'shard', split_axis=0, concat_axis=0, tiled=True)  191 us
    psum x1, waiting for transfers between devices, body(): summed = lax.psum(grad_rows, 'grp')  59.2 us
    dot_general x8, matrix products, one_block(): return jnp.dot(hits, slot_grads, preferred_element_type=jnp.float32)  42.7 us
    scatter x1, other arithmetic, body(): jnp.zeros((shards * slots_each, width), jnp.bfloat16).at[slot]  37.7 us
    scatter x1, local copies, waits for them, and re-layouts, body(): jnp.full((shards * slots_each,), -1, jnp.int32).at[slot].set(ids % rows_dev)  16.1 us
    scatter x1, other arithmetic, body(): new_table = table.at[listed].set(rows_next)  15.9 us
    all_to_all x1, starting transfers between devices, body(): lax.all_to_all(send_rows, 'shard', split_axis=0, concat_axis=0, tiled=True)  11.9 us
    all_to_all x1, starting transfers between devices, body(): lax.all_to_all(send_grads, 'shard', split_axis=0, concat_axis=0, tiled=True)  9.66 us
  transfers between devices with their start and end apart: 3, of which 2 were waited for; matrix products, arithmetic and copies ran while one was open for 10% of the time, Pallas kernels for 0%

commit v1 on v0

v1 whole, which is shorter than its diff:
```python
import jax
import jax.numpy as jnp
from jax import lax
from jax.experimental import pallas as pl
from jax.experimental.pallas import tpu as pltpu
from jax.sharding import PartitionSpec as P

E = 256
ROWS_DEV = 4096
TOUCH = 1024
HALF = TOUCH // 2
QUART = TOUCH // 8
LOOK = 4096
B_DEV = 512
LANES = 128
BLOCKS = 64
KEY_ROWS = 72
NZ, NX, NY, NC = 8, 4, 4, 2
F32 = jnp.float32
BF16 = jnp.bfloat16
I32 = jnp.int32
NT = (((1,), (1,)), ((), ()))
TN = (((0,), (0,)), ((), ()))


def iota(shape, dim):
    return lax.broadcasted_iota(I32, shape, dim)


def one_hot(mask):
    return jnp.where(mask, 1.0, 0.0).astype(BF16)


def pack_kernel(ids_ref, bags_ref, g_ref, keys_ref, gt_ref, a_ref, b_ref, o_ref):
    groups = LOOK // LANES
    ids = ids_ref[...]
    owner = ids >> 12
    owners = iota((32, LANES), 0)
    running = jnp.zeros((32, LANES), F32)
    for i in range(groups):
        hit = jnp.where(owner[i:i + 1, :] == owners, 1.0, 0.0)
        o_ref[i * 32:(i + 1) * 32, 0:LANES] = hit.astype(BF16)
        o_ref[i * 32:(i + 1) * 32, LANES:2 * LANES] = running.astype(BF16)
        running = running + hit
    before = one_hot(iota((LANES, LANES), 0) < iota((LANES, LANES), 1))
    weights = jnp.concatenate([before, jnp.ones((LANES, LANES), BF16)], axis=0)
    prefix = jnp.dot(o_ref[...], weights, preferred_element_type=F32)
    totals = jnp.concatenate([running, jnp.zeros((LANES - 32, LANES), F32)], axis=0)
    count_row = lax.dot_general(jnp.ones((8, LANES), BF16), totals.astype(BF16), NT,
                                preferred_element_type=F32).astype(I32)
    blocks_row = (count_row + (LANES - 1)) >> 7
    start_row = jnp.dot(blocks_row.astype(F32).astype(BF16), before, preferred_element_type=F32)
    start_col = jnp.sum(
        jnp.where(iota((32, LANES), 1) < iota((32, LANES), 0),
                  jnp.broadcast_to(blocks_row[0:1, :].astype(F32), (32, LANES)), 0.0),
        axis=1, keepdims=True) * float(LANES)
    start_all = jnp.broadcast_to(start_col, (32, LANES))
    for i in range(groups):
        hit = owner[i:i + 1, :] == owners
        pos = jnp.sum(jnp.where(hit, prefix[i * 32:(i + 1) * 32, :] + start_all, 0.0),
                      axis=0, keepdims=True).astype(I32)
        key = (((ids[i:i + 1, :] & (ROWS_DEV - 1)) << 9) | bags_ref[i:i + 1, :]) + 1
        at_hi = (pos >> 7) == iota((BLOCKS, LANES), 0)
        for piece in range(3):
            part = ((key >> (8 * piece)) & 255).astype(F32)
            a_ref[piece * BLOCKS:(piece + 1) * BLOCKS, i * LANES:(i + 1) * LANES] = jnp.where(
                at_hi, part, 0.0).astype(BF16)
        b_ref[:, i * LANES:(i + 1) * LANES] = one_hot((pos & (LANES - 1)) == iota((LANES, LANES), 0))
    placed = lax.dot_general(a_ref[...], b_ref[...], NT, preferred_element_type=F32).astype(I32)
    keys = (placed[0:BLOCKS] + (placed[BLOCKS:2 * BLOCKS] << 8)
            + (placed[2 * BLOCKS:3 * BLOCKS] << 16)) - 1
    keys_ref[0:BLOCKS, :] = keys
    keys_ref[BLOCKS:KEY_ROWS, :] = jnp.where(iota((8, LANES), 0) == 0, start_row.astype(I32), blocks_row)
    eye = one_hot(iota((E, E), 0) == iota((E, E), 1))
    gt_ref[...] = lax.dot_general(eye, g_ref[...], NT, preferred_element_type=F32).astype(BF16)


def pack(ids, bags, grads):
    return pl.pallas_call(
        pack_kernel,
        out_shape=(jax.ShapeDtypeStruct((KEY_ROWS, LANES), I32),
                   jax.ShapeDtypeStruct((E, B_DEV), BF16)),
        scratch_shapes=[pltpu.VMEM((3 * BLOCKS, LOOK), BF16),
                        pltpu.VMEM((LANES, LOOK), BF16),
                        pltpu.VMEM((TOUCH, 2 * LANES), BF16)],
        name="pack",
    )(ids, bags, grads)


def owner_kernel(*refs):
    meta_ref, shard_ref, rows_ref = refs[0:3]
    gts = refs[3:3 + NZ]
    keys = refs[3 + NZ:3 + 2 * NZ]
    send_ref, keep_ref, x_ref, k_ref = refs[3 + 2 * NZ:]
    shard = shard_ref[0]
    filled = jnp.int32(0)
    for d in range(NZ):
        first = meta_ref[2 * d, shard]
        many = meta_ref[2 * d + 1, shard]

        def gather(j, _, d=d, first=first, filled=filled):
            row = keys[d][pl.ds(first + j, 1), :]
            bag = row & (B_DEV - 1)
            picks = one_hot(bag == iota((B_DEV, LANES), 0))
            slot = filled + j
            x_ref[slot] = jnp.dot(gts[d][...], picks, preferred_element_type=F32).astype(BF16)
            k_ref[pl.ds(slot, 1), :] = row >> 9
            return 0

        lax.fori_loop(0, many, gather, 0)
        filled = filled + many
    rounds = (filled + 3) >> 2

    def blank(j, _):
        x_ref[j] = jnp.zeros((E, LANES), BF16)
        k_ref[pl.ds(j, 1), :] = jnp.full((1, LANES), -1, I32)
        return 0

    lax.fori_loop(filled, rounds * 4, blank, 0)
    send_ref[...] = jnp.zeros((HALF, E), F32)
    keep_ref[...] = jnp.zeros((HALF, E), F32)

    def accumulate(r, _):
        xs = jnp.concatenate([x_ref[4 * r + j] for j in range(4)], axis=1)
        rows4 = [k_ref[pl.ds(4 * r + j, 1), :] for j in range(4)]
        for out_ref, base in ((send_ref, 0), (keep_ref, HALF)):
            mine = rows_ref[base:base + HALF, :]
            hits = jnp.concatenate([one_hot(mine == row) for row in rows4], axis=1)
            out_ref[...] += lax.dot_general(hits, xs, NT, preferred_element_type=F32)
        return 0

    lax.fori_loop(0, rounds, accumulate, 0)


def owner_sums(meta, shard, rows, gts, keys):
    smem = pl.BlockSpec(memory_space=pltpu.SMEM)
    vmem = pl.BlockSpec(memory_space=pltpu.VMEM)
    return pl.pallas_call(
        owner_kernel,
        out_shape=(jax.ShapeDtypeStruct((HALF, E), F32), jax.ShapeDtypeStruct((HALF, E), F32)),
        in_specs=[smem, smem, vmem] + [vmem] * (2 * NZ),
        scratch_shapes=[pltpu.VMEM((4 * NZ, E, LANES), BF16), pltpu.VMEM((4 * NZ, LANES), I32)],
        name="owner_sums",
    )(meta, shard, rows, *gts, *keys)


def listed_accum_kernel(rows_ref, accum_ref, out_ref):
    rows = rows_ref[...]
    hi = jnp.where((rows >> 7) == iota((TOUCH, LANES), 1), 1.0, 0.0)
    padded = jnp.concatenate([accum_ref[...], jnp.zeros((LANES - 32, LANES), F32)], axis=0)
    line = jnp.dot(hi, padded, precision=lax.Precision.HIGHEST, preferred_element_type=F32)
    mine = jnp.where((rows & (LANES - 1)) == iota((TOUCH, LANES), 1), line, 0.0)
    out_ref[...] = jnp.broadcast_to(jnp.sum(mine, axis=1, keepdims=True), (TOUCH, LANES))


def listed_accum(rows, accum):
    return pl.pallas_call(
        listed_accum_kernel,
        out_shape=jax.ShapeDtypeStruct((TOUCH, LANES), F32),
        name="listed_accum",
    )(rows, accum)


def update_kernel(*refs):
    list_ref, table_ref, accum_ref, listed_ref, rows_ref = refs[0:5]
    chunks = refs[5:13]
    table_out, accum_out, u_ref, lhs_ref, rhs_ref = refs[13:]
    lane = iota((QUART, LANES), 1)
    for n in range(8):
        at = slice(n * QUART, (n + 1) * QUART)
        g = chunks[n][...]
        mean = jnp.sum(g * g, axis=1, keepdims=True) * (1.0 / E)
        now = listed_ref[at, 0:1] + mean
        u_ref[at, :] = 0.5 * g / (jnp.sqrt(now) + 1e-08)
        rows = rows_ref[at, :]
        lhs_ref[at, :] = jnp.where((rows >> 7) == lane, mean, 0.0)
        rhs_ref[at, :] = jnp.where((rows & (LANES - 1)) == lane, 1.0, 0.0)
    added = lax.dot_general(lhs_ref[...], rhs_ref[...], TN, precision=lax.Precision.HIGHEST,
                            preferred_element_type=F32)
    accum_out[...] = accum_ref[...] + added[0:32, :]
    table_out[...] = table_ref[...]

    def step(i, _):
        for j in range(8):
            p = i * 8 + j
            row = list_ref[i >> 4, (i & 15) * 8 + j]
            table_out[pl.ds(row, 1), :] = table_out[pl.ds(row, 1), :] - u_ref[pl.ds(p, 1), :]
        return 0

    lax.fori_loop(0, TOUCH // 8, step, 0)


def update(order, table, accum, listed, rows, chunks):
    vmem = pl.BlockSpec(memory_space=pltpu.VMEM)
    return pl.pallas_call(
        update_kernel,
        out_shape=(jax.ShapeDtypeStruct((ROWS_DEV, E), F32), jax.ShapeDtypeStruct((32, LANES), F32)),
        in_specs=[pl.BlockSpec(memory_space=pltpu.SMEM)] + [vmem] * 12,
        scratch_shapes=[pltpu.VMEM((TOUCH, E), F32), pltpu.VMEM((TOUCH, LANES), F32),
                        pltpu.VMEM((TOUCH, LANES), F32)],
        name="update",
    )(order, table, accum, listed, rows, *chunks)


def z_pairs(k):
    return [(z * NX + x, ((z + k) % NZ) * NX + x) for z in range(NZ) for x in range(NX)]


def x_pairs(k):
    return [(z * NX + x, z * NX + (x + k) % NX) for z in range(NZ) for x in range(NX)]


def y_pairs(k):
    return [(y * NC + c, ((y + k) % NY) * NC + c) for y in range(NY) for c in range(NC)]


C_PAIRS = [(y * NC + c, y * NC + 1 - c) for y in range(NY) for c in range(NC)]


def body(table, accum, pooled_grad, row_ids, bag_ids, touched):
    grp = lax.axis_index("grp")
    me = lax.axis_index("shard")
    y, c = grp // NC, grp % NC
    z, x = me // NX, me % NX
    keys, gt = pack(row_ids.reshape(32, LANES), bag_ids.reshape(32, LANES),
                    pooled_grad.reshape(B_DEV, E))
    gts, all_keys = [gt], [keys]
    for step in (1, -1):
        g_now, k_now = gt, keys
        for _ in range(NZ // 2 if step == 1 else NZ // 2 - 1):
            g_now = lax.ppermute(g_now, "shard", z_pairs(step))
            k_now = lax.ppermute(k_now, "shard", z_pairs(step))
            gts.append(g_now)
            all_keys.append(k_now)
    meta = jnp.concatenate([k[BLOCKS:BLOCKS + 2] for k in all_keys], axis=0)

    def ordered(listed):
        halves = listed.reshape(NC, NY, QUART)
        halves = jnp.where(c == 0, halves[::-1], halves)
        doubled = jnp.concatenate([halves, halves], axis=1)
        return lax.dynamic_slice(doubled, (0, y, 0), (NC, NY, QUART)).reshape(TOUCH)

    own_list = touched.reshape(TOUCH)
    lists = [ordered(own_list)]
    for k in range(1, NX):
        lists.append(ordered(lax.ppermute(own_list, "shard", x_pairs(-k))))
    rows = [jnp.broadcast_to(t[:, None], (TOUCH, LANES)) for t in lists]
    listed = listed_accum(rows[0], accum.reshape(32, LANES))

    arrived = []
    own = None
    for k in (2, 1, 3, 0):
        shard = (z * NX + (x + k) % NX).reshape(1)
        send, keep = owner_sums(meta, shard, rows[k], gts, all_keys)
        both = keep + lax.ppermute(send, "grp", C_PAIRS)
        if k:
            arrived.append(lax.ppermute(both, "shard", x_pairs(k)))
        else:
            own = both
    total = own + arrived[0] + arrived[1] + arrived[2]
    part = total[0:QUART]
    for j in range(1, NY):
        part = part + lax.ppermute(total[j * QUART:(j + 1) * QUART], "grp", y_pairs(j))
    mine = [part] + [lax.ppermute(part, "grp", y_pairs(-j)) for j in range(1, NY)]
    other = [lax.ppermute(m, "grp", C_PAIRS) for m in mine]
    new_table, new_accum = update(lists[0].reshape(8, LANES), table, accum.reshape(32, LANES),
                                  listed, rows[0], other + mine)
    return (new_table, new_accum.reshape(ROWS_DEV))


def solution(mesh):
    return jax.shard_map(
        body,
        mesh=mesh,
        in_specs=(
            P("shard", None),
            P("shard"),
            P("grp", "shard", None, None),
            P("grp", "shard", None),
            P("grp", "shard", None),
            P("shard", None),
        ),
        out_specs=(P("shard", None), P("shard")),
        check_vma=False,
    )
```

time: 429 us -> 150 us (0.35)
  waiting for transfers between devices: 250 us -> 46.2 us
  other arithmetic: 65.2 us -> 0.52 us
  matrix products: 42.7 us -> 0 us
  Pallas kernels: 0 us -> 39.7 us
  starting transfers between devices: 21.6 us -> 56 us
  local copies, waits for them, and re-layouts: 32.9 us -> 6.72 us
  between operations: 14.2 us -> 1.01 us
    all_to_all x2 -> x0, waiting for transfers between devices: 191 us -> none  [the longest x1 191 us: body(): lax.all_to_all(send_grads, 'shard', split_axis=0, concat_axis=0, tiled=True)]
    psum x1 -> x0, waiting for transfers between devices: 59.2 us -> none  [body(): summed = lax.psum(grad_rows, 'grp')]
    ppermute x0 -> x34, starting transfers between devices: none -> 56 us  [the longest x3 11.6 us: body(): lax.ppermute(total[j * QUART:(j + 1) * QUART], 'grp', y_pairs(j))]
    scatter x2 -> x0, other arithmetic: 53.6 us -> none  [the longest x1 37.7 us: body(): jnp.zeros((shards * slots_each, width), jnp.bfloat16).at[slot]]
    ppermute x0 -> x34, waiting for transfers between devices: none -> 46.2 us  [the longest x3 22.4 us: body(): arrived.append(lax.ppermute(both, 'shard', x_pairs(k)))]
    dot_general x8 -> x0, matrix products: 42.7 us -> none  [one_block(): return jnp.dot(hits, slot_grads, preferred_element_type=jnp.float32)]
    pallas_call x0 -> x7, Pallas kernels: none -> 39.7 us  [the longest x4 22.1 us: owner_sums(): pl.pallas_call(owner_kernel, out_shape=(jax.ShapeDtypeStruct((HALF, E), F...]
    all_to_all x2 -> x0, starting transfers between devices: 21.5 us -> none  [the longest x1 11.9 us: body(): lax.all_to_all(send_rows, 'shard', split_axis=0, concat_axis=0, tiled=True)]
  transfers between devices with their start and end apart: 3 -> 34, of which waited for: 2 -> 14; matrix products, arithmetic and copies ran while one was open for 10% -> 3% of each run, Pallas kernels for 0% -> 13%
where the time goes in v1:
time: 150 us
  starting transfers between devices  56 us (37%)
  waiting for transfers between devices  46.2 us (31%)
  Pallas kernels  39.7 us (26%)
  local copies, waits for them, and re-layouts  6.72 us (4%)
    ppermute x3, waiting for transfers between devices, body(): arrived.append(lax.ppermute(both, 'shard', x_pairs(k)))  22.4 us
    pallas_call x4, Pallas kernels, owner_sums(): pl.pallas_call(owner_kernel, out_shape=(jax.ShapeDtypeStruct((HALF, E), F...  22.1 us
    pallas_call x1, Pallas kernels, update(): pl.pallas_call(update_kernel, out_shape=(jax.ShapeDtypeStruct((ROWS_DEV,...  11.9 us
    ppermute x3, starting transfers between devices, body(): lax.ppermute(total[j * QUART:(j + 1) * QUART], 'grp', y_pairs(j))  11.6 us
    ppermute x7, starting transfers between devices, body(): g_now = lax.ppermute(g_now, 'shard', z_pairs(step))  10.5 us
    ppermute x4, starting transfers between devices, body(): other = [lax.ppermute(m, 'grp', C_PAIRS) for m in mine]  10.1 us
    ppermute x7, starting transfers between devices, body(): k_now = lax.ppermute(k_now, 'shard', z_pairs(step))  8.14 us
    ppermute x7, waiting for transfers between devices, body(): g_now = lax.ppermute(g_now, 'shard', z_pairs(step))  8.12 us
  transfers between devices with their start and end apart: 34, of which 14 were waited for; matrix products, arithmetic and copies ran while one was open for 3% of the time, Pallas kernels for 13%

profile of v1, /device:TPU:1, one launch (start us, length us, event | category | flops | bytes accessed | tf_op | source)
XLA Modules:
  0.0 150.1 jit_solution(13689012738839658948)
XLA Ops:
  0.6 3.2 %pack.1 = (s32[72,128]{1,0:T(8,128)}, bf16[256,512]{1,0:T(8,128)(2,1)}) custom-call(s32[32,128]{1,0:T(8,128)} %bitcast.27, s32[32,128]{1,0:T(8,128)} %bitcast.28, bf16[512,256]{1,0:T(8,128)(2,1)} %bitcast.19), custom_call_target="tpu_custom_call" | custom-call | tf_op jit(solution)/shard_map/pack/pallas_call | solution.py:79
  3.9 2.5 %collective-permute-start.7 = (bf16[256,512]{1,0:T(8,128)(2,1)}, bf16[256,512]{1,0:T(8,128)(2,1)S(1)}, u32[]{:S(2)}, u32[]{:S(2)}) collective-permute-start(bf16[256,512]{1,0:T(8,128)(2,1)} %get-tuple-element.15.refs_3_), channel_id=1, source_target_pairs={{0,4},{1,5},{2,6},{3,7},{4,8},{5,9},{6,10},{7,11},{8,12},{9,13},{1... | collective-permute-start | bytes 786440 | tf_op jit(solution)/shard_map/ppermute | solution.py:231
  6.3 3.9 %collective-permute-start.11 = (bf16[256,512]{1,0:T(8,128)(2,1)}, bf16[256,512]{1,0:T(8,128)(2,1)S(1)}, u32[]{:S(2)}, u32[]{:S(2)}) collective-permute-start(bf16[256,512]{1,0:T(8,128)(2,1)} %get-tuple-element.15.refs_3_), channel_id=1, source_target_pairs={{0,28},{1,29},{2,30},{3,31},{4,0},{5,1},{6,2},{7,3},{8,4},{9,5},{1... | collective-permute-start | bytes 786440 | tf_op jit(solution)/shard_map/ppermute | solution.py:231
  10.3 6.2 %collective-permute-done.7.refs_4_ = bf16[256,512]{1,0:T(8,128)(2,1)S(1)} collective-permute-done((bf16[256,512]{1,0:T(8,128)(2,1)}, bf16[256,512]{1,0:T(8,128)(2,1)S(1)}, u32[]{:S(2)}, u32[]{:S(2)}) %collective-permute-start.7) | collective-permute-done | bytes 262176 | tf_op jit(solution)/shard_map/ppermute | solution.py:231
  16.5 2.7 %collective-permute-start.4 = (s32[72,128]{1,0:T(8,128)}, s32[72,128]{1,0:T(8,128)S(1)}, u32[]{:S(2)}, u32[]{:S(2)}) collective-permute-start(s32[72,128]{1,0:T(8,128)} %get-tuple-element.14.refs_11_), channel_id=1, source_target_pairs={{0,28},{1,29},{2,30},{3,31},{4,0},{5,1},{6,2},{7,3},{8,4},{9,5},{1... | collective-permute-start | bytes 110600 | tf_op jit(solution)/shard_map/ppermute | solution.py:232
  21.1 2.3 %collective-permute-done.21 = s32[1024]{0:T(1024)S(1)} collective-permute-done((s32[1024]{0:T(1024)}, s32[1024]{0:T(1024)S(1)}, u32[]{:S(2)}, u32[]{:S(2)}) %collective-permute-start.21) | collective-permute-done | bytes 4128 | tf_op jit(solution)/shard_map/ppermute | solution.py:246
  29.9 2.7 %collective-permute-start.13 = (bf16[256,512]{1,0:T(8,128)(2,1)S(1)}, bf16[256,512]{1,0:T(8,128)(2,1)S(1)}, u32[]{:S(2)}, u32[]{:S(2)}) collective-permute-start(bf16[256,512]{1,0:T(8,128)(2,1)S(1)} %collective-permute-done.12.refs_9_), channel_id=1, source_target_pairs={{0,28},{1,29},{2,30},{3,31},{4,0},{5,1},{6,2},{7,3},{8,4},{9,5},{1... | collective-permute-start | bytes 786440 | tf_op jit(solution)/shard_map/ppermute | solution.py:231
  32.6 2.7 %collective-permute-start.5 = (s32[72,128]{1,0:T(8,128)S(1)}, s32[72,128]{1,0:T(8,128)S(1)}, u32[]{:S(2)}, u32[]{:S(2)}) collective-permute-start(s32[72,128]{1,0:T(8,128)S(1)} %collective-permute-done.4.refs_16_), channel_id=1, source_target_pairs={{0,28},{1,29},{2,30},{3,31},{4,0},{5,1},{6,2},{7,3},{8,4},{9,5},{1... | collective-permute-start | bytes 110600 | tf_op jit(solution)/shard_map/ppermute | solution.py:232
  36.8 2.6 %collective-permute-start.6 = (s32[72,128]{1,0:T(8,128)S(1)}, s32[72,128]{1,0:T(8,128)S(1)}, u32[]{:S(2)}, u32[]{:S(2)}) collective-permute-start(s32[72,128]{1,0:T(8,128)S(1)} %collective-permute-done.5.refs_17_), channel_id=1, source_target_pairs={{0,28},{1,29},{2,30},{3,31},{4,0},{5,1},{6,2},{7,3},{8,4},{9,5},{1... | collective-permute-start | bytes 110600 | tf_op jit(solution)/shard_map/ppermute | solution.py:232
  40.7 4.1 %collective-permute-done.3.refs_15_ = s32[72,128]{1,0:T(8,128)S(1)} collective-permute-done((s32[72,128]{1,0:T(8,128)S(1)}, s32[72,128]{1,0:T(8,128)S(1)}, u32[]{:S(2)}, u32[]{:S(2)}) %collective-permute-start.3) | collective-permute-done | bytes 36896 | tf_op jit(solution)/shard_map/ppermute | solution.py:232
  47.1 5.5 %owner_sums.7 = (f32[512,256]{1,0:T(8,128)}, f32[512,256]{1,0:T(8,128)}) custom-call(s32[16,128]{1,0:T(8,128)} %concatenate.16.refs_0_, s32[1]{0:T(128)} %bitcast.15.refs_1_, s32[1024,128]{1,0:T(8,128)} %broadcast_in_dim.35.refs_2_, bf16[256,512]{1,0:T(8,128)(2,1)} %get-tuple-element.15.refs_3_, bf16[256,512]{1,0:T(8,128)(2,1)} %copy-done, ...), custom_call_target="tpu_custom_call" | custom-call | tf_op jit(solution)/shard_map/owner_sums/pallas_call | solution.py:138
  52.7 6.5 %collective-permute-start.22 = (f32[512,256]{1,0:T(8,128)}, f32[512,256]{1,0:T(8,128)S(1)}, u32[]{:S(2)}, u32[]{:S(2)}) collective-permute-start(f32[512,256]{1,0:T(8,128)} %get-tuple-element.23), channel_id=1, source_target_pairs={{0,32},{32,0},{64,96},{96,64},{128,160},{160,128},{192,224},{224,1... | collective-permute-start | bytes 1572872 | tf_op jit(solution)/shard_map/ppermute | solution.py:255
  60.1 5.5 %owner_sums.6 = (f32[512,256]{1,0:T(8,128)}, f32[512,256]{1,0:T(8,128)}) custom-call(s32[16,128]{1,0:T(8,128)} %concatenate.16.refs_0_, s32[1]{0:T(128)} %bitcast.12.refs_1_, s32[1024,128]{1,0:T(8,128)} %broadcast_in_dim.33.refs_2_, bf16[256,512]{1,0:T(8,128)(2,1)} %get-tuple-element.15.refs_3_, bf16[256,512]{1,0:T(8,128)(2,1)} %copy-done, ...), custom_call_target="tpu_custom_call" | custom-call | tf_op jit(solution)/shard_map/owner_sums/pallas_call | solution.py:138
  66.8 5.5 %owner_sums.5 = (f32[512,256]{1,0:T(8,128)}, f32[512,256]{1,0:T(8,128)}) custom-call(s32[16,128]{1,0:T(8,128)} %concatenate.16.refs_0_, s32[1]{0:T(128)} %bitcast.8.refs_1_, s32[1024,128]{1,0:T(8,128)} %broadcast_in_dim.31.refs_2_, bf16[256,512]{1,0:T(8,128)(2,1)} %get-tuple-element.15.refs_3_, bf16[256,512]{1,0:T(8,128)(2,1)} %copy-done, ...), custom_call_target="tpu_custom_call" | custom-call | tf_op jit(solution)/shard_map/owner_sums/pallas_call | solution.py:138
  73.9 5.5 %owner_sums.4 = (f32[512,256]{1,0:T(8,128)}, f32[512,256]{1,0:T(8,128)}) custom-call(s32[16,128]{1,0:T(8,128)} %concatenate.16.refs_0_, s32[1]{0:T(128)} %bitcast.7.refs_1_, s32[1024,128]{1,0:T(8,128)} %broadcast_in_dim.29.rows_ref.refs_2_.refs_4_, bf16[256,512]{1,0:T(8,128)(2,1)} %get-tuple-element.15.refs_3_, bf16[256,512]{1,0:T(8,128)(2,1)} %copy-done, ...), custom_call_target="tpu_custom_call" | custom-call | tf_op jit(solution)/shard_map/owner_sums/pallas_call | solution.py:138
  82.6 10.2 %collective-permute-done.23 = f32[512,256]{1,0:T(8,128)S(1)} collective-permute-done((f32[512,256]{1,0:T(8,128)S(1)}, f32[512,256]{1,0:T(8,128)S(1)}, u32[]{:S(2)}, u32[]{:S(2)}) %collective-permute-start.23) | collective-permute-done | bytes 524320 | tf_op jit(solution)/shard_map/ppermute | solution.py:257
  94.7 10.3 %collective-permute-done.17 = f32[512,256]{1,0:T(8,128)S(1)} collective-permute-done((f32[512,256]{1,0:T(8,128)S(1)}, f32[512,256]{1,0:T(8,128)S(1)}, u32[]{:S(2)}, u32[]{:S(2)}) %collective-permute-start.17) | collective-permute-done | bytes 524320 | tf_op jit(solution)/shard_map/ppermute | solution.py:257
  105.3 10.9 %collective-permute-start.26 = (f32[128,256]{1,0:T(8,128)S(1)}, f32[128,256]{1,0:T(8,128)S(1)}, u32[]{:S(2)}, u32[]{:S(2)}) collective-permute-start(f32[128,256]{1,0:T(8,128)S(1)} %get-tuple-element.27), channel_id=1, source_target_pairs={{0,192},{32,224},{64,0},{96,32},{128,64},{160,96},{192,128},{224,1... | collective-permute-start | bytes 393224 | tf_op jit(solution)/shard_map/ppermute | solution.py:263
  116.8 2.2 %collective-permute-done.26 = f32[128,256]{1,0:T(8,128)S(1)} collective-permute-done((f32[128,256]{1,0:T(8,128)S(1)}, f32[128,256]{1,0:T(8,128)S(1)}, u32[]{:S(2)}, u32[]{:S(2)}) %collective-permute-start.26) | collective-permute-done | bytes 131104 | tf_op jit(solution)/shard_map/ppermute | solution.py:263
  119.0 2.5 %collective-permute-done.25 = f32[128,256]{1,0:T(8,128)S(1)} collective-permute-done((f32[128,256]{1,0:T(8,128)S(1)}, f32[128,256]{1,0:T(8,128)S(1)}, u32[]{:S(2)}, u32[]{:S(2)}) %collective-permute-start.25) | collective-permute-done | bytes 131104 | tf_op jit(solution)/shard_map/ppermute | solution.py:263
  124.8 3.8 %collective-permute-start.27 = (f32[128,256]{1,0:T(8,128)S(1)}, f32[128,256]{1,0:T(8,128)S(1)}, u32[]{:S(2)}, u32[]{:S(2)}) collective-permute-start(f32[128,256]{1,0:T(8,128)S(1)} %fusion.1.refs_9_), channel_id=1, source_target_pairs={{0,32},{32,0},{64,96},{96,64},{128,160},{160,128},{192,224},{224,1... | collective-permute-start | bytes 393224 | tf_op jit(solution)/shard_map/ppermute | solution.py:265
  128.6 2.8 %collective-permute-start.29 = (f32[128,256]{1,0:T(8,128)S(1)}, f32[128,256]{1,0:T(8,128)S(1)}, u32[]{:S(2)}, u32[]{:S(2)}) collective-permute-start(f32[128,256]{1,0:T(8,128)S(1)} %collective-permute-done.28.refs_10_), channel_id=1, source_target_pairs={{0,32},{32,0},{64,96},{96,64},{128,160},{160,128},{192,224},{224,1... | collective-permute-start | bytes 393224 | tf_op jit(solution)/shard_map/ppermute | solution.py:265
  134.9 2.5 %listed_accum.1.refs_3_ = f32[1024,128]{1,0:T(8,128)} custom-call(s32[1024,128]{1,0:T(8,128)} %broadcast_in_dim.29.rows_ref.refs_2_.refs_4_, f32[32,128]{1,0:T(8,128)} %bitcast.20), custom_call_target="tpu_custom_call" | custom-call | tf_op jit(solution)/shard_map/listed_accum/pallas_call | solution.py:157
  138.2 11.9 %update.1 = (f32[4096,256]{1,0:T(8,128)}, f32[32,128]{1,0:T(8,128)}) custom-call(s32[8,128]{1,0:T(8,128)} %bitcast.23, f32[4096,256]{1,0:T(8,128)} %refs_1_.1, f32[32,128]{1,0:T(8,128)} %bitcast.21, f32[1024,128]{1,0:T(8,128)} %listed_accum.1.refs_3_, s32[1024,128]{1,0:T(8,128)} %broadcast_in_dim.29.rows_ref.refs_2_.refs_4_, f32[128,256]{1,0:T(8,128)} %copy-done.22, ...), custom_call_target="tpu_custom_call" | custom-call | tf_op jit(solution)/shard_map/update/pallas_call | solution.py:195
  (133 shorter events, 30.5 us)
Async XLA Ops:
  3.9 12.6 %collective-permute-start.7 = (bf16[256,512]{1,0:T(8,128)(2,1)}, bf16[256,512]{1,0:T(8,128)(2,1)S(1)}, u32[]{:S(2)}, u32[]{:S(2)}) collective-permute-start(bf16[256,512]{1,0:T(8,128)(2,1)} %get-tuple-element.15.refs_3_), channel_id=1, source_target_pairs={{0,4},{1,5},{2,6},{3,7},{4,8},{5,9},{6,10},{7,11},{8,12},{9,13},{1... | collective-permute-start | bytes 786440 | tf_op jit(solution)/shard_map/ppermute | solution.py:231
  6.3 18.3 %collective-permute-start.11 = (bf16[256,512]{1,0:T(8,128)(2,1)}, bf16[256,512]{1,0:T(8,128)(2,1)S(1)}, u32[]{:S(2)}, u32[]{:S(2)}) collective-permute-start(bf16[256,512]{1,0:T(8,128)(2,1)} %get-tuple-element.15.refs_3_), channel_id=1, source_target_pairs={{0,28},{1,29},{2,30},{3,31},{4,0},{5,1},{6,2},{7,3},{8,4},{9,5},{1... | collective-permute-start | bytes 786440 | tf_op jit(solution)/shard_map/ppermute | solution.py:231
  16.5 9.6 %collective-permute-start.8 = (bf16[256,512]{1,0:T(8,128)(2,1)S(1)}, bf16[256,512]{1,0:T(8,128)(2,1)S(1)}, u32[]{:S(2)}, u32[]{:S(2)}) collective-permute-start(bf16[256,512]{1,0:T(8,128)(2,1)S(1)} %collective-permute-done.7.refs_4_), channel_id=1, source_target_pairs={{0,4},{1,5},{2,6},{3,7},{4,8},{5,9},{6,10},{7,11},{8,12},{9,13},{1... | collective-permute-start | bytes 786440 | tf_op jit(solution)/shard_map/ppermute | solution.py:231
  16.5 11.4 %collective-permute-start = (s32[72,128]{1,0:T(8,128)}, s32[72,128]{1,0:T(8,128)S(1)}, u32[]{:S(2)}, u32[]{:S(2)}) collective-permute-start(s32[72,128]{1,0:T(8,128)} %get-tuple-element.14.refs_11_), channel_id=1, source_target_pairs={{0,4},{1,5},{2,6},{3,7},{4,8},{5,9},{6,10},{7,11},{8,12},{9,13},{1... | collective-permute-start | bytes 110600 | tf_op jit(solution)/shard_map/ppermute | solution.py:232
  16.5 16.1 %collective-permute-start.4 = (s32[72,128]{1,0:T(8,128)}, s32[72,128]{1,0:T(8,128)S(1)}, u32[]{:S(2)}, u32[]{:S(2)}) collective-permute-start(s32[72,128]{1,0:T(8,128)} %get-tuple-element.14.refs_11_), channel_id=1, source_target_pairs={{0,28},{1,29},{2,30},{3,31},{4,0},{5,1},{6,2},{7,3},{8,4},{9,5},{1... | collective-permute-start | bytes 110600 | tf_op jit(solution)/shard_map/ppermute | solution.py:232
  26.1 6.4 %collective-permute-start.9 = (bf16[256,512]{1,0:T(8,128)(2,1)S(1)}, bf16[256,512]{1,0:T(8,128)(2,1)S(1)}, u32[]{:S(2)}, u32[]{:S(2)}) collective-permute-start(bf16[256,512]{1,0:T(8,128)(2,1)S(1)} %collective-permute-done.8.refs_5_), channel_id=1, source_target_pairs={{0,4},{1,5},{2,6},{3,7},{4,8},{5,9},{6,10},{7,11},{8,12},{9,13},{1... | collective-permute-start | bytes 786440 | tf_op jit(solution)/shard_map/ppermute | solution.py:231
  26.3 6.2 %collective-permute-start.15 = (s32[1024]{0:T(1024)}, s32[1024]{0:T(1024)S(1)}, u32[]{:S(2)}, u32[]{:S(2)}) collective-permute-start(s32[1024]{0:T(1024)} %bitcast.31), channel_id=1, source_target_pairs={{0,2},{1,3},{2,0},{3,1},{4,6},{5,7},{6,4},{7,5},{8,10},{9,11},{10,... | collective-permute-start | bytes 12296 | tf_op jit(solution)/shard_map/ppermute | solution.py:246
  27.9 7.4 %collective-permute-start.1 = (s32[72,128]{1,0:T(8,128)S(1)}, s32[72,128]{1,0:T(8,128)S(1)}, u32[]{:S(2)}, u32[]{:S(2)}) collective-permute-start(s32[72,128]{1,0:T(8,128)S(1)} %collective-permute-done.refs_12_), channel_id=1, source_target_pairs={{0,4},{1,5},{2,6},{3,7},{4,8},{5,9},{6,10},{7,11},{8,12},{9,13},{1... | collective-permute-start | bytes 110600 | tf_op jit(solution)/shard_map/ppermute | solution.py:232
  29.9 16.2 %collective-permute-start.13 = (bf16[256,512]{1,0:T(8,128)(2,1)S(1)}, bf16[256,512]{1,0:T(8,128)(2,1)S(1)}, u32[]{:S(2)}, u32[]{:S(2)}) collective-permute-start(bf16[256,512]{1,0:T(8,128)(2,1)S(1)} %collective-permute-done.12.refs_9_), channel_id=1, source_target_pairs={{0,28},{1,29},{2,30},{3,31},{4,0},{5,1},{6,2},{7,3},{8,4},{9,5},{1... | collective-permute-start | bytes 786440 | tf_op jit(solution)/shard_map/ppermute | solution.py:231
  32.5 13.5 %collective-permute-start.10 = (bf16[256,512]{1,0:T(8,128)(2,1)S(1)}, bf16[256,512]{1,0:T(8,128)(2,1)S(1)}, u32[]{:S(2)}, u32[]{:S(2)}) collective-permute-start(bf16[256,512]{1,0:T(8,128)(2,1)S(1)} %collective-permute-done.9.refs_6_), channel_id=1, source_target_pairs={{0,4},{1,5},{2,6},{3,7},{4,8},{5,9},{6,10},{7,11},{8,12},{9,13},{1... | collective-permute-start | bytes 786440 | tf_op jit(solution)/shard_map/ppermute | solution.py:231
  52.7 26.9 %collective-permute-start.22 = (f32[512,256]{1,0:T(8,128)}, f32[512,256]{1,0:T(8,128)S(1)}, u32[]{:S(2)}, u32[]{:S(2)}) collective-permute-start(f32[512,256]{1,0:T(8,128)} %get-tuple-element.23), channel_id=1, source_target_pairs={{0,32},{32,0},{64,96},{96,64},{128,160},{160,128},{192,224},{224,1... | collective-permute-start | bytes 1572872 | tf_op jit(solution)/shard_map/ppermute | solution.py:255
  65.7 14.4 %collective-permute-start.19 = (f32[512,256]{1,0:T(8,128)}, f32[512,256]{1,0:T(8,128)S(1)}, u32[]{:S(2)}, u32[]{:S(2)}) collective-permute-start(f32[512,256]{1,0:T(8,128)} %get-tuple-element.21), channel_id=1, source_target_pairs={{0,32},{32,0},{64,96},{96,64},{128,160},{160,128},{192,224},{224,1... | collective-permute-start | bytes 1572872 | tf_op jit(solution)/shard_map/ppermute | solution.py:255
  72.3 9.0 %collective-permute-start.16 = (f32[512,256]{1,0:T(8,128)}, f32[512,256]{1,0:T(8,128)S(1)}, u32[]{:S(2)}, u32[]{:S(2)}) collective-permute-start(f32[512,256]{1,0:T(8,128)} %get-tuple-element.19), channel_id=1, source_target_pairs={{0,32},{32,0},{64,96},{96,64},{128,160},{160,128},{192,224},{224,1... | collective-permute-start | bytes 1572872 | tf_op jit(solution)/shard_map/ppermute | solution.py:255
  79.6 13.1 %collective-permute-start.23 = (f32[512,256]{1,0:T(8,128)S(1)}, f32[512,256]{1,0:T(8,128)S(1)}, u32[]{:S(2)}, u32[]{:S(2)}) collective-permute-start(f32[512,256]{1,0:T(8,128)S(1)} %add.97), channel_id=1, source_target_pairs={{0,3},{1,0},{2,1},{3,2},{4,7},{5,4},{6,5},{7,6},{8,11},{9,8},{10,9... | collective-permute-start | bytes 1572872 | tf_op jit(solution)/shard_map/ppermute | solution.py:257
  80.2 14.5 %collective-permute-start.20 = (f32[512,256]{1,0:T(8,128)S(1)}, f32[512,256]{1,0:T(8,128)S(1)}, u32[]{:S(2)}, u32[]{:S(2)}) collective-permute-start(f32[512,256]{1,0:T(8,128)S(1)} %add.92), channel_id=1, source_target_pairs={{0,1},{1,2},{2,3},{3,0},{4,5},{5,6},{6,7},{7,4},{8,9},{9,10},{10,1... | collective-permute-start | bytes 1572872 | tf_op jit(solution)/shard_map/ppermute | solution.py:257
  81.4 23.6 %collective-permute-start.17 = (f32[512,256]{1,0:T(8,128)S(1)}, f32[512,256]{1,0:T(8,128)S(1)}, u32[]{:S(2)}, u32[]{:S(2)}) collective-permute-start(f32[512,256]{1,0:T(8,128)S(1)} %add.87), channel_id=1, source_target_pairs={{0,2},{1,3},{2,0},{3,1},{4,6},{5,7},{6,4},{7,5},{8,10},{9,11},{10,... | collective-permute-start | bytes 1572872 | tf_op jit(solution)/shard_map/ppermute | solution.py:257
  105.3 13.8 %collective-permute-start.26 = (f32[128,256]{1,0:T(8,128)S(1)}, f32[128,256]{1,0:T(8,128)S(1)}, u32[]{:S(2)}, u32[]{:S(2)}) collective-permute-start(f32[128,256]{1,0:T(8,128)S(1)} %get-tuple-element.27), channel_id=1, source_target_pairs={{0,192},{32,224},{64,0},{96,32},{128,64},{160,96},{192,128},{224,1... | collective-permute-start | bytes 393224 | tf_op jit(solution)/shard_map/ppermute | solution.py:263
  116.2 5.4 %collective-permute-start.25 = (f32[128,256]{1,0:T(8,128)S(1)}, f32[128,256]{1,0:T(8,128)S(1)}, u32[]{:S(2)}, u32[]{:S(2)}) collective-permute-start(f32[128,256]{1,0:T(8,128)S(1)} %get-tuple-element.28), channel_id=1, source_target_pairs={{0,128},{32,160},{64,192},{96,224},{128,0},{160,32},{192,64},{224,... | collective-permute-start | bytes 393224 | tf_op jit(solution)/shard_map/ppermute | solution.py:263
  116.6 6.6 %collective-permute-start.24 = (f32[128,256]{1,0:T(8,128)S(1)}, f32[128,256]{1,0:T(8,128)S(1)}, u32[]{:S(2)}, u32[]{:S(2)}) collective-permute-start(f32[128,256]{1,0:T(8,128)S(1)} %get-tuple-element.26), channel_id=1, source_target_pairs={{0,64},{32,96},{64,128},{96,160},{128,192},{160,224},{192,0},{224,... | collective-permute-start | bytes 393224 | tf_op jit(solution)/shard_map/ppermute | solution.py:263
  123.6 7.9 %collective-permute-start.30 = (f32[128,256]{1,0:T(8,128)S(1)}, f32[128,256]{1,0:T(8,128)S(1)}, u32[]{:S(2)}, u32[]{:S(2)}) collective-permute-start(f32[128,256]{1,0:T(8,128)S(1)} %fusion.1.refs_9_), channel_id=1, source_target_pairs={{0,128},{32,160},{64,192},{96,224},{128,0},{160,32},{192,64},{224,... | collective-permute-start | bytes 393224 | tf_op jit(solution)/shard_map/ppermute | solution.py:264
  124.1 9.5 %collective-permute-start.32 = (f32[128,256]{1,0:T(8,128)S(1)}, f32[128,256]{1,0:T(8,128)S(1)}, u32[]{:S(2)}, u32[]{:S(2)}) collective-permute-start(f32[128,256]{1,0:T(8,128)S(1)} %fusion.1.refs_9_), channel_id=1, source_target_pairs={{0,64},{32,96},{64,128},{96,160},{128,192},{160,224},{192,0},{224,... | collective-permute-start | bytes 393224 | tf_op jit(solution)/shard_map/ppermute | solution.py:264
  124.8 12.6 %collective-permute-start.27 = (f32[128,256]{1,0:T(8,128)S(1)}, f32[128,256]{1,0:T(8,128)S(1)}, u32[]{:S(2)}, u32[]{:S(2)}) collective-permute-start(f32[128,256]{1,0:T(8,128)S(1)} %fusion.1.refs_9_), channel_id=1, source_target_pairs={{0,32},{32,0},{64,96},{96,64},{128,160},{160,128},{192,224},{224,1... | collective-permute-start | bytes 393224 | tf_op jit(solution)/shard_map/ppermute | solution.py:265
  128.6 8.8 %collective-permute-start.29 = (f32[128,256]{1,0:T(8,128)S(1)}, f32[128,256]{1,0:T(8,128)S(1)}, u32[]{:S(2)}, u32[]{:S(2)}) collective-permute-start(f32[128,256]{1,0:T(8,128)S(1)} %collective-permute-done.28.refs_10_), channel_id=1, source_target_pairs={{0,32},{32,0},{64,96},{96,64},{128,160},{160,128},{192,224},{224,1... | collective-permute-start | bytes 393224 | tf_op jit(solution)/shard_map/ppermute | solution.py:265
  131.5 6.0 %collective-permute-start.31 = (f32[128,256]{1,0:T(8,128)S(1)}, f32[128,256]{1,0:T(8,128)S(1)}, u32[]{:S(2)}, u32[]{:S(2)}) collective-permute-start(f32[128,256]{1,0:T(8,128)S(1)} %collective-permute-done.30.refs_11_), channel_id=1, source_target_pairs={{0,32},{32,0},{64,96},{96,64},{128,160},{160,128},{192,224},{224,1... | collective-permute-start | bytes 393224 | tf_op jit(solution)/shard_map/ppermute | solution.py:265
  (38 other events, 372.9 us)

commit v2 on v1

v2 whole, which is shorter than its diff:
```python
import jax
import jax.numpy as jnp
from jax import lax
from jax.experimental import pallas as pl
from jax.experimental.pallas import tpu as pltpu
from jax.sharding import PartitionSpec as P


E = 256
ROWS_DEV = 4096
TOUCH = 1024
HALF = TOUCH // 2
QUART = TOUCH // 8
LOOK = 4096
B_DEV = 512
LANES = 128
BLOCKS = 128
KEY_ROWS = 24
NZ, NX, NY, NC = 8, 4, 4, 2
F32 = jnp.float32
BF16 = jnp.bfloat16
I32 = jnp.int32
NT = (((1,), (1,)), ((), ()))
TN = (((0,), (0,)), ((), ()))
FIRST_ROWS = pl.BlockSpec((1, TOUCH, LANES), lambda i: (0, 0, 0))


def iota(shape, dim):
    return lax.broadcasted_iota(I32, shape, dim)


def one_hot(mask):
    return jnp.where(mask, 1.0, 0.0).astype(BF16)


def pack_kernel(z_ref, ids_ref, bags_ref, keys_ref, a_ref, b_ref, o_ref):
    groups = LOOK // LANES
    ids = ids_ref[...]
    owner = ((ids >> 12) - NX * z_ref[0]) & (NZ * NX - 1)
    owners = iota((32, LANES), 0)
    running = jnp.zeros((32, LANES), F32)
    for i in range(groups):
        hit = jnp.where(owner[i:i + 1, :] == owners, 1.0, 0.0)
        o_ref[i * 32:(i + 1) * 32, 0:LANES] = hit.astype(BF16)
        o_ref[i * 32:(i + 1) * 32, LANES:2 * LANES] = running.astype(BF16)
        running = running + hit
    before = one_hot(iota((LANES, LANES), 0) < iota((LANES, LANES), 1))
    weights = jnp.concatenate([before, jnp.ones((LANES, LANES), BF16)], axis=0)
    prefix = jnp.dot(o_ref[...], weights, preferred_element_type=F32)
    counts = jnp.sum(running, axis=1, keepdims=True).astype(I32)
    blocks = jnp.broadcast_to((counts + (LANES - 1)) >> 7, (32, LANES))
    for i in range(groups):
        hit = owner[i:i + 1, :] == owners
        rank = jnp.sum(jnp.where(hit, prefix[i * 32:(i + 1) * 32, :], 0.0),
                       axis=0, keepdims=True).astype(I32)
        key = (((ids[i:i + 1, :] & (ROWS_DEV - 1)) << 9) | bags_ref[i:i + 1, :]) + 1
        at_hi = ((owner[i:i + 1, :] << 2) + (rank >> 7)) == iota((BLOCKS, LANES), 0)
        for piece in range(3):
            part = ((key >> (8 * piece)) & 255).astype(F32)
            a_ref[piece * BLOCKS:(piece + 1) * BLOCKS, i * LANES:(i + 1) * LANES] = jnp.where(
                at_hi, part, 0.0).astype(BF16)
        b_ref[:, i * LANES:(i + 1) * LANES] = one_hot((rank & (LANES - 1)) == iota((LANES, LANES), 0))
    placed = lax.dot_general(a_ref[...], b_ref[...], NT, preferred_element_type=F32).astype(I32)
    keys = (placed[0:BLOCKS] + (placed[BLOCKS:2 * BLOCKS] << 8)
            + (placed[2 * BLOCKS:3 * BLOCKS] << 16)) - 1
    for n in range(NZ):
        keys_ref[n, 0:16, :] = keys[16 * n:16 * (n + 1), :]
        keys_ref[n, 16:20, :] = blocks[4 * n:4 * (n + 1), :]
        keys_ref[n, 20:24, :] = blocks[4 * n:4 * (n + 1), :]


def pack(z, ids, bags):
    vmem = pl.BlockSpec(memory_space=pltpu.VMEM)
    return pl.pallas_call(
        pack_kernel,
        out_shape=jax.ShapeDtypeStruct((NZ, KEY_ROWS, LANES), I32),
        in_specs=[pl.BlockSpec(memory_space=pltpu.SMEM), vmem, vmem],
        scratch_shapes=[pltpu.VMEM((3 * BLOCKS, LOOK), BF16),
                        pltpu.VMEM((LANES, LOOK), BF16),
                        pltpu.VMEM((TOUCH, 2 * LANES), BF16)],
        cost_estimate=cost(4),
        name="pack",
    )(z, ids, bags)


def sums_kernel(*refs, sources, base, fresh):
    x_ref, refs = refs[0], list(refs[1:])
    take = lambda n: [refs.pop(0) for _ in range(n)]
    metas, grads, keys = take(sources), take(sources), take(sources)
    rows_ref = refs.pop(0)
    old_ref = None if fresh else refs.pop(0)
    gt_ref, xs_ref, k_ref = refs[-3:]
    outs = refs[:-3]
    if len(outs) == 1:
        outs = [outs[0].at[0, 0], outs[0].at[0, 1]]
    shard = pl.program_id(0)

    @pl.when(shard == 0)
    def _():
        eye = one_hot(iota((E, E), 0) == iota((E, E), 1))
        for d in range(sources):
            gt_ref[d] = lax.dot_general(eye, grads[d][...], NT, preferred_element_type=F32).astype(BF16)

    column = (x_ref[0] + base + shard) & (NX - 1)
    filled = jnp.int32(0)
    for d in range(sources):
        many = metas[d][column, 0]

        def gather(j, _, d=d, filled=filled):
            row = keys[d][pl.ds(4 * column + j, 1), :]
            picks = one_hot((row & (B_DEV - 1)) == iota((B_DEV, LANES), 0))
            slot = filled + j
            xs_ref[slot] = jnp.dot(gt_ref[d], picks, preferred_element_type=F32).astype(BF16)
            k_ref[pl.ds(slot, 1), :] = row >> 9
            return 0

        lax.fori_loop(0, many, gather, 0)
        filled = filled + many
    xs_ref[filled] = jnp.zeros((E, LANES), BF16)
    k_ref[pl.ds(filled, 1), :] = jnp.full((1, LANES), -1, I32)
    for h in range(2):
        outs[h][...] = jnp.zeros((HALF, E), F32) if fresh else old_ref[0, h]

    def accumulate(r, _):
        xs = jnp.concatenate([xs_ref[2 * r], xs_ref[2 * r + 1]], axis=1)
        pair = [k_ref[pl.ds(2 * r + j, 1), :] for j in range(2)]
        for h in range(2):
            mine = rows_ref[0, h * HALF:(h + 1) * HALF, :]
            hits = jnp.concatenate([one_hot(mine == row) for row in pair], axis=1)
            outs[h][...] += lax.dot_general(hits, xs, NT, preferred_element_type=F32)
        return 0

    lax.fori_loop(0, (filled + 1) >> 1, accumulate, 0)


def cost(us):
    return pl.CostEstimate(flops=int(us * 6e8), bytes_accessed=int(us * 3e6), transcendentals=0)


def sums(x, base, metas, grads, keys, rows, old, last):
    smem = pl.BlockSpec(memory_space=pltpu.SMEM)
    count = len(grads)
    whole = lambda shape: pl.BlockSpec(shape, lambda k: (0,) * len(shape))
    acc_spec = pl.BlockSpec((1, 2, HALF, E), lambda k: (base + k, 0, 0, 0))
    in_specs = ([smem] * (1 + count) + [whole((B_DEV, E))] * count + [whole((KEY_ROWS, LANES))] * count
                + [pl.BlockSpec((1, TOUCH, LANES), lambda k: (base + k, 0, 0))])
    if last:
        out_shape = [jax.ShapeDtypeStruct((HALF, E), F32)] * 2
        out_specs = [whole((HALF, E))] * 2
    else:
        out_shape = jax.ShapeDtypeStruct((NX, 2, HALF, E), F32)
        out_specs = acc_spec
    return pl.pallas_call(
        lambda *refs: sums_kernel(*refs, sources=count, base=base, fresh=old is None),
        grid=(1 if last else NX,),
        out_shape=out_shape,
        in_specs=in_specs + ([] if old is None else [acc_spec]),
        out_specs=out_specs,
        scratch_shapes=[pltpu.VMEM((count, E, B_DEV), BF16),
                        pltpu.VMEM((4 * count + 1, E, LANES), BF16),
                        pltpu.VMEM((4 * count + 8, LANES), I32)],
        cost_estimate=cost(3 if last else 6),
    )(x, *metas, *grads, *keys, rows, *([] if old is None else [old]))


def listed_kernel(list_ref, rows_ref, accum_ref, table_ref, accum_out, table_out):
    rows = rows_ref[0]
    hi = jnp.where((rows >> 7) == iota((TOUCH, LANES), 1), 1.0, 0.0)
    padded = jnp.concatenate([accum_ref[...], jnp.zeros((LANES - 32, LANES), F32)], axis=0)
    line = jnp.dot(hi, padded, precision=lax.Precision.HIGHEST, preferred_element_type=F32)
    mine = jnp.where((rows & (LANES - 1)) == iota((TOUCH, LANES), 1), line, 0.0)
    accum_out[...] = jnp.broadcast_to(jnp.sum(mine, axis=1, keepdims=True), (TOUCH, LANES))

    def step(i, _):
        for j in range(16):
            row = list_ref[i >> 3, (i & 7) * 16 + j]
            table_out[pl.ds(i * 16 + j, 1), :] = table_ref[pl.ds(row, 1), :]
        return 0

    lax.fori_loop(0, TOUCH // 16, step, 0)


def listed_values(order, rows, accum, table):
    vmem = pl.BlockSpec(memory_space=pltpu.VMEM)
    return pl.pallas_call(
        listed_kernel,
        out_shape=(jax.ShapeDtypeStruct((TOUCH, LANES), F32), jax.ShapeDtypeStruct((TOUCH, E), F32)),
        grid=(1,),
        in_specs=[pl.BlockSpec(memory_space=pltpu.SMEM), FIRST_ROWS, vmem, vmem],
        cost_estimate=cost(7),
        name="listed_values",
    )(order, rows, accum, table)


def update_kernel(*refs):
    list_ref, table_ref, accum_ref, listed_ref, old_ref, rows_ref = refs[0:6]
    chunks = refs[6:14]
    table_out, accum_out, new_ref, u_ref, lhs_ref, rhs_ref, sem = refs[14:]
    load = pltpu.make_async_copy(table_ref, new_ref, sem)
    load.start()
    lane = iota((QUART, LANES), 1)
    for n in range(8):
        at = slice(n * QUART, (n + 1) * QUART)
        g = chunks[n][...]
        mean = jnp.sum(g * g, axis=1, keepdims=True) * (1.0 / E)
        now = listed_ref[at, 0:1] + mean
        u_ref[at, :] = old_ref[at, :] - 0.5 * g / (jnp.sqrt(now) + 1e-08)
        rows = rows_ref[0, at, :]
        lhs_ref[at, :] = jnp.where((rows >> 7) == lane, mean, 0.0)
        rhs_ref[at, :] = jnp.where((rows & (LANES - 1)) == lane, 1.0, 0.0)
    added = lax.dot_general(lhs_ref[...], rhs_ref[...], TN, precision=lax.Precision.HIGHEST,
                            preferred_element_type=F32)
    accum_out[...] = accum_ref[...] + added[0:32, :]
    load.wait()

    def step(i, _):
        for j in range(16):
            row = list_ref[i >> 3, (i & 7) * 16 + j]
            new_ref[pl.ds(row, 1), :] = u_ref[pl.ds(i * 16 + j, 1), :]
        return 0

    lax.fori_loop(0, TOUCH // 16, step, 0)
    store = pltpu.make_async_copy(new_ref, table_out, sem)
    store.start()
    store.wait()


def update(order, table, accum, listed, old, rows, chunks):
    vmem = pl.BlockSpec(memory_space=pltpu.VMEM)
    hbm = pl.BlockSpec(memory_space=pl.ANY)
    return pl.pallas_call(
        update_kernel,
        out_shape=(jax.ShapeDtypeStruct((ROWS_DEV, E), F32), jax.ShapeDtypeStruct((32, LANES), F32)),
        grid=(1,),
        in_specs=[pl.BlockSpec(memory_space=pltpu.SMEM), hbm] + [vmem] * 3 + [FIRST_ROWS] + [vmem] * 8,
        out_specs=(hbm, vmem),
        scratch_shapes=[pltpu.VMEM((ROWS_DEV, E), F32), pltpu.VMEM((TOUCH, E), F32),
                        pltpu.VMEM((TOUCH, LANES), F32), pltpu.VMEM((TOUCH, LANES), F32),
                        pltpu.SemaphoreType.DMA],
        name="update",
    )(order, table, accum, listed, old, rows, *chunks)


def z_pairs(k):
    return [(z * NX + x, ((z + k) % NZ) * NX + x) for z in range(NZ) for x in range(NX)]


def x_pairs(k):
    return [(z * NX + x, z * NX + (x + k) % NX) for z in range(NZ) for x in range(NX)]


def y_pairs(k):
    return [(y * NC + c, ((y + k) % NY) * NC + c) for y in range(NY) for c in range(NC)]


C_PAIRS = [(y * NC + c, y * NC + 1 - c) for y in range(NY) for c in range(NC)]


def body(table, accum, pooled_grad, row_ids, bag_ids, touched):
    grp = lax.axis_index("grp")
    me = lax.axis_index("shard")
    y, c = grp // NC, grp % NC
    z, x = me // NX, me % NX
    grads = pooled_grad.reshape(B_DEV, E)

    def ordered(listed):
        halves = listed.reshape(NC, NY, QUART)
        halves = jnp.where(c == 0, halves[::-1], halves)
        doubled = jnp.concatenate([halves, halves], axis=1)
        return lax.dynamic_slice(doubled, (0, y, 0), (NC, NY, QUART)).reshape(TOUCH)

    own_list = touched.reshape(TOUCH)
    lists = [ordered(own_list)]
    for k in range(1, NX):
        lists.append(ordered(lax.ppermute(own_list, "shard", x_pairs(-k))))
    rows = jnp.broadcast_to(jnp.stack(lists)[:, :, None], (NX, TOUCH, LANES))

    keys = pack(z.reshape(1), row_ids.reshape(32, LANES), bag_ids.reshape(32, LANES))
    key_of = {0: keys[0]}
    for k in (1, -1, 2, -2, 3, -3, 4):
        key_of[-k] = lax.ppermute(keys[k % NZ], "shard", z_pairs(k))
    grad_of = {0: grads}
    for k in range(1, 5):
        grad_of[-k] = lax.ppermute(grad_of[1 - k], "shard", z_pairs(1))
        if k < 4:
            grad_of[k] = lax.ppermute(grad_of[k - 1], "shard", z_pairs(-1))

    order = lists[0].reshape(8, LANES)
    listed, old = listed_values(order, rows, accum.reshape(32, LANES), table)
    at = x.reshape(1)

    def add(sources, base, old, last):
        return sums(at, base, [key_of[d][16:24] for d in sources], [grad_of[d] for d in sources],
                    [key_of[d] for d in sources], rows, old, last)

    acc = add((0,), 0, None, False)
    acc = add((-1, 1), 0, acc, False)
    acc = add((-2, 2), 0, acc, False)
    acc = add((-3, 3), 0, acc, False)

    arrived = []
    own = None
    for k in (2, 1, 3, 0):
        send, keep = add((-4,), k, acc, True)
        both = keep + lax.ppermute(send, "grp", C_PAIRS)
        if k:
            arrived.append(lax.ppermute(both, "shard", x_pairs(k)))
        else:
            own = both
    total = own + arrived[0] + arrived[1] + arrived[2]
    part = total[0:QUART]
    for j in range(1, NY):
        part = part + lax.ppermute(total[j * QUART:(j + 1) * QUART], "grp", y_pairs(j))
    mine = [part] + [lax.ppermute(part, "grp", y_pairs(-j)) for j in range(1, NY)]
    other = [lax.ppermute(m, "grp", C_PAIRS) for m in mine]
    new_table, new_accum = update(order, table, accum.reshape(32, LANES),
                                  listed, old, rows, other + mine)
    return (new_table, new_accum.reshape(ROWS_DEV))


def solution(mesh):
    return jax.shard_map(
        body,
        mesh=mesh,
        in_specs=(
            P("shard", None),
            P("shard"),
            P("grp", "shard", None, None),
            P("grp", "shard", None),
            P("grp", "shard", None),
            P("shard", None),
        ),
        out_specs=(P("shard", None), P("shard")),
        check_vma=False,
    )
```

time: 150 us -> 168 us (1.12)
  Pallas kernels: 39.7 us -> 65.8 us
  waiting for transfers between devices: 46.2 us -> 27.8 us
  local copies, waits for them, and re-layouts: 6.72 us -> 12.3 us
  starting transfers between devices: 56 us -> 59 us
    pallas_call x6 -> x10, Pallas kernels: 27.8 us -> 54.1 us  [the longest x8 41.4 us: sums(): pl.pallas_call(lambda *refs: sums_kernel(*refs, sources=count, base=base,...]
    ppermute x14, waiting for transfers between devices: 14.9 us -> 0.04 us  [the longest x7 0.02 us: body(): key_of[-k] = lax.ppermute(keys[k % NZ], 'shard', z_pairs(k))]
    ppermute x3, starting transfers between devices: 11.6 us -> 4.94 us  [body(): lax.ppermute(total[j * QUART:(j + 1) * QUART], 'grp', y_pairs(j))]
    slice x8, local copies, waits for them, and re-layouts: 0.7 us -> 5.43 us  [add(): key_of[d][16:24]]
    ppermute x14, starting transfers between devices: 18.7 us -> 22.3 us  [the longest x7 15.2 us: body(): key_of[-k] = lax.ppermute(keys[k % NZ], 'shard', z_pairs(k))]
    ppermute x4, starting transfers between devices: 7.29 us -> 10 us  [body(): both = keep + lax.ppermute(send, 'grp', C_PAIRS)]
    ppermute x3, waiting for transfers between devices: 2.49 us -> 0.01 us  [body(): lists.append(ordered(lax.ppermute(own_list, 'shard', x_pairs(-k))))]
    unnamed x56 -> x58, local copies, waits for them, and re-layouts: 0.79 us -> 3.22 us
  transfers between devices with their start and end apart: 34 -> 34, of which waited for: 14 -> 6; matrix products, arithmetic and copies ran while one was open for 3% -> 6% of each run, Pallas kernels for 13% -> 30%
where the time goes in v2:
time: 168 us; the launch traced here: 167 us
  Pallas kernels  65.8 us (39%)
  starting transfers between devices  59 us (35%)
  waiting for transfers between devices  27.8 us (17%)
  local copies, waits for them, and re-layouts  12.3 us (7%)
    pallas_call x8, Pallas kernels, sums(): pl.pallas_call(lambda *refs: sums_kernel(*refs, sources=count, base=base,...  41.4 us
    ppermute x3, waiting for transfers between devices, body(): arrived.append(lax.ppermute(both, 'shard', x_pairs(k)))  23.1 us
    ppermute x7, starting transfers between devices, body(): key_of[-k] = lax.ppermute(keys[k % NZ], 'shard', z_pairs(k))  15.2 us
    pallas_call x1, Pallas kernels, update(): pl.pallas_call(update_kernel, out_shape=(jax.ShapeDtypeStruct((ROWS_DEV,...  11.7 us
    ppermute x4, starting transfers between devices, body(): both = keep + lax.ppermute(send, 'grp', C_PAIRS)  10 us
    pallas_call x1, Pallas kernels, listed_values(): pl.pallas_call(listed_kernel, out_shape=(jax.ShapeDtypeStruct((TOUCH, LAN...  9.3 us
    ppermute x4, starting transfers between devices, body(): other = [lax.ppermute(m, 'grp', C_PAIRS) for m in mine]  9.24 us
    ppermute x3, starting transfers between devices, body(): grad_of[k] = lax.ppermute(grad_of[k - 1], 'shard', z_pairs(-1))  6.23 us
  transfers between devices with their start and end apart: 34, of which 6 were waited for; matrix products, arithmetic and copies ran while one was open for 6% of the time, Pallas kernels for 30%

profile of v2, /device:TPU:1, one launch (start us, length us, event | category | flops | bytes accessed | tf_op | source)
XLA Modules:
  0.0 166.6 jit_solution(5431829610667935644)
XLA Ops:
  2.7 2.5 %collective-permute-start.1 = (s32[1024]{0:T(1024)}, s32[1024]{0:T(1024)S(1)}, u32[]{:S(2)}, u32[]{:S(2)}) collective-permute-start(s32[1024]{0:T(1024)} %bitcast.44), channel_id=1, source_target_pairs={{0,2},{1,3},{2,0},{3,1},{4,6},{5,7},{6,4},{7,5},{8,10},{9,11},{10,... | collective-permute-start | bytes 12296 | tf_op jit(solution)/shard_map/ppermute | solution.py:275
  6.3 3.4 %pack.1 = s32[8,24,128]{2,1,0:T(8,128)} custom-call(s32[1]{0:T(128)} %bitcast.12.z_ref, s32[32,128]{1,0:T(8,128)} %bitcast.53, s32[32,128]{1,0:T(8,128)} %bitcast.54), custom_call_target="tpu_custom_call" | custom-call | flops 2400000000 | bytes 12000000 | tf_op jit(solution)/shard_map/pack/pallas_call | solution.py:74
  11.2 5.6 %collective-permute-start.16 = (s32[24,128]{1,0:T(8,128)S(1)}, s32[24,128]{1,0:T(8,128)S(1)}, u32[]{:S(2)}, u32[]{:S(2)}) collective-permute-start(s32[24,128]{1,0:T(8,128)S(1)} %get-tuple-element.30), channel_id=1, source_target_pairs={{0,28},{1,29},{2,30},{3,31},{4,0},{5,1},{6,2},{7,3},{8,4},{9,5},{1... | collective-permute-start | bytes 36872 | tf_op jit(solution)/shard_map/ppermute | solution.py:281
  18.1 2.7 %collective-permute-start.10 = (bf16[512,256]{1,0:T(8,128)(2,1)S(1)}, bf16[512,256]{1,0:T(8,128)(2,1)S(1)}, u32[]{:S(2)}, u32[]{:S(2)}) collective-permute-start(bf16[512,256]{1,0:T(8,128)(2,1)S(1)} %bitcast.51), channel_id=1, source_target_pairs={{0,28},{1,29},{2,30},{3,31},{4,0},{5,1},{6,2},{7,3},{8,4},{9,5},{1... | collective-permute-start | bytes 786440 | tf_op jit(solution)/shard_map/ppermute | solution.py:286
  20.9 3.6 %collective-permute-start.14 = (s32[24,128]{1,0:T(8,128)S(1)}, s32[24,128]{1,0:T(8,128)S(1)}, u32[]{:S(2)}, u32[]{:S(2)}) collective-permute-start(s32[24,128]{1,0:T(8,128)S(1)} %get-tuple-element.32), channel_id=1, source_target_pairs={{0,24},{1,25},{2,26},{3,27},{4,28},{5,29},{6,30},{7,31},{8,0},{9,1... | collective-permute-start | bytes 36872 | tf_op jit(solution)/shard_map/ppermute | solution.py:281
  26.2 3.0 %collective-permute-start.9 = (s32[24,128]{1,0:T(8,128)S(1)}, s32[24,128]{1,0:T(8,128)S(1)}, u32[]{:S(2)}, u32[]{:S(2)}) collective-permute-start(s32[24,128]{1,0:T(8,128)S(1)} %get-tuple-element.34), channel_id=1, source_target_pairs={{0,20},{1,21},{2,22},{3,23},{4,24},{5,25},{6,26},{7,27},{8,28},{9,... | collective-permute-start | bytes 36872 | tf_op jit(solution)/shard_map/ppermute | solution.py:281
  32.9 5.8 %shard_map.77.refs_8_ = f32[4,2,512,256]{3,2,1,0:T(8,128)} custom-call(s32[1]{0:T(128)} %bitcast.11.refs_0_, s32[8,128]{1,0:T(8,128)} %slice_bitcast_fusion.8.refs_1_, bf16[512,256]{1,0:T(8,128)(2,1)} %bitcast.50, s32[24,128]{1,0:T(8,128)} %get-tuple-element.29.refs_3_, s32[4,1024,128]{2,1,0:T(8,128)} %broadcast_in_dim.2.rows_ref.refs_4_.refs_7_.refs_5_), custom_call_target="tpu_custom_call" | custom-call | flops 3600000000 | bytes 18000000 | tf_op jit(solution)/shard_map/pallas_call | solution.py:153
  44.8 7.3 %shard_map.78.refs_8_ = f32[4,2,512,256]{3,2,1,0:T(8,128)} custom-call(s32[1]{0:T(128)} %bitcast.11.refs_0_, s32[8,128]{1,0:T(8,128)} %slice.99.refs_1_, s32[8,128]{1,0:T(8,128)} %slice.101.refs_2_, bf16[512,256]{1,0:T(8,128)(2,1)} %copy-done.23, bf16[512,256]{1,0:T(8,128)(2,1)} %copy-done.22, s32[24,128]{1,0:T(8,128)} %copy-done.15, s32[24,128]{1,0:T(8,128)} %copy-done.14, ...), custom_call_target="tpu_custom_call" | custom-call | flops 3600000000 | bytes 18000000 | tf_op jit(solution)/shard_map/pallas_call | solution.py:153
  55.0 7.4 %shard_map.79.refs_8_ = f32[4,2,512,256]{3,2,1,0:T(8,128)} custom-call(s32[1]{0:T(128)} %bitcast.11.refs_0_, s32[8,128]{1,0:T(8,128)} %slice.95.refs_1_, s32[8,128]{1,0:T(8,128)} %slice.97.refs_2_, bf16[512,256]{1,0:T(8,128)(2,1)} %copy-done.27, bf16[512,256]{1,0:T(8,128)(2,1)} %copy-done.24, s32[24,128]{1,0:T(8,128)} %copy-done.16, s32[24,128]{1,0:T(8,128)} %copy-done.17, ...), custom_call_target="tpu_custom_call" | custom-call | flops 3600000000 | bytes 18000000 | tf_op jit(solution)/shard_map/pallas_call | solution.py:153
  63.7 7.3 %shard_map.80.refs_5_ = f32[4,2,512,256]{3,2,1,0:T(8,128)} custom-call(s32[1]{0:T(128)} %bitcast.11.refs_0_, s32[8,128]{1,0:T(8,128)} %slice.91.refs_1_, s32[8,128]{1,0:T(8,128)} %slice.93.refs_2_, bf16[512,256]{1,0:T(8,128)(2,1)} %copy-done.26, bf16[512,256]{1,0:T(8,128)(2,1)} %copy-done.28, s32[24,128]{1,0:T(8,128)} %copy-done.19, s32[24,128]{1,0:T(8,128)} %copy-done.20, ...), custom_call_target="tpu_custom_call" | custom-call | flops 3600000000 | bytes 18000000 | tf_op jit(solution)/shard_map/pallas_call | solution.py:153
  71.8 3.4 %shard_map.82 = (f32[512,256]{1,0:T(8,128)}, f32[512,256]{1,0:T(8,128)}) custom-call(s32[1]{0:T(128)} %bitcast.11.refs_0_, s32[8,128]{1,0:T(8,128)} %slice.89.refs_1_, bf16[512,256]{1,0:T(8,128)(2,1)} %copy-done.25, s32[24,128]{1,0:T(8,128)} %copy-done.18, s32[4,1024,128]{2,1,0:T(8,128)} %broadcast_in_dim.2.rows_ref.refs_4_.refs_7_.refs_5_, ...), custom_call_target="tpu_custom_call" | custom-call | flops 1800000000 | bytes 9000000 | tf_op jit(solution)/shard_map/pallas_call | solution.py:153
  75.1 9.4 %collective-permute-start.18 = (f32[512,256]{1,0:T(8,128)}, f32[512,256]{1,0:T(8,128)S(1)}, u32[]{:S(2)}, u32[]{:S(2)}) collective-permute-start(f32[512,256]{1,0:T(8,128)} %get-tuple-element.19), channel_id=1, source_target_pairs={{0,32},{32,0},{64,96},{96,64},{128,160},{160,128},{192,224},{224,1... | collective-permute-start | bytes 1572872 | tf_op jit(solution)/shard_map/ppermute | solution.py:305
  84.5 3.5 %shard_map.83 = (f32[512,256]{1,0:T(8,128)}, f32[512,256]{1,0:T(8,128)}) custom-call(s32[1]{0:T(128)} %bitcast.11.refs_0_, s32[8,128]{1,0:T(8,128)} %slice.89.refs_1_, bf16[512,256]{1,0:T(8,128)(2,1)} %copy-done.25, s32[24,128]{1,0:T(8,128)} %copy-done.18, s32[4,1024,128]{2,1,0:T(8,128)} %broadcast_in_dim.2.rows_ref.refs_4_.refs_7_.refs_5_, ...), custom_call_target="tpu_custom_call" | custom-call | flops 1800000000 | bytes 9000000 | tf_op jit(solution)/shard_map/pallas_call | solution.py:153
  88.0 3.3 %shard_map.84 = (f32[512,256]{1,0:T(8,128)}, f32[512,256]{1,0:T(8,128)}) custom-call(s32[1]{0:T(128)} %bitcast.11.refs_0_, s32[8,128]{1,0:T(8,128)} %slice.89.refs_1_, bf16[512,256]{1,0:T(8,128)(2,1)} %copy-done.25, s32[24,128]{1,0:T(8,128)} %copy-done.18, s32[4,1024,128]{2,1,0:T(8,128)} %broadcast_in_dim.2.rows_ref.refs_4_.refs_7_.refs_5_, ...), custom_call_target="tpu_custom_call" | custom-call | flops 1800000000 | bytes 9000000 | tf_op jit(solution)/shard_map/pallas_call | solution.py:153
  91.9 3.4 %shard_map.81 = (f32[512,256]{1,0:T(8,128)}, f32[512,256]{1,0:T(8,128)}) custom-call(s32[1]{0:T(128)} %bitcast.11.refs_0_, s32[8,128]{1,0:T(8,128)} %slice.89.refs_1_, bf16[512,256]{1,0:T(8,128)(2,1)} %copy-done.25, s32[24,128]{1,0:T(8,128)} %copy-done.18, s32[4,1024,128]{2,1,0:T(8,128)} %broadcast_in_dim.2.rows_ref.refs_4_.refs_7_.refs_5_, ...), custom_call_target="tpu_custom_call" | custom-call | flops 1800000000 | bytes 9000000 | tf_op jit(solution)/shard_map/pallas_call | solution.py:153
  96.2 2.7 %collective-permute-start.23 = (f32[512,256]{1,0:T(8,128)S(1)}, f32[512,256]{1,0:T(8,128)S(1)}, u32[]{:S(2)}, u32[]{:S(2)}) collective-permute-start(f32[512,256]{1,0:T(8,128)S(1)} %add.53), channel_id=1, source_target_pairs={{0,3},{1,0},{2,1},{3,2},{4,7},{5,4},{6,5},{7,6},{8,11},{9,8},{10,9... | collective-permute-start | bytes 1572872 | tf_op jit(solution)/shard_map/ppermute | solution.py:307
  98.8 11.3 %collective-permute-done.19 = f32[512,256]{1,0:T(8,128)S(1)} collective-permute-done((f32[512,256]{1,0:T(8,128)S(1)}, f32[512,256]{1,0:T(8,128)S(1)}, u32[]{:S(2)}, u32[]{:S(2)}) %collective-permute-start.19) | collective-permute-done | bytes 524320 | tf_op jit(solution)/shard_map/ppermute | solution.py:307
  110.2 11.8 %collective-permute-done.21 = f32[512,256]{1,0:T(8,128)S(1)} collective-permute-done((f32[512,256]{1,0:T(8,128)S(1)}, f32[512,256]{1,0:T(8,128)S(1)}, u32[]{:S(2)}, u32[]{:S(2)}) %collective-permute-start.21) | collective-permute-done | bytes 524320 | tf_op jit(solution)/shard_map/ppermute | solution.py:307
  122.3 3.3 %collective-permute-start.25 = (f32[128,256]{1,0:T(8,128)S(1)}, f32[128,256]{1,0:T(8,128)S(1)}, u32[]{:S(2)}, u32[]{:S(2)}) collective-permute-start(f32[128,256]{1,0:T(8,128)S(1)} %get-tuple-element.28), channel_id=1, source_target_pairs={{0,128},{32,160},{64,192},{96,224},{128,0},{160,32},{192,64},{224,... | collective-permute-start | bytes 393224 | tf_op jit(solution)/shard_map/ppermute | solution.py:313
  128.0 3.5 %collective-permute-done.25 = f32[128,256]{1,0:T(8,128)S(1)} collective-permute-done((f32[128,256]{1,0:T(8,128)S(1)}, f32[128,256]{1,0:T(8,128)S(1)}, u32[]{:S(2)}, u32[]{:S(2)}) %collective-permute-start.25) | collective-permute-done | bytes 131104 | tf_op jit(solution)/shard_map/ppermute | solution.py:313
  131.5 2.8 %collective-permute-start.28 = (f32[128,256]{1,0:T(8,128)S(1)}, f32[128,256]{1,0:T(8,128)S(1)}, u32[]{:S(2)}, u32[]{:S(2)}) collective-permute-start(f32[128,256]{1,0:T(8,128)S(1)} %fusion.1.refs_10_), channel_id=1, source_target_pairs={{0,192},{32,224},{64,0},{96,32},{128,64},{160,96},{192,128},{224,1... | collective-permute-start | bytes 393224 | tf_op jit(solution)/shard_map/ppermute | solution.py:314
  137.6 3.3 %collective-permute-start.29 = (f32[128,256]{1,0:T(8,128)S(1)}, f32[128,256]{1,0:T(8,128)S(1)}, u32[]{:S(2)}, u32[]{:S(2)}) collective-permute-start(f32[128,256]{1,0:T(8,128)S(1)} %collective-permute-done.28.refs_11_), channel_id=1, source_target_pairs={{0,32},{32,0},{64,96},{96,64},{128,160},{160,128},{192,224},{224,1... | collective-permute-start | bytes 393224 | tf_op jit(solution)/shard_map/ppermute | solution.py:315
  144.6 9.3 %listed_values.1 = (f32[1024,128]{1,0:T(8,128)}, f32[1024,256]{1,0:T(8,128)}) custom-call(s32[8,128]{1,0:T(8,128)} %bitcast.36, s32[4,1024,128]{2,1,0:T(8,128)} %broadcast_in_dim.2.rows_ref.refs_4_.refs_7_.refs_5_, f32[32,128]{1,0:T(8,128)} %bitcast.38, f32[4096,256]{1,0:T(8,128)} %refs_1_.1), custom_call_target="tpu_custom_call" | custom-call | flops 4200000000 | bytes 21000000 | tf_op jit(solution)/shard_map/listed_values/pallas_call | solution.py:185
  154.7 11.7 %update.1 = (f32[4096,256]{1,0:T(8,128)}, f32[32,128]{1,0:T(8,128)}) custom-call(s32[8,128]{1,0:T(8,128)} %bitcast.37, f32[4096,256]{1,0:T(8,128)} %refs_1_.1, f32[32,128]{1,0:T(8,128)} %bitcast.39, f32[1024,128]{1,0:T(8,128)} %get-tuple-element.14.refs_3_, f32[1024,256]{1,0:T(8,128)} %get-tuple-element.15.refs_4_, ...), custom_call_target="tpu_custom_call" | custom-call | tf_op jit(solution)/shard_map/update/pallas_call | solution.py:231
  (136 shorter events, 34.2 us)
Async XLA Ops:
  0.6 17.4 %collective-permute-start.2 = (s32[1024]{0:T(1024)}, s32[1024]{0:T(1024)S(1)}, u32[]{:S(2)}, u32[]{:S(2)}) collective-permute-start(s32[1024]{0:T(1024)} %bitcast.43), channel_id=1, source_target_pairs={{0,1},{1,2},{2,3},{3,0},{4,5},{5,6},{6,7},{7,4},{8,9},{9,10},{10,1... | collective-permute-start | bytes 12296 | tf_op jit(solution)/shard_map/ppermute | solution.py:275
  2.7 18.1 %collective-permute-start.1 = (s32[1024]{0:T(1024)}, s32[1024]{0:T(1024)S(1)}, u32[]{:S(2)}, u32[]{:S(2)}) collective-permute-start(s32[1024]{0:T(1024)} %bitcast.44), channel_id=1, source_target_pairs={{0,2},{1,3},{2,0},{3,1},{4,6},{5,7},{6,4},{7,5},{8,10},{9,11},{10,... | collective-permute-start | bytes 12296 | tf_op jit(solution)/shard_map/ppermute | solution.py:275
  5.2 15.7 %collective-permute-start = (s32[1024]{0:T(1024)}, s32[1024]{0:T(1024)S(1)}, u32[]{:S(2)}, u32[]{:S(2)}) collective-permute-start(s32[1024]{0:T(1024)} %bitcast.45), channel_id=1, source_target_pairs={{0,3},{1,0},{2,1},{3,2},{4,7},{5,4},{6,5},{7,6},{8,11},{9,8},{10,9... | collective-permute-start | bytes 12296 | tf_op jit(solution)/shard_map/ppermute | solution.py:275
  11.2 13.3 %collective-permute-start.16 = (s32[24,128]{1,0:T(8,128)S(1)}, s32[24,128]{1,0:T(8,128)S(1)}, u32[]{:S(2)}, u32[]{:S(2)}) collective-permute-start(s32[24,128]{1,0:T(8,128)S(1)} %get-tuple-element.30), channel_id=1, source_target_pairs={{0,28},{1,29},{2,30},{3,31},{4,0},{5,1},{6,2},{7,3},{8,4},{9,5},{1... | collective-permute-start | bytes 36872 | tf_op jit(solution)/shard_map/ppermute | solution.py:281
  18.1 24.9 %collective-permute-start.10 = (bf16[512,256]{1,0:T(8,128)(2,1)S(1)}, bf16[512,256]{1,0:T(8,128)(2,1)S(1)}, u32[]{:S(2)}, u32[]{:S(2)}) collective-permute-start(bf16[512,256]{1,0:T(8,128)(2,1)S(1)} %bitcast.51), channel_id=1, source_target_pairs={{0,28},{1,29},{2,30},{3,31},{4,0},{5,1},{6,2},{7,3},{8,4},{9,5},{1... | collective-permute-start | bytes 786440 | tf_op jit(solution)/shard_map/ppermute | solution.py:286
  20.9 8.3 %collective-permute-start.14 = (s32[24,128]{1,0:T(8,128)S(1)}, s32[24,128]{1,0:T(8,128)S(1)}, u32[]{:S(2)}, u32[]{:S(2)}) collective-permute-start(s32[24,128]{1,0:T(8,128)S(1)} %get-tuple-element.32), channel_id=1, source_target_pairs={{0,24},{1,25},{2,26},{3,27},{4,28},{5,29},{6,30},{7,31},{8,0},{9,1... | collective-permute-start | bytes 36872 | tf_op jit(solution)/shard_map/ppermute | solution.py:281
  24.5 19.6 %collective-permute-start.4 = (bf16[512,256]{1,0:T(8,128)(2,1)S(1)}, bf16[512,256]{1,0:T(8,128)(2,1)S(1)}, u32[]{:S(2)}, u32[]{:S(2)}) collective-permute-start(bf16[512,256]{1,0:T(8,128)(2,1)S(1)} %bitcast.52), channel_id=1, source_target_pairs={{0,4},{1,5},{2,6},{3,7},{4,8},{5,9},{6,10},{7,11},{8,12},{9,13},{1... | collective-permute-start | bytes 786440 | tf_op jit(solution)/shard_map/ppermute | solution.py:284
  24.6 16.5 %collective-permute-start.8 = (s32[24,128]{1,0:T(8,128)S(1)}, s32[24,128]{1,0:T(8,128)S(1)}, u32[]{:S(2)}, u32[]{:S(2)}) collective-permute-start(s32[24,128]{1,0:T(8,128)S(1)} %get-tuple-element.35), channel_id=1, source_target_pairs={{0,12},{1,13},{2,14},{3,15},{4,16},{5,17},{6,18},{7,19},{8,20},{9,... | collective-permute-start | bytes 36872 | tf_op jit(solution)/shard_map/ppermute | solution.py:281
  26.2 15.5 %collective-permute-start.9 = (s32[24,128]{1,0:T(8,128)S(1)}, s32[24,128]{1,0:T(8,128)S(1)}, u32[]{:S(2)}, u32[]{:S(2)}) collective-permute-start(s32[24,128]{1,0:T(8,128)S(1)} %get-tuple-element.34), channel_id=1, source_target_pairs={{0,20},{1,21},{2,22},{3,23},{4,24},{5,25},{6,26},{7,27},{8,28},{9,... | collective-permute-start | bytes 36872 | tf_op jit(solution)/shard_map/ppermute | solution.py:281
  29.2 13.1 %collective-permute-start.3 = (s32[24,128]{1,0:T(8,128)S(1)}, s32[24,128]{1,0:T(8,128)S(1)}, u32[]{:S(2)}, u32[]{:S(2)}) collective-permute-start(s32[24,128]{1,0:T(8,128)S(1)} %get-tuple-element.36), channel_id=1, source_target_pairs={{0,16},{1,17},{2,18},{3,19},{4,20},{5,21},{6,22},{7,23},{8,24},{9,... | collective-permute-start | bytes 36872 | tf_op jit(solution)/shard_map/ppermute | solution.py:281
  42.9 9.7 %collective-permute-start.11 = (bf16[512,256]{1,0:T(8,128)(2,1)S(1)}, bf16[512,256]{1,0:T(8,128)(2,1)S(1)}, u32[]{:S(2)}, u32[]{:S(2)}) collective-permute-start(bf16[512,256]{1,0:T(8,128)(2,1)S(1)} %collective-permute-done.10.refs_4_), channel_id=1, source_target_pairs={{0,28},{1,29},{2,30},{3,31},{4,0},{5,1},{6,2},{7,3},{8,4},{9,5},{1... | collective-permute-start | bytes 786440 | tf_op jit(solution)/shard_map/ppermute | solution.py:286
  52.2 10.1 %collective-permute-start.6 = (bf16[512,256]{1,0:T(8,128)(2,1)S(1)}, bf16[512,256]{1,0:T(8,128)(2,1)S(1)}, u32[]{:S(2)}, u32[]{:S(2)}) collective-permute-start(bf16[512,256]{1,0:T(8,128)(2,1)S(1)} %collective-permute-done.5.refs_3_), channel_id=1, source_target_pairs={{0,4},{1,5},{2,6},{3,7},{4,8},{5,9},{6,10},{7,11},{8,12},{9,13},{1... | collective-permute-start | bytes 786440 | tf_op jit(solution)/shard_map/ppermute | solution.py:284
  52.7 9.8 %collective-permute-start.12 = (bf16[512,256]{1,0:T(8,128)(2,1)S(1)}, bf16[512,256]{1,0:T(8,128)(2,1)S(1)}, u32[]{:S(2)}, u32[]{:S(2)}) collective-permute-start(bf16[512,256]{1,0:T(8,128)(2,1)S(1)} %collective-permute-done.11.refs_4_), channel_id=1, source_target_pairs={{0,28},{1,29},{2,30},{3,31},{4,0},{5,1},{6,2},{7,3},{8,4},{9,5},{1... | collective-permute-start | bytes 786440 | tf_op jit(solution)/shard_map/ppermute | solution.py:286
  62.3 8.7 %collective-permute-start.7 = (bf16[512,256]{1,0:T(8,128)(2,1)S(1)}, bf16[512,256]{1,0:T(8,128)(2,1)S(1)}, u32[]{:S(2)}, u32[]{:S(2)}) collective-permute-start(bf16[512,256]{1,0:T(8,128)(2,1)S(1)} %collective-permute-done.6.refs_3_), channel_id=1, source_target_pairs={{0,4},{1,5},{2,6},{3,7},{4,8},{5,9},{6,10},{7,11},{8,12},{9,13},{1... | collective-permute-start | bytes 786440 | tf_op jit(solution)/shard_map/ppermute | solution.py:284
  75.1 20.2 %collective-permute-start.18 = (f32[512,256]{1,0:T(8,128)}, f32[512,256]{1,0:T(8,128)S(1)}, u32[]{:S(2)}, u32[]{:S(2)}) collective-permute-start(f32[512,256]{1,0:T(8,128)} %get-tuple-element.19), channel_id=1, source_target_pairs={{0,32},{32,0},{64,96},{96,64},{128,160},{160,128},{192,224},{224,1... | collective-permute-start | bytes 1572872 | tf_op jit(solution)/shard_map/ppermute | solution.py:305
  95.4 14.7 %collective-permute-start.19 = (f32[512,256]{1,0:T(8,128)S(1)}, f32[512,256]{1,0:T(8,128)S(1)}, u32[]{:S(2)}, u32[]{:S(2)}) collective-permute-start(f32[512,256]{1,0:T(8,128)S(1)} %add.49), channel_id=1, source_target_pairs={{0,2},{1,3},{2,0},{3,1},{4,6},{5,7},{6,4},{7,5},{8,10},{9,11},{10,... | collective-permute-start | bytes 1572872 | tf_op jit(solution)/shard_map/ppermute | solution.py:307
  95.6 26.3 %collective-permute-start.21 = (f32[512,256]{1,0:T(8,128)S(1)}, f32[512,256]{1,0:T(8,128)S(1)}, u32[]{:S(2)}, u32[]{:S(2)}) collective-permute-start(f32[512,256]{1,0:T(8,128)S(1)} %add.51), channel_id=1, source_target_pairs={{0,1},{1,2},{2,3},{3,0},{4,5},{5,6},{6,7},{7,4},{8,9},{9,10},{10,1... | collective-permute-start | bytes 1572872 | tf_op jit(solution)/shard_map/ppermute | solution.py:307
  96.2 25.8 %collective-permute-start.23 = (f32[512,256]{1,0:T(8,128)S(1)}, f32[512,256]{1,0:T(8,128)S(1)}, u32[]{:S(2)}, u32[]{:S(2)}) collective-permute-start(f32[512,256]{1,0:T(8,128)S(1)} %add.53), channel_id=1, source_target_pairs={{0,3},{1,0},{2,1},{3,2},{4,7},{5,4},{6,5},{7,6},{8,11},{9,8},{10,9... | collective-permute-start | bytes 1572872 | tf_op jit(solution)/shard_map/ppermute | solution.py:307
  122.3 9.2 %collective-permute-start.25 = (f32[128,256]{1,0:T(8,128)S(1)}, f32[128,256]{1,0:T(8,128)S(1)}, u32[]{:S(2)}, u32[]{:S(2)}) collective-permute-start(f32[128,256]{1,0:T(8,128)S(1)} %get-tuple-element.28), channel_id=1, source_target_pairs={{0,128},{32,160},{64,192},{96,224},{128,0},{160,32},{192,64},{224,... | collective-permute-start | bytes 393224 | tf_op jit(solution)/shard_map/ppermute | solution.py:313
  135.0 8.4 %collective-permute-start.32 = (f32[128,256]{1,0:T(8,128)S(1)}, f32[128,256]{1,0:T(8,128)S(1)}, u32[]{:S(2)}, u32[]{:S(2)}) collective-permute-start(f32[128,256]{1,0:T(8,128)S(1)} %fusion.1.refs_10_), channel_id=1, source_target_pairs={{0,64},{32,96},{64,128},{96,160},{128,192},{160,224},{192,0},{224,... | collective-permute-start | bytes 393224 | tf_op jit(solution)/shard_map/ppermute | solution.py:314
  135.0 18.9 %collective-permute-start.27 = (f32[128,256]{1,0:T(8,128)S(1)}, f32[128,256]{1,0:T(8,128)S(1)}, u32[]{:S(2)}, u32[]{:S(2)}) collective-permute-start(f32[128,256]{1,0:T(8,128)S(1)} %fusion.1.refs_10_), channel_id=1, source_target_pairs={{0,32},{32,0},{64,96},{96,64},{128,160},{160,128},{192,224},{224,1... | collective-permute-start | bytes 393224 | tf_op jit(solution)/shard_map/ppermute | solution.py:315
  137.6 16.4 %collective-permute-start.29 = (f32[128,256]{1,0:T(8,128)S(1)}, f32[128,256]{1,0:T(8,128)S(1)}, u32[]{:S(2)}, u32[]{:S(2)}) collective-permute-start(f32[128,256]{1,0:T(8,128)S(1)} %collective-permute-done.28.refs_11_), channel_id=1, source_target_pairs={{0,32},{32,0},{64,96},{96,64},{128,160},{160,128},{192,224},{224,1... | collective-permute-start | bytes 393224 | tf_op jit(solution)/shard_map/ppermute | solution.py:315
  140.9 13.0 %collective-permute-start.31 = (f32[128,256]{1,0:T(8,128)S(1)}, f32[128,256]{1,0:T(8,128)S(1)}, u32[]{:S(2)}, u32[]{:S(2)}) collective-permute-start(f32[128,256]{1,0:T(8,128)S(1)} %collective-permute-done.30.refs_12_), channel_id=1, source_target_pairs={{0,32},{32,0},{64,96},{96,64},{128,160},{160,128},{192,224},{224,1... | collective-permute-start | bytes 393224 | tf_op jit(solution)/shard_map/ppermute | solution.py:315
  143.4 10.6 %collective-permute-start.33 = (f32[128,256]{1,0:T(8,128)S(1)}, f32[128,256]{1,0:T(8,128)S(1)}, u32[]{:S(2)}, u32[]{:S(2)}) collective-permute-start(f32[128,256]{1,0:T(8,128)S(1)} %collective-permute-done.32.refs_13_), channel_id=1, source_target_pairs={{0,32},{32,0},{64,96},{96,64},{128,160},{160,128},{192,224},{224,1... | collective-permute-start | bytes 393224 | tf_op jit(solution)/shard_map/ppermute | solution.py:315
  (39 other events, 298.6 us)

commit v3 on v1

v3 whole, which is shorter than its diff:
```python
import jax
import jax.numpy as jnp
from jax import lax
from jax.experimental import pallas as pl
from jax.experimental.pallas import tpu as pltpu
from jax.sharding import PartitionSpec as P


E = 256
ROWS_DEV = 4096
TOUCH = 1024
HALF = TOUCH // 2
QUART = TOUCH // 8
TILE = 512
LOOK = 4096
B_DEV = 512
LANES = 128
BLOCKS = 64
WIDTH = B_DEV + LANES
NZ, NX, NY, NC = 8, 4, 4, 2
F32 = jnp.float32
BF16 = jnp.bfloat16
I32 = jnp.int32
NT = (((1,), (1,)), ((), ()))
TN = (((0,), (0,)), ((), ()))
ORDER = (2, 1, 3, 0)
OWN_ROWS = pl.BlockSpec((1, TOUCH, LANES), lambda i: (3, 0, 0))


def iota(shape, dim):
    return lax.broadcasted_iota(I32, shape, dim)


def one_hot(mask):
    return jnp.where(mask, 1.0, 0.0).astype(BF16)


def pack_kernel(ids_ref, bags_ref, g_ref, out_ref, a_ref, b_ref, o_ref):
    groups = LOOK // LANES
    ids = ids_ref[...]
    owner = ids >> 12
    owners = iota((32, LANES), 0)
    running = jnp.zeros((32, LANES), F32)
    for i in range(groups):
        hit = jnp.where(owner[i:i + 1, :] == owners, 1.0, 0.0)
        o_ref[i * 32:(i + 1) * 32, 0:LANES] = hit.astype(BF16)
        o_ref[i * 32:(i + 1) * 32, LANES:2 * LANES] = running.astype(BF16)
        running = running + hit
    before = one_hot(iota((LANES, LANES), 0) < iota((LANES, LANES), 1))
    weights = jnp.concatenate([before, jnp.ones((LANES, LANES), BF16)], axis=0)
    prefix = jnp.dot(o_ref[...], weights, preferred_element_type=F32)
    totals = jnp.concatenate([running, jnp.zeros((LANES - 32, LANES), F32)], axis=0)
    count_row = lax.dot_general(jnp.ones((8, LANES), BF16), totals.astype(BF16), NT,
                                preferred_element_type=F32).astype(I32)
    blocks_row = (count_row + (LANES - 1)) >> 7
    start_row = jnp.dot(blocks_row.astype(F32).astype(BF16), before, preferred_element_type=F32)
    start_col = jnp.sum(
        jnp.where(iota((32, LANES), 1) < iota((32, LANES), 0),
                  jnp.broadcast_to(blocks_row[0:1, :].astype(F32), (32, LANES)), 0.0),
        axis=1, keepdims=True) * float(LANES)
    start_all = jnp.broadcast_to(start_col, (32, LANES))
    for i in range(groups):
        hit = owner[i:i + 1, :] == owners
        pos = jnp.sum(jnp.where(hit, prefix[i * 32:(i + 1) * 32, :] + start_all, 0.0),
                      axis=0, keepdims=True).astype(I32)
        key = (((ids[i:i + 1, :] & (ROWS_DEV - 1)) << 9) | bags_ref[i:i + 1, :]) + 1
        at_hi = (pos >> 7) == iota((BLOCKS, LANES), 0)
        for piece in range(3):
            part = ((key >> (8 * piece)) & 255).astype(F32)
            a_ref[piece * BLOCKS:(piece + 1) * BLOCKS, i * LANES:(i + 1) * LANES] = jnp.where(
                at_hi, part, 0.0).astype(BF16)
        b_ref[:, i * LANES:(i + 1) * LANES] = one_hot((pos & (LANES - 1)) == iota((LANES, LANES), 0))
    placed = lax.dot_general(a_ref[...], b_ref[...], NT, preferred_element_type=F32)
    out_ref[0:3 * BLOCKS, B_DEV:WIDTH] = placed.astype(BF16)
    meta = jnp.where(iota((16, LANES), 0) < 8,
                     jnp.concatenate([start_row, start_row], axis=0),
                     jnp.concatenate([blocks_row, blocks_row], axis=0).astype(F32))
    out_ref[3 * BLOCKS:3 * BLOCKS + 16, B_DEV:WIDTH] = meta.astype(BF16)
    out_ref[3 * BLOCKS + 16:E, B_DEV:WIDTH] = jnp.zeros((E - 3 * BLOCKS - 16, LANES), BF16)
    eye = one_hot(iota((E, E), 0) == iota((E, E), 1))
    out_ref[:, 0:B_DEV] = lax.dot_general(eye, g_ref[...], NT, preferred_element_type=F32).astype(BF16)


def pack(ids, bags, grads):
    return pl.pallas_call(
        pack_kernel,
        out_shape=jax.ShapeDtypeStruct((E, WIDTH), BF16),
        scratch_shapes=[pltpu.VMEM((3 * BLOCKS, LOOK), BF16),
                        pltpu.VMEM((LANES, LOOK), BF16),
                        pltpu.VMEM((TOUCH, 2 * LANES), BF16)],
        cost_estimate=cost(4),
        name="pack",
    )(ids, bags, grads)


def gather_kernel(z_ref, *refs, count):
    packets = refs[0:count]
    x_ref, k_ref, m_ref, all_ref, scalar_ref, sem = refs[count:]
    for d in range(count):
        side = packets[d][3 * BLOCKS:3 * BLOCKS + 16, B_DEV:WIDTH].astype(F32).astype(I32)
        m_ref[d] = jnp.where(iota((8, LANES), 0) == 0, side[0:8], side[8:16])
        copy = pltpu.make_async_copy(m_ref.at[d], scalar_ref.at[d], sem.at[d])
        copy.start()
        pieces = packets[d][0:3 * BLOCKS, B_DEV:WIDTH].astype(F32).astype(I32)
        all_ref[d] = (pieces[0:BLOCKS] + (pieces[BLOCKS:2 * BLOCKS] << 8)
                      + (pieces[2 * BLOCKS:3 * BLOCKS] << 16)) - 1
        copy.wait()

        def column(n, _, d=d):
            first = scalar_ref[d, 0, NX * z_ref[0] + n]

            def block(j, _):
                row = all_ref[d, pl.ds(first + j, 1), :]
                picks = one_hot((row & (B_DEV - 1)) == iota((B_DEV, LANES), 0))
                x_ref[d, 4 * n + j] = jnp.dot(packets[d][:, 0:B_DEV], picks,
                                              preferred_element_type=F32).astype(BF16)
                k_ref[d, pl.ds(4 * n + j, 1), :] = row >> 9
                return 0

            lax.fori_loop(0, scalar_ref[d, 1, NX * z_ref[0] + n], block, 0)
            return 0

        lax.fori_loop(0, NX, column, 0)


def gather(z, packets):
    count = len(packets)
    vmem = pl.BlockSpec(memory_space=pltpu.VMEM)
    return pl.pallas_call(
        lambda *refs: gather_kernel(*refs, count=count),
        out_shape=(jax.ShapeDtypeStruct((count, 16, E, LANES), BF16),
                   jax.ShapeDtypeStruct((count, 16, LANES), I32),
                   jax.ShapeDtypeStruct((count, 8, LANES), I32)),
        in_specs=[pl.BlockSpec(memory_space=pltpu.SMEM)] + [vmem] * count,
        scratch_shapes=[pltpu.VMEM((count, BLOCKS, LANES), I32), pltpu.SMEM((count, 8, LANES), I32),
                        pltpu.SemaphoreType.DMA((count,))],
        cost_estimate=cost(2 + 2 * count),
    )(z, *packets)


def sums_kernel(at_ref, *refs, counts, base):
    groups = len(counts)
    metas, xs, keys = refs[0:groups], refs[groups:2 * groups], refs[2 * groups:3 * groups]
    rows_ref, send_ref, keep_ref, all_ref, k_ref = refs[3 * groups:]
    column = at_ref[base + pl.program_id(0)]
    shard = at_ref[4] + column
    filled = jnp.int32(0)
    for n in range(groups):
        for d in range(counts[n]):
            many = metas[n][d, 1, shard]

            def move(j, _, n=n, d=d, filled=filled):
                all_ref[filled + j] = xs[n][d, j]
                k_ref[pl.ds(filled + j, 1), :] = keys[n][d, pl.ds(4 * column + j, 1), :]
                return 0

            lax.fori_loop(0, many, move, 0)
            filled = filled + many
    rounds = (filled + 7) >> 3

    def blank(j, _):
        all_ref[j] = jnp.zeros((E, LANES), BF16)
        k_ref[pl.ds(j, 1), :] = jnp.full((1, LANES), -1, I32)
        return 0

    lax.fori_loop(filled, rounds * 8, blank, 0)
    outs = (send_ref.at[0], keep_ref.at[0])
    for out in outs:
        out[...] = jnp.zeros((HALF, E), F32)

    def accumulate(r, _):
        wide = jnp.concatenate([all_ref[8 * r + j] for j in range(8)], axis=1)
        lines = [k_ref[pl.ds(8 * r + j, 1), :] for j in range(8)]
        for h in range(2):
            mine = rows_ref[0, h * HALF:(h + 1) * HALF, :]
            hits = jnp.concatenate([one_hot(mine == line) for line in lines], axis=1)
            outs[h][...] += lax.dot_general(hits, wide, NT, preferred_element_type=F32)
        return 0

    lax.fori_loop(0, rounds, accumulate, 0)


def cost(us):
    return pl.CostEstimate(flops=int(us * 6e8), bytes_accessed=int(us * 3e6), transcendentals=0)


def sums(at, base, many, gathered, rows):
    counts = tuple(g[0].shape[0] for g in gathered)
    total = sum(counts)
    smem = pl.BlockSpec(memory_space=pltpu.SMEM)
    out = pl.BlockSpec((1, HALF, E), lambda k, at: (k, 0, 0))
    in_specs = [smem] * len(counts)
    in_specs += [pl.BlockSpec((n, 4, E, LANES), lambda k, at: (0, at[base + k], 0, 0)) for n in counts]
    in_specs += [pl.BlockSpec((n, 16, LANES), lambda k, at: (0, 0, 0)) for n in counts]
    in_specs += [pl.BlockSpec((1, TOUCH, LANES), lambda k, at: (base + k, 0, 0))]
    return pl.pallas_call(
        lambda *refs: sums_kernel(*refs, counts=counts, base=base),
        grid_spec=pltpu.PrefetchScalarGridSpec(
            num_scalar_prefetch=1,
            grid=(many,),
            in_specs=in_specs,
            out_specs=[out, out],
            scratch_shapes=[pltpu.VMEM((4 * total, E, LANES), BF16), pltpu.VMEM((4 * total, LANES), I32)],
        ),
        out_shape=[jax.ShapeDtypeStruct((many, HALF, E), F32)] * 2,
        cost_estimate=cost(3 * many),
    )(at, *[g[2] for g in gathered], *[g[0] for g in gathered], *[g[1] for g in gathered], rows)


def listed_kernel(list_ref, rows_ref, accum_ref, table_ref, accum_out, table_out):
    rows = rows_ref[0]
    hi = jnp.where((rows >> 7) == iota((TOUCH, LANES), 1), 1.0, 0.0)
    padded = jnp.concatenate([accum_ref[...], jnp.zeros((LANES - 32, LANES), F32)], axis=0)
    line = jnp.dot(hi, padded, precision=lax.Precision.HIGHEST, preferred_element_type=F32)
    mine = jnp.where((rows & (LANES - 1)) == iota((TOUCH, LANES), 1), line, 0.0)
    accum_out[...] = jnp.broadcast_to(jnp.sum(mine, axis=1, keepdims=True), (TOUCH, LANES))

    def step(i, _):
        for j in range(16):
            row = list_ref[i >> 3, (i & 7) * 16 + j]
            table_out[pl.ds(i * 16 + j, 1), :] = table_ref[pl.ds(row, 1), :]
        return 0

    lax.fori_loop(0, TOUCH // 16, step, 0)


def listed_values(order, rows, accum, table):
    vmem = pl.BlockSpec(memory_space=pltpu.VMEM)
    return pl.pallas_call(
        listed_kernel,
        out_shape=(jax.ShapeDtypeStruct((TOUCH, LANES), F32), jax.ShapeDtypeStruct((TOUCH, E), F32)),
        grid=(1,),
        in_specs=[pl.BlockSpec(memory_space=pltpu.SMEM), OWN_ROWS, vmem, vmem],
        cost_estimate=cost(7),
        name="listed_values",
    )(order, rows, accum, table)


def update_kernel(*refs):
    plan_ref, list_ref, table_ref, accum_ref, listed_ref, old_ref, rows_ref = refs[0:7]
    chunks = refs[7:15]
    table_out, accum_out, u_ref, lhs_ref, rhs_ref = refs[15:]
    block = pl.program_id(0)

    @pl.when(block == 0)
    def _():
        lane = iota((QUART, LANES), 1)
        for n in range(8):
            at = slice(n * QUART, (n + 1) * QUART)
            g = chunks[n][...]
            mean = jnp.sum(g * g, axis=1, keepdims=True) * (1.0 / E)
            now = listed_ref[at, 0:1] + mean
            place = pl.multiple_of(plan_ref[16 + n] * QUART, QUART)
            u_ref[pl.ds(place, QUART), :] = old_ref[at, :] - 0.5 * g / (jnp.sqrt(now) + 1e-08)
            rows = rows_ref[0, at, :]
            lhs_ref[at, :] = jnp.where((rows >> 7) == lane, mean, 0.0)
            rhs_ref[at, :] = jnp.where((rows & (LANES - 1)) == lane, 1.0, 0.0)
        added = lax.dot_general(lhs_ref[...], rhs_ref[...], TN, precision=lax.Precision.HIGHEST,
                                preferred_element_type=F32)
        accum_out[...] = accum_ref[...] + added[0:32, :]

    table_out[...] = table_ref[...]
    first, last = plan_ref[block], plan_ref[block + 1]

    def put(n):
        row = list_ref[n >> 7, n & (LANES - 1)] - block * TILE
        table_out[pl.ds(row, 1), :] = u_ref[pl.ds(n, 1), :]

    def step(i, _):
        for j in range(8):
            put(first + i * 8 + j)
        return 0

    whole = (last - first) >> 3
    lax.fori_loop(0, whole, step, 0)
    lax.fori_loop(first + whole * 8, last, lambda n, _: (put(n), 0)[1], 0)


def update(plan, natural, table, accum, listed, old, rows, chunks):
    smem = pl.BlockSpec(memory_space=pltpu.SMEM)
    tile = pl.BlockSpec((TILE, E), lambda i: (i, 0))
    whole = lambda *shape: pl.BlockSpec(shape, lambda i: (0,) * len(shape))
    return pl.pallas_call(
        update_kernel,
        grid=(ROWS_DEV // TILE,),
        out_shape=(jax.ShapeDtypeStruct((ROWS_DEV, E), F32), jax.ShapeDtypeStruct((32, LANES), F32)),
        in_specs=[smem, smem, tile, whole(32, LANES), whole(TOUCH, LANES), whole(TOUCH, E), OWN_ROWS]
        + [whole(QUART, E)] * 8,
        out_specs=(tile, whole(32, LANES)),
        scratch_shapes=[pltpu.VMEM((TOUCH, E), F32), pltpu.VMEM((TOUCH, LANES), F32),
                        pltpu.VMEM((TOUCH, LANES), F32)],
        name="update",
    )(plan, natural, table, accum, listed, old, rows, *chunks)


def z_pairs(k):
    return [(z * NX + x, ((z + k) % NZ) * NX + x) for z in range(NZ) for x in range(NX)]


def x_pairs(k):
    return [(z * NX + x, z * NX + (x + k) % NX) for z in range(NZ) for x in range(NX)]


def y_pairs(k):
    return [(y * NC + c, ((y + k) % NY) * NC + c) for y in range(NY) for c in range(NC)]


C_PAIRS = [(y * NC + c, y * NC + 1 - c) for y in range(NY) for c in range(NC)]


def body(table, accum, pooled_grad, row_ids, bag_ids, touched):
    grp = lax.axis_index("grp")
    me = lax.axis_index("shard")
    y, c = grp // NC, grp % NC
    z, x = me // NX, me % NX

    def ordered(listed):
        halves = listed.reshape(NC, NY, QUART)
        halves = jnp.where(c == 0, halves[::-1], halves)
        doubled = jnp.concatenate([halves, halves], axis=1)
        return lax.dynamic_slice(doubled, (0, y, 0), (NC, NY, QUART)).reshape(TOUCH)

    own_list = touched.reshape(TOUCH)
    lists = {0: ordered(own_list)}
    for k in range(1, NX):
        lists[k] = ordered(lax.ppermute(own_list, "shard", x_pairs(-k)))
    stacked = jnp.stack([lists[k] for k in ORDER])[:, :, None]
    rows = jnp.broadcast_to(stacked, (NX, TOUCH, LANES))
    order = lists[0].reshape(8, LANES)
    bounds = jnp.sum((own_list[None, :] < TILE * jnp.arange(16, dtype=I32)[:, None]).astype(I32), axis=1)
    turn = (y + jnp.arange(NY, dtype=I32)) % NY
    plan = jnp.concatenate([bounds, (1 - c) * NY + turn, c * NY + turn])

    packet = pack(row_ids.reshape(32, LANES), bag_ids.reshape(32, LANES),
                  pooled_grad.reshape(B_DEV, E))
    got = {0: packet}
    for k in range(1, 5):
        got[-k] = lax.ppermute(got[1 - k], "shard", z_pairs(1))
        if k < 4:
            got[k] = lax.ppermute(got[k - 1], "shard", z_pairs(-1))
    gathered = []
    for sources in ((0,), (-1, 1), (-2, 2), (-3, 3), (-4,)):
        gathered.append(gather(z.reshape(1), [got[k] for k in sources]))

    listed, old = listed_values(order, rows, accum.reshape(32, LANES), table)
    at = jnp.concatenate([(x + jnp.array(ORDER, I32)) % NX, (NX * z).reshape(1)])
    both = {}
    for base, ks in ((0, (2,)), (1, (1, 3)), (3, (0,))):
        send, keep = sums(at, base, len(ks), gathered, rows)
        swapped = lax.ppermute(send, "grp", C_PAIRS)
        total = keep + swapped
        for n, k in enumerate(ks):
            both[k] = total[n]
    low = lax.ppermute(both[2][:HALF // 2], "shard", x_pairs(1))
    high = lax.ppermute(both[2][HALF // 2:], "shard", x_pairs(-1))
    up = jnp.concatenate([both[1][:HALF // 2] + low, both[1][HALF // 2:]], axis=0)
    down = jnp.concatenate([both[3][:HALF // 2], both[3][HALF // 2:] + high], axis=0)
    up = lax.ppermute(up, "shard", x_pairs(1))
    down = lax.ppermute(down, "shard", x_pairs(-1))
    total = both[0] + up + down
    part = total[0:QUART]
    for j in range(1, NY):
        part = part + lax.ppermute(total[j * QUART:(j + 1) * QUART], "grp", y_pairs(j))
    mine = [part] + [lax.ppermute(part, "grp", y_pairs(-j)) for j in range(1, NY)]
    other = [lax.ppermute(m, "grp", C_PAIRS) for m in mine]
    new_table, new_accum = update(plan, own_list.reshape(8, LANES), table, accum.reshape(32, LANES),
                                  listed, old, rows, other + mine)
    return (new_table, new_accum.reshape(ROWS_DEV))


def solution(mesh):
    return jax.shard_map(
        body,
        mesh=mesh,
        in_specs=(
            P("shard", None),
            P("shard"),
            P("grp", "shard", None, None),
            P("grp", "shard", None),
            P("grp", "shard", None),
            P("shard", None),
        ),
        out_specs=(P("shard", None), P("shard")),
        check_vma=False,
    )
```

time: 150 us -> 144 us (0.960)
  waiting for transfers between devices: 46.2 us -> 23.4 us
  Pallas kernels: 39.7 us -> 62 us
  starting transfers between devices: 56 us -> 47.1 us
  other arithmetic: 0.52 us -> 3.05 us
    pallas_call x7 -> x11, Pallas kernels: 39.7 us -> 62 us  [the longest x5 23.7 us: gather(): pl.pallas_call(lambda *refs: gather_kernel(*refs, count=count), out_shape...]
    ppermute x24 -> x17, waiting for transfers between devices: 39.8 us -> 18.9 us  [the longest x1 9.96 us: body(): down = lax.ppermute(down, 'shard', x_pairs(-1))]
    ppermute x24 -> x17, starting transfers between devices: 32.8 us -> 27.7 us  [the longest x3 10.9 us: body(): got[k] = lax.ppermute(got[k - 1], 'shard', z_pairs(-1))]
    unnamed x56 -> x40, local copies, waits for them, and re-layouts: 0.79 us -> 4.47 us
    ppermute x3, starting transfers between devices: 11.6 us -> 8.17 us  [body(): lax.ppermute(total[j * QUART:(j + 1) * QUART], 'grp', y_pairs(j))]
    ppermute x3, waiting for transfers between devices: 6.37 us -> 4.51 us  [body(): lax.ppermute(total[j * QUART:(j + 1) * QUART], 'grp', y_pairs(j))]
    broadcast_in_dim x4 -> x1, local copies, waits for them, and re-layouts: 3.99 us -> 2.24 us  [body(): rows = jnp.broadcast_to(stacked, (NX, TOUCH, LANES))]
    ppermute x4, starting transfers between devices: 10.1 us -> 8.49 us  [body(): other = [lax.ppermute(m, 'grp', C_PAIRS) for m in mine]]
  transfers between devices with their start and end apart: 34 -> 27, of which waited for: 14 -> 9; matrix products, arithmetic and copies ran while one was open for 3% -> 2% of each run, Pallas kernels for 13% -> 29%
where the time goes in v3:
time: 144 us
  Pallas kernels  62 us (43%)
  starting transfers between devices  47.1 us (33%)
  waiting for transfers between devices  23.4 us (16%)
  local copies, waits for them, and re-layouts  6.82 us (5%)
  other arithmetic  3.05 us (2%)
    pallas_call x5, Pallas kernels, gather(): pl.pallas_call(lambda *refs: gather_kernel(*refs, count=count), out_shape...  23.7 us
    pallas_call x3, Pallas kernels, sums(): pl.pallas_call(lambda *refs: sums_kernel(*refs, counts=counts, base=base)...  14.2 us
    pallas_call x1, Pallas kernels, update(): pl.pallas_call(update_kernel, grid=(ROWS_DEV // TILE,), out_shape=(jax.Sh...  11.5 us
    ppermute x3, starting transfers between devices, body(): got[k] = lax.ppermute(got[k - 1], 'shard', z_pairs(-1))  10.9 us
    ppermute x1, waiting for transfers between devices, body(): down = lax.ppermute(down, 'shard', x_pairs(-1))  9.96 us
    pallas_call x1, Pallas kernels, listed_values(): pl.pallas_call(listed_kernel, out_shape=(jax.ShapeDtypeStruct((TOUCH, LAN...  9.24 us
    ppermute x4, starting transfers between devices, body(): other = [lax.ppermute(m, 'grp', C_PAIRS) for m in mine]  8.49 us
    ppermute x3, starting transfers between devices, body(): lax.ppermute(total[j * QUART:(j + 1) * QUART], 'grp', y_pairs(j))  8.17 us
  transfers between devices with their start and end apart: 27, of which 9 were waited for; matrix products, arithmetic and copies ran while one was open for 2% of the time, Pallas kernels for 29%

profile of v3, /device:TPU:1, one launch (start us, length us, event | category | flops | bytes accessed | tf_op | source)
XLA Modules:
  0.0 143.5 jit_solution(16698881956397983479)
XLA Ops:
  0.6 2.1 %collective-permute-start.2 = (s32[1024]{0:T(1024)}, s32[1024]{0:T(1024)S(1)}, u32[]{:S(2)}, u32[]{:S(2)}) collective-permute-start(s32[1024]{0:T(1024)} %bitcast.38), channel_id=1, source_target_pairs={{0,1},{1,2},{2,3},{3,0},{4,5},{5,6},{6,7},{7,4},{8,9},{9,10},{10,1... | collective-permute-start | bytes 12296 | tf_op jit(solution)/shard_map/ppermute | solution.py:326
  5.7 3.3 %pack.1.refs_1_ = bf16[256,640]{1,0:T(8,128)(2,1)} custom-call(s32[32,128]{1,0:T(8,128)} %bitcast.55, s32[32,128]{1,0:T(8,128)} %bitcast.56, bf16[512,256]{1,0:T(8,128)(2,1)} %bitcast.54), custom_call_target="tpu_custom_call" | custom-call | flops 2400000000 | bytes 12000000 | tf_op jit(solution)/shard_map/pack/pallas_call | solution.py:85
  9.1 5.6 %collective-permute-start.4 = (bf16[256,640]{1,0:T(8,128)(2,1)}, bf16[256,640]{1,0:T(8,128)(2,1)S(1)}, u32[]{:S(2)}, u32[]{:S(2)}) collective-permute-start(bf16[256,640]{1,0:T(8,128)(2,1)} %pack.1.refs_1_), channel_id=1, source_target_pairs={{0,28},{1,29},{2,30},{3,31},{4,0},{5,1},{6,2},{7,3},{8,4},{9,5},{1... | collective-permute-start | bytes 983048 | tf_op jit(solution)/shard_map/ppermute | solution.py:340
  14.6 3.5 %shard_map.86 = (bf16[1,16,256,128]{3,2,1,0:T(8,128)(2,1)}, s32[1,16,128]{2,1,0:T(8,128)}, s32[1,8,128]{2,1,0:T(8,128)}) custom-call(s32[1]{0:T(128)} %bitcast.13.refs_0_, bf16[256,640]{1,0:T(8,128)(2,1)} %pack.1.refs_1_), custom_call_target="tpu_custom_call" | custom-call | flops 2400000000 | bytes 12000000 | tf_op jit(solution)/shard_map/pallas_call | solution.py:129
  20.5 3.3 %collective-permute-start.6 = (bf16[256,640]{1,0:T(8,128)(2,1)S(1)}, bf16[256,640]{1,0:T(8,128)(2,1)S(1)}, u32[]{:S(2)}, u32[]{:S(2)}) collective-permute-start(bf16[256,640]{1,0:T(8,128)(2,1)S(1)} %collective-permute-done.4.refs_2_), channel_id=1, source_target_pairs={{0,28},{1,29},{2,30},{3,31},{4,0},{5,1},{6,2},{7,3},{8,4},{9,5},{1... | collective-permute-start | bytes 983048 | tf_op jit(solution)/shard_map/ppermute | solution.py:340
  24.6 5.5 %shard_map.87 = (bf16[2,16,256,128]{3,2,1,0:T(8,128)(2,1)}, s32[2,16,128]{2,1,0:T(8,128)}, s32[2,8,128]{2,1,0:T(8,128)}) custom-call(s32[1]{0:T(128)} %bitcast.13.refs_0_, bf16[256,640]{1,0:T(8,128)(2,1)} %copy-done.12, bf16[256,640]{1,0:T(8,128)(2,1)} %copy-done.13), custom_call_target="tpu_custom_call" | custom-call | flops 3600000000 | bytes 18000000 | tf_op jit(solution)/shard_map/pallas_call | solution.py:129
  32.9 5.5 %shard_map.88 = (bf16[2,16,256,128]{3,2,1,0:T(8,128)(2,1)}, s32[2,16,128]{2,1,0:T(8,128)}, s32[2,8,128]{2,1,0:T(8,128)}) custom-call(s32[1]{0:T(128)} %bitcast.13.refs_0_, bf16[256,640]{1,0:T(8,128)(2,1)} %copy-done.16, bf16[256,640]{1,0:T(8,128)(2,1)} %copy-done.14), custom_call_target="tpu_custom_call" | custom-call | flops 3600000000 | bytes 18000000 | tf_op jit(solution)/shard_map/pallas_call | solution.py:129
  40.7 5.5 %shard_map.89 = (bf16[2,16,256,128]{3,2,1,0:T(8,128)(2,1)}, s32[2,16,128]{2,1,0:T(8,128)}, s32[2,8,128]{2,1,0:T(8,128)}) custom-call(s32[1]{0:T(128)} %bitcast.13.refs_0_, bf16[256,640]{1,0:T(8,128)(2,1)} %copy-done.17, bf16[256,640]{1,0:T(8,128)(2,1)} %copy-done.15), custom_call_target="tpu_custom_call" | custom-call | flops 3600000000 | bytes 18000000 | tf_op jit(solution)/shard_map/pallas_call | solution.py:129
  47.3 3.6 %shard_map.90 = (bf16[1,16,256,128]{3,2,1,0:T(8,128)(2,1)}, s32[1,16,128]{2,1,0:T(8,128)}, s32[1,8,128]{2,1,0:T(8,128)}) custom-call(s32[1]{0:T(128)} %bitcast.13.refs_0_, bf16[256,640]{1,0:T(8,128)(2,1)} %copy-done.18), custom_call_target="tpu_custom_call" | custom-call | flops 2400000000 | bytes 12000000 | tf_op jit(solution)/shard_map/pallas_call | solution.py:129
  50.9 2.2 %broadcast_in_dim.2.rows_ref.refs_16_.refs_6_ = s32[4,1024,128]{2,1,0:T(8,128)} broadcast(s32[4,1024]{1,0:T(4,128)S(1)} %pad_add_fusion), dimensions={0,1} | broadcast | bytes 2113536 | tf_op jit(solution)/shard_map/broadcast_in_dim | solution.py:328
  53.1 5.4 %shard_map.92 = (f32[2,512,256]{2,1,0:T(8,128)}, f32[2,512,256]{2,1,0:T(8,128)}) custom-call(s32[5]{0:T(128)} %pad_add_fusion.2.refs_0_, s32[1,8,128]{2,1,0:T(8,128)} %get-tuple-element.29.refs_1_, s32[2,8,128]{2,1,0:T(8,128)} %get-tuple-element.30.refs_2_, s32[2,8,128]{2,1,0:T(8,128)} %get-tuple-element.31.refs_3_, s32[2,8,128]{2,1,0:T(8,128)} %get-tuple-element.32.refs_4_, ...), custom_call_target="tpu_custom_call" | custom-call | flops 3600000000 | bytes 18000000 | tf_op jit(solution)/shard_map/pallas_call | solution.py:196
  58.5 5.7 %collective-permute-start.11 = (f32[2,512,256]{2,1,0:T(8,128)}, f32[2,512,256]{2,1,0:T(8,128)S(1)}, u32[]{:S(2)}, u32[]{:S(2)}) collective-permute-start(f32[2,512,256]{2,1,0:T(8,128)} %get-tuple-element.47), channel_id=1, source_target_pairs={{0,32},{32,0},{64,96},{96,64},{128,160},{160,128},{192,224},{224,1... | collective-permute-start | bytes 3145736 | tf_op jit(solution)/shard_map/ppermute | solution.py:350
  64.2 4.5 %shard_map.93 = (f32[1,512,256]{2,1,0:T(8,128)}, f32[1,512,256]{2,1,0:T(8,128)}) custom-call(s32[5]{0:T(128)} %pad_add_fusion.2.refs_0_, s32[1,8,128]{2,1,0:T(8,128)} %get-tuple-element.29.refs_1_, s32[2,8,128]{2,1,0:T(8,128)} %get-tuple-element.30.refs_2_, s32[2,8,128]{2,1,0:T(8,128)} %get-tuple-element.31.refs_3_, s32[2,8,128]{2,1,0:T(8,128)} %get-tuple-element.32.refs_4_, ...), custom_call_target="tpu_custom_call" | custom-call | flops 1800000000 | bytes 9000000 | tf_op jit(solution)/shard_map/pallas_call | solution.py:196
  68.8 2.1 %collective-permute-done.12 = f32[1,512,256]{2,1,0:T(8,128)S(1)} collective-permute-done((f32[1,512,256]{2,1,0:T(8,128)}, f32[1,512,256]{2,1,0:T(8,128)S(1)}, u32[]{:S(2)}, u32[]{:S(2)}) %collective-permute-start.12) | collective-permute-done | bytes 524320 | tf_op jit(solution)/shard_map/ppermute | solution.py:350
  72.4 2.3 %collective-permute-start.15 = (f32[256,256]{1,0:T(8,128)S(1)}, f32[256,256]{1,0:T(8,128)S(1)}, u32[]{:S(2)}, u32[]{:S(2)}) collective-permute-start(f32[256,256]{1,0:T(8,128)S(1)} %get-tuple-element.60), channel_id=1, source_target_pairs={{0,3},{1,0},{2,1},{3,2},{4,7},{5,4},{6,5},{7,6},{8,11},{9,8},{10,9... | collective-permute-start | bytes 786440 | tf_op jit(solution)/shard_map/ppermute | solution.py:355
  74.8 4.3 %shard_map.91 = (f32[1,512,256]{2,1,0:T(8,128)}, f32[1,512,256]{2,1,0:T(8,128)}) custom-call(s32[5]{0:T(128)} %pad_add_fusion.2.refs_0_, s32[1,8,128]{2,1,0:T(8,128)} %get-tuple-element.29.refs_1_, s32[2,8,128]{2,1,0:T(8,128)} %get-tuple-element.30.refs_2_, s32[2,8,128]{2,1,0:T(8,128)} %get-tuple-element.31.refs_3_, s32[2,8,128]{2,1,0:T(8,128)} %get-tuple-element.32.refs_4_, ...), custom_call_target="tpu_custom_call" | custom-call | flops 1800000000 | bytes 9000000 | tf_op jit(solution)/shard_map/pallas_call | solution.py:196
  81.1 2.5 %collective-permute-start.16 = (f32[512,256]{1,0:T(8,128)S(1)}, f32[512,256]{1,0:T(8,128)S(1)}, u32[]{:S(2)}, u32[]{:S(2)}) collective-permute-start(f32[512,256]{1,0:T(8,128)S(1)} %pad_maximum_fusion.1), channel_id=1, source_target_pairs={{0,3},{1,0},{2,1},{3,2},{4,7},{5,4},{6,5},{7,6},{8,11},{9,8},{10,9... | collective-permute-start | bytes 1572872 | tf_op jit(solution)/shard_map/ppermute | solution.py:359
  83.8 10.0 %collective-permute-done.16 = f32[512,256]{1,0:T(8,128)S(1)} collective-permute-done((f32[512,256]{1,0:T(8,128)S(1)}, f32[512,256]{1,0:T(8,128)S(1)}, u32[]{:S(2)}, u32[]{:S(2)}) %collective-permute-start.16) | collective-permute-done | bytes 524320 | tf_op jit(solution)/shard_map/ppermute | solution.py:359
  93.7 3.2 %collective-permute-done.14 = f32[512,256]{1,0:T(8,128)S(1)} collective-permute-done((f32[512,256]{1,0:T(8,128)S(1)}, f32[512,256]{1,0:T(8,128)S(1)}, u32[]{:S(2)}, u32[]{:S(2)}) %collective-permute-start.14) | collective-permute-done | bytes 524320 | tf_op jit(solution)/shard_map/ppermute | solution.py:358
  98.4 5.7 %collective-permute-start.19 = (f32[128,256]{1,0:T(8,128)S(1)}, f32[128,256]{1,0:T(8,128)S(1)}, u32[]{:S(2)}, u32[]{:S(2)}) collective-permute-start(f32[128,256]{1,0:T(8,128)S(1)} %get-tuple-element.57), channel_id=1, source_target_pairs={{0,192},{32,224},{64,0},{96,32},{128,64},{160,96},{192,128},{224,1... | collective-permute-start | bytes 393224 | tf_op jit(solution)/shard_map/ppermute | solution.py:363
  106.4 3.5 %collective-permute-done.18 = f32[128,256]{1,0:T(8,128)S(1)} collective-permute-done((f32[128,256]{1,0:T(8,128)S(1)}, f32[128,256]{1,0:T(8,128)S(1)}, u32[]{:S(2)}, u32[]{:S(2)}) %collective-permute-start.18) | collective-permute-done | bytes 131104 | tf_op jit(solution)/shard_map/ppermute | solution.py:363
  113.3 4.7 %collective-permute-start.20 = (f32[128,256]{1,0:T(8,128)S(1)}, f32[128,256]{1,0:T(8,128)S(1)}, u32[]{:S(2)}, u32[]{:S(2)}) collective-permute-start(f32[128,256]{1,0:T(8,128)S(1)} %fusion.4.refs_11_), channel_id=1, source_target_pairs={{0,32},{32,0},{64,96},{96,64},{128,160},{160,128},{192,224},{224,1... | collective-permute-start | bytes 393224 | tf_op jit(solution)/shard_map/ppermute | solution.py:365
  121.9 9.2 %listed_values.1 = (f32[1024,128]{1,0:T(8,128)}, f32[1024,256]{1,0:T(8,128)}) custom-call(s32[8,128]{1,0:T(8,128)} %bitcast.47, s32[4,1024,128]{2,1,0:T(8,128)} %broadcast_in_dim.2.rows_ref.refs_16_.refs_6_, f32[32,128]{1,0:T(8,128)} %bitcast.44, f32[4096,256]{1,0:T(8,128)} %refs_2_.1), custom_call_target="tpu_custom_call" | custom-call | flops 4200000000 | bytes 21000000 | tf_op jit(solution)/shard_map/listed_values/pallas_call | solution.py:229
  131.9 11.5 %update.1 = (f32[4096,256]{1,0:T(8,128)}, f32[32,128]{1,0:T(8,128)}) custom-call(s32[24]{0:T(128)} %pad_add_fusion.1.refs_0_, s32[8,128]{1,0:T(8,128)} %bitcast.41, f32[4096,256]{1,0:T(8,128)} %refs_2_.1, f32[32,128]{1,0:T(8,128)} %bitcast.45, f32[1024,128]{1,0:T(8,128)} %get-tuple-element.27.refs_4_, f32[1024,256]{1,0:T(8,128)} %get-tuple-element.28.refs_5_, ...), custom_call_target="tpu_custom_call" | custom-call | tf_op jit(solution)/shard_map/update/pallas_call | solution.py:283
  (105 shorter events, 27.5 us)
Async XLA Ops:
  0.6 18.2 %collective-permute-start.2 = (s32[1024]{0:T(1024)}, s32[1024]{0:T(1024)S(1)}, u32[]{:S(2)}, u32[]{:S(2)}) collective-permute-start(s32[1024]{0:T(1024)} %bitcast.38), channel_id=1, source_target_pairs={{0,1},{1,2},{2,3},{3,0},{4,5},{5,6},{6,7},{7,4},{8,9},{9,10},{10,1... | collective-permute-start | bytes 12296 | tf_op jit(solution)/shard_map/ppermute | solution.py:326
  2.7 16.1 %collective-permute-start.1 = (s32[1024]{0:T(1024)}, s32[1024]{0:T(1024)S(1)}, u32[]{:S(2)}, u32[]{:S(2)}) collective-permute-start(s32[1024]{0:T(1024)} %bitcast.39), channel_id=1, source_target_pairs={{0,3},{1,0},{2,1},{3,2},{4,7},{5,4},{6,5},{7,6},{8,11},{9,8},{10,9... | collective-permute-start | bytes 12296 | tf_op jit(solution)/shard_map/ppermute | solution.py:326
  4.1 14.8 %collective-permute-start = (s32[1024]{0:T(1024)}, s32[1024]{0:T(1024)S(1)}, u32[]{:S(2)}, u32[]{:S(2)}) collective-permute-start(s32[1024]{0:T(1024)} %bitcast.40), channel_id=1, source_target_pairs={{0,2},{1,3},{2,0},{3,1},{4,6},{5,7},{6,4},{7,5},{8,10},{9,11},{10,... | collective-permute-start | bytes 12296 | tf_op jit(solution)/shard_map/ppermute | solution.py:326
  9.1 11.4 %collective-permute-start.4 = (bf16[256,640]{1,0:T(8,128)(2,1)}, bf16[256,640]{1,0:T(8,128)(2,1)S(1)}, u32[]{:S(2)}, u32[]{:S(2)}) collective-permute-start(bf16[256,640]{1,0:T(8,128)(2,1)} %pack.1.refs_1_), channel_id=1, source_target_pairs={{0,28},{1,29},{2,30},{3,31},{4,0},{5,1},{6,2},{7,3},{8,4},{9,5},{1... | collective-permute-start | bytes 983048 | tf_op jit(solution)/shard_map/ppermute | solution.py:340
  14.6 9.2 %collective-permute-start.3 = (bf16[256,640]{1,0:T(8,128)(2,1)}, bf16[256,640]{1,0:T(8,128)(2,1)S(1)}, u32[]{:S(2)}, u32[]{:S(2)}) collective-permute-start(bf16[256,640]{1,0:T(8,128)(2,1)} %pack.1.refs_1_), channel_id=1, source_target_pairs={{0,4},{1,5},{2,6},{3,7},{4,8},{5,9},{6,10},{7,11},{8,12},{9,13},{1... | collective-permute-start | bytes 983048 | tf_op jit(solution)/shard_map/ppermute | solution.py:338
  20.5 9.6 %collective-permute-start.6 = (bf16[256,640]{1,0:T(8,128)(2,1)S(1)}, bf16[256,640]{1,0:T(8,128)(2,1)S(1)}, u32[]{:S(2)}, u32[]{:S(2)}) collective-permute-start(bf16[256,640]{1,0:T(8,128)(2,1)S(1)} %collective-permute-done.4.refs_2_), channel_id=1, source_target_pairs={{0,28},{1,29},{2,30},{3,31},{4,0},{5,1},{6,2},{7,3},{8,4},{9,5},{1... | collective-permute-start | bytes 983048 | tf_op jit(solution)/shard_map/ppermute | solution.py:340
  23.8 8.3 %collective-permute-start.5 = (bf16[256,640]{1,0:T(8,128)(2,1)S(1)}, bf16[256,640]{1,0:T(8,128)(2,1)S(1)}, u32[]{:S(2)}, u32[]{:S(2)}) collective-permute-start(bf16[256,640]{1,0:T(8,128)(2,1)S(1)} %collective-permute-done.3.refs_1_), channel_id=1, source_target_pairs={{0,4},{1,5},{2,6},{3,7},{4,8},{5,9},{6,10},{7,11},{8,12},{9,13},{1... | collective-permute-start | bytes 983048 | tf_op jit(solution)/shard_map/ppermute | solution.py:338
  30.1 9.2 %collective-permute-start.8 = (bf16[256,640]{1,0:T(8,128)(2,1)S(1)}, bf16[256,640]{1,0:T(8,128)(2,1)S(1)}, u32[]{:S(2)}, u32[]{:S(2)}) collective-permute-start(bf16[256,640]{1,0:T(8,128)(2,1)S(1)} %collective-permute-done.6.refs_2_), channel_id=1, source_target_pairs={{0,28},{1,29},{2,30},{3,31},{4,0},{5,1},{6,2},{7,3},{8,4},{9,5},{1... | collective-permute-start | bytes 983048 | tf_op jit(solution)/shard_map/ppermute | solution.py:340
  32.1 7.1 %collective-permute-start.7 = (bf16[256,640]{1,0:T(8,128)(2,1)S(1)}, bf16[256,640]{1,0:T(8,128)(2,1)S(1)}, u32[]{:S(2)}, u32[]{:S(2)}) collective-permute-start(bf16[256,640]{1,0:T(8,128)(2,1)S(1)} %collective-permute-done.5.refs_1_), channel_id=1, source_target_pairs={{0,4},{1,5},{2,6},{3,7},{4,8},{5,9},{6,10},{7,11},{8,12},{9,13},{1... | collective-permute-start | bytes 983048 | tf_op jit(solution)/shard_map/ppermute | solution.py:338
  39.3 7.3 %collective-permute-start.9 = (bf16[256,640]{1,0:T(8,128)(2,1)S(1)}, bf16[256,640]{1,0:T(8,128)(2,1)S(1)}, u32[]{:S(2)}, u32[]{:S(2)}) collective-permute-start(bf16[256,640]{1,0:T(8,128)(2,1)S(1)} %collective-permute-done.7.refs_1_), channel_id=1, source_target_pairs={{0,4},{1,5},{2,6},{3,7},{4,8},{5,9},{6,10},{7,11},{8,12},{9,13},{1... | collective-permute-start | bytes 983048 | tf_op jit(solution)/shard_map/ppermute | solution.py:338
  58.5 21.2 %collective-permute-start.11 = (f32[2,512,256]{2,1,0:T(8,128)}, f32[2,512,256]{2,1,0:T(8,128)S(1)}, u32[]{:S(2)}, u32[]{:S(2)}) collective-permute-start(f32[2,512,256]{2,1,0:T(8,128)} %get-tuple-element.47), channel_id=1, source_target_pairs={{0,32},{32,0},{64,96},{96,64},{128,160},{160,128},{192,224},{224,1... | collective-permute-start | bytes 3145736 | tf_op jit(solution)/shard_map/ppermute | solution.py:350
  72.0 9.0 %collective-permute-start.13 = (f32[256,256]{1,0:T(8,128)S(1)}, f32[256,256]{1,0:T(8,128)S(1)}, u32[]{:S(2)}, u32[]{:S(2)}) collective-permute-start(f32[256,256]{1,0:T(8,128)S(1)} %get-tuple-element.59), channel_id=1, source_target_pairs={{0,1},{1,2},{2,3},{3,0},{4,5},{5,6},{6,7},{7,4},{8,9},{9,10},{10,1... | collective-permute-start | bytes 786440 | tf_op jit(solution)/shard_map/ppermute | solution.py:354
  72.4 8.6 %collective-permute-start.15 = (f32[256,256]{1,0:T(8,128)S(1)}, f32[256,256]{1,0:T(8,128)S(1)}, u32[]{:S(2)}, u32[]{:S(2)}) collective-permute-start(f32[256,256]{1,0:T(8,128)S(1)} %get-tuple-element.60), channel_id=1, source_target_pairs={{0,3},{1,0},{2,1},{3,2},{4,7},{5,4},{6,5},{7,6},{8,11},{9,8},{10,9... | collective-permute-start | bytes 786440 | tf_op jit(solution)/shard_map/ppermute | solution.py:355
  81.1 12.6 %collective-permute-start.16 = (f32[512,256]{1,0:T(8,128)S(1)}, f32[512,256]{1,0:T(8,128)S(1)}, u32[]{:S(2)}, u32[]{:S(2)}) collective-permute-start(f32[512,256]{1,0:T(8,128)S(1)} %pad_maximum_fusion.1), channel_id=1, source_target_pairs={{0,3},{1,0},{2,1},{3,2},{4,7},{5,4},{6,5},{7,6},{8,11},{9,8},{10,9... | collective-permute-start | bytes 1572872 | tf_op jit(solution)/shard_map/ppermute | solution.py:359
  83.7 13.2 %collective-permute-start.14 = (f32[512,256]{1,0:T(8,128)S(1)}, f32[512,256]{1,0:T(8,128)S(1)}, u32[]{:S(2)}, u32[]{:S(2)}) collective-permute-start(f32[512,256]{1,0:T(8,128)S(1)} %pad_maximum_fusion), channel_id=1, source_target_pairs={{0,1},{1,2},{2,3},{3,0},{4,5},{5,6},{6,7},{7,4},{8,9},{9,10},{10,1... | collective-permute-start | bytes 1572872 | tf_op jit(solution)/shard_map/ppermute | solution.py:358
  97.0 9.3 %collective-permute-start.17 = (f32[128,256]{1,0:T(8,128)S(1)}, f32[128,256]{1,0:T(8,128)S(1)}, u32[]{:S(2)}, u32[]{:S(2)}) collective-permute-start(f32[128,256]{1,0:T(8,128)S(1)} %get-tuple-element.56), channel_id=1, source_target_pairs={{0,64},{32,96},{64,128},{96,160},{128,192},{160,224},{192,0},{224,... | collective-permute-start | bytes 393224 | tf_op jit(solution)/shard_map/ppermute | solution.py:363
  98.4 8.0 %collective-permute-start.19 = (f32[128,256]{1,0:T(8,128)S(1)}, f32[128,256]{1,0:T(8,128)S(1)}, u32[]{:S(2)}, u32[]{:S(2)}) collective-permute-start(f32[128,256]{1,0:T(8,128)S(1)} %get-tuple-element.57), channel_id=1, source_target_pairs={{0,192},{32,224},{64,0},{96,32},{128,64},{160,96},{192,128},{224,1... | collective-permute-start | bytes 393224 | tf_op jit(solution)/shard_map/ppermute | solution.py:363
  110.0 8.1 %collective-permute-start.25 = (f32[128,256]{1,0:T(8,128)S(1)}, f32[128,256]{1,0:T(8,128)S(1)}, u32[]{:S(2)}, u32[]{:S(2)}) collective-permute-start(f32[128,256]{1,0:T(8,128)S(1)} %fusion.4.refs_11_), channel_id=1, source_target_pairs={{0,64},{32,96},{64,128},{96,160},{128,192},{160,224},{192,0},{224,... | collective-permute-start | bytes 393224 | tf_op jit(solution)/shard_map/ppermute | solution.py:364
  110.1 9.5 %collective-permute-start.23 = (f32[128,256]{1,0:T(8,128)S(1)}, f32[128,256]{1,0:T(8,128)S(1)}, u32[]{:S(2)}, u32[]{:S(2)}) collective-permute-start(f32[128,256]{1,0:T(8,128)S(1)} %fusion.4.refs_11_), channel_id=1, source_target_pairs={{0,128},{32,160},{64,192},{96,224},{128,0},{160,32},{192,64},{224,... | collective-permute-start | bytes 393224 | tf_op jit(solution)/shard_map/ppermute | solution.py:364
  112.1 9.0 %collective-permute-start.21 = (f32[128,256]{1,0:T(8,128)S(1)}, f32[128,256]{1,0:T(8,128)S(1)}, u32[]{:S(2)}, u32[]{:S(2)}) collective-permute-start(f32[128,256]{1,0:T(8,128)S(1)} %fusion.4.refs_11_), channel_id=1, source_target_pairs={{0,192},{32,224},{64,0},{96,32},{128,64},{160,96},{192,128},{224,1... | collective-permute-start | bytes 393224 | tf_op jit(solution)/shard_map/ppermute | solution.py:364
  113.3 17.8 %collective-permute-start.20 = (f32[128,256]{1,0:T(8,128)S(1)}, f32[128,256]{1,0:T(8,128)S(1)}, u32[]{:S(2)}, u32[]{:S(2)}) collective-permute-start(f32[128,256]{1,0:T(8,128)S(1)} %fusion.4.refs_11_), channel_id=1, source_target_pairs={{0,32},{32,0},{64,96},{96,64},{128,160},{160,128},{192,224},{224,1... | collective-permute-start | bytes 393224 | tf_op jit(solution)/shard_map/ppermute | solution.py:365
  118.1 13.0 %collective-permute-start.26 = (f32[128,256]{1,0:T(8,128)S(1)}, f32[128,256]{1,0:T(8,128)S(1)}, u32[]{:S(2)}, u32[]{:S(2)}) collective-permute-start(f32[128,256]{1,0:T(8,128)S(1)} %collective-permute-done.25.refs_14_), channel_id=1, source_target_pairs={{0,32},{32,0},{64,96},{96,64},{128,160},{160,128},{192,224},{224,1... | collective-permute-start | bytes 393224 | tf_op jit(solution)/shard_map/ppermute | solution.py:365
  119.6 11.6 %collective-permute-start.24 = (f32[128,256]{1,0:T(8,128)S(1)}, f32[128,256]{1,0:T(8,128)S(1)}, u32[]{:S(2)}, u32[]{:S(2)}) collective-permute-start(f32[128,256]{1,0:T(8,128)S(1)} %collective-permute-done.23.refs_13_), channel_id=1, source_target_pairs={{0,32},{32,0},{64,96},{96,64},{128,160},{160,128},{192,224},{224,1... | collective-permute-start | bytes 393224 | tf_op jit(solution)/shard_map/ppermute | solution.py:365
  121.2 10.0 %collective-permute-start.22 = (f32[128,256]{1,0:T(8,128)S(1)}, f32[128,256]{1,0:T(8,128)S(1)}, u32[]{:S(2)}, u32[]{:S(2)}) collective-permute-start(f32[128,256]{1,0:T(8,128)S(1)} %collective-permute-done.21.refs_12_), channel_id=1, source_target_pairs={{0,32},{32,0},{64,96},{96,64},{128,160},{160,128},{192,224},{224,1... | collective-permute-start | bytes 393224 | tf_op jit(solution)/shard_map/ppermute | solution.py:365
  (23 other events, 122.6 us)

commit v4 on v3

--- a/solution.py
+++ b/solution.py
@@ -24,7 +24,9 @@
 NT = (((1,), (1,)), ((), ()))
 TN = (((0,), (0,)), ((), ()))
 ORDER = (2, 1, 3, 0)
-OWN_ROWS = pl.BlockSpec((1, TOUCH, LANES), lambda i: (3, 0, 0))
+SMEM = pl.BlockSpec(memory_space=pltpu.SMEM)
+VMEM = pl.BlockSpec(memory_space=pltpu.VMEM)
+PARAMS = pltpu.CompilerParams(vmem_limit_bytes=26 << 20)
 
 
 def iota(shape, dim):
@@ -89,6 +91,7 @@
                         pltpu.VMEM((LANES, LOOK), BF16),
                         pltpu.VMEM((TOUCH, 2 * LANES), BF16)],
         cost_estimate=cost(4),
+        compiler_params=PARAMS,
         name="pack",
     )(ids, bags, grads)
 
@@ -125,59 +128,58 @@
 
 def gather(z, packets):
     count = len(packets)
-    vmem = pl.BlockSpec(memory_space=pltpu.VMEM)
     return pl.pallas_call(
         lambda *refs: gather_kernel(*refs, count=count),
         out_shape=(jax.ShapeDtypeStruct((count, 16, E, LANES), BF16),
                    jax.ShapeDtypeStruct((count, 16, LANES), I32),
                    jax.ShapeDtypeStruct((count, 8, LANES), I32)),
-        in_specs=[pl.BlockSpec(memory_space=pltpu.SMEM)] + [vmem] * count,
+        in_specs=[SMEM] + [VMEM] * count,
         scratch_shapes=[pltpu.VMEM((count, BLOCKS, LANES), I32), pltpu.SMEM((count, 8, LANES), I32),
                         pltpu.SemaphoreType.DMA((count,))],
-        cost_estimate=cost(2 + 2 * count),
+        cost_estimate=cost(2 + count),
+        compiler_params=PARAMS,
     )(z, *packets)
 
 
-def sums_kernel(at_ref, *refs, counts, base):
+def sums_kernel(at_ref, *refs, counts, base, many):
     groups = len(counts)
     metas, xs, keys = refs[0:groups], refs[groups:2 * groups], refs[2 * groups:3 * groups]
     rows_ref, send_ref, keep_ref, all_ref, k_ref = refs[3 * groups:]
-    column = at_ref[base + pl.program_id(0)]
-    shard = at_ref[4] + column
-    filled = jnp.int32(0)
-    for n in range(groups):
-        for d in range(counts[n]):
-            many = metas[n][d, 1, shard]
-
-            def move(j, _, n=n, d=d, filled=filled):
-                all_ref[filled + j] = xs[n][d, j]
-                k_ref[pl.ds(filled + j, 1), :] = keys[n][d, pl.ds(4 * column + j, 1), :]
-                return 0
-
-            lax.fori_loop(0, many, move, 0)
-            filled = filled + many
-    rounds = (filled + 7) >> 3
-
-    def blank(j, _):
-        all_ref[j] = jnp.zeros((E, LANES), BF16)
-        k_ref[pl.ds(j, 1), :] = jnp.full((1, LANES), -1, I32)
-        return 0
-
-    lax.fori_loop(filled, rounds * 8, blank, 0)
-    outs = (send_ref.at[0], keep_ref.at[0])
-    for out in outs:
-        out[...] = jnp.zeros((HALF, E), F32)
-
-    def accumulate(r, _):
-        wide = jnp.concatenate([all_ref[8 * r + j] for j in range(8)], axis=1)
-        lines = [k_ref[pl.ds(8 * r + j, 1), :] for j in range(8)]
-        for h in range(2):
-            mine = rows_ref[0, h * HALF:(h + 1) * HALF, :]
-            hits = jnp.concatenate([one_hot(mine == line) for line in lines], axis=1)
-            outs[h][...] += lax.dot_general(hits, wide, NT, preferred_element_type=F32)
-        return 0
-
-    lax.fori_loop(0, rounds, accumulate, 0)
+    for m in range(many):
+        column = at_ref[base + m]
+        filled = jnp.int32(0)
+        for n in range(groups):
+            for d in range(counts[n]):
+                found = metas[n][d, 1, at_ref[4] + column]
+
+                def move(j, _, n=n, d=d, filled=filled, column=column):
+                    all_ref[filled + j] = xs[n][d, 4 * column + j]
+                    k_ref[pl.ds(filled + j, 1), :] = keys[n][d, pl.ds(4 * column + j, 1), :]
+                    return 0
+
+                lax.fori_loop(0, found, move, 0)
+                filled = filled + found
+        rounds = (filled + 7) >> 3
+
+        def blank(j, _):
+            all_ref[j] = jnp.zeros((E, LANES), BF16)
+            k_ref[pl.ds(j, 1), :] = jnp.full((1, LANES), -1, I32)
+            return 0
+
+        lax.fori_loop(filled, rounds * 8, blank, 0)
+        send_ref[m] = jnp.zeros((HALF, E), F32)
+        keep_ref[m] = jnp.zeros((HALF, E), F32)
+
+        def accumulate(r, _, m=m):
+            wide = jnp.concatenate([all_ref[8 * r + j] for j in range(8)], axis=1)
+            lines = [k_ref[pl.ds(8 * r + j, 1), :] for j in range(8)]
+            for h, out_ref in enumerate((send_ref, keep_ref)):
+                mine = rows_ref[base + m, h * HALF:(h + 1) * HALF, :]
+                hits = jnp.concatenate([one_hot(mine == line) for line in lines], axis=1)
+                out_ref[m] += lax.dot_general(hits, wide, NT, preferred_element_type=F32)
+            return 0
+
+        lax.fori_loop(0, rounds, accumulate, 0)
 
 
 def cost(us):
@@ -187,28 +189,18 @@
 def sums(at, base, many, gathered, rows):
     counts = tuple(g[0].shape[0] for g in gathered)
     total = sum(counts)
-    smem = pl.BlockSpec(memory_space=pltpu.SMEM)
-    out = pl.BlockSpec((1, HALF, E), lambda k, at: (k, 0, 0))
-    in_specs = [smem] * len(counts)
-    in_specs += [pl.BlockSpec((n, 4, E, LANES), lambda k, at: (0, at[base + k], 0, 0)) for n in counts]
-    in_specs += [pl.BlockSpec((n, 16, LANES), lambda k, at: (0, 0, 0)) for n in counts]
-    in_specs += [pl.BlockSpec((1, TOUCH, LANES), lambda k, at: (base + k, 0, 0))]
-    return pl.pallas_call(
-        lambda *refs: sums_kernel(*refs, counts=counts, base=base),
-        grid_spec=pltpu.PrefetchScalarGridSpec(
-            num_scalar_prefetch=1,
-            grid=(many,),
-            in_specs=in_specs,
-            out_specs=[out, out],
-            scratch_shapes=[pltpu.VMEM((4 * total, E, LANES), BF16), pltpu.VMEM((4 * total, LANES), I32)],
-        ),
+    return pl.pallas_call(
+        lambda *refs: sums_kernel(*refs, counts=counts, base=base, many=many),
+        in_specs=[SMEM] * (1 + len(counts)) + [VMEM] * (2 * len(counts) + 1),
+        scratch_shapes=[pltpu.VMEM((4 * total, E, LANES), BF16), pltpu.VMEM((4 * total, LANES), I32)],
         out_shape=[jax.ShapeDtypeStruct((many, HALF, E), F32)] * 2,
-        cost_estimate=cost(3 * many),
+        cost_estimate=cost(2 * many),
+        compiler_params=PARAMS,
     )(at, *[g[2] for g in gathered], *[g[0] for g in gathered], *[g[1] for g in gathered], rows)
 
 
 def listed_kernel(list_ref, rows_ref, accum_ref, table_ref, accum_out, table_out):
-    rows = rows_ref[0]
+    rows = rows_ref[NX - 1]
     hi = jnp.where((rows >> 7) == iota((TOUCH, LANES), 1), 1.0, 0.0)
     padded = jnp.concatenate([accum_ref[...], jnp.zeros((LANES - 32, LANES), F32)], axis=0)
     line = jnp.dot(hi, padded, precision=lax.Precision.HIGHEST, preferred_element_type=F32)
@@ -225,13 +217,12 @@
 
 
 def listed_values(order, rows, accum, table):
-    vmem = pl.BlockSpec(memory_space=pltpu.VMEM)
     return pl.pallas_call(
         listed_kernel,
         out_shape=(jax.ShapeDtypeStruct((TOUCH, LANES), F32), jax.ShapeDtypeStruct((TOUCH, E), F32)),
-        grid=(1,),
-        in_specs=[pl.BlockSpec(memory_space=pltpu.SMEM), OWN_ROWS, vmem, vmem],
-        cost_estimate=cost(7),
+        in_specs=[SMEM, VMEM, VMEM, VMEM],
+        cost_estimate=cost(6),
+        compiler_params=PARAMS,
         name="listed_values",
     )(order, rows, accum, table)
 
@@ -252,14 +243,14 @@
             now = listed_ref[at, 0:1] + mean
             place = pl.multiple_of(plan_ref[16 + n] * QUART, QUART)
             u_ref[pl.ds(place, QUART), :] = old_ref[at, :] - 0.5 * g / (jnp.sqrt(now) + 1e-08)
-            rows = rows_ref[0, at, :]
+            rows = rows_ref[NX - 1, at, :]
             lhs_ref[at, :] = jnp.where((rows >> 7) == lane, mean, 0.0)
             rhs_ref[at, :] = jnp.where((rows & (LANES - 1)) == lane, 1.0, 0.0)
         added = lax.dot_general(lhs_ref[...], rhs_ref[...], TN, precision=lax.Precision.HIGHEST,
                                 preferred_element_type=F32)
         accum_out[...] = accum_ref[...] + added[0:32, :]
 
-    table_out[...] = table_ref[...]
+    table_out[...] = table_ref[pl.ds(pl.multiple_of(block * TILE, TILE), TILE), :]
     first, last = plan_ref[block], plan_ref[block + 1]
 
     def put(n):
@@ -277,18 +268,15 @@
 
 
 def update(plan, natural, table, accum, listed, old, rows, chunks):
-    smem = pl.BlockSpec(memory_space=pltpu.SMEM)
-    tile = pl.BlockSpec((TILE, E), lambda i: (i, 0))
-    whole = lambda *shape: pl.BlockSpec(shape, lambda i: (0,) * len(shape))
     return pl.pallas_call(
         update_kernel,
         grid=(ROWS_DEV // TILE,),
         out_shape=(jax.ShapeDtypeStruct((ROWS_DEV, E), F32), jax.ShapeDtypeStruct((32, LANES), F32)),
-        in_specs=[smem, smem, tile, whole(32, LANES), whole(TOUCH, LANES), whole(TOUCH, E), OWN_ROWS]
-        + [whole(QUART, E)] * 8,
-        out_specs=(tile, whole(32, LANES)),
+        in_specs=[SMEM, SMEM] + [VMEM] * 13,
+        out_specs=(pl.BlockSpec((TILE, E), lambda i: (i, 0)), pl.BlockSpec((32, LANES), lambda i: (0, 0))),
         scratch_shapes=[pltpu.VMEM((TOUCH, E), F32), pltpu.VMEM((TOUCH, LANES), F32),
                         pltpu.VMEM((TOUCH, LANES), F32)],
+        compiler_params=PARAMS,
         name="update",
     )(plan, natural, table, accum, listed, old, rows, *chunks)
 
@@ -342,6 +330,7 @@
     for sources in ((0,), (-1, 1), (-2, 2), (-3, 3), (-4,)):
         gathered.append(gather(z.reshape(1), [got[k] for k in sources]))
 
+    table = pltpu.with_memory_space_constraint(table, pltpu.VMEM)
     listed, old = listed_values(order, rows, accum.reshape(32, LANES), table)
     at = jnp.concatenate([(x + jnp.array(ORDER, I32)) % NX, (NX * z).reshape(1)])
     both = {}

time: 144 us -> 128 us (0.89)
  Pallas kernels: 62 us -> 36.1 us
  waiting for transfers between devices: 23.4 us -> 36.9 us
  other arithmetic: 3.05 us -> 1.06 us
    ppermute x4, waiting for transfers between devices: 1.12 us -> 14.5 us  [body(): got[-k] = lax.ppermute(got[1 - k], 'shard', z_pairs(1))]
    pallas_call x5, Pallas kernels: 23.7 us -> 12.3 us  [gather(): pl.pallas_call(lambda *refs: gather_kernel(*refs, count=count), out_shape...]
    pallas_call x3, Pallas kernels: 14.2 us -> 7.08 us  [sums(): pl.pallas_call(lambda *refs: sums_kernel(*refs, counts=counts, base=base,...]
    pallas_call x1, Pallas kernels: 9.24 us -> 6.28 us  [listed_values(): pl.pallas_call(listed_kernel, out_shape=(jax.ShapeDtypeStruct((TOUCH, LAN...]
    pallas_call x1, Pallas kernels: 11.5 us -> 8.84 us  [update(): pl.pallas_call(update_kernel, grid=(ROWS_DEV // TILE,), out_shape=(jax.Sh...]
    ppermute x1, waiting for transfers between devices: 1.03 us -> 3.19 us  [body(): low = lax.ppermute(both[2][:HALF // 2], 'shard', x_pairs(1))]
    ppermute x3, starting transfers between devices: 8.17 us -> 6.16 us  [body(): lax.ppermute(total[j * QUART:(j + 1) * QUART], 'grp', y_pairs(j))]
    pallas_call x1, Pallas kernels: 3.33 us -> 1.61 us  [pack(): pl.pallas_call(pack_kernel, out_shape=jax.ShapeDtypeStruct((E, WIDTH), BF...]
  transfers between devices with their start and end apart: 27 -> 27, of which waited for: 9 -> 10; matrix products, arithmetic and copies ran while one was open for 2% -> 1% of each run, Pallas kernels for 29% -> 18%
where the time goes in v4:
time: 128 us
  starting transfers between devices  46.8 us (37%)
  waiting for transfers between devices  36.9 us (29%)
  Pallas kernels  36.1 us (28%)
  local copies, waits for them, and re-layouts  5.94 us (5%)
    ppermute x4, waiting for transfers between devices, body(): got[-k] = lax.ppermute(got[1 - k], 'shard', z_pairs(1))  14.5 us
    pallas_call x5, Pallas kernels, gather(): pl.pallas_call(lambda *refs: gather_kernel(*refs, count=count), out_shape...  12.3 us
    ppermute x3, starting transfers between devices, body(): got[k] = lax.ppermute(got[k - 1], 'shard', z_pairs(-1))  11.1 us
    ppermute x1, waiting for transfers between devices, body(): down = lax.ppermute(down, 'shard', x_pairs(-1))  9.95 us
    ppermute x4, starting transfers between devices, body(): other = [lax.ppermute(m, 'grp', C_PAIRS) for m in mine]  8.94 us
    pallas_call x1, Pallas kernels, update(): pl.pallas_call(update_kernel, grid=(ROWS_DEV // TILE,), out_shape=(jax.Sh...  8.84 us
    pallas_call x3, Pallas kernels, sums(): pl.pallas_call(lambda *refs: sums_kernel(*refs, counts=counts, base=base,...  7.08 us
    ppermute x3, starting transfers between devices, body(): swapped = lax.ppermute(send, 'grp', C_PAIRS)  6.99 us
  transfers between devices with their start and end apart: 27, of which 10 were waited for; matrix products, arithmetic and copies ran while one was open for 1% of the time, Pallas kernels for 18%

profile of v4, /device:TPU:1, one launch (start us, length us, event | category | flops | bytes accessed | tf_op | source)
XLA Modules:
  0.0 127.7 jit_solution(4302129715782148940)
XLA Ops:
  0.6 2.1 %collective-permute-start.2 = (s32[1024]{0:T(1024)}, s32[1024]{0:T(1024)S(1)}, u32[]{:S(2)}, u32[]{:S(2)}) collective-permute-start(s32[1024]{0:T(1024)} %bitcast.38), channel_id=1, source_target_pairs={{0,1},{1,2},{2,3},{3,0},{4,5},{5,6},{6,7},{7,4},{8,9},{9,10},{10,1... | collective-permute-start | bytes 12296 | tf_op jit(solution)/shard_map/ppermute | solution.py:314
  9.7 5.7 %collective-permute-start.4 = (bf16[256,640]{1,0:T(8,128)(2,1)S(1)}, bf16[256,640]{1,0:T(8,128)(2,1)S(1)}, u32[]{:S(2)}, u32[]{:S(2)}) collective-permute-start(bf16[256,640]{1,0:T(8,128)(2,1)S(1)} %pack.1.refs_1_), channel_id=1, source_target_pairs={{0,28},{1,29},{2,30},{3,31},{4,0},{5,1},{6,2},{7,3},{8,4},{9,5},{1... | collective-permute-start | bytes 983048 | tf_op jit(solution)/shard_map/ppermute | solution.py:328
  17.1 7.0 %collective-permute-done.3.refs_1_ = bf16[256,640]{1,0:T(8,128)(2,1)S(1)} collective-permute-done((bf16[256,640]{1,0:T(8,128)(2,1)S(1)}, bf16[256,640]{1,0:T(8,128)(2,1)S(1)}, u32[]{:S(2)}, u32[]{:S(2)}) %collective-permute-start.3) | collective-permute-done | bytes 327712 | tf_op jit(solution)/shard_map/ppermute | solution.py:326
  24.1 2.7 %collective-permute-start.6 = (bf16[256,640]{1,0:T(8,128)(2,1)S(1)}, bf16[256,640]{1,0:T(8,128)(2,1)S(1)}, u32[]{:S(2)}, u32[]{:S(2)}) collective-permute-start(bf16[256,640]{1,0:T(8,128)(2,1)S(1)} %collective-permute-done.4.refs_2_), channel_id=1, source_target_pairs={{0,28},{1,29},{2,30},{3,31},{4,0},{5,1},{6,2},{7,3},{8,4},{9,5},{1... | collective-permute-start | bytes 983048 | tf_op jit(solution)/shard_map/ppermute | solution.py:328
  26.9 5.0 %collective-permute-done.5.refs_1_ = bf16[256,640]{1,0:T(8,128)(2,1)S(1)} collective-permute-done((bf16[256,640]{1,0:T(8,128)(2,1)S(1)}, bf16[256,640]{1,0:T(8,128)(2,1)S(1)}, u32[]{:S(2)}, u32[]{:S(2)}) %collective-permute-start.5) | collective-permute-done | bytes 327712 | tf_op jit(solution)/shard_map/ppermute | solution.py:326
  31.9 2.7 %collective-permute-start.8 = (bf16[256,640]{1,0:T(8,128)(2,1)S(1)}, bf16[256,640]{1,0:T(8,128)(2,1)S(1)}, u32[]{:S(2)}, u32[]{:S(2)}) collective-permute-start(bf16[256,640]{1,0:T(8,128)(2,1)S(1)} %collective-permute-done.6.refs_2_), channel_id=1, source_target_pairs={{0,28},{1,29},{2,30},{3,31},{4,0},{5,1},{6,2},{7,3},{8,4},{9,5},{1... | collective-permute-start | bytes 983048 | tf_op jit(solution)/shard_map/ppermute | solution.py:328
  34.7 3.1 %shard_map.87 = (bf16[2,16,256,128]{3,2,1,0:T(8,128)(2,1)S(1)}, s32[2,16,128]{2,1,0:T(8,128)S(1)}, s32[2,8,128]{2,1,0:T(8,128)S(1)}) custom-call(s32[1]{0:T(128)} %bitcast.13.refs_0_, bf16[256,640]{1,0:T(8,128)(2,1)S(1)} %collective-permute-done.3.refs_1_, bf16[256,640]{1,0:T(8,128)(2,1)S(1)} %collective-permute-done.4.refs_2_), custom_call_target="tpu_custom_call" | custom-call | flops 2400000000 | bytes 12000000 | tf_op jit(solution)/shard_map/pallas_call | solution.py:131
  39.0 3.1 %shard_map.88 = (bf16[2,16,256,128]{3,2,1,0:T(8,128)(2,1)S(1)}, s32[2,16,128]{2,1,0:T(8,128)S(1)}, s32[2,8,128]{2,1,0:T(8,128)S(1)}) custom-call(s32[1]{0:T(128)} %bitcast.13.refs_0_, bf16[256,640]{1,0:T(8,128)(2,1)S(1)} %collective-permute-done.5.refs_1_, bf16[256,640]{1,0:T(8,128)(2,1)S(1)} %collective-permute-done.6.refs_2_), custom_call_target="tpu_custom_call" | custom-call | flops 2400000000 | bytes 12000000 | tf_op jit(solution)/shard_map/pallas_call | solution.py:131
  42.1 3.1 %shard_map.89 = (bf16[2,16,256,128]{3,2,1,0:T(8,128)(2,1)S(1)}, s32[2,16,128]{2,1,0:T(8,128)S(1)}, s32[2,8,128]{2,1,0:T(8,128)S(1)}) custom-call(s32[1]{0:T(128)} %bitcast.13.refs_0_, bf16[256,640]{1,0:T(8,128)(2,1)S(1)} %collective-permute-done.7.refs_1_, bf16[256,640]{1,0:T(8,128)(2,1)S(1)} %collective-permute-done.8.refs_2_), custom_call_target="tpu_custom_call" | custom-call | flops 2400000000 | bytes 12000000 | tf_op jit(solution)/shard_map/pallas_call | solution.py:131
  48.6 3.0 %shard_map.92 = (f32[2,512,256]{2,1,0:T(8,128)S(1)}, f32[2,512,256]{2,1,0:T(8,128)S(1)}) custom-call(s32[5]{0:T(128)S(1)} %pad_add_fusion.2.refs_0_, s32[1,8,128]{2,1,0:T(8,128)S(1)} %get-tuple-element.29.refs_1_, s32[2,8,128]{2,1,0:T(8,128)S(1)} %get-tuple-element.30.refs_2_, s32[2,8,128]{2,1,0:T(8,128)S(1)} %get-tuple-element.31.refs_3_, ...), custom_call_target="tpu_custom_call" | custom-call | flops 2400000000 | bytes 12000000 | tf_op jit(solution)/shard_map/pallas_call | solution.py:192
  51.7 6.1 %collective-permute-start.11 = (f32[2,512,256]{2,1,0:T(8,128)S(1)}, f32[2,512,256]{2,1,0:T(8,128)S(1)}, u32[]{:S(2)}, u32[]{:S(2)}) collective-permute-start(f32[2,512,256]{2,1,0:T(8,128)S(1)} %get-tuple-element.47), channel_id=1, source_target_pairs={{0,32},{32,0},{64,96},{96,64},{128,160},{160,128},{192,224},{224,1... | collective-permute-start | bytes 3145736 | tf_op jit(solution)/shard_map/ppermute | solution.py:339
  62.3 2.4 %collective-permute-start.15 = (f32[256,256]{1,0:T(8,128)S(1)}, f32[256,256]{1,0:T(8,128)S(1)}, u32[]{:S(2)}, u32[]{:S(2)}) collective-permute-start(f32[256,256]{1,0:T(8,128)S(1)} %get-tuple-element.60), channel_id=1, source_target_pairs={{0,3},{1,0},{2,1},{3,2},{4,7},{5,4},{6,5},{7,6},{8,11},{9,8},{10,9... | collective-permute-start | bytes 786440 | tf_op jit(solution)/shard_map/ppermute | solution.py:344
  64.7 2.0 %shard_map.91 = (f32[1,512,256]{2,1,0:T(8,128)S(1)}, f32[1,512,256]{2,1,0:T(8,128)S(1)}) custom-call(s32[5]{0:T(128)S(1)} %pad_add_fusion.2.refs_0_, s32[1,8,128]{2,1,0:T(8,128)S(1)} %get-tuple-element.29.refs_1_, s32[2,8,128]{2,1,0:T(8,128)S(1)} %get-tuple-element.30.refs_2_, s32[2,8,128]{2,1,0:T(8,128)S(1)} %get-tuple-element.31.refs_3_, ...), custom_call_target="tpu_custom_call" | custom-call | flops 1200000000 | bytes 6000000 | tf_op jit(solution)/shard_map/pallas_call | solution.py:192
  67.7 3.2 %collective-permute-done.13 = f32[256,256]{1,0:T(8,128)S(1)} collective-permute-done((f32[256,256]{1,0:T(8,128)S(1)}, f32[256,256]{1,0:T(8,128)S(1)}, u32[]{:S(2)}, u32[]{:S(2)}) %collective-permute-start.13) | collective-permute-done | bytes 262176 | tf_op jit(solution)/shard_map/ppermute | solution.py:343
  71.1 2.5 %collective-permute-start.16 = (f32[512,256]{1,0:T(8,128)S(1)}, f32[512,256]{1,0:T(8,128)S(1)}, u32[]{:S(2)}, u32[]{:S(2)}) collective-permute-start(f32[512,256]{1,0:T(8,128)S(1)} %pad_maximum_fusion.1), channel_id=1, source_target_pairs={{0,3},{1,0},{2,1},{3,2},{4,7},{5,4},{6,5},{7,6},{8,11},{9,8},{10,9... | collective-permute-start | bytes 1572872 | tf_op jit(solution)/shard_map/ppermute | solution.py:348
  73.7 9.9 %collective-permute-done.16 = f32[512,256]{1,0:T(8,128)S(1)} collective-permute-done((f32[512,256]{1,0:T(8,128)S(1)}, f32[512,256]{1,0:T(8,128)S(1)}, u32[]{:S(2)}, u32[]{:S(2)}) %collective-permute-start.16) | collective-permute-done | bytes 524320 | tf_op jit(solution)/shard_map/ppermute | solution.py:348
  83.6 3.2 %collective-permute-done.14 = f32[512,256]{1,0:T(8,128)S(1)} collective-permute-done((f32[512,256]{1,0:T(8,128)S(1)}, f32[512,256]{1,0:T(8,128)S(1)}, u32[]{:S(2)}, u32[]{:S(2)}) %collective-permute-start.14) | collective-permute-done | bytes 524320 | tf_op jit(solution)/shard_map/ppermute | solution.py:347
  88.9 3.7 %collective-permute-start.19 = (f32[128,256]{1,0:T(8,128)S(1)}, f32[128,256]{1,0:T(8,128)S(1)}, u32[]{:S(2)}, u32[]{:S(2)}) collective-permute-start(f32[128,256]{1,0:T(8,128)S(1)} %get-tuple-element.57), channel_id=1, source_target_pairs={{0,192},{32,224},{64,0},{96,32},{128,64},{160,96},{192,128},{224,1... | collective-permute-start | bytes 393224 | tf_op jit(solution)/shard_map/ppermute | solution.py:352
  95.2 3.0 %collective-permute-done.18 = f32[128,256]{1,0:T(8,128)S(1)} collective-permute-done((f32[128,256]{1,0:T(8,128)S(1)}, f32[128,256]{1,0:T(8,128)S(1)}, u32[]{:S(2)}, u32[]{:S(2)}) %collective-permute-start.18) | collective-permute-done | bytes 131104 | tf_op jit(solution)/shard_map/ppermute | solution.py:352
  98.6 2.4 %collective-permute-start.23 = (f32[128,256]{1,0:T(8,128)S(1)}, f32[128,256]{1,0:T(8,128)S(1)}, u32[]{:S(2)}, u32[]{:S(2)}) collective-permute-start(f32[128,256]{1,0:T(8,128)S(1)} %fusion.4.refs_11_), channel_id=1, source_target_pairs={{0,128},{32,160},{64,192},{96,224},{128,0},{160,32},{192,64},{224,... | collective-permute-start | bytes 393224 | tf_op jit(solution)/shard_map/ppermute | solution.py:353
  101.4 4.8 %collective-permute-start.20 = (f32[128,256]{1,0:T(8,128)S(1)}, f32[128,256]{1,0:T(8,128)S(1)}, u32[]{:S(2)}, u32[]{:S(2)}) collective-permute-start(f32[128,256]{1,0:T(8,128)S(1)} %fusion.4.refs_11_), channel_id=1, source_target_pairs={{0,32},{32,0},{64,96},{96,64},{128,160},{160,128},{192,224},{224,1... | collective-permute-start | bytes 393224 | tf_op jit(solution)/shard_map/ppermute | solution.py:354
  110.4 2.2 %copy-done = f32[4096,256]{1,0:T(8,128)S(1)} copy-done((f32[4096,256]{1,0:T(8,128)S(1)}, f32[4096,256]{1,0:T(8,128)}, u32[]{:S(2)}) %copy-start) | copy-done | bytes 4194328
  112.6 6.3 %listed_values.1 = (f32[1024,128]{1,0:T(8,128)S(1)}, f32[1024,256]{1,0:T(8,128)S(1)}) custom-call(s32[8,128]{1,0:T(8,128)S(1)} %bitcast.47, s32[4,1024,128]{2,1,0:T(8,128)S(1)} %broadcast_in_dim.2.rows_ref.refs_16_.refs_6_, f32[32,128]{1,0:T(8,128)S(1)} %bitcast.44, f32[4096,256]{1,0:T(8,128)S(1)} %copy-done), custom_call_target="tpu_custom_call" | custom-call | flops 3600000000 | bytes 18000000 | tf_op jit(solution)/shard_map/listed_values/pallas_call | solution.py:220
  118.9 8.8 %update.1 = (f32[4096,256]{1,0:T(8,128)}, f32[32,128]{1,0:T(8,128)}) custom-call(s32[24]{0:T(128)S(1)} %pad_add_fusion.1.refs_0_, s32[8,128]{1,0:T(8,128)S(1)} %bitcast.43, f32[4096,256]{1,0:T(8,128)S(1)} %copy-done.1, f32[32,128]{1,0:T(8,128)S(1)} %bitcast.45, f32[1024,128]{1,0:T(8,128)S(1)} %get-tuple-element.27.refs_4_, ...), custom_call_target="tpu_custom_call" | custom-call | tf_op jit(solution)/shard_map/update/pallas_call | solution.py:271
  (81 shorter events, 28.9 us)
Async XLA Ops:
  0.6 16.4 %collective-permute-start.2 = (s32[1024]{0:T(1024)}, s32[1024]{0:T(1024)S(1)}, u32[]{:S(2)}, u32[]{:S(2)}) collective-permute-start(s32[1024]{0:T(1024)} %bitcast.38), channel_id=1, source_target_pairs={{0,1},{1,2},{2,3},{3,0},{4,5},{5,6},{6,7},{7,4},{8,9},{9,10},{10,1... | collective-permute-start | bytes 12296 | tf_op jit(solution)/shard_map/ppermute | solution.py:314
  2.7 14.3 %collective-permute-start.1 = (s32[1024]{0:T(1024)}, s32[1024]{0:T(1024)S(1)}, u32[]{:S(2)}, u32[]{:S(2)}) collective-permute-start(s32[1024]{0:T(1024)} %bitcast.39), channel_id=1, source_target_pairs={{0,3},{1,0},{2,1},{3,2},{4,7},{5,4},{6,5},{7,6},{8,11},{9,8},{10,9... | collective-permute-start | bytes 12296 | tf_op jit(solution)/shard_map/ppermute | solution.py:314
  4.1 20.0 %collective-permute-start = (s32[1024]{0:T(1024)}, s32[1024]{0:T(1024)S(1)}, u32[]{:S(2)}, u32[]{:S(2)}) collective-permute-start(s32[1024]{0:T(1024)} %bitcast.40), channel_id=1, source_target_pairs={{0,2},{1,3},{2,0},{3,1},{4,6},{5,7},{6,4},{7,5},{8,10},{9,11},{10,... | collective-permute-start | bytes 12296 | tf_op jit(solution)/shard_map/ppermute | solution.py:314
  9.7 14.4 %collective-permute-start.4 = (bf16[256,640]{1,0:T(8,128)(2,1)S(1)}, bf16[256,640]{1,0:T(8,128)(2,1)S(1)}, u32[]{:S(2)}, u32[]{:S(2)}) collective-permute-start(bf16[256,640]{1,0:T(8,128)(2,1)S(1)} %pack.1.refs_1_), channel_id=1, source_target_pairs={{0,28},{1,29},{2,30},{3,31},{4,0},{5,1},{6,2},{7,3},{8,4},{9,5},{1... | collective-permute-start | bytes 983048 | tf_op jit(solution)/shard_map/ppermute | solution.py:328
  15.4 8.7 %collective-permute-start.3 = (bf16[256,640]{1,0:T(8,128)(2,1)S(1)}, bf16[256,640]{1,0:T(8,128)(2,1)S(1)}, u32[]{:S(2)}, u32[]{:S(2)}) collective-permute-start(bf16[256,640]{1,0:T(8,128)(2,1)S(1)} %pack.1.refs_1_), channel_id=1, source_target_pairs={{0,4},{1,5},{2,6},{3,7},{4,8},{5,9},{6,10},{7,11},{8,12},{9,13},{1... | collective-permute-start | bytes 983048 | tf_op jit(solution)/shard_map/ppermute | solution.py:326
  24.1 7.8 %collective-permute-start.5 = (bf16[256,640]{1,0:T(8,128)(2,1)S(1)}, bf16[256,640]{1,0:T(8,128)(2,1)S(1)}, u32[]{:S(2)}, u32[]{:S(2)}) collective-permute-start(bf16[256,640]{1,0:T(8,128)(2,1)S(1)} %collective-permute-done.3.refs_1_), channel_id=1, source_target_pairs={{0,4},{1,5},{2,6},{3,7},{4,8},{5,9},{6,10},{7,11},{8,12},{9,13},{1... | collective-permute-start | bytes 983048 | tf_op jit(solution)/shard_map/ppermute | solution.py:326
  24.1 7.8 %collective-permute-start.6 = (bf16[256,640]{1,0:T(8,128)(2,1)S(1)}, bf16[256,640]{1,0:T(8,128)(2,1)S(1)}, u32[]{:S(2)}, u32[]{:S(2)}) collective-permute-start(bf16[256,640]{1,0:T(8,128)(2,1)S(1)} %collective-permute-done.4.refs_2_), channel_id=1, source_target_pairs={{0,28},{1,29},{2,30},{3,31},{4,0},{5,1},{6,2},{7,3},{8,4},{9,5},{1... | collective-permute-start | bytes 983048 | tf_op jit(solution)/shard_map/ppermute | solution.py:328
  31.9 7.1 %collective-permute-start.7 = (bf16[256,640]{1,0:T(8,128)(2,1)S(1)}, bf16[256,640]{1,0:T(8,128)(2,1)S(1)}, u32[]{:S(2)}, u32[]{:S(2)}) collective-permute-start(bf16[256,640]{1,0:T(8,128)(2,1)S(1)} %collective-permute-done.5.refs_1_), channel_id=1, source_target_pairs={{0,4},{1,5},{2,6},{3,7},{4,8},{5,9},{6,10},{7,11},{8,12},{9,13},{1... | collective-permute-start | bytes 983048 | tf_op jit(solution)/shard_map/ppermute | solution.py:326
  31.9 10.2 %collective-permute-start.8 = (bf16[256,640]{1,0:T(8,128)(2,1)S(1)}, bf16[256,640]{1,0:T(8,128)(2,1)S(1)}, u32[]{:S(2)}, u32[]{:S(2)}) collective-permute-start(bf16[256,640]{1,0:T(8,128)(2,1)S(1)} %collective-permute-done.6.refs_2_), channel_id=1, source_target_pairs={{0,28},{1,29},{2,30},{3,31},{4,0},{5,1},{6,2},{7,3},{8,4},{9,5},{1... | collective-permute-start | bytes 983048 | tf_op jit(solution)/shard_map/ppermute | solution.py:328
  39.0 7.5 %collective-permute-start.9 = (bf16[256,640]{1,0:T(8,128)(2,1)S(1)}, bf16[256,640]{1,0:T(8,128)(2,1)S(1)}, u32[]{:S(2)}, u32[]{:S(2)}) collective-permute-start(bf16[256,640]{1,0:T(8,128)(2,1)S(1)} %collective-permute-done.7.refs_1_), channel_id=1, source_target_pairs={{0,4},{1,5},{2,6},{3,7},{4,8},{5,9},{6,10},{7,11},{8,12},{9,13},{1... | collective-permute-start | bytes 983048 | tf_op jit(solution)/shard_map/ppermute | solution.py:326
  51.7 15.8 %collective-permute-start.11 = (f32[2,512,256]{2,1,0:T(8,128)S(1)}, f32[2,512,256]{2,1,0:T(8,128)S(1)}, u32[]{:S(2)}, u32[]{:S(2)}) collective-permute-start(f32[2,512,256]{2,1,0:T(8,128)S(1)} %get-tuple-element.47), channel_id=1, source_target_pairs={{0,32},{32,0},{64,96},{96,64},{128,160},{160,128},{192,224},{224,1... | collective-permute-start | bytes 3145736 | tf_op jit(solution)/shard_map/ppermute | solution.py:339
  61.9 9.0 %collective-permute-start.13 = (f32[256,256]{1,0:T(8,128)S(1)}, f32[256,256]{1,0:T(8,128)S(1)}, u32[]{:S(2)}, u32[]{:S(2)}) collective-permute-start(f32[256,256]{1,0:T(8,128)S(1)} %get-tuple-element.59), channel_id=1, source_target_pairs={{0,1},{1,2},{2,3},{3,0},{4,5},{5,6},{6,7},{7,4},{8,9},{9,10},{10,1... | collective-permute-start | bytes 786440 | tf_op jit(solution)/shard_map/ppermute | solution.py:343
  62.3 8.6 %collective-permute-start.15 = (f32[256,256]{1,0:T(8,128)S(1)}, f32[256,256]{1,0:T(8,128)S(1)}, u32[]{:S(2)}, u32[]{:S(2)}) collective-permute-start(f32[256,256]{1,0:T(8,128)S(1)} %get-tuple-element.60), channel_id=1, source_target_pairs={{0,3},{1,0},{2,1},{3,2},{4,7},{5,4},{6,5},{7,6},{8,11},{9,8},{10,9... | collective-permute-start | bytes 786440 | tf_op jit(solution)/shard_map/ppermute | solution.py:344
  66.7 7.0 %collective-permute-start.10 = (f32[1,512,256]{2,1,0:T(8,128)S(1)}, f32[1,512,256]{2,1,0:T(8,128)S(1)}, u32[]{:S(2)}, u32[]{:S(2)}) collective-permute-start(f32[1,512,256]{2,1,0:T(8,128)S(1)} %get-tuple-element.45), channel_id=1, source_target_pairs={{0,32},{32,0},{64,96},{96,64},{128,160},{160,128},{192,224},{224,1... | collective-permute-start | bytes 1572872 | tf_op jit(solution)/shard_map/ppermute | solution.py:339
  71.1 12.6 %collective-permute-start.16 = (f32[512,256]{1,0:T(8,128)S(1)}, f32[512,256]{1,0:T(8,128)S(1)}, u32[]{:S(2)}, u32[]{:S(2)}) collective-permute-start(f32[512,256]{1,0:T(8,128)S(1)} %pad_maximum_fusion.1), channel_id=1, source_target_pairs={{0,3},{1,0},{2,1},{3,2},{4,7},{5,4},{6,5},{7,6},{8,11},{9,8},{10,9... | collective-permute-start | bytes 1572872 | tf_op jit(solution)/shard_map/ppermute | solution.py:348
  73.6 13.2 %collective-permute-start.14 = (f32[512,256]{1,0:T(8,128)S(1)}, f32[512,256]{1,0:T(8,128)S(1)}, u32[]{:S(2)}, u32[]{:S(2)}) collective-permute-start(f32[512,256]{1,0:T(8,128)S(1)} %pad_maximum_fusion), channel_id=1, source_target_pairs={{0,1},{1,2},{2,3},{3,0},{4,5},{5,6},{6,7},{7,4},{8,9},{9,10},{10,1... | collective-permute-start | bytes 1572872 | tf_op jit(solution)/shard_map/ppermute | solution.py:347
  87.6 7.5 %collective-permute-start.17 = (f32[128,256]{1,0:T(8,128)}, f32[128,256]{1,0:T(8,128)S(1)}, u32[]{:S(2)}, u32[]{:S(2)}) collective-permute-start(f32[128,256]{1,0:T(8,128)} %get-tuple-element.56), channel_id=1, source_target_pairs={{0,64},{32,96},{64,128},{96,160},{128,192},{160,224},{192,0},{224,... | collective-permute-start | bytes 393224 | tf_op jit(solution)/shard_map/ppermute | solution.py:352
  98.2 8.0 %collective-permute-start.25 = (f32[128,256]{1,0:T(8,128)S(1)}, f32[128,256]{1,0:T(8,128)S(1)}, u32[]{:S(2)}, u32[]{:S(2)}) collective-permute-start(f32[128,256]{1,0:T(8,128)S(1)} %fusion.4.refs_11_), channel_id=1, source_target_pairs={{0,64},{32,96},{64,128},{96,160},{128,192},{160,224},{192,0},{224,... | collective-permute-start | bytes 393224 | tf_op jit(solution)/shard_map/ppermute | solution.py:353
  98.6 9.4 %collective-permute-start.23 = (f32[128,256]{1,0:T(8,128)S(1)}, f32[128,256]{1,0:T(8,128)S(1)}, u32[]{:S(2)}, u32[]{:S(2)}) collective-permute-start(f32[128,256]{1,0:T(8,128)S(1)} %fusion.4.refs_11_), channel_id=1, source_target_pairs={{0,128},{32,160},{64,192},{96,224},{128,0},{160,32},{192,64},{224,... | collective-permute-start | bytes 393224 | tf_op jit(solution)/shard_map/ppermute | solution.py:353
  101.0 8.7 %collective-permute-start.21 = (f32[128,256]{1,0:T(8,128)S(1)}, f32[128,256]{1,0:T(8,128)S(1)}, u32[]{:S(2)}, u32[]{:S(2)}) collective-permute-start(f32[128,256]{1,0:T(8,128)S(1)} %fusion.4.refs_11_), channel_id=1, source_target_pairs={{0,192},{32,224},{64,0},{96,32},{128,64},{160,96},{192,128},{224,1... | collective-permute-start | bytes 393224 | tf_op jit(solution)/shard_map/ppermute | solution.py:353
  101.4 17.4 %collective-permute-start.20 = (f32[128,256]{1,0:T(8,128)S(1)}, f32[128,256]{1,0:T(8,128)S(1)}, u32[]{:S(2)}, u32[]{:S(2)}) collective-permute-start(f32[128,256]{1,0:T(8,128)S(1)} %fusion.4.refs_11_), channel_id=1, source_target_pairs={{0,32},{32,0},{64,96},{96,64},{128,160},{160,128},{192,224},{224,1... | collective-permute-start | bytes 393224 | tf_op jit(solution)/shard_map/ppermute | solution.py:354
  106.2 12.7 %collective-permute-start.26 = (f32[128,256]{1,0:T(8,128)S(1)}, f32[128,256]{1,0:T(8,128)S(1)}, u32[]{:S(2)}, u32[]{:S(2)}) collective-permute-start(f32[128,256]{1,0:T(8,128)S(1)} %collective-permute-done.25.refs_14_), channel_id=1, source_target_pairs={{0,32},{32,0},{64,96},{96,64},{128,160},{160,128},{192,224},{224,1... | collective-permute-start | bytes 393224 | tf_op jit(solution)/shard_map/ppermute | solution.py:354
  108.1 10.8 %collective-permute-start.24 = (f32[128,256]{1,0:T(8,128)S(1)}, f32[128,256]{1,0:T(8,128)S(1)}, u32[]{:S(2)}, u32[]{:S(2)}) collective-permute-start(f32[128,256]{1,0:T(8,128)S(1)} %collective-permute-done.23.refs_13_), channel_id=1, source_target_pairs={{0,32},{32,0},{64,96},{96,64},{128,160},{160,128},{192,224},{224,1... | collective-permute-start | bytes 393224 | tf_op jit(solution)/shard_map/ppermute | solution.py:354
  109.7 9.1 %collective-permute-start.22 = (f32[128,256]{1,0:T(8,128)S(1)}, f32[128,256]{1,0:T(8,128)S(1)}, u32[]{:S(2)}, u32[]{:S(2)}) collective-permute-start(f32[128,256]{1,0:T(8,128)S(1)} %collective-permute-done.21.refs_12_), channel_id=1, source_target_pairs={{0,32},{32,0},{64,96},{96,64},{128,160},{160,128},{192,224},{224,1... | collective-permute-start | bytes 393224 | tf_op jit(solution)/shard_map/ppermute | solution.py:354
  (11 other events, 64.6 us)

commit v5 on v4

--- a/solution.py
+++ b/solution.py
@@ -26,6 +26,7 @@
 ORDER = (2, 1, 3, 0)
 SMEM = pl.BlockSpec(memory_space=pltpu.SMEM)
 VMEM = pl.BlockSpec(memory_space=pltpu.VMEM)
+HBM = pl.BlockSpec(memory_space=pltpu.HBM)
 PARAMS = pltpu.CompilerParams(vmem_limit_bytes=26 << 20)
 
 
@@ -37,7 +38,17 @@
     return jnp.where(mask, 1.0, 0.0).astype(BF16)
 
 
-def pack_kernel(ids_ref, bags_ref, g_ref, out_ref, a_ref, b_ref, o_ref):
+def in_hbm(array):
+    return pltpu.with_memory_space_constraint(array, pltpu.HBM)
+
+
+def pack_kernel(ids_hbm, bags_hbm, g_hbm, out_ref, a_ref, b_ref, o_ref, ids_ref, bags_ref, g_ref, sem):
+    loads = [pltpu.make_async_copy(src, dst, sem.at[n])
+             for n, (src, dst) in enumerate(((ids_hbm, ids_ref), (bags_hbm, bags_ref), (g_hbm, g_ref)))]
+    for load in loads:
+        load.start()
+    for load in loads:
+        load.wait()
     groups = LOOK // LANES
     ids = ids_ref[...]
     owner = ids >> 12
@@ -87,13 +98,16 @@
     return pl.pallas_call(
         pack_kernel,
         out_shape=jax.ShapeDtypeStruct((E, WIDTH), BF16),
+        in_specs=[HBM] * 3,
         scratch_shapes=[pltpu.VMEM((3 * BLOCKS, LOOK), BF16),
                         pltpu.VMEM((LANES, LOOK), BF16),
-                        pltpu.VMEM((TOUCH, 2 * LANES), BF16)],
+                        pltpu.VMEM((TOUCH, 2 * LANES), BF16),
+                        pltpu.VMEM((32, LANES), I32), pltpu.VMEM((32, LANES), I32),
+                        pltpu.VMEM((B_DEV, E), BF16), pltpu.SemaphoreType.DMA((3,))],
         cost_estimate=cost(4),
         compiler_params=PARAMS,
         name="pack",
-    )(ids, bags, grads)
+    )(*[in_hbm(a) for a in (ids, bags, grads)])
 
 
 def gather_kernel(z_ref, *refs, count):
@@ -199,18 +213,20 @@
     )(at, *[g[2] for g in gathered], *[g[0] for g in gathered], *[g[1] for g in gathered], rows)
 
 
-def listed_kernel(list_ref, rows_ref, accum_ref, table_ref, accum_out, table_out):
+def listed_kernel(list_ref, rows_ref, accum_ref, table_ref, out_ref):
     rows = rows_ref[NX - 1]
     hi = jnp.where((rows >> 7) == iota((TOUCH, LANES), 1), 1.0, 0.0)
     padded = jnp.concatenate([accum_ref[...], jnp.zeros((LANES - 32, LANES), F32)], axis=0)
     line = jnp.dot(hi, padded, precision=lax.Precision.HIGHEST, preferred_element_type=F32)
     mine = jnp.where((rows & (LANES - 1)) == iota((TOUCH, LANES), 1), line, 0.0)
-    accum_out[...] = jnp.broadcast_to(jnp.sum(mine, axis=1, keepdims=True), (TOUCH, LANES))
+    out_ref[0:TOUCH, E:] = jnp.broadcast_to(jnp.sum(mine, axis=1, keepdims=True), (TOUCH, LANES))
+    out_ref[TOUCH:, E:] = accum_ref[...]
+    out_ref[TOUCH:, 0:E] = jnp.zeros((32, E), F32)
 
     def step(i, _):
         for j in range(16):
             row = list_ref[i >> 3, (i & 7) * 16 + j]
-            table_out[pl.ds(i * 16 + j, 1), :] = table_ref[pl.ds(row, 1), :]
+            out_ref[pl.ds(i * 16 + j, 1), 0:E] = table_ref[pl.ds(row, 1), :]
         return 0
 
     lax.fori_loop(0, TOUCH // 16, step, 0)
@@ -219,7 +235,7 @@
 def listed_values(order, rows, accum, table):
     return pl.pallas_call(
         listed_kernel,
-        out_shape=(jax.ShapeDtypeStruct((TOUCH, LANES), F32), jax.ShapeDtypeStruct((TOUCH, E), F32)),
+        out_shape=jax.ShapeDtypeStruct((TOUCH + 32, E + LANES), F32),
         in_specs=[SMEM, VMEM, VMEM, VMEM],
         cost_estimate=cost(6),
         compiler_params=PARAMS,
@@ -228,57 +244,74 @@
 
 
 def update_kernel(*refs):
-    plan_ref, list_ref, table_ref, accum_ref, listed_ref, old_ref, rows_ref = refs[0:7]
-    chunks = refs[7:15]
-    table_out, accum_out, u_ref, lhs_ref, rhs_ref = refs[15:]
-    block = pl.program_id(0)
-
-    @pl.when(block == 0)
-    def _():
-        lane = iota((QUART, LANES), 1)
-        for n in range(8):
-            at = slice(n * QUART, (n + 1) * QUART)
-            g = chunks[n][...]
-            mean = jnp.sum(g * g, axis=1, keepdims=True) * (1.0 / E)
-            now = listed_ref[at, 0:1] + mean
-            place = pl.multiple_of(plan_ref[16 + n] * QUART, QUART)
-            u_ref[pl.ds(place, QUART), :] = old_ref[at, :] - 0.5 * g / (jnp.sqrt(now) + 1e-08)
-            rows = rows_ref[NX - 1, at, :]
-            lhs_ref[at, :] = jnp.where((rows >> 7) == lane, mean, 0.0)
-            rhs_ref[at, :] = jnp.where((rows & (LANES - 1)) == lane, 1.0, 0.0)
-        added = lax.dot_general(lhs_ref[...], rhs_ref[...], TN, precision=lax.Precision.HIGHEST,
-                                preferred_element_type=F32)
-        accum_out[...] = accum_ref[...] + added[0:32, :]
-
-    table_out[...] = table_ref[pl.ds(pl.multiple_of(block * TILE, TILE), TILE), :]
-    first, last = plan_ref[block], plan_ref[block + 1]
+    plan_ref, list_ref, table_ref, listed_hbm, rows_ref = refs[0:5]
+    chunks = refs[5:13]
+    table_out, accum_out, new_ref, listed_ref, u_ref, lhs_ref, rhs_ref, load_sem, store_sem = refs[13:]
+    loads = [pltpu.make_async_copy(src, dst, load_sem.at[n])
+             for n, (src, dst) in enumerate(((listed_hbm, listed_ref), (table_ref, new_ref)))]
+    for load in loads:
+        load.start()
+    lane = iota((QUART, LANES), 1)
+    means = []
+    for n in range(8):
+        at = slice(n * QUART, (n + 1) * QUART)
+        g = chunks[n][...]
+        mean = jnp.sum(g * g, axis=1, keepdims=True) * (1.0 / E)
+        means.append(mean)
+        rows = rows_ref[NX - 1, at, :]
+        lhs_ref[at, :] = jnp.where((rows >> 7) == lane, mean, 0.0)
+        rhs_ref[at, :] = jnp.where((rows & (LANES - 1)) == lane, 1.0, 0.0)
+    loads[0].wait()
+    for n in range(8):
+        at = slice(n * QUART, (n + 1) * QUART)
+        now = listed_ref[at, E:E + 1] + means[n]
+        place = pl.multiple_of(plan_ref[16 + n] * QUART, QUART)
+        u_ref[pl.ds(place, QUART), :] = (
+            listed_ref[at, 0:E] - 0.5 * chunks[n][...] / (jnp.sqrt(now) + 1e-08))
+    loads[1].wait()
 
     def put(n):
-        row = list_ref[n >> 7, n & (LANES - 1)] - block * TILE
-        table_out[pl.ds(row, 1), :] = u_ref[pl.ds(n, 1), :]
-
-    def step(i, _):
-        for j in range(8):
-            put(first + i * 8 + j)
+        new_ref[pl.ds(list_ref[n], 1), :] = u_ref[pl.ds(n, 1), :]
+
+    def store(b):
+        tile = pl.ds(pl.multiple_of(b * TILE, TILE), TILE)
+        return pltpu.make_async_copy(new_ref.at[tile], table_out.at[tile], store_sem.at[b])
+
+    def tile(b, _):
+        first, last = plan_ref[b], plan_ref[b + 1]
+        whole = (last - first) >> 3
+
+        def step(i, _):
+            for j in range(8):
+                put(first + i * 8 + j)
+            return 0
+
+        lax.fori_loop(0, whole, step, 0)
+        lax.fori_loop(first + whole * 8, last, lambda n, _: (put(n), 0)[1], 0)
+        store(b).start()
         return 0
 
-    whole = (last - first) >> 3
-    lax.fori_loop(0, whole, step, 0)
-    lax.fori_loop(first + whole * 8, last, lambda n, _: (put(n), 0)[1], 0)
-
-
-def update(plan, natural, table, accum, listed, old, rows, chunks):
+    lax.fori_loop(0, ROWS_DEV // TILE, tile, 0)
+    added = lax.dot_general(lhs_ref[...], rhs_ref[...], TN, precision=lax.Precision.HIGHEST,
+                            preferred_element_type=F32)
+    accum_out[...] = listed_ref[TOUCH:, E:] + added[0:32, :]
+    for b in range(ROWS_DEV // TILE):
+        store(b).wait()
+
+
+def update(plan, natural, table, listed, rows, chunks):
     return pl.pallas_call(
         update_kernel,
-        grid=(ROWS_DEV // TILE,),
         out_shape=(jax.ShapeDtypeStruct((ROWS_DEV, E), F32), jax.ShapeDtypeStruct((32, LANES), F32)),
-        in_specs=[SMEM, SMEM] + [VMEM] * 13,
-        out_specs=(pl.BlockSpec((TILE, E), lambda i: (i, 0)), pl.BlockSpec((32, LANES), lambda i: (0, 0))),
-        scratch_shapes=[pltpu.VMEM((TOUCH, E), F32), pltpu.VMEM((TOUCH, LANES), F32),
-                        pltpu.VMEM((TOUCH, LANES), F32)],
+        in_specs=[SMEM, SMEM, HBM, HBM] + [VMEM] * 9,
+        out_specs=(HBM, VMEM),
+        scratch_shapes=[pltpu.VMEM((ROWS_DEV, E), F32), pltpu.VMEM((TOUCH + 32, E + LANES), F32),
+                        pltpu.VMEM((TOUCH, E), F32),
+                        pltpu.VMEM((TOUCH, LANES), F32), pltpu.VMEM((TOUCH, LANES), F32),
+                        pltpu.SemaphoreType.DMA((2,)), pltpu.SemaphoreType.DMA((ROWS_DEV // TILE,))],
         compiler_params=PARAMS,
         name="update",
-    )(plan, natural, table, accum, listed, old, rows, *chunks)
+    )(plan, natural, in_hbm(table), in_hbm(listed), rows, *chunks)
 
 
 def z_pairs(k):
@@ -330,8 +363,7 @@
     for sources in ((0,), (-1, 1), (-2, 2), (-3, 3), (-4,)):
         gathered.append(gather(z.reshape(1), [got[k] for k in sources]))
 
-    table = pltpu.with_memory_space_constraint(table, pltpu.VMEM)
-    listed, old = listed_values(order, rows, accum.reshape(32, LANES), table)
+    listed = listed_values(order, rows, accum.reshape(32, LANES), table)
     at = jnp.concatenate([(x + jnp.array(ORDER, I32)) % NX, (NX * z).reshape(1)])
     both = {}
     for base, ks in ((0, (2,)), (1, (1, 3)), (3, (0,))):
@@ -340,20 +372,15 @@
         total = keep + swapped
         for n, k in enumerate(ks):
             both[k] = total[n]
-    low = lax.ppermute(both[2][:HALF // 2], "shard", x_pairs(1))
-    high = lax.ppermute(both[2][HALF // 2:], "shard", x_pairs(-1))
-    up = jnp.concatenate([both[1][:HALF // 2] + low, both[1][HALF // 2:]], axis=0)
-    down = jnp.concatenate([both[3][:HALF // 2], both[3][HALF // 2:] + high], axis=0)
-    up = lax.ppermute(up, "shard", x_pairs(1))
-    down = lax.ppermute(down, "shard", x_pairs(-1))
-    total = both[0] + up + down
+    total = both[0]
+    for k in (2, 1, 3):
+        total = total + lax.ppermute(both[k], "shard", x_pairs(k))
     part = total[0:QUART]
     for j in range(1, NY):
         part = part + lax.ppermute(total[j * QUART:(j + 1) * QUART], "grp", y_pairs(j))
     mine = [part] + [lax.ppermute(part, "grp", y_pairs(-j)) for j in range(1, NY)]
     other = [lax.ppermute(m, "grp", C_PAIRS) for m in mine]
-    new_table, new_accum = update(plan, own_list.reshape(8, LANES), table, accum.reshape(32, LANES),
-                                  listed, old, rows, other + mine)
+    new_table, new_accum = update(plan, own_list, table, listed, rows, other + mine)
     return (new_table, new_accum.reshape(ROWS_DEV))
 
 

time: 128 us -> 130 us (1.016)
  waiting for transfers between devices: 36.9 us -> 44.9 us
  starting transfers between devices: 46.8 us -> 41.8 us
    ppermute x4 -> x3, waiting for transfers between devices: 16.3 us -> 22.2 us  [body(): total = total + lax.ppermute(both[k], 'shard', x_pairs(k))]
    ppermute x4, starting transfers between devices: 8.94 us -> 5.4 us  [body(): other = [lax.ppermute(m, 'grp', C_PAIRS) for m in mine]]
    ppermute x3, waiting for transfers between devices: 0.01 us -> 2.19 us  [body(): lax.ppermute(part, 'grp', y_pairs(-j))]
    ppermute x3, waiting for transfers between devices: 1.89 us -> 0.01 us  [body(): swapped = lax.ppermute(send, 'grp', C_PAIRS)]
    ppermute x3, waiting for transfers between devices: 4.15 us -> 5.92 us  [body(): lax.ppermute(total[j * QUART:(j + 1) * QUART], 'grp', y_pairs(j))]
    unnamed x16 -> x10, local copies, waits for them, and re-layouts: 4.59 us -> 3.38 us
    ppermute x4 -> x3, starting transfers between devices: 5.31 us -> 4.27 us  [body(): total = total + lax.ppermute(both[k], 'shard', x_pairs(k))]
  transfers between devices with their start and end apart: 27 -> 26, of which waited for: 10 -> 9; matrix products, arithmetic and copies ran while one was open for 1% -> 1% of each run, Pallas kernels for 18% -> 18%
where the time goes in v5:
time: 130 us
  waiting for transfers between devices  44.9 us (35%)
  starting transfers between devices  41.8 us (32%)
  Pallas kernels  36.8 us (28%)
  local copies, waits for them, and re-layouts  4.72 us (4%)
    ppermute x3, waiting for transfers between devices, body(): total = total + lax.ppermute(both[k], 'shard', x_pairs(k))  22.2 us
    ppermute x4, waiting for transfers between devices, body(): got[-k] = lax.ppermute(got[1 - k], 'shard', z_pairs(1))  14.5 us
    pallas_call x5, Pallas kernels, gather(): pl.pallas_call(lambda *refs: gather_kernel(*refs, count=count), out_shape...  12.3 us
    ppermute x3, starting transfers between devices, body(): got[k] = lax.ppermute(got[k - 1], 'shard', z_pairs(-1))  11.1 us
    pallas_call x1, Pallas kernels, update(): pl.pallas_call(update_kernel, out_shape=(jax.ShapeDtypeStruct((ROWS_DEV,...  8.5 us
    pallas_call x3, Pallas kernels, sums(): pl.pallas_call(lambda *refs: sums_kernel(*refs, counts=counts, base=base,...  7.09 us
    ppermute x3, starting transfers between devices, body(): swapped = lax.ppermute(send, 'grp', C_PAIRS)  6.8 us
    pallas_call x1, Pallas kernels, listed_values(): pl.pallas_call(listed_kernel, out_shape=jax.ShapeDtypeStruct((TOUCH + 32,...  6.32 us
  transfers between devices with their start and end apart: 26, of which 9 were waited for; matrix products, arithmetic and copies ran while one was open for 1% of the time, Pallas kernels for 18%

profile of v5, /device:TPU:1, one launch (start us, length us, event | category | flops | bytes accessed | tf_op | source)
XLA Modules:
  0.0 130.1 jit_solution(7313680339784786291)
XLA Ops:
  0.6 2.1 %collective-permute-start.2 = (s32[1024]{0:T(1024)}, s32[1024]{0:T(1024)S(1)}, u32[]{:S(2)}, u32[]{:S(2)}) collective-permute-start(s32[1024]{0:T(1024)} %bitcast.29), channel_id=1, source_target_pairs={{0,1},{1,2},{2,3},{3,0},{4,5},{5,6},{6,7},{7,4},{8,9},{9,10},{10,1... | collective-permute-start | bytes 12296 | tf_op jit(solution)/shard_map/ppermute | solution.py:347
  5.7 2.6 %pack.1.refs_1_ = bf16[256,640]{1,0:T(8,128)(2,1)S(1)} custom-call(s32[32,128]{1,0:T(8,128)} %bitcast.45, s32[32,128]{1,0:T(8,128)} %bitcast.46, bf16[512,256]{1,0:T(8,128)(2,1)} %bitcast.44), custom_call_target="tpu_custom_call" | custom-call | flops 2400000000 | bytes 12000000 | tf_op jit(solution)/shard_map/pack/pallas_call | solution.py:98
  8.4 5.7 %collective-permute-start.4 = (bf16[256,640]{1,0:T(8,128)(2,1)S(1)}, bf16[256,640]{1,0:T(8,128)(2,1)S(1)}, u32[]{:S(2)}, u32[]{:S(2)}) collective-permute-start(bf16[256,640]{1,0:T(8,128)(2,1)S(1)} %pack.1.refs_1_), channel_id=1, source_target_pairs={{0,28},{1,29},{2,30},{3,31},{4,0},{5,1},{6,2},{7,3},{8,4},{9,5},{1... | collective-permute-start | bytes 983048 | tf_op jit(solution)/shard_map/ppermute | solution.py:361
  15.7 7.0 %collective-permute-done.3.refs_1_ = bf16[256,640]{1,0:T(8,128)(2,1)S(1)} collective-permute-done((bf16[256,640]{1,0:T(8,128)(2,1)S(1)}, bf16[256,640]{1,0:T(8,128)(2,1)S(1)}, u32[]{:S(2)}, u32[]{:S(2)}) %collective-permute-start.3) | collective-permute-done | bytes 327712 | tf_op jit(solution)/shard_map/ppermute | solution.py:359
  22.7 2.7 %collective-permute-start.6 = (bf16[256,640]{1,0:T(8,128)(2,1)S(1)}, bf16[256,640]{1,0:T(8,128)(2,1)S(1)}, u32[]{:S(2)}, u32[]{:S(2)}) collective-permute-start(bf16[256,640]{1,0:T(8,128)(2,1)S(1)} %collective-permute-done.4.refs_2_), channel_id=1, source_target_pairs={{0,28},{1,29},{2,30},{3,31},{4,0},{5,1},{6,2},{7,3},{8,4},{9,5},{1... | collective-permute-start | bytes 983048 | tf_op jit(solution)/shard_map/ppermute | solution.py:361
  25.5 5.0 %collective-permute-done.5.refs_1_ = bf16[256,640]{1,0:T(8,128)(2,1)S(1)} collective-permute-done((bf16[256,640]{1,0:T(8,128)(2,1)S(1)}, bf16[256,640]{1,0:T(8,128)(2,1)S(1)}, u32[]{:S(2)}, u32[]{:S(2)}) %collective-permute-start.5) | collective-permute-done | bytes 327712 | tf_op jit(solution)/shard_map/ppermute | solution.py:359
  30.6 2.7 %collective-permute-start.8 = (bf16[256,640]{1,0:T(8,128)(2,1)S(1)}, bf16[256,640]{1,0:T(8,128)(2,1)S(1)}, u32[]{:S(2)}, u32[]{:S(2)}) collective-permute-start(bf16[256,640]{1,0:T(8,128)(2,1)S(1)} %collective-permute-done.6.refs_2_), channel_id=1, source_target_pairs={{0,28},{1,29},{2,30},{3,31},{4,0},{5,1},{6,2},{7,3},{8,4},{9,5},{1... | collective-permute-start | bytes 983048 | tf_op jit(solution)/shard_map/ppermute | solution.py:361
  33.3 3.1 %shard_map.87 = (bf16[2,16,256,128]{3,2,1,0:T(8,128)(2,1)S(1)}, s32[2,16,128]{2,1,0:T(8,128)S(1)}, s32[2,8,128]{2,1,0:T(8,128)S(1)}) custom-call(s32[1]{0:T(128)} %bitcast.12.refs_0_, bf16[256,640]{1,0:T(8,128)(2,1)S(1)} %collective-permute-done.3.refs_1_, bf16[256,640]{1,0:T(8,128)(2,1)S(1)} %collective-permute-done.4.refs_2_), custom_call_target="tpu_custom_call" | custom-call | flops 2400000000 | bytes 12000000 | tf_op jit(solution)/shard_map/pallas_call | solution.py:145
  37.7 3.1 %shard_map.88 = (bf16[2,16,256,128]{3,2,1,0:T(8,128)(2,1)S(1)}, s32[2,16,128]{2,1,0:T(8,128)S(1)}, s32[2,8,128]{2,1,0:T(8,128)S(1)}) custom-call(s32[1]{0:T(128)} %bitcast.12.refs_0_, bf16[256,640]{1,0:T(8,128)(2,1)S(1)} %collective-permute-done.5.refs_1_, bf16[256,640]{1,0:T(8,128)(2,1)S(1)} %collective-permute-done.6.refs_2_), custom_call_target="tpu_custom_call" | custom-call | flops 2400000000 | bytes 12000000 | tf_op jit(solution)/shard_map/pallas_call | solution.py:145
  40.8 3.1 %shard_map.89 = (bf16[2,16,256,128]{3,2,1,0:T(8,128)(2,1)S(1)}, s32[2,16,128]{2,1,0:T(8,128)S(1)}, s32[2,8,128]{2,1,0:T(8,128)S(1)}) custom-call(s32[1]{0:T(128)} %bitcast.12.refs_0_, bf16[256,640]{1,0:T(8,128)(2,1)S(1)} %collective-permute-done.7.refs_1_, bf16[256,640]{1,0:T(8,128)(2,1)S(1)} %collective-permute-done.8.refs_2_), custom_call_target="tpu_custom_call" | custom-call | flops 2400000000 | bytes 12000000 | tf_op jit(solution)/shard_map/pallas_call | solution.py:145
  47.3 3.0 %shard_map.93 = (f32[2,512,256]{2,1,0:T(8,128)S(1)}, f32[2,512,256]{2,1,0:T(8,128)S(1)}) custom-call(s32[5]{0:T(128)S(1)} %pad_add_fusion.2.refs_0_, s32[1,8,128]{2,1,0:T(8,128)S(1)} %get-tuple-element.25.refs_1_, s32[2,8,128]{2,1,0:T(8,128)S(1)} %get-tuple-element.26.refs_2_, s32[2,8,128]{2,1,0:T(8,128)S(1)} %get-tuple-element.27.refs_3_, ...), custom_call_target="tpu_custom_call" | custom-call | flops 2400000000 | bytes 12000000 | tf_op jit(solution)/shard_map/pallas_call | solution.py:206
  50.3 6.1 %collective-permute-start.13 = (f32[2,512,256]{2,1,0:T(8,128)S(1)}, f32[2,512,256]{2,1,0:T(8,128)S(1)}, u32[]{:S(2)}, u32[]{:S(2)}) collective-permute-start(f32[2,512,256]{2,1,0:T(8,128)S(1)} %get-tuple-element.45), channel_id=1, source_target_pairs={{0,32},{32,0},{64,96},{96,64},{128,160},{160,128},{192,224},{224,1... | collective-permute-start | bytes 3145736 | tf_op jit(solution)/shard_map/ppermute | solution.py:371
  63.1 2.7 %collective-permute-start.15 = (f32[512,256]{1,0:T(8,128)S(1)}, f32[512,256]{1,0:T(8,128)S(1)}, u32[]{:S(2)}, u32[]{:S(2)}) collective-permute-start(f32[512,256]{1,0:T(8,128)S(1)} %get-tuple-element.49), channel_id=1, source_target_pairs={{0,3},{1,0},{2,1},{3,2},{4,7},{5,4},{6,5},{7,6},{8,11},{9,8},{10,9... | collective-permute-start | bytes 1572872 | tf_op jit(solution)/shard_map/ppermute | solution.py:377
  65.8 10.6 %collective-permute-done.12 = f32[512,256]{1,0:T(8,128)S(1)} collective-permute-done((f32[512,256]{1,0:T(8,128)S(1)}, f32[512,256]{1,0:T(8,128)S(1)}, u32[]{:S(2)}, u32[]{:S(2)}) %collective-permute-start.12) | collective-permute-done | bytes 524320 | tf_op jit(solution)/shard_map/ppermute | solution.py:377
  76.3 11.6 %collective-permute-done.14 = f32[512,256]{1,0:T(8,128)S(1)} collective-permute-done((f32[512,256]{1,0:T(8,128)S(1)}, f32[512,256]{1,0:T(8,128)S(1)}, u32[]{:S(2)}, u32[]{:S(2)}) %collective-permute-start.14) | collective-permute-done | bytes 524320 | tf_op jit(solution)/shard_map/ppermute | solution.py:377
  90.1 3.6 %collective-permute-start.18 = (f32[128,256]{1,0:T(8,128)S(1)}, f32[128,256]{1,0:T(8,128)S(1)}, u32[]{:S(2)}, u32[]{:S(2)}) collective-permute-start(f32[128,256]{1,0:T(8,128)S(1)} %get-tuple-element.51), channel_id=1, source_target_pairs={{0,192},{32,224},{64,0},{96,32},{128,64},{160,96},{192,128},{224,1... | collective-permute-start | bytes 393224 | tf_op jit(solution)/shard_map/ppermute | solution.py:380
  95.1 2.2 %collective-permute-done.16 = f32[128,256]{1,0:T(8,128)S(1)} collective-permute-done((f32[128,256]{1,0:T(8,128)}, f32[128,256]{1,0:T(8,128)S(1)}, u32[]{:S(2)}, u32[]{:S(2)}) %collective-permute-start.16) | collective-permute-done | bytes 131104 | tf_op jit(solution)/shard_map/ppermute | solution.py:380
  97.3 3.7 %collective-permute-done.17 = f32[128,256]{1,0:T(8,128)S(1)} collective-permute-done((f32[128,256]{1,0:T(8,128)S(1)}, f32[128,256]{1,0:T(8,128)S(1)}, u32[]{:S(2)}, u32[]{:S(2)}) %collective-permute-start.17) | collective-permute-done | bytes 131104 | tf_op jit(solution)/shard_map/ppermute | solution.py:380
  104.1 2.2 %collective-permute-start.19 = (f32[128,256]{1,0:T(8,128)S(1)}, f32[128,256]{1,0:T(8,128)S(1)}, u32[]{:S(2)}, u32[]{:S(2)}) collective-permute-start(f32[128,256]{1,0:T(8,128)S(1)} %fusion.3.refs_9_), channel_id=1, source_target_pairs={{0,32},{32,0},{64,96},{96,64},{128,160},{160,128},{192,224},{224,1... | collective-permute-start | bytes 393224 | tf_op jit(solution)/shard_map/ppermute | solution.py:382
  106.3 2.2 %collective-permute-done.24.refs_12_ = f32[128,256]{1,0:T(8,128)S(1)} collective-permute-done((f32[128,256]{1,0:T(8,128)S(1)}, f32[128,256]{1,0:T(8,128)S(1)}, u32[]{:S(2)}, u32[]{:S(2)}) %collective-permute-start.24) | collective-permute-done | bytes 131104 | tf_op jit(solution)/shard_map/ppermute | solution.py:381
  108.5 2.6 %collective-permute-start.25 = (f32[128,256]{1,0:T(8,128)S(1)}, f32[128,256]{1,0:T(8,128)S(1)}, u32[]{:S(2)}, u32[]{:S(2)}) collective-permute-start(f32[128,256]{1,0:T(8,128)S(1)} %collective-permute-done.24.refs_12_), channel_id=1, source_target_pairs={{0,32},{32,0},{64,96},{96,64},{128,160},{160,128},{192,224},{224,1... | collective-permute-start | bytes 393224 | tf_op jit(solution)/shard_map/ppermute | solution.py:382
  111.7 2.2 %copy-done = f32[4096,256]{1,0:T(8,128)S(1)} copy-done((f32[4096,256]{1,0:T(8,128)S(1)}, f32[4096,256]{1,0:T(8,128)}, u32[]{:S(2)}) %copy-start) | copy-done | bytes 4194328
  113.9 6.3 %listed_values.1.refs_3_ = f32[1056,384]{1,0:T(8,128)S(1)} custom-call(s32[8,128]{1,0:T(8,128)S(1)} %bitcast.36, s32[4,1024,128]{2,1,0:T(8,128)S(1)} %broadcast_in_dim.2.rows_ref.refs_16_.refs_4_, f32[32,128]{1,0:T(8,128)S(1)} %bitcast.37, f32[4096,256]{1,0:T(8,128)S(1)} %copy-done), custom_call_target="tpu_custom_call" | custom-call | flops 3600000000 | bytes 18000000 | tf_op jit(solution)/shard_map/listed_values/pallas_call | solution.py:236
  121.4 8.5 %update.1 = (f32[4096,256]{1,0:T(8,128)}, f32[32,128]{1,0:T(8,128)}) custom-call(s32[24]{0:T(128)S(1)} %pad_add_fusion.1.refs_0_, s32[1024]{0:T(1024)S(1)} %bitcast.34, f32[4096,256]{1,0:T(8,128)} %refs_2_.1, f32[1056,384]{1,0:T(8,128)} %copy-done.1, s32[4,1024,128]{2,1,0:T(8,128)S(1)} %broadcast_in_dim.2.rows_ref.refs_16_.refs_4_, ...), custom_call_target="tpu_custom_call" | custom-call | tf_op jit(solution)/shard_map/update/pallas_call | solution.py:303
  (69 shorter events, 24.5 us)
Async XLA Ops:
  0.6 15.1 %collective-permute-start.2 = (s32[1024]{0:T(1024)}, s32[1024]{0:T(1024)S(1)}, u32[]{:S(2)}, u32[]{:S(2)}) collective-permute-start(s32[1024]{0:T(1024)} %bitcast.29), channel_id=1, source_target_pairs={{0,1},{1,2},{2,3},{3,0},{4,5},{5,6},{6,7},{7,4},{8,9},{9,10},{10,1... | collective-permute-start | bytes 12296 | tf_op jit(solution)/shard_map/ppermute | solution.py:347
  2.7 13.0 %collective-permute-start.1 = (s32[1024]{0:T(1024)}, s32[1024]{0:T(1024)S(1)}, u32[]{:S(2)}, u32[]{:S(2)}) collective-permute-start(s32[1024]{0:T(1024)} %bitcast.30), channel_id=1, source_target_pairs={{0,3},{1,0},{2,1},{3,2},{4,7},{5,4},{6,5},{7,6},{8,11},{9,8},{10,9... | collective-permute-start | bytes 12296 | tf_op jit(solution)/shard_map/ppermute | solution.py:347
  4.1 18.6 %collective-permute-start = (s32[1024]{0:T(1024)}, s32[1024]{0:T(1024)S(1)}, u32[]{:S(2)}, u32[]{:S(2)}) collective-permute-start(s32[1024]{0:T(1024)} %bitcast.31), channel_id=1, source_target_pairs={{0,2},{1,3},{2,0},{3,1},{4,6},{5,7},{6,4},{7,5},{8,10},{9,11},{10,... | collective-permute-start | bytes 12296 | tf_op jit(solution)/shard_map/ppermute | solution.py:347
  8.4 14.3 %collective-permute-start.4 = (bf16[256,640]{1,0:T(8,128)(2,1)S(1)}, bf16[256,640]{1,0:T(8,128)(2,1)S(1)}, u32[]{:S(2)}, u32[]{:S(2)}) collective-permute-start(bf16[256,640]{1,0:T(8,128)(2,1)S(1)} %pack.1.refs_1_), channel_id=1, source_target_pairs={{0,28},{1,29},{2,30},{3,31},{4,0},{5,1},{6,2},{7,3},{8,4},{9,5},{1... | collective-permute-start | bytes 983048 | tf_op jit(solution)/shard_map/ppermute | solution.py:361
  14.0 8.7 %collective-permute-start.3 = (bf16[256,640]{1,0:T(8,128)(2,1)S(1)}, bf16[256,640]{1,0:T(8,128)(2,1)S(1)}, u32[]{:S(2)}, u32[]{:S(2)}) collective-permute-start(bf16[256,640]{1,0:T(8,128)(2,1)S(1)} %pack.1.refs_1_), channel_id=1, source_target_pairs={{0,4},{1,5},{2,6},{3,7},{4,8},{5,9},{6,10},{7,11},{8,12},{9,13},{1... | collective-permute-start | bytes 983048 | tf_op jit(solution)/shard_map/ppermute | solution.py:359
  22.7 7.8 %collective-permute-start.5 = (bf16[256,640]{1,0:T(8,128)(2,1)S(1)}, bf16[256,640]{1,0:T(8,128)(2,1)S(1)}, u32[]{:S(2)}, u32[]{:S(2)}) collective-permute-start(bf16[256,640]{1,0:T(8,128)(2,1)S(1)} %collective-permute-done.3.refs_1_), channel_id=1, source_target_pairs={{0,4},{1,5},{2,6},{3,7},{4,8},{5,9},{6,10},{7,11},{8,12},{9,13},{1... | collective-permute-start | bytes 983048 | tf_op jit(solution)/shard_map/ppermute | solution.py:359
  22.7 7.8 %collective-permute-start.6 = (bf16[256,640]{1,0:T(8,128)(2,1)S(1)}, bf16[256,640]{1,0:T(8,128)(2,1)S(1)}, u32[]{:S(2)}, u32[]{:S(2)}) collective-permute-start(bf16[256,640]{1,0:T(8,128)(2,1)S(1)} %collective-permute-done.4.refs_2_), channel_id=1, source_target_pairs={{0,28},{1,29},{2,30},{3,31},{4,0},{5,1},{6,2},{7,3},{8,4},{9,5},{1... | collective-permute-start | bytes 983048 | tf_op jit(solution)/shard_map/ppermute | solution.py:361
  30.5 7.1 %collective-permute-start.7 = (bf16[256,640]{1,0:T(8,128)(2,1)S(1)}, bf16[256,640]{1,0:T(8,128)(2,1)S(1)}, u32[]{:S(2)}, u32[]{:S(2)}) collective-permute-start(bf16[256,640]{1,0:T(8,128)(2,1)S(1)} %collective-permute-done.5.refs_1_), channel_id=1, source_target_pairs={{0,4},{1,5},{2,6},{3,7},{4,8},{5,9},{6,10},{7,11},{8,12},{9,13},{1... | collective-permute-start | bytes 983048 | tf_op jit(solution)/shard_map/ppermute | solution.py:359
  30.6 10.2 %collective-permute-start.8 = (bf16[256,640]{1,0:T(8,128)(2,1)S(1)}, bf16[256,640]{1,0:T(8,128)(2,1)S(1)}, u32[]{:S(2)}, u32[]{:S(2)}) collective-permute-start(bf16[256,640]{1,0:T(8,128)(2,1)S(1)} %collective-permute-done.6.refs_2_), channel_id=1, source_target_pairs={{0,28},{1,29},{2,30},{3,31},{4,0},{5,1},{6,2},{7,3},{8,4},{9,5},{1... | collective-permute-start | bytes 983048 | tf_op jit(solution)/shard_map/ppermute | solution.py:361
  37.7 7.5 %collective-permute-start.9 = (bf16[256,640]{1,0:T(8,128)(2,1)S(1)}, bf16[256,640]{1,0:T(8,128)(2,1)S(1)}, u32[]{:S(2)}, u32[]{:S(2)}) collective-permute-start(bf16[256,640]{1,0:T(8,128)(2,1)S(1)} %collective-permute-done.7.refs_1_), channel_id=1, source_target_pairs={{0,4},{1,5},{2,6},{3,7},{4,8},{5,9},{6,10},{7,11},{8,12},{9,13},{1... | collective-permute-start | bytes 983048 | tf_op jit(solution)/shard_map/ppermute | solution.py:359
  50.3 12.5 %collective-permute-start.13 = (f32[2,512,256]{2,1,0:T(8,128)S(1)}, f32[2,512,256]{2,1,0:T(8,128)S(1)}, u32[]{:S(2)}, u32[]{:S(2)}) collective-permute-start(f32[2,512,256]{2,1,0:T(8,128)S(1)} %get-tuple-element.45), channel_id=1, source_target_pairs={{0,32},{32,0},{64,96},{96,64},{128,160},{160,128},{192,224},{224,1... | collective-permute-start | bytes 3145736 | tf_op jit(solution)/shard_map/ppermute | solution.py:371
  61.3 15.1 %collective-permute-start.12 = (f32[512,256]{1,0:T(8,128)S(1)}, f32[512,256]{1,0:T(8,128)S(1)}, u32[]{:S(2)}, u32[]{:S(2)}) collective-permute-start(f32[512,256]{1,0:T(8,128)S(1)} %add_bitcast_fusion), channel_id=1, source_target_pairs={{0,2},{1,3},{2,0},{3,1},{4,6},{5,7},{6,4},{7,5},{8,10},{9,11},{10,... | collective-permute-start | bytes 1572872 | tf_op jit(solution)/shard_map/ppermute | solution.py:377
  63.0 25.0 %collective-permute-start.14 = (f32[512,256]{1,0:T(8,128)S(1)}, f32[512,256]{1,0:T(8,128)S(1)}, u32[]{:S(2)}, u32[]{:S(2)}) collective-permute-start(f32[512,256]{1,0:T(8,128)S(1)} %get-tuple-element.48), channel_id=1, source_target_pairs={{0,1},{1,2},{2,3},{3,0},{4,5},{5,6},{6,7},{7,4},{8,9},{9,10},{10,1... | collective-permute-start | bytes 1572872 | tf_op jit(solution)/shard_map/ppermute | solution.py:377
  63.1 24.9 %collective-permute-start.15 = (f32[512,256]{1,0:T(8,128)S(1)}, f32[512,256]{1,0:T(8,128)S(1)}, u32[]{:S(2)}, u32[]{:S(2)}) collective-permute-start(f32[512,256]{1,0:T(8,128)S(1)} %get-tuple-element.49), channel_id=1, source_target_pairs={{0,3},{1,0},{2,1},{3,2},{4,7},{5,4},{6,5},{7,6},{8,11},{9,8},{10,9... | collective-permute-start | bytes 1572872 | tf_op jit(solution)/shard_map/ppermute | solution.py:377
  88.8 8.5 %collective-permute-start.16 = (f32[128,256]{1,0:T(8,128)}, f32[128,256]{1,0:T(8,128)S(1)}, u32[]{:S(2)}, u32[]{:S(2)}) collective-permute-start(f32[128,256]{1,0:T(8,128)} %get-tuple-element.50), channel_id=1, source_target_pairs={{0,64},{32,96},{64,128},{96,160},{128,192},{160,224},{192,0},{224,... | collective-permute-start | bytes 393224 | tf_op jit(solution)/shard_map/ppermute | solution.py:380
  90.1 7.2 %collective-permute-start.18 = (f32[128,256]{1,0:T(8,128)S(1)}, f32[128,256]{1,0:T(8,128)S(1)}, u32[]{:S(2)}, u32[]{:S(2)}) collective-permute-start(f32[128,256]{1,0:T(8,128)S(1)} %get-tuple-element.51), channel_id=1, source_target_pairs={{0,192},{32,224},{64,0},{96,32},{128,64},{160,96},{192,128},{224,1... | collective-permute-start | bytes 393224 | tf_op jit(solution)/shard_map/ppermute | solution.py:380
  93.7 7.3 %collective-permute-start.17 = (f32[128,256]{1,0:T(8,128)S(1)}, f32[128,256]{1,0:T(8,128)S(1)}, u32[]{:S(2)}, u32[]{:S(2)}) collective-permute-start(f32[128,256]{1,0:T(8,128)S(1)} %get-tuple-element.52), channel_id=1, source_target_pairs={{0,128},{32,160},{64,192},{96,224},{128,0},{160,32},{192,64},{224,... | collective-permute-start | bytes 393224 | tf_op jit(solution)/shard_map/ppermute | solution.py:380
  101.1 7.4 %collective-permute-start.24 = (f32[128,256]{1,0:T(8,128)S(1)}, f32[128,256]{1,0:T(8,128)S(1)}, u32[]{:S(2)}, u32[]{:S(2)}) collective-permute-start(f32[128,256]{1,0:T(8,128)S(1)} %fusion.3.refs_9_), channel_id=1, source_target_pairs={{0,64},{32,96},{64,128},{96,160},{128,192},{160,224},{192,0},{224,... | collective-permute-start | bytes 393224 | tf_op jit(solution)/shard_map/ppermute | solution.py:381
  101.5 9.6 %collective-permute-start.22 = (f32[128,256]{1,0:T(8,128)S(1)}, f32[128,256]{1,0:T(8,128)S(1)}, u32[]{:S(2)}, u32[]{:S(2)}) collective-permute-start(f32[128,256]{1,0:T(8,128)S(1)} %fusion.3.refs_9_), channel_id=1, source_target_pairs={{0,128},{32,160},{64,192},{96,224},{128,0},{160,32},{192,64},{224,... | collective-permute-start | bytes 393224 | tf_op jit(solution)/shard_map/ppermute | solution.py:381
  101.9 9.2 %collective-permute-start.20 = (f32[128,256]{1,0:T(8,128)S(1)}, f32[128,256]{1,0:T(8,128)S(1)}, u32[]{:S(2)}, u32[]{:S(2)}) collective-permute-start(f32[128,256]{1,0:T(8,128)S(1)} %fusion.3.refs_9_), channel_id=1, source_target_pairs={{0,192},{32,224},{64,0},{96,32},{128,64},{160,96},{192,128},{224,1... | collective-permute-start | bytes 393224 | tf_op jit(solution)/shard_map/ppermute | solution.py:381
  104.1 17.3 %collective-permute-start.19 = (f32[128,256]{1,0:T(8,128)S(1)}, f32[128,256]{1,0:T(8,128)S(1)}, u32[]{:S(2)}, u32[]{:S(2)}) collective-permute-start(f32[128,256]{1,0:T(8,128)S(1)} %fusion.3.refs_9_), channel_id=1, source_target_pairs={{0,32},{32,0},{64,96},{96,64},{128,160},{160,128},{192,224},{224,1... | collective-permute-start | bytes 393224 | tf_op jit(solution)/shard_map/ppermute | solution.py:382
  108.5 12.9 %collective-permute-start.25 = (f32[128,256]{1,0:T(8,128)S(1)}, f32[128,256]{1,0:T(8,128)S(1)}, u32[]{:S(2)}, u32[]{:S(2)}) collective-permute-start(f32[128,256]{1,0:T(8,128)S(1)} %collective-permute-done.24.refs_12_), channel_id=1, source_target_pairs={{0,32},{32,0},{64,96},{96,64},{128,160},{160,128},{192,224},{224,1... | collective-permute-start | bytes 393224 | tf_op jit(solution)/shard_map/ppermute | solution.py:382
  111.1 10.3 %collective-permute-start.23 = (f32[128,256]{1,0:T(8,128)S(1)}, f32[128,256]{1,0:T(8,128)S(1)}, u32[]{:S(2)}, u32[]{:S(2)}) collective-permute-start(f32[128,256]{1,0:T(8,128)S(1)} %collective-permute-done.22.refs_11_), channel_id=1, source_target_pairs={{0,32},{32,0},{64,96},{96,64},{128,160},{160,128},{192,224},{224,1... | collective-permute-start | bytes 393224 | tf_op jit(solution)/shard_map/ppermute | solution.py:382
  111.1 10.3 %collective-permute-start.21 = (f32[128,256]{1,0:T(8,128)S(1)}, f32[128,256]{1,0:T(8,128)S(1)}, u32[]{:S(2)}, u32[]{:S(2)}) collective-permute-start(f32[128,256]{1,0:T(8,128)S(1)} %collective-permute-done.20.refs_10_), channel_id=1, source_target_pairs={{0,32},{32,0},{64,96},{96,64},{128,160},{160,128},{192,224},{224,1... | collective-permute-start | bytes 393224 | tf_op jit(solution)/shard_map/ppermute | solution.py:382
  (7 other events, 38.1 us)

commit v6 on v5

--- a/solution.py
+++ b/solution.py
@@ -11,6 +11,7 @@
 TOUCH = 1024
 HALF = TOUCH // 2
 QUART = TOUCH // 8
+PIECE = QUART // 2
 TILE = 512
 LOOK = 4096
 B_DEV = 512
@@ -27,7 +28,7 @@
 SMEM = pl.BlockSpec(memory_space=pltpu.SMEM)
 VMEM = pl.BlockSpec(memory_space=pltpu.VMEM)
 HBM = pl.BlockSpec(memory_space=pltpu.HBM)
-PARAMS = pltpu.CompilerParams(vmem_limit_bytes=26 << 20)
+PARAMS = pltpu.CompilerParams(vmem_limit_bytes=14 << 20)
 
 
 def iota(shape, dim):
@@ -110,45 +111,52 @@
     )(*[in_hbm(a) for a in (ids, bags, grads)])
 
 
-def gather_kernel(z_ref, *refs, count):
-    packets = refs[0:count]
-    x_ref, k_ref, m_ref, all_ref, scalar_ref, sem = refs[count:]
+def gather_kernel(z_ref, *refs, count, split):
+    packets = refs[0:count + split]
+    x_ref, k_ref, m_ref, all_ref, scalar_ref, sem = refs[count + split:]
+    copies = []
     for d in range(count):
-        side = packets[d][3 * BLOCKS:3 * BLOCKS + 16, B_DEV:WIDTH].astype(F32).astype(I32)
+        tail = packets[d + split][3 * BLOCKS - 128 * split:3 * BLOCKS + 16 - 128 * split, B_DEV:WIDTH]
+        side = tail.astype(F32).astype(I32)
         m_ref[d] = jnp.where(iota((8, LANES), 0) == 0, side[0:8], side[8:16])
-        copy = pltpu.make_async_copy(m_ref.at[d], scalar_ref.at[d], sem.at[d])
-        copy.start()
-        pieces = packets[d][0:3 * BLOCKS, B_DEV:WIDTH].astype(F32).astype(I32)
-        all_ref[d] = (pieces[0:BLOCKS] + (pieces[BLOCKS:2 * BLOCKS] << 8)
-                      + (pieces[2 * BLOCKS:3 * BLOCKS] << 16)) - 1
+        copies.append(pltpu.make_async_copy(m_ref.at[d], scalar_ref.at[d], sem.at[d]))
+        copies[d].start()
+    for d in range(count):
+        low = packets[d][0:2 * BLOCKS, B_DEV:WIDTH].astype(F32).astype(I32)
+        top = packets[d + split][2 * BLOCKS - 128 * split:3 * BLOCKS - 128 * split, B_DEV:WIDTH]
+        all_ref[d, 0:BLOCKS] = (low[0:BLOCKS] + (low[BLOCKS:2 * BLOCKS] << 8)
+                                + (top.astype(F32).astype(I32) << 16)) - 1
+        all_ref[d, BLOCKS:BLOCKS + 16] = jnp.zeros((16, LANES), I32)
+    for copy in copies:
         copy.wait()
-
-        def column(n, _, d=d):
-            first = scalar_ref[d, 0, NX * z_ref[0] + n]
-
-            def block(j, _):
-                row = all_ref[d, pl.ds(first + j, 1), :]
-                picks = one_hot((row & (B_DEV - 1)) == iota((B_DEV, LANES), 0))
-                x_ref[d, 4 * n + j] = jnp.dot(packets[d][:, 0:B_DEV], picks,
-                                              preferred_element_type=F32).astype(BF16)
-                k_ref[d, pl.ds(4 * n + j, 1), :] = row >> 9
-                return 0
-
-            lax.fori_loop(0, scalar_ref[d, 1, NX * z_ref[0] + n], block, 0)
+    for d in range(count):
+        first = scalar_ref[d, 0, NX * z_ref[0]]
+        last = scalar_ref[d, 0, NX * z_ref[0] + NX - 1] + scalar_ref[d, 1, NX * z_ref[0] + NX - 1]
+        k_ref[d] = all_ref[d, pl.ds(first, 16), :] >> 9
+
+        def pair(j, _, d=d, first=first):
+            lines = [all_ref[d, pl.ds(first + 2 * j + i, 1), :] & (B_DEV - 1) for i in range(2)]
+            picks = jnp.concatenate([one_hot(line == iota((B_DEV, LANES), 0)) for line in lines], axis=1)
+            for part in range(1 + split):
+                rows = E >> split
+                got = jnp.dot(packets[d + part][:, 0:B_DEV], picks,
+                              preferred_element_type=F32).astype(BF16)
+                for i in range(2):
+                    x_ref[d, 2 * j + i, part * rows:(part + 1) * rows] = got[:, i * LANES:(i + 1) * LANES]
             return 0
 
-        lax.fori_loop(0, NX, column, 0)
-
-
-def gather(z, packets):
-    count = len(packets)
+        lax.fori_loop(0, (last - first + 1) >> 1, pair, 0)
+
+
+def gather(z, packets, split):
+    count = len(packets) - split
     return pl.pallas_call(
-        lambda *refs: gather_kernel(*refs, count=count),
+        lambda *refs: gather_kernel(*refs, count=count, split=split),
         out_shape=(jax.ShapeDtypeStruct((count, 16, E, LANES), BF16),
                    jax.ShapeDtypeStruct((count, 16, LANES), I32),
                    jax.ShapeDtypeStruct((count, 8, LANES), I32)),
-        in_specs=[SMEM] + [VMEM] * count,
-        scratch_shapes=[pltpu.VMEM((count, BLOCKS, LANES), I32), pltpu.SMEM((count, 8, LANES), I32),
+        in_specs=[SMEM] + [VMEM] * len(packets),
+        scratch_shapes=[pltpu.VMEM((count, BLOCKS + 16, LANES), I32), pltpu.SMEM((count, 8, LANES), I32),
                         pltpu.SemaphoreType.DMA((count,))],
         cost_estimate=cost(2 + count),
         compiler_params=PARAMS,
@@ -165,10 +173,11 @@
         for n in range(groups):
             for d in range(counts[n]):
                 found = metas[n][d, 1, at_ref[4] + column]
-
-                def move(j, _, n=n, d=d, filled=filled, column=column):
-                    all_ref[filled + j] = xs[n][d, 4 * column + j]
-                    k_ref[pl.ds(filled + j, 1), :] = keys[n][d, pl.ds(4 * column + j, 1), :]
+                first = metas[n][d, 0, at_ref[4] + column] - metas[n][d, 0, at_ref[4]]
+
+                def move(j, _, n=n, d=d, filled=filled, first=first):
+                    all_ref[filled + j] = xs[n][d, first + j]
+                    k_ref[pl.ds(filled + j, 1), :] = keys[n][d, pl.ds(first + j, 1), :]
                     return 0
 
                 lax.fori_loop(0, found, move, 0)
@@ -247,35 +256,43 @@
     plan_ref, list_ref, table_ref, listed_hbm, rows_ref = refs[0:5]
     chunks = refs[5:13]
     table_out, accum_out, new_ref, listed_ref, u_ref, lhs_ref, rhs_ref, load_sem, store_sem = refs[13:]
-    loads = [pltpu.make_async_copy(src, dst, load_sem.at[n])
-             for n, (src, dst) in enumerate(((listed_hbm, listed_ref), (table_ref, new_ref)))]
-    for load in loads:
-        load.start()
-    lane = iota((QUART, LANES), 1)
-    means = []
+    tiles = ROWS_DEV // TILE
+    listed_load = pltpu.make_async_copy(listed_hbm, listed_ref, load_sem.at[tiles])
+    listed_load.start()
+
+    def load(b):
+        at = pl.ds(b * TILE if isinstance(b, int) else pl.multiple_of(b * TILE, TILE), TILE)
+        return pltpu.make_async_copy(table_ref.at[at], new_ref.at[at], load_sem.at[b])
+
+    for b in range(tiles):
+        load(b).start()
+    lane = iota((PIECE, LANES), 1)
+    pieces = []
     for n in range(8):
-        at = slice(n * QUART, (n + 1) * QUART)
-        g = chunks[n][...]
-        mean = jnp.sum(g * g, axis=1, keepdims=True) * (1.0 / E)
-        means.append(mean)
-        rows = rows_ref[NX - 1, at, :]
-        lhs_ref[at, :] = jnp.where((rows >> 7) == lane, mean, 0.0)
-        rhs_ref[at, :] = jnp.where((rows & (LANES - 1)) == lane, 1.0, 0.0)
-    loads[0].wait()
-    for n in range(8):
-        at = slice(n * QUART, (n + 1) * QUART)
-        now = listed_ref[at, E:E + 1] + means[n]
-        place = pl.multiple_of(plan_ref[16 + n] * QUART, QUART)
-        u_ref[pl.ds(place, QUART), :] = (
-            listed_ref[at, 0:E] - 0.5 * chunks[n][...] / (jnp.sqrt(now) + 1e-08))
-    loads[1].wait()
+        for half in range(2):
+            start = (n >> 2) * HALF + half * (HALF // 2) + (n & 3) * PIECE
+            at = slice(start, start + PIECE)
+            g = chunks[n][half * PIECE:(half + 1) * PIECE, :]
+            mean = jnp.sum(g * g, axis=1, keepdims=True) * (1.0 / E)
+            rows = rows_ref[NX - 1, at, :]
+            lhs_ref[at, :] = jnp.where((rows >> 7) == lane, mean, 0.0)
+            rhs_ref[at, :] = jnp.where((rows & (LANES - 1)) == lane, 1.0, 0.0)
+            pieces.append((n, half, at, mean))
+    listed_load.wait()
+    for n, half, at, mean in pieces:
+        now = listed_ref[at, E:E + 1] + mean
+        place = plan_ref[16 + n]
+        place = (place >> 2) * HALF + half * (HALF // 2) + (place & 3) * PIECE
+        u_ref[pl.ds(pl.multiple_of(place, PIECE), PIECE), :] = (
+            listed_ref[at, 0:E]
+            - 0.5 * chunks[n][half * PIECE:(half + 1) * PIECE, :] / (jnp.sqrt(now) + 1e-08))
 
     def put(n):
         new_ref[pl.ds(list_ref[n], 1), :] = u_ref[pl.ds(n, 1), :]
 
     def store(b):
-        tile = pl.ds(pl.multiple_of(b * TILE, TILE), TILE)
-        return pltpu.make_async_copy(new_ref.at[tile], table_out.at[tile], store_sem.at[b])
+        at = pl.ds(b * TILE if isinstance(b, int) else pl.multiple_of(b * TILE, TILE), TILE)
+        return pltpu.make_async_copy(new_ref.at[at], table_out.at[at], store_sem.at[b])
 
     def tile(b, _):
         first, last = plan_ref[b], plan_ref[b + 1]
@@ -286,6 +303,7 @@
                 put(first + i * 8 + j)
             return 0
 
+        load(b).wait()
         lax.fori_loop(0, whole, step, 0)
         lax.fori_loop(first + whole * 8, last, lambda n, _: (put(n), 0)[1], 0)
         store(b).start()
@@ -308,7 +326,8 @@
         scratch_shapes=[pltpu.VMEM((ROWS_DEV, E), F32), pltpu.VMEM((TOUCH + 32, E + LANES), F32),
                         pltpu.VMEM((TOUCH, E), F32),
                         pltpu.VMEM((TOUCH, LANES), F32), pltpu.VMEM((TOUCH, LANES), F32),
-                        pltpu.SemaphoreType.DMA((2,)), pltpu.SemaphoreType.DMA((ROWS_DEV // TILE,))],
+                        pltpu.SemaphoreType.DMA((ROWS_DEV // TILE + 1,)),
+                        pltpu.SemaphoreType.DMA((ROWS_DEV // TILE,))],
         compiler_params=PARAMS,
         name="update",
     )(plan, natural, in_hbm(table), in_hbm(listed), rows, *chunks)
@@ -336,10 +355,10 @@
     z, x = me // NX, me % NX
 
     def ordered(listed):
-        halves = listed.reshape(NC, NY, QUART)
+        halves = listed.reshape(NC, 2, NY, PIECE)
         halves = jnp.where(c == 0, halves[::-1], halves)
-        doubled = jnp.concatenate([halves, halves], axis=1)
-        return lax.dynamic_slice(doubled, (0, y, 0), (NC, NY, QUART)).reshape(TOUCH)
+        doubled = jnp.concatenate([halves, halves], axis=2)
+        return lax.dynamic_slice(doubled, (0, 0, y, 0), (NC, 2, NY, PIECE)).reshape(TOUCH)
 
     own_list = touched.reshape(TOUCH)
     lists = {0: ordered(own_list)}
@@ -355,29 +374,39 @@
     packet = pack(row_ids.reshape(32, LANES), bag_ids.reshape(32, LANES),
                   pooled_grad.reshape(B_DEV, E))
     got = {0: packet}
-    for k in range(1, 5):
+    for k in range(1, 4):
         got[-k] = lax.ppermute(got[1 - k], "shard", z_pairs(1))
-        if k < 4:
-            got[k] = lax.ppermute(got[k - 1], "shard", z_pairs(-1))
+        got[k] = lax.ppermute(got[k - 1], "shard", z_pairs(-1))
+    last = [lax.ppermute(got[-3][:E // 2], "shard", z_pairs(1))]
+    last.append(lax.ppermute(got[3][E // 2:], "shard", z_pairs(-1)))
     gathered = []
-    for sources in ((0,), (-1, 1), (-2, 2), (-3, 3), (-4,)):
-        gathered.append(gather(z.reshape(1), [got[k] for k in sources]))
+    for sources in ((0,), (-1, 1), (-2, 2), (-3, 3), None):
+        packets = [got[k] for k in sources] if sources else last
+        gathered.append(gather(z.reshape(1), packets, int(sources is None)))
 
     listed = listed_values(order, rows, accum.reshape(32, LANES), table)
     at = jnp.concatenate([(x + jnp.array(ORDER, I32)) % NX, (NX * z).reshape(1)])
-    both = {}
+    first, second = {}, {}
     for base, ks in ((0, (2,)), (1, (1, 3)), (3, (0,))):
         send, keep = sums(at, base, len(ks), gathered, rows)
         swapped = lax.ppermute(send, "grp", C_PAIRS)
-        total = keep + swapped
         for n, k in enumerate(ks):
-            both[k] = total[n]
-    total = both[0]
+            first[k] = keep[n, :HALF // 2] + swapped[n, :HALF // 2]
+            if k:
+                first[k] = lax.ppermute(first[k], "shard", x_pairs(k))
+            second[k] = (keep[n, HALF // 2:] + swapped[n, HALF // 2:]).reshape(NY, PIECE, E)
+    side = [jnp.stack([second[k][j] for k in range(NX)]) for j in range(NY)]
+    for j in (2, 1, 3):
+        side[j] = lax.ppermute(side[j], "grp", y_pairs(j))
+    low = (first[0] + first[2] + first[1] + first[3]).reshape(NY, PIECE, E)
+    part_low = low[0]
+    for j in (2, 1, 3):
+        part_low = part_low + lax.ppermute(low[j], "grp", y_pairs(j))
+    high = side[0] + side[2] + side[1] + side[3]
+    part_high = high[0]
     for k in (2, 1, 3):
-        total = total + lax.ppermute(both[k], "shard", x_pairs(k))
-    part = total[0:QUART]
-    for j in range(1, NY):
-        part = part + lax.ppermute(total[j * QUART:(j + 1) * QUART], "grp", y_pairs(j))
+        part_high = part_high + lax.ppermute(high[k], "shard", x_pairs(k))
+    part = jnp.concatenate([part_low, part_high], axis=0)
     mine = [part] + [lax.ppermute(part, "grp", y_pairs(-j)) for j in range(1, NY)]
     other = [lax.ppermute(m, "grp", C_PAIRS) for m in mine]
     new_table, new_accum = update(plan, own_list, table, listed, rows, other + mine)

time: 130 us -> 124 us (0.954)
  waiting for transfers between devices: 44.9 us -> 22.5 us
  starting transfers between devices: 41.8 us -> 55.2 us
  Pallas kernels: 36.8 us -> 31.1 us
  other arithmetic: 0.85 us -> 6.31 us
  local copies, waits for them, and re-layouts: 4.72 us -> 7.23 us
    ppermute x4 -> x3, waiting for transfers between devices: 14.5 us -> 0.01 us  [body(): got[-k] = lax.ppermute(got[1 - k], 'shard', z_pairs(1))]
    ppermute x6 -> x14, waiting for transfers between devices: 28.1 us -> 14 us  [the longest x3 4.46 us: body(): side[j] = lax.ppermute(side[j], 'grp', y_pairs(j))]
    ppermute x6 -> x14, starting transfers between devices: 10.4 us -> 20.4 us  [the longest x3 5.58 us: body(): side[j] = lax.ppermute(side[j], 'grp', y_pairs(j))]
    ppermute x3, waiting for transfers between devices: 0.01 us -> 7.76 us  [body(): got[k] = lax.ppermute(got[k - 1], 'shard', z_pairs(-1))]
    pallas_call x5, Pallas kernels: 12.3 us -> 7.15 us  [gather(): pl.pallas_call(lambda *refs: gather_kernel(*refs, count=count, split=spli...]
    add x3 -> x7, other arithmetic: 0.34 us -> 3 us  [the longest x2 1.61 us: body(): first[k] = keep[n, :HALF // 2] + swapped[n, :HALF // 2]]
    ppermute x4, starting transfers between devices: 5.4 us -> 7.89 us  [body(): other = [lax.ppermute(m, 'grp', C_PAIRS) for m in mine]]
    ppermute x3, waiting for transfers between devices: 2.19 us -> 0.01 us  [body(): lax.ppermute(part, 'grp', y_pairs(-j))]
  transfers between devices with their start and end apart: 26 -> 33, of which waited for: 9 -> 13; matrix products, arithmetic and copies ran while one was open for 1% -> 5% of each run, Pallas kernels for 18% -> 16%
where the time goes in v6:
time: 124 us; the launch traced here: 123 us
  starting transfers between devices  55.2 us (45%)
  Pallas kernels  31.1 us (25%)
  waiting for transfers between devices  22.5 us (18%)
  local copies, waits for them, and re-layouts  7.23 us (6%)
  other arithmetic  6.31 us (5%)
    ppermute x3, starting transfers between devices, body(): got[k] = lax.ppermute(got[k - 1], 'shard', z_pairs(-1))  12.5 us
    ppermute x4, starting transfers between devices, body(): other = [lax.ppermute(m, 'grp', C_PAIRS) for m in mine]  7.89 us
    ppermute x3, waiting for transfers between devices, body(): got[k] = lax.ppermute(got[k - 1], 'shard', z_pairs(-1))  7.76 us
    pallas_call x1, Pallas kernels, update(): pl.pallas_call(update_kernel, out_shape=(jax.ShapeDtypeStruct((ROWS_DEV,...  7.69 us
    pallas_call x3, Pallas kernels, sums(): pl.pallas_call(lambda *refs: sums_kernel(*refs, counts=counts, base=base,...  7.29 us
    pallas_call x5, Pallas kernels, gather(): pl.pallas_call(lambda *refs: gather_kernel(*refs, count=count, split=spli...  7.15 us
    ppermute x3, starting transfers between devices, body(): swapped = lax.ppermute(send, 'grp', C_PAIRS)  6.48 us
    pallas_call x1, Pallas kernels, listed_values(): pl.pallas_call(listed_kernel, out_shape=jax.ShapeDtypeStruct((TOUCH + 32,...  6.32 us
  transfers between devices with their start and end apart: 33, of which 13 were waited for; matrix products, arithmetic and copies ran while one was open for 5% of the time, Pallas kernels for 16%

profile of v6, /device:TPU:1, one launch (start us, length us, event | category | flops | bytes accessed | tf_op | source)
XLA Modules:
  0.0 123.5 jit_solution(16623107656133174270)
XLA Ops:
  0.6 2.1 %collective-permute-start.2 = (s32[1024]{0:T(1024)}, s32[1024]{0:T(1024)S(1)}, u32[]{:S(2)}, u32[]{:S(2)}) collective-permute-start(s32[1024]{0:T(1024)} %bitcast.36), channel_id=1, source_target_pairs={{0,1},{1,2},{2,3},{3,0},{4,5},{5,6},{6,7},{7,4},{8,9},{9,10},{10,1... | collective-permute-start | bytes 12296 | tf_op jit(solution)/shard_map/ppermute | solution.py:366
  5.7 2.6 %pack.1.refs_1_ = bf16[256,640]{1,0:T(8,128)(2,1)S(1)} custom-call(s32[32,128]{1,0:T(8,128)} %bitcast.43, s32[32,128]{1,0:T(8,128)} %bitcast.44, bf16[512,256]{1,0:T(8,128)(2,1)} %bitcast.42), custom_call_target="tpu_custom_call" | custom-call | flops 2400000000 | bytes 12000000 | tf_op jit(solution)/shard_map/pack/pallas_call | solution.py:99
  8.4 5.7 %collective-permute-start.4 = (bf16[256,640]{1,0:T(8,128)(2,1)S(1)}, bf16[256,640]{1,0:T(8,128)(2,1)S(1)}, u32[]{:S(2)}, u32[]{:S(2)}) collective-permute-start(bf16[256,640]{1,0:T(8,128)(2,1)S(1)} %pack.1.refs_1_), channel_id=1, source_target_pairs={{0,28},{1,29},{2,30},{3,31},{4,0},{5,1},{6,2},{7,3},{8,4},{9,5},{1... | collective-permute-start | bytes 983048 | tf_op jit(solution)/shard_map/ppermute | solution.py:379
  16.8 2.8 %collective-permute-done.4.refs_2_ = bf16[256,640]{1,0:T(8,128)(2,1)S(1)} collective-permute-done((bf16[256,640]{1,0:T(8,128)(2,1)S(1)}, bf16[256,640]{1,0:T(8,128)(2,1)S(1)}, u32[]{:S(2)}, u32[]{:S(2)}) %collective-permute-start.4) | collective-permute-done | bytes 327712 | tf_op jit(solution)/shard_map/ppermute | solution.py:379
  19.6 3.4 %collective-permute-start.6 = (bf16[256,640]{1,0:T(8,128)(2,1)S(1)}, bf16[256,640]{1,0:T(8,128)(2,1)S(1)}, u32[]{:S(2)}, u32[]{:S(2)}) collective-permute-start(bf16[256,640]{1,0:T(8,128)(2,1)S(1)} %collective-permute-done.4.refs_2_), channel_id=1, source_target_pairs={{0,28},{1,29},{2,30},{3,31},{4,0},{5,1},{6,2},{7,3},{8,4},{9,5},{1... | collective-permute-start | bytes 983048 | tf_op jit(solution)/shard_map/ppermute | solution.py:379
  23.4 4.3 %collective-permute-done.6.refs_2_ = bf16[256,640]{1,0:T(8,128)(2,1)S(1)} collective-permute-done((bf16[256,640]{1,0:T(8,128)(2,1)S(1)}, bf16[256,640]{1,0:T(8,128)(2,1)S(1)}, u32[]{:S(2)}, u32[]{:S(2)}) %collective-permute-start.6) | collective-permute-done | bytes 327712 | tf_op jit(solution)/shard_map/ppermute | solution.py:379
  27.7 3.4 %collective-permute-start.8 = (bf16[256,640]{1,0:T(8,128)(2,1)S(1)}, bf16[256,640]{1,0:T(8,128)(2,1)S(1)}, u32[]{:S(2)}, u32[]{:S(2)}) collective-permute-start(bf16[256,640]{1,0:T(8,128)(2,1)S(1)} %collective-permute-done.6.refs_2_), channel_id=1, source_target_pairs={{0,28},{1,29},{2,30},{3,31},{4,0},{5,1},{6,2},{7,3},{8,4},{9,5},{1... | collective-permute-start | bytes 983048 | tf_op jit(solution)/shard_map/ppermute | solution.py:379
  35.1 3.2 %collective-permute-start.10 = (bf16[128,640]{1,0:T(8,128)(2,1)S(1)}, bf16[128,640]{1,0:T(8,128)(2,1)S(1)}, u32[]{:S(2)}, u32[]{:S(2)}) collective-permute-start(bf16[128,640]{1,0:T(8,128)(2,1)S(1)} %slice.205), channel_id=1, source_target_pairs={{0,28},{1,29},{2,30},{3,31},{4,0},{5,1},{6,2},{7,3},{8,4},{9,5},{1... | collective-permute-start | bytes 491528 | tf_op jit(solution)/shard_map/ppermute | solution.py:381
  40.6 3.4 %collective-permute-done.9.refs_1_ = bf16[128,640]{1,0:T(8,128)(2,1)S(1)} collective-permute-done((bf16[128,640]{1,0:T(8,128)(2,1)S(1)}, bf16[128,640]{1,0:T(8,128)(2,1)S(1)}, u32[]{:S(2)}, u32[]{:S(2)}) %collective-permute-start.9) | collective-permute-done | bytes 163872 | tf_op jit(solution)/shard_map/ppermute | solution.py:380
  45.7 2.2 %shard_map.92 = (f32[1,512,256]{2,1,0:T(8,128)S(1)}, f32[1,512,256]{2,1,0:T(8,128)S(1)}) custom-call(s32[5]{0:T(128)S(1)} %pad_add_fusion.2.refs_0_, s32[1,8,128]{2,1,0:T(8,128)S(1)} %get-tuple-element.25.refs_1_, s32[2,8,128]{2,1,0:T(8,128)S(1)} %get-tuple-element.26.refs_2_, s32[2,8,128]{2,1,0:T(8,128)S(1)} %get-tuple-element.27.refs_3_, ...), custom_call_target="tpu_custom_call" | custom-call | flops 1200000000 | bytes 6000000 | tf_op jit(solution)/shard_map/pallas_call | solution.py:215
  47.9 5.8 %collective-permute-start.12 = (f32[1,512,256]{2,1,0:T(8,128)S(1)}, f32[1,512,256]{2,1,0:T(8,128)S(1)}, u32[]{:S(2)}, u32[]{:S(2)}) collective-permute-start(f32[1,512,256]{2,1,0:T(8,128)S(1)} %get-tuple-element.43), channel_id=1, source_target_pairs={{0,32},{32,0},{64,96},{96,64},{128,160},{160,128},{192,224},{224,1... | collective-permute-start | bytes 1572872 | tf_op jit(solution)/shard_map/ppermute | solution.py:392
  53.7 3.0 %shard_map.93 = (f32[2,512,256]{2,1,0:T(8,128)S(1)}, f32[2,512,256]{2,1,0:T(8,128)S(1)}) custom-call(s32[5]{0:T(128)S(1)} %pad_add_fusion.2.refs_0_, s32[1,8,128]{2,1,0:T(8,128)S(1)} %get-tuple-element.25.refs_1_, s32[2,8,128]{2,1,0:T(8,128)S(1)} %get-tuple-element.26.refs_2_, s32[2,8,128]{2,1,0:T(8,128)S(1)} %get-tuple-element.27.refs_3_, ...), custom_call_target="tpu_custom_call" | custom-call | flops 2400000000 | bytes 12000000 | tf_op jit(solution)/shard_map/pallas_call | solution.py:215
  64.6 2.9 %collective-permute-start.20 = (f32[4,64,256]{2,1,0:T(8,128)}, f32[4,64,256]{2,1,0:T(8,128)}, u32[]{:S(2)}, u32[]{:S(2)}) collective-permute-start(f32[4,64,256]{2,1,0:T(8,128)} %pad_maximum_fusion), channel_id=1, source_target_pairs={{0,128},{32,160},{64,192},{96,224},{128,0},{160,32},{192,64},{224,... | collective-permute-start | bytes 786440 | tf_op jit(solution)/shard_map/ppermute | solution.py:400
  69.4 2.2 %collective-permute-start.22 = (f32[4,64,256]{2,1,0:T(8,128)}, f32[4,64,256]{2,1,0:T(8,128)}, u32[]{:S(2)}, u32[]{:S(2)}) collective-permute-start(f32[4,64,256]{2,1,0:T(8,128)} %pad_maximum_fusion.2), channel_id=1, source_target_pairs={{0,192},{32,224},{64,0},{96,32},{128,64},{160,96},{192,128},{224,1... | collective-permute-start | bytes 786440 | tf_op jit(solution)/shard_map/ppermute | solution.py:400
  73.9 2.2 %collective-permute-start.16 = (f32[256,256]{1,0:T(8,128)S(1)}, f32[256,256]{1,0:T(8,128)S(1)}, u32[]{:S(2)}, u32[]{:S(2)}) collective-permute-start(f32[256,256]{1,0:T(8,128)S(1)} %get-tuple-element.51), channel_id=1, source_target_pairs={{0,3},{1,0},{2,1},{3,2},{4,7},{5,4},{6,5},{7,6},{8,11},{9,8},{10,9... | collective-permute-start | bytes 786440 | tf_op jit(solution)/shard_map/ppermute | solution.py:396
  76.1 4.1 %collective-permute-done.21 = f32[4,64,256]{2,1,0:T(8,128)} collective-permute-done((f32[4,64,256]{2,1,0:T(8,128)}, f32[4,64,256]{2,1,0:T(8,128)}, u32[]{:S(2)}, u32[]{:S(2)}) %collective-permute-start.21) | collective-permute-done | bytes 262176 | tf_op jit(solution)/shard_map/ppermute | solution.py:400
  81.5 3.8 %collective-permute-start.23 = (f32[64,256]{1,0:T(8,128)S(1)}, f32[64,256]{1,0:T(8,128)S(1)}, u32[]{:S(2)}, u32[]{:S(2)}) collective-permute-start(f32[64,256]{1,0:T(8,128)S(1)} %get-tuple-element.57), channel_id=1, source_target_pairs={{0,2},{1,3},{2,0},{3,1},{4,6},{5,7},{6,4},{7,5},{8,10},{9,11},{10,... | collective-permute-start | bytes 196616 | tf_op jit(solution)/shard_map/ppermute | solution.py:408
  88.4 2.2 %collective-permute-start.19 = (f32[64,256]{1,0:T(8,128)S(1)}, f32[64,256]{1,0:T(8,128)S(1)}, u32[]{:S(2)}, u32[]{:S(2)}) collective-permute-start(f32[64,256]{1,0:T(8,128)S(1)} %get-tuple-element.55), channel_id=1, source_target_pairs={{0,192},{32,224},{64,0},{96,32},{128,64},{160,96},{192,128},{224,1... | collective-permute-start | bytes 196616 | tf_op jit(solution)/shard_map/ppermute | solution.py:404
  90.8 2.2 %collective-permute-done.17 = f32[64,256]{1,0:T(8,128)S(1)} collective-permute-done((f32[64,256]{1,0:T(8,128)S(1)}, f32[64,256]{1,0:T(8,128)S(1)}, u32[]{:S(2)}, u32[]{:S(2)}) %collective-permute-start.17) | collective-permute-done | bytes 65568 | tf_op jit(solution)/shard_map/ppermute | solution.py:404
  98.0 3.6 %collective-permute-start.26 = (f32[128,256]{1,0:T(8,128)S(1)}, f32[128,256]{1,0:T(8,128)S(1)}, u32[]{:S(2)}, u32[]{:S(2)}) collective-permute-start(f32[128,256]{1,0:T(8,128)S(1)} %pad_maximum_fusion.3.refs_9_), channel_id=1, source_target_pairs={{0,32},{32,0},{64,96},{96,64},{128,160},{160,128},{192,224},{224,1... | collective-permute-start | bytes 393224 | tf_op jit(solution)/shard_map/ppermute | solution.py:411
  101.6 3.4 %collective-permute-start.32 = (f32[128,256]{1,0:T(8,128)S(1)}, f32[128,256]{1,0:T(8,128)S(1)}, u32[]{:S(2)}, u32[]{:S(2)}) collective-permute-start(f32[128,256]{1,0:T(8,128)S(1)} %collective-permute-done.31.refs_12_), channel_id=1, source_target_pairs={{0,32},{32,0},{64,96},{96,64},{128,160},{160,128},{192,224},{224,1... | collective-permute-start | bytes 393224 | tf_op jit(solution)/shard_map/ppermute | solution.py:411
  105.9 2.2 %copy-done = f32[4096,256]{1,0:T(8,128)S(1)} copy-done((f32[4096,256]{1,0:T(8,128)S(1)}, f32[4096,256]{1,0:T(8,128)}, u32[]{:S(2)}) %copy-start) | copy-done | bytes 4194328
  108.1 6.3 %listed_values.1.refs_3_ = f32[1056,384]{1,0:T(8,128)S(1)} custom-call(s32[8,128]{1,0:T(8,128)S(1)} %reshape_reshape.7.list_ref, s32[4,1024,128]{2,1,0:T(8,128)S(1)} %broadcast_in_dim.2.rows_ref.refs_16_.refs_4_, f32[32,128]{1,0:T(8,128)S(1)} %bitcast.41, f32[4096,256]{1,0:T(8,128)S(1)} %copy-done), custom_call_target="tpu_custom_call" | custom-call | flops 3600000000 | bytes 18000000 | tf_op jit(solution)/shard_map/listed_values/pallas_call | solution.py:245
  115.6 7.7 %update.1 = (f32[4096,256]{1,0:T(8,128)}, f32[32,128]{1,0:T(8,128)}) custom-call(s32[24]{0:T(128)S(1)} %pad_add_fusion.1.refs_0_, s32[1024]{0:T(1024)S(1)} %bitcast.40, f32[4096,256]{1,0:T(8,128)} %refs_2_.1, f32[1056,384]{1,0:T(8,128)} %copy-done.1, s32[4,1024,128]{2,1,0:T(8,128)S(1)} %broadcast_in_dim.2.rows_ref.refs_16_.refs_4_, ...), custom_call_target="tpu_custom_call" | custom-call | tf_op jit(solution)/shard_map/update/pallas_call | solution.py:321
  (111 shorter events, 37.7 us)
Async XLA Ops:
  0.6 15.9 %collective-permute-start.2 = (s32[1024]{0:T(1024)}, s32[1024]{0:T(1024)S(1)}, u32[]{:S(2)}, u32[]{:S(2)}) collective-permute-start(s32[1024]{0:T(1024)} %bitcast.36), channel_id=1, source_target_pairs={{0,1},{1,2},{2,3},{3,0},{4,5},{5,6},{6,7},{7,4},{8,9},{9,10},{10,1... | collective-permute-start | bytes 12296 | tf_op jit(solution)/shard_map/ppermute | solution.py:366
  2.7 13.9 %collective-permute-start.1 = (s32[1024]{0:T(1024)}, s32[1024]{0:T(1024)S(1)}, u32[]{:S(2)}, u32[]{:S(2)}) collective-permute-start(s32[1024]{0:T(1024)} %bitcast.37), channel_id=1, source_target_pairs={{0,3},{1,0},{2,1},{3,2},{4,7},{5,4},{6,5},{7,6},{8,11},{9,8},{10,9... | collective-permute-start | bytes 12296 | tf_op jit(solution)/shard_map/ppermute | solution.py:366
  4.1 12.6 %collective-permute-start = (s32[1024]{0:T(1024)}, s32[1024]{0:T(1024)S(1)}, u32[]{:S(2)}, u32[]{:S(2)}) collective-permute-start(s32[1024]{0:T(1024)} %bitcast.38), channel_id=1, source_target_pairs={{0,2},{1,3},{2,0},{3,1},{4,6},{5,7},{6,4},{7,5},{8,10},{9,11},{10,... | collective-permute-start | bytes 12296 | tf_op jit(solution)/shard_map/ppermute | solution.py:366
  8.4 11.2 %collective-permute-start.4 = (bf16[256,640]{1,0:T(8,128)(2,1)S(1)}, bf16[256,640]{1,0:T(8,128)(2,1)S(1)}, u32[]{:S(2)}, u32[]{:S(2)}) collective-permute-start(bf16[256,640]{1,0:T(8,128)(2,1)S(1)} %pack.1.refs_1_), channel_id=1, source_target_pairs={{0,28},{1,29},{2,30},{3,31},{4,0},{5,1},{6,2},{7,3},{8,4},{9,5},{1... | collective-permute-start | bytes 983048 | tf_op jit(solution)/shard_map/ppermute | solution.py:379
  14.0 9.0 %collective-permute-start.3 = (bf16[256,640]{1,0:T(8,128)(2,1)S(1)}, bf16[256,640]{1,0:T(8,128)(2,1)S(1)}, u32[]{:S(2)}, u32[]{:S(2)}) collective-permute-start(bf16[256,640]{1,0:T(8,128)(2,1)S(1)} %pack.1.refs_1_), channel_id=1, source_target_pairs={{0,4},{1,5},{2,6},{3,7},{4,8},{5,9},{6,10},{7,11},{8,12},{9,13},{1... | collective-permute-start | bytes 983048 | tf_op jit(solution)/shard_map/ppermute | solution.py:378
  19.6 8.1 %collective-permute-start.6 = (bf16[256,640]{1,0:T(8,128)(2,1)S(1)}, bf16[256,640]{1,0:T(8,128)(2,1)S(1)}, u32[]{:S(2)}, u32[]{:S(2)}) collective-permute-start(bf16[256,640]{1,0:T(8,128)(2,1)S(1)} %collective-permute-done.4.refs_2_), channel_id=1, source_target_pairs={{0,28},{1,29},{2,30},{3,31},{4,0},{5,1},{6,2},{7,3},{8,4},{9,5},{1... | collective-permute-start | bytes 983048 | tf_op jit(solution)/shard_map/ppermute | solution.py:379
  23.0 8.1 %collective-permute-start.5 = (bf16[256,640]{1,0:T(8,128)(2,1)S(1)}, bf16[256,640]{1,0:T(8,128)(2,1)S(1)}, u32[]{:S(2)}, u32[]{:S(2)}) collective-permute-start(bf16[256,640]{1,0:T(8,128)(2,1)S(1)} %collective-permute-done.3.refs_1_), channel_id=1, source_target_pairs={{0,4},{1,5},{2,6},{3,7},{4,8},{5,9},{6,10},{7,11},{8,12},{9,13},{1... | collective-permute-start | bytes 983048 | tf_op jit(solution)/shard_map/ppermute | solution.py:378
  27.7 7.4 %collective-permute-start.8 = (bf16[256,640]{1,0:T(8,128)(2,1)S(1)}, bf16[256,640]{1,0:T(8,128)(2,1)S(1)}, u32[]{:S(2)}, u32[]{:S(2)}) collective-permute-start(bf16[256,640]{1,0:T(8,128)(2,1)S(1)} %collective-permute-done.6.refs_2_), channel_id=1, source_target_pairs={{0,28},{1,29},{2,30},{3,31},{4,0},{5,1},{6,2},{7,3},{8,4},{9,5},{1... | collective-permute-start | bytes 983048 | tf_op jit(solution)/shard_map/ppermute | solution.py:379
  31.1 7.2 %collective-permute-start.7 = (bf16[256,640]{1,0:T(8,128)(2,1)S(1)}, bf16[256,640]{1,0:T(8,128)(2,1)S(1)}, u32[]{:S(2)}, u32[]{:S(2)}) collective-permute-start(bf16[256,640]{1,0:T(8,128)(2,1)S(1)} %collective-permute-done.5.refs_1_), channel_id=1, source_target_pairs={{0,4},{1,5},{2,6},{3,7},{4,8},{5,9},{6,10},{7,11},{8,12},{9,13},{1... | collective-permute-start | bytes 983048 | tf_op jit(solution)/shard_map/ppermute | solution.py:378
  47.9 11.6 %collective-permute-start.12 = (f32[1,512,256]{2,1,0:T(8,128)S(1)}, f32[1,512,256]{2,1,0:T(8,128)S(1)}, u32[]{:S(2)}, u32[]{:S(2)}) collective-permute-start(f32[1,512,256]{2,1,0:T(8,128)S(1)} %get-tuple-element.43), channel_id=1, source_target_pairs={{0,32},{32,0},{64,96},{96,64},{128,160},{160,128},{192,224},{224,1... | collective-permute-start | bytes 1572872 | tf_op jit(solution)/shard_map/ppermute | solution.py:392
  64.6 9.3 %collective-permute-start.20 = (f32[4,64,256]{2,1,0:T(8,128)}, f32[4,64,256]{2,1,0:T(8,128)}, u32[]{:S(2)}, u32[]{:S(2)}) collective-permute-start(f32[4,64,256]{2,1,0:T(8,128)} %pad_maximum_fusion), channel_id=1, source_target_pairs={{0,128},{32,160},{64,192},{96,224},{128,0},{160,32},{192,64},{224,... | collective-permute-start | bytes 786440 | tf_op jit(solution)/shard_map/ppermute | solution.py:400
  68.2 12.0 %collective-permute-start.21 = (f32[4,64,256]{2,1,0:T(8,128)}, f32[4,64,256]{2,1,0:T(8,128)}, u32[]{:S(2)}, u32[]{:S(2)}) collective-permute-start(f32[4,64,256]{2,1,0:T(8,128)} %pad_maximum_fusion.1), channel_id=1, source_target_pairs={{0,64},{32,96},{64,128},{96,160},{128,192},{160,224},{192,0},{224,... | collective-permute-start | bytes 786440 | tf_op jit(solution)/shard_map/ppermute | solution.py:400
  69.4 10.8 %collective-permute-start.22 = (f32[4,64,256]{2,1,0:T(8,128)}, f32[4,64,256]{2,1,0:T(8,128)}, u32[]{:S(2)}, u32[]{:S(2)}) collective-permute-start(f32[4,64,256]{2,1,0:T(8,128)} %pad_maximum_fusion.2), channel_id=1, source_target_pairs={{0,192},{32,224},{64,0},{96,32},{128,64},{160,96},{192,128},{224,1... | collective-permute-start | bytes 786440 | tf_op jit(solution)/shard_map/ppermute | solution.py:400
  71.8 14.6 %collective-permute-start.13 = (f32[256,256]{1,0:T(8,128)}, f32[256,256]{1,0:T(8,128)S(1)}, u32[]{:S(2)}, u32[]{:S(2)}) collective-permute-start(f32[256,256]{1,0:T(8,128)} %get-tuple-element.52), channel_id=1, source_target_pairs={{0,2},{1,3},{2,0},{3,1},{4,6},{5,7},{6,4},{7,5},{8,10},{9,11},{10,... | collective-permute-start | bytes 786440 | tf_op jit(solution)/shard_map/ppermute | solution.py:396
  73.4 14.7 %collective-permute-start.15 = (f32[256,256]{1,0:T(8,128)}, f32[256,256]{1,0:T(8,128)S(1)}, u32[]{:S(2)}, u32[]{:S(2)}) collective-permute-start(f32[256,256]{1,0:T(8,128)} %get-tuple-element.48), channel_id=1, source_target_pairs={{0,1},{1,2},{2,3},{3,0},{4,5},{5,6},{6,7},{7,4},{8,9},{9,10},{10,1... | collective-permute-start | bytes 786440 | tf_op jit(solution)/shard_map/ppermute | solution.py:396
  73.9 14.3 %collective-permute-start.16 = (f32[256,256]{1,0:T(8,128)S(1)}, f32[256,256]{1,0:T(8,128)S(1)}, u32[]{:S(2)}, u32[]{:S(2)}) collective-permute-start(f32[256,256]{1,0:T(8,128)S(1)} %get-tuple-element.51), channel_id=1, source_target_pairs={{0,3},{1,0},{2,1},{3,2},{4,7},{5,4},{6,5},{7,6},{8,11},{9,8},{10,9... | collective-permute-start | bytes 786440 | tf_op jit(solution)/shard_map/ppermute | solution.py:396
  81.5 9.0 %collective-permute-start.23 = (f32[64,256]{1,0:T(8,128)S(1)}, f32[64,256]{1,0:T(8,128)S(1)}, u32[]{:S(2)}, u32[]{:S(2)}) collective-permute-start(f32[64,256]{1,0:T(8,128)S(1)} %get-tuple-element.57), channel_id=1, source_target_pairs={{0,2},{1,3},{2,0},{3,1},{4,6},{5,7},{6,4},{7,5},{8,10},{9,11},{10,... | collective-permute-start | bytes 196616 | tf_op jit(solution)/shard_map/ppermute | solution.py:408
  94.9 6.7 %collective-permute-start.31 = (f32[128,256]{1,0:T(8,128)S(1)}, f32[128,256]{1,0:T(8,128)S(1)}, u32[]{:S(2)}, u32[]{:S(2)}) collective-permute-start(f32[128,256]{1,0:T(8,128)S(1)} %pad_maximum_fusion.3.refs_9_), channel_id=1, source_target_pairs={{0,64},{32,96},{64,128},{96,160},{128,192},{160,224},{192,0},{224,... | collective-permute-start | bytes 393224 | tf_op jit(solution)/shard_map/ppermute | solution.py:410
  95.0 10.0 %collective-permute-start.29 = (f32[128,256]{1,0:T(8,128)S(1)}, f32[128,256]{1,0:T(8,128)S(1)}, u32[]{:S(2)}, u32[]{:S(2)}) collective-permute-start(f32[128,256]{1,0:T(8,128)S(1)} %pad_maximum_fusion.3.refs_9_), channel_id=1, source_target_pairs={{0,128},{32,160},{64,192},{96,224},{128,0},{160,32},{192,64},{224,... | collective-permute-start | bytes 393224 | tf_op jit(solution)/shard_map/ppermute | solution.py:410
  96.8 8.3 %collective-permute-start.27 = (f32[128,256]{1,0:T(8,128)S(1)}, f32[128,256]{1,0:T(8,128)S(1)}, u32[]{:S(2)}, u32[]{:S(2)}) collective-permute-start(f32[128,256]{1,0:T(8,128)S(1)} %pad_maximum_fusion.3.refs_9_), channel_id=1, source_target_pairs={{0,192},{32,224},{64,0},{96,32},{128,64},{160,96},{192,128},{224,1... | collective-permute-start | bytes 393224 | tf_op jit(solution)/shard_map/ppermute | solution.py:410
  98.0 17.6 %collective-permute-start.26 = (f32[128,256]{1,0:T(8,128)S(1)}, f32[128,256]{1,0:T(8,128)S(1)}, u32[]{:S(2)}, u32[]{:S(2)}) collective-permute-start(f32[128,256]{1,0:T(8,128)S(1)} %pad_maximum_fusion.3.refs_9_), channel_id=1, source_target_pairs={{0,32},{32,0},{64,96},{96,64},{128,160},{160,128},{192,224},{224,1... | collective-permute-start | bytes 393224 | tf_op jit(solution)/shard_map/ppermute | solution.py:411
  101.6 14.0 %collective-permute-start.32 = (f32[128,256]{1,0:T(8,128)S(1)}, f32[128,256]{1,0:T(8,128)S(1)}, u32[]{:S(2)}, u32[]{:S(2)}) collective-permute-start(f32[128,256]{1,0:T(8,128)S(1)} %collective-permute-done.31.refs_12_), channel_id=1, source_target_pairs={{0,32},{32,0},{64,96},{96,64},{128,160},{160,128},{192,224},{224,1... | collective-permute-start | bytes 393224 | tf_op jit(solution)/shard_map/ppermute | solution.py:411
  105.0 10.6 %collective-permute-start.30 = (f32[128,256]{1,0:T(8,128)S(1)}, f32[128,256]{1,0:T(8,128)S(1)}, u32[]{:S(2)}, u32[]{:S(2)}) collective-permute-start(f32[128,256]{1,0:T(8,128)S(1)} %collective-permute-done.29.refs_11_), channel_id=1, source_target_pairs={{0,32},{32,0},{64,96},{96,64},{128,160},{160,128},{192,224},{224,1... | collective-permute-start | bytes 393224 | tf_op jit(solution)/shard_map/ppermute | solution.py:411
  105.0 10.6 %collective-permute-start.28 = (f32[128,256]{1,0:T(8,128)S(1)}, f32[128,256]{1,0:T(8,128)S(1)}, u32[]{:S(2)}, u32[]{:S(2)}) collective-permute-start(f32[128,256]{1,0:T(8,128)S(1)} %collective-permute-done.27.refs_10_), channel_id=1, source_target_pairs={{0,32},{32,0},{64,96},{96,64},{128,160},{160,128},{192,224},{224,1... | collective-permute-start | bytes 393224 | tf_op jit(solution)/shard_map/ppermute | solution.py:411
  (16 other events, 109.6 us)

commit v7 on v6

--- a/solution.py
+++ b/solution.py
@@ -11,7 +11,6 @@
 TOUCH = 1024
 HALF = TOUCH // 2
 QUART = TOUCH // 8
-PIECE = QUART // 2
 TILE = 512
 LOOK = 4096
 B_DEV = 512
@@ -116,33 +115,35 @@
     x_ref, k_ref, m_ref, all_ref, scalar_ref, sem = refs[count + split:]
     copies = []
     for d in range(count):
-        tail = packets[d + split][3 * BLOCKS - 128 * split:3 * BLOCKS + 16 - 128 * split, B_DEV:WIDTH]
-        side = tail.astype(F32).astype(I32)
+        cut = 128 if split and d == count - 1 else 0
+        tail = packets[-1] if cut else packets[d]
+        side = tail[3 * BLOCKS - cut:3 * BLOCKS + 16 - cut, B_DEV:WIDTH].astype(F32).astype(I32)
         m_ref[d] = jnp.where(iota((8, LANES), 0) == 0, side[0:8], side[8:16])
         copies.append(pltpu.make_async_copy(m_ref.at[d], scalar_ref.at[d], sem.at[d]))
         copies[d].start()
     for d in range(count):
+        cut = 128 if split and d == count - 1 else 0
+        tail = packets[-1] if cut else packets[d]
         low = packets[d][0:2 * BLOCKS, B_DEV:WIDTH].astype(F32).astype(I32)
-        top = packets[d + split][2 * BLOCKS - 128 * split:3 * BLOCKS - 128 * split, B_DEV:WIDTH]
-        all_ref[d, 0:BLOCKS] = (low[0:BLOCKS] + (low[BLOCKS:2 * BLOCKS] << 8)
-                                + (top.astype(F32).astype(I32) << 16)) - 1
+        top = tail[2 * BLOCKS - cut:3 * BLOCKS - cut, B_DEV:WIDTH].astype(F32).astype(I32)
+        all_ref[d, 0:BLOCKS] = (low[0:BLOCKS] + (low[BLOCKS:2 * BLOCKS] << 8) + (top << 16)) - 1
         all_ref[d, BLOCKS:BLOCKS + 16] = jnp.zeros((16, LANES), I32)
     for copy in copies:
         copy.wait()
     for d in range(count):
+        parts = packets[d:] if split and d == count - 1 else packets[d:d + 1]
         first = scalar_ref[d, 0, NX * z_ref[0]]
         last = scalar_ref[d, 0, NX * z_ref[0] + NX - 1] + scalar_ref[d, 1, NX * z_ref[0] + NX - 1]
         k_ref[d] = all_ref[d, pl.ds(first, 16), :] >> 9
 
-        def pair(j, _, d=d, first=first):
+        def pair(j, _, d=d, first=first, parts=parts):
             lines = [all_ref[d, pl.ds(first + 2 * j + i, 1), :] & (B_DEV - 1) for i in range(2)]
             picks = jnp.concatenate([one_hot(line == iota((B_DEV, LANES), 0)) for line in lines], axis=1)
-            for part in range(1 + split):
-                rows = E >> split
-                got = jnp.dot(packets[d + part][:, 0:B_DEV], picks,
-                              preferred_element_type=F32).astype(BF16)
+            rows = E // len(parts)
+            for n, part in enumerate(parts):
+                got = jnp.dot(part[:, 0:B_DEV], picks, preferred_element_type=F32).astype(BF16)
                 for i in range(2):
-                    x_ref[d, 2 * j + i, part * rows:(part + 1) * rows] = got[:, i * LANES:(i + 1) * LANES]
+                    x_ref[d, 2 * j + i, n * rows:(n + 1) * rows] = got[:, i * LANES:(i + 1) * LANES]
             return 0
 
         lax.fori_loop(0, (last - first + 1) >> 1, pair, 0)
@@ -166,7 +167,7 @@
 def sums_kernel(at_ref, *refs, counts, base, many):
     groups = len(counts)
     metas, xs, keys = refs[0:groups], refs[groups:2 * groups], refs[2 * groups:3 * groups]
-    rows_ref, send_ref, keep_ref, all_ref, k_ref = refs[3 * groups:]
+    rows_ref, out_ref, all_ref, k_ref = refs[3 * groups:]
     for m in range(many):
         column = at_ref[base + m]
         filled = jnp.int32(0)
@@ -190,16 +191,14 @@
             return 0
 
         lax.fori_loop(filled, rounds * 8, blank, 0)
-        send_ref[m] = jnp.zeros((HALF, E), F32)
-        keep_ref[m] = jnp.zeros((HALF, E), F32)
+        out_ref[m] = jnp.zeros((HALF, E), F32)
 
         def accumulate(r, _, m=m):
             wide = jnp.concatenate([all_ref[8 * r + j] for j in range(8)], axis=1)
             lines = [k_ref[pl.ds(8 * r + j, 1), :] for j in range(8)]
-            for h, out_ref in enumerate((send_ref, keep_ref)):
-                mine = rows_ref[base + m, h * HALF:(h + 1) * HALF, :]
-                hits = jnp.concatenate([one_hot(mine == line) for line in lines], axis=1)
-                out_ref[m] += lax.dot_general(hits, wide, NT, preferred_element_type=F32)
+            mine = rows_ref[base + m]
+            hits = jnp.concatenate([one_hot(mine == line) for line in lines], axis=1)
+            out_ref[m] += lax.dot_general(hits, wide, NT, preferred_element_type=F32)
             return 0
 
         lax.fori_loop(0, rounds, accumulate, 0)
@@ -216,14 +215,14 @@
         lambda *refs: sums_kernel(*refs, counts=counts, base=base, many=many),
         in_specs=[SMEM] * (1 + len(counts)) + [VMEM] * (2 * len(counts) + 1),
         scratch_shapes=[pltpu.VMEM((4 * total, E, LANES), BF16), pltpu.VMEM((4 * total, LANES), I32)],
-        out_shape=[jax.ShapeDtypeStruct((many, HALF, E), F32)] * 2,
+        out_shape=jax.ShapeDtypeStruct((many, HALF, E), F32),
         cost_estimate=cost(2 * many),
         compiler_params=PARAMS,
     )(at, *[g[2] for g in gathered], *[g[0] for g in gathered], *[g[1] for g in gathered], rows)
 
 
 def listed_kernel(list_ref, rows_ref, accum_ref, table_ref, out_ref):
-    rows = rows_ref[NX - 1]
+    rows = rows_ref[...]
     hi = jnp.where((rows >> 7) == iota((TOUCH, LANES), 1), 1.0, 0.0)
     padded = jnp.concatenate([accum_ref[...], jnp.zeros((LANES - 32, LANES), F32)], axis=0)
     line = jnp.dot(hi, padded, precision=lax.Precision.HIGHEST, preferred_element_type=F32)
@@ -266,26 +265,21 @@
 
     for b in range(tiles):
         load(b).start()
-    lane = iota((PIECE, LANES), 1)
-    pieces = []
+    lane = iota((QUART, LANES), 1)
+    means = []
     for n in range(8):
-        for half in range(2):
-            start = (n >> 2) * HALF + half * (HALF // 2) + (n & 3) * PIECE
-            at = slice(start, start + PIECE)
-            g = chunks[n][half * PIECE:(half + 1) * PIECE, :]
-            mean = jnp.sum(g * g, axis=1, keepdims=True) * (1.0 / E)
-            rows = rows_ref[NX - 1, at, :]
-            lhs_ref[at, :] = jnp.where((rows >> 7) == lane, mean, 0.0)
-            rhs_ref[at, :] = jnp.where((rows & (LANES - 1)) == lane, 1.0, 0.0)
-            pieces.append((n, half, at, mean))
+        at = slice(n * QUART, (n + 1) * QUART)
+        g = chunks[n][...]
+        means.append(jnp.sum(g * g, axis=1, keepdims=True) * (1.0 / E))
+        rows = rows_ref[at, :]
+        lhs_ref[at, :] = jnp.where((rows >> 7) == lane, means[n], 0.0)
+        rhs_ref[at, :] = jnp.where((rows & (LANES - 1)) == lane, 1.0, 0.0)
     listed_load.wait()
-    for n, half, at, mean in pieces:
-        now = listed_ref[at, E:E + 1] + mean
-        place = plan_ref[16 + n]
-        place = (place >> 2) * HALF + half * (HALF // 2) + (place & 3) * PIECE
-        u_ref[pl.ds(pl.multiple_of(place, PIECE), PIECE), :] = (
-            listed_ref[at, 0:E]
-            - 0.5 * chunks[n][half * PIECE:(half + 1) * PIECE, :] / (jnp.sqrt(now) + 1e-08))
+    for n in range(8):
+        at = slice(n * QUART, (n + 1) * QUART)
+        now = listed_ref[at, E:E + 1] + means[n]
+        u_ref[pl.ds(pl.multiple_of(plan_ref[16 + n] * QUART, QUART), QUART), :] = (
+            listed_ref[at, 0:E] - 0.5 * chunks[n][...] / (jnp.sqrt(now) + 1e-08))
 
     def put(n):
         new_ref[pl.ds(list_ref[n], 1), :] = u_ref[pl.ds(n, 1), :]
@@ -355,17 +349,18 @@
     z, x = me // NX, me % NX
 
     def ordered(listed):
-        halves = listed.reshape(NC, 2, NY, PIECE)
+        halves = listed.reshape(NC, NY, QUART)
         halves = jnp.where(c == 0, halves[::-1], halves)
-        doubled = jnp.concatenate([halves, halves], axis=2)
-        return lax.dynamic_slice(doubled, (0, 0, y, 0), (NC, 2, NY, PIECE)).reshape(TOUCH)
+        doubled = jnp.concatenate([halves, halves], axis=1)
+        return lax.dynamic_slice(doubled, (0, y, 0), (NC, NY, QUART)).reshape(TOUCH)
 
     own_list = touched.reshape(TOUCH)
     lists = {0: ordered(own_list)}
     for k in range(1, NX):
         lists[k] = ordered(lax.ppermute(own_list, "shard", x_pairs(-k)))
-    stacked = jnp.stack([lists[k] for k in ORDER])[:, :, None]
-    rows = jnp.broadcast_to(stacked, (NX, TOUCH, LANES))
+    stacked = jnp.stack([lists[k][HALF:] for k in ORDER])[:, :, None]
+    rows = jnp.broadcast_to(stacked, (NX, HALF, LANES))
+    all_rows = jnp.broadcast_to(lists[0][:, None], (TOUCH, LANES))
     order = lists[0].reshape(8, LANES)
     bounds = jnp.sum((own_list[None, :] < TILE * jnp.arange(16, dtype=I32)[:, None]).astype(I32), axis=1)
     turn = (y + jnp.arange(NY, dtype=I32)) % NY
@@ -373,43 +368,42 @@
 
     packet = pack(row_ids.reshape(32, LANES), bag_ids.reshape(32, LANES),
                   pooled_grad.reshape(B_DEV, E))
-    got = {0: packet}
-    for k in range(1, 4):
-        got[-k] = lax.ppermute(got[1 - k], "shard", z_pairs(1))
-        got[k] = lax.ppermute(got[k - 1], "shard", z_pairs(-1))
-    last = [lax.ppermute(got[-3][:E // 2], "shard", z_pairs(1))]
-    last.append(lax.ppermute(got[3][E // 2:], "shard", z_pairs(-1)))
-    gathered = []
-    for sources in ((0,), (-1, 1), (-2, 2), (-3, 3), None):
-        packets = [got[k] for k in sources] if sources else last
-        gathered.append(gather(z.reshape(1), packets, int(sources is None)))
-
-    listed = listed_values(order, rows, accum.reshape(32, LANES), table)
+
+    def swap(packets):
+        return [lax.ppermute(p, "grp", C_PAIRS) for p in packets]
+
+    def gather_of(packets, split):
+        return gather(z.reshape(1), packets, split)
+
+    up = down = packet
+    other = swap([packet])
+    gathered = [gather_of([packet], 0)]
+    for _ in range(1, 4):
+        up = lax.ppermute(up, "shard", z_pairs(1))
+        down = lax.ppermute(down, "shard", z_pairs(-1))
+        gathered.append(gather_of([up, down] + other, 0))
+        other = swap([up, down])
+    up = lax.ppermute(up[:E // 2], "shard", z_pairs(1))
+    down = lax.ppermute(down[E // 2:], "shard", z_pairs(-1))
+    gathered.append(gather_of(other + [up, down], 1))
+    gathered.append(gather_of(swap([up, down]), 1))
+
+    listed = listed_values(order, all_rows, accum.reshape(32, LANES), table)
     at = jnp.concatenate([(x + jnp.array(ORDER, I32)) % NX, (NX * z).reshape(1)])
-    first, second = {}, {}
+    both = {}
     for base, ks in ((0, (2,)), (1, (1, 3)), (3, (0,))):
-        send, keep = sums(at, base, len(ks), gathered, rows)
-        swapped = lax.ppermute(send, "grp", C_PAIRS)
+        found = sums(at, base, len(ks), gathered, rows)
         for n, k in enumerate(ks):
-            first[k] = keep[n, :HALF // 2] + swapped[n, :HALF // 2]
+            both[k] = found[n]
             if k:
-                first[k] = lax.ppermute(first[k], "shard", x_pairs(k))
-            second[k] = (keep[n, HALF // 2:] + swapped[n, HALF // 2:]).reshape(NY, PIECE, E)
-    side = [jnp.stack([second[k][j] for k in range(NX)]) for j in range(NY)]
+                both[k] = lax.ppermute(both[k], "shard", x_pairs(k))
+    total = both[0] + both[2] + both[1] + both[3]
+    part = total[0:QUART]
     for j in (2, 1, 3):
-        side[j] = lax.ppermute(side[j], "grp", y_pairs(j))
-    low = (first[0] + first[2] + first[1] + first[3]).reshape(NY, PIECE, E)
-    part_low = low[0]
-    for j in (2, 1, 3):
-        part_low = part_low + lax.ppermute(low[j], "grp", y_pairs(j))
-    high = side[0] + side[2] + side[1] + side[3]
-    part_high = high[0]
-    for k in (2, 1, 3):
-        part_high = part_high + lax.ppermute(high[k], "shard", x_pairs(k))
-    part = jnp.concatenate([part_low, part_high], axis=0)
+        part = part + lax.ppermute(total[j * QUART:(j + 1) * QUART], "grp", y_pairs(j))
     mine = [part] + [lax.ppermute(part, "grp", y_pairs(-j)) for j in range(1, NY)]
     other = [lax.ppermute(m, "grp", C_PAIRS) for m in mine]
-    new_table, new_accum = update(plan, own_list, table, listed, rows, other + mine)
+    new_table, new_accum = update(plan, own_list, table, listed, all_rows, other + mine)
     return (new_table, new_accum.reshape(ROWS_DEV))
 
 

time: 124 us -> 129 us (1.040)
  waiting for transfers between devices: 22.5 us -> 35.6 us
  Pallas kernels: 31.1 us -> 39 us
  other arithmetic: 6.31 us -> 0.64 us
  starting transfers between devices: 55.2 us -> 49.7 us
  local copies, waits for them, and re-layouts: 7.23 us -> 1.86 us
    ppermute x23, waiting for transfers between devices: 22.5 us -> 34.6 us  [the longest x3 19.4 us: body(): both[k] = lax.ppermute(both[k], 'shard', x_pairs(k))]
    ppermute x23, starting transfers between devices: 39.3 us -> 33 us  [the longest x3 10.4 us: body(): down = lax.ppermute(down, 'shard', z_pairs(-1))]
    pallas_call x5 -> x6, Pallas kernels: 7.15 us -> 12.3 us  [gather(): pl.pallas_call(lambda *refs: gather_kernel(*refs, count=count, split=spli...]
    add x7 -> x2, other arithmetic: 3 us -> 0.17 us  [the longest x1 0.13 us: body(): total = both[0] + both[2] + both[1] + both[3]]
    pallas_call x3, Pallas kernels: 7.29 us -> 10 us  [sums(): pl.pallas_call(lambda *refs: sums_kernel(*refs, counts=counts, base=base,...]
    unnamed x15 -> x10, local copies, waits for them, and re-layouts: 3.9 us -> 1.22 us
    another operation x4 -> x1, other arithmetic: 2.18 us -> 0.01 us  [body(): stacked = jnp.stack([lists[k][HALF:] for k in ORDER])[:, :, None]]
    slice x7 -> x4, local copies, waits for them, and re-layouts: 2 us -> 0.06 us  [the longest x1 0.03 us: body(): total[j * QUART:(j + 1) * QUART]]
  transfers between devices with their start and end apart: 33 -> 33, of which waited for: 13 -> 6; matrix products, arithmetic and copies ran while one was open for 5% -> 1% of each run, Pallas kernels for 16% -> 18%
where the time goes in v7:
time: 129 us; the launch traced here: 128 us
  starting transfers between devices  49.7 us (39%)
  Pallas kernels  39 us (30%)
  waiting for transfers between devices  35.6 us (28%)
  local copies, waits for them, and re-layouts  1.86 us (1%)
    ppermute x3, waiting for transfers between devices, body(): both[k] = lax.ppermute(both[k], 'shard', x_pairs(k))  19.4 us
    pallas_call x6, Pallas kernels, gather(): pl.pallas_call(lambda *refs: gather_kernel(*refs, count=count, split=spli...  12.3 us
    ppermute x3, waiting for transfers between devices, body(): up = lax.ppermute(up, 'shard', z_pairs(1))  10.7 us
    ppermute x3, starting transfers between devices, body(): down = lax.ppermute(down, 'shard', z_pairs(-1))  10.4 us
    pallas_call x3, Pallas kernels, sums(): pl.pallas_call(lambda *refs: sums_kernel(*refs, counts=counts, base=base,...  10 us
    ppermute x4, starting transfers between devices, body(): other = [lax.ppermute(m, 'grp', C_PAIRS) for m in mine]  8.27 us
    ppermute x9, starting transfers between devices, swap(): return [lax.ppermute(p, 'grp', C_PAIRS) for p in packets]  7.72 us
    pallas_call x1, Pallas kernels, update(): pl.pallas_call(update_kernel, out_shape=(jax.ShapeDtypeStruct((ROWS_DEV,...  7.67 us
  transfers between devices with their start and end apart: 33, of which 6 were waited for; matrix products, arithmetic and copies ran while one was open for 1% of the time, Pallas kernels for 18%

profile of v7, /device:TPU:1, one launch (start us, length us, event | category | flops | bytes accessed | tf_op | source)
XLA Modules:
  0.0 127.9 jit_solution(8225595157869476974)
XLA Ops:
  5.7 2.6 %pack.1.refs_1_ = bf16[256,640]{1,0:T(8,128)(2,1)S(1)} custom-call(s32[32,128]{1,0:T(8,128)} %bitcast.47, s32[32,128]{1,0:T(8,128)} %bitcast.48, bf16[512,256]{1,0:T(8,128)(2,1)} %bitcast.46), custom_call_target="tpu_custom_call" | custom-call | flops 2400000000 | bytes 12000000 | tf_op jit(solution)/shard_map/pack/pallas_call | solution.py:98
  10.1 4.0 %collective-permute-start.1 = (bf16[256,640]{1,0:T(8,128)(2,1)S(1)}, bf16[256,640]{1,0:T(8,128)(2,1)S(1)}, u32[]{:S(2)}, u32[]{:S(2)}) collective-permute-start(bf16[256,640]{1,0:T(8,128)(2,1)S(1)} %pack.1.refs_1_), channel_id=1, source_target_pairs={{0,28},{1,29},{2,30},{3,31},{4,0},{5,1},{6,2},{7,3},{8,4},{9,5},{1... | collective-permute-start | bytes 983048 | tf_op jit(solution)/shard_map/ppermute | solution.py:383
  17.3 3.3 %collective-permute-done.refs_1_ = bf16[256,640]{1,0:T(8,128)(2,1)S(1)} collective-permute-done((bf16[256,640]{1,0:T(8,128)(2,1)S(1)}, bf16[256,640]{1,0:T(8,128)(2,1)S(1)}, u32[]{:S(2)}, u32[]{:S(2)}) %collective-permute-start) | collective-permute-done | bytes 327712 | tf_op jit(solution)/shard_map/ppermute | solution.py:382
  22.7 3.0 %collective-permute-start.4 = (bf16[256,640]{1,0:T(8,128)(2,1)S(1)}, bf16[256,640]{1,0:T(8,128)(2,1)S(1)}, u32[]{:S(2)}, u32[]{:S(2)}) collective-permute-start(bf16[256,640]{1,0:T(8,128)(2,1)S(1)} %collective-permute-done.1.refs_2_), channel_id=1, source_target_pairs={{0,28},{1,29},{2,30},{3,31},{4,0},{5,1},{6,2},{7,3},{8,4},{9,5},{1... | collective-permute-start | bytes 983048 | tf_op jit(solution)/shard_map/ppermute | solution.py:383
  26.0 2.2 %shard_map.87 = (bf16[3,16,256,128]{3,2,1,0:T(8,128)(2,1)S(1)}, s32[3,16,128]{2,1,0:T(8,128)S(1)}, s32[3,8,128]{2,1,0:T(8,128)S(1)}) custom-call(s32[1]{0:T(128)} %bitcast.6.refs_0_, bf16[256,640]{1,0:T(8,128)(2,1)S(1)} %collective-permute-done.refs_1_, bf16[256,640]{1,0:T(8,128)(2,1)S(1)} %collective-permute-done.1.refs_2_, ...), custom_call_target="tpu_custom_call" | custom-call | flops 3000000000 | bytes 15000000 | tf_op jit(solution)/shard_map/pallas_call | solution.py:154
  28.2 4.5 %collective-permute-done.4.refs_2_ = bf16[256,640]{1,0:T(8,128)(2,1)S(1)} collective-permute-done((bf16[256,640]{1,0:T(8,128)(2,1)S(1)}, bf16[256,640]{1,0:T(8,128)(2,1)S(1)}, u32[]{:S(2)}, u32[]{:S(2)}) %collective-permute-start.4) | collective-permute-done | bytes 327712 | tf_op jit(solution)/shard_map/ppermute | solution.py:383
  32.7 3.4 %collective-permute-start.8 = (bf16[256,640]{1,0:T(8,128)(2,1)S(1)}, bf16[256,640]{1,0:T(8,128)(2,1)S(1)}, u32[]{:S(2)}, u32[]{:S(2)}) collective-permute-start(bf16[256,640]{1,0:T(8,128)(2,1)S(1)} %collective-permute-done.4.refs_2_), channel_id=1, source_target_pairs={{0,28},{1,29},{2,30},{3,31},{4,0},{5,1},{6,2},{7,3},{8,4},{9,5},{1... | collective-permute-start | bytes 983048 | tf_op jit(solution)/shard_map/ppermute | solution.py:383
  37.4 3.0 %shard_map.88 = (bf16[4,16,256,128]{3,2,1,0:T(8,128)(2,1)S(1)}, s32[4,16,128]{2,1,0:T(8,128)S(1)}, s32[4,8,128]{2,1,0:T(8,128)S(1)}) custom-call(s32[1]{0:T(128)} %bitcast.6.refs_0_, bf16[256,640]{1,0:T(8,128)(2,1)S(1)} %collective-permute-done.3.refs_1_, bf16[256,640]{1,0:T(8,128)(2,1)S(1)} %collective-permute-done.4.refs_2_, ...), custom_call_target="tpu_custom_call" | custom-call | flops 3600000000 | bytes 18000000 | tf_op jit(solution)/shard_map/pallas_call | solution.py:154
  40.4 7.4 %collective-permute-done.7.refs_1_ = bf16[256,640]{1,0:T(8,128)(2,1)S(1)} collective-permute-done((bf16[256,640]{1,0:T(8,128)(2,1)S(1)}, bf16[256,640]{1,0:T(8,128)(2,1)S(1)}, u32[]{:S(2)}, u32[]{:S(2)}) %collective-permute-start.7) | collective-permute-done | bytes 327712 | tf_op jit(solution)/shard_map/ppermute | solution.py:382
  47.9 2.7 %collective-permute-start.14 = (bf16[128,640]{1,0:T(8,128)(2,1)S(1)}, bf16[128,640]{1,0:T(8,128)(2,1)S(1)}, u32[]{:S(2)}, u32[]{:S(2)}) collective-permute-start(bf16[128,640]{1,0:T(8,128)(2,1)S(1)} %slice.53), channel_id=1, source_target_pairs={{0,28},{1,29},{2,30},{3,31},{4,0},{5,1},{6,2},{7,3},{8,4},{9,5},{1... | collective-permute-start | bytes 491528 | tf_op jit(solution)/shard_map/ppermute | solution.py:387
  52.1 2.8 %shard_map.89 = (bf16[4,16,256,128]{3,2,1,0:T(8,128)(2,1)S(1)}, s32[4,16,128]{2,1,0:T(8,128)S(1)}, s32[4,8,128]{2,1,0:T(8,128)S(1)}) custom-call(s32[1]{0:T(128)} %bitcast.6.refs_0_, bf16[256,640]{1,0:T(8,128)(2,1)S(1)} %collective-permute-done.7.refs_1_, bf16[256,640]{1,0:T(8,128)(2,1)S(1)} %collective-permute-done.8.refs_2_, ...), custom_call_target="tpu_custom_call" | custom-call | flops 3600000000 | bytes 18000000 | tf_op jit(solution)/shard_map/pallas_call | solution.py:154
  55.7 2.2 %shard_map.90 = (bf16[3,16,256,128]{3,2,1,0:T(8,128)(2,1)S(1)}, s32[3,16,128]{2,1,0:T(8,128)S(1)}, s32[3,8,128]{2,1,0:T(8,128)S(1)}) custom-call(s32[1]{0:T(128)} %bitcast.6.refs_0_, bf16[256,640]{1,0:T(8,128)(2,1)S(1)} %collective-permute-done.11.refs_1_, bf16[256,640]{1,0:T(8,128)(2,1)S(1)} %collective-permute-done.12.refs_2_, ...), custom_call_target="tpu_custom_call" | custom-call | flops 3000000000 | bytes 15000000 | tf_op jit(solution)/shard_map/pallas_call | solution.py:154
  59.4 2.9 %shard_map.93 = f32[1,512,256]{2,1,0:T(8,128)S(1)} custom-call(s32[5]{0:T(128)S(1)} %pad_add_fusion.2.refs_0_, s32[1,8,128]{2,1,0:T(8,128)S(1)} %get-tuple-element.22.refs_1_, s32[3,8,128]{2,1,0:T(8,128)S(1)} %get-tuple-element.23.refs_2_, s32[4,8,128]{2,1,0:T(8,128)S(1)} %get-tuple-element.24.refs_3_, s32[4,8,128]{2,1,0:T(8,128)S(1)} %get-tuple-element.25.refs_4_, ...), custom_call_target="tpu_custom_call" | custom-call | flops 1200000000 | bytes 6000000 | tf_op jit(solution)/shard_map/pallas_call | solution.py:214
  62.3 4.2 %shard_map.94 = f32[2,512,256]{2,1,0:T(8,128)S(1)} custom-call(s32[5]{0:T(128)S(1)} %pad_add_fusion.2.refs_0_, s32[1,8,128]{2,1,0:T(8,128)S(1)} %get-tuple-element.22.refs_1_, s32[3,8,128]{2,1,0:T(8,128)S(1)} %get-tuple-element.23.refs_2_, s32[4,8,128]{2,1,0:T(8,128)S(1)} %get-tuple-element.24.refs_3_, s32[4,8,128]{2,1,0:T(8,128)S(1)} %get-tuple-element.25.refs_4_, ...), custom_call_target="tpu_custom_call" | custom-call | flops 2400000000 | bytes 12000000 | tf_op jit(solution)/shard_map/pallas_call | solution.py:214
  68.2 2.6 %collective-permute-start.22 = (f32[512,256]{1,0:T(8,128)S(1)}, f32[512,256]{1,0:T(8,128)S(1)}, u32[]{:S(2)}, u32[]{:S(2)}) collective-permute-start(f32[512,256]{1,0:T(8,128)S(1)} %get-tuple-element.43), channel_id=1, source_target_pairs={{0,3},{1,0},{2,1},{3,2},{4,7},{5,4},{6,5},{7,6},{8,11},{9,8},{10,9... | collective-permute-start | bytes 1572872 | tf_op jit(solution)/shard_map/ppermute | solution.py:399
  70.9 2.9 %shard_map.92 = f32[1,512,256]{2,1,0:T(8,128)S(1)} custom-call(s32[5]{0:T(128)S(1)} %pad_add_fusion.2.refs_0_, s32[1,8,128]{2,1,0:T(8,128)S(1)} %get-tuple-element.22.refs_1_, s32[3,8,128]{2,1,0:T(8,128)S(1)} %get-tuple-element.23.refs_2_, s32[4,8,128]{2,1,0:T(8,128)S(1)} %get-tuple-element.24.refs_3_, s32[4,8,128]{2,1,0:T(8,128)S(1)} %get-tuple-element.25.refs_4_, ...), custom_call_target="tpu_custom_call" | custom-call | flops 1200000000 | bytes 6000000 | tf_op jit(solution)/shard_map/pallas_call | solution.py:214
  73.8 7.3 %collective-permute-done.20 = f32[512,256]{1,0:T(8,128)S(1)} collective-permute-done((f32[512,256]{1,0:T(8,128)S(1)}, f32[512,256]{1,0:T(8,128)S(1)}, u32[]{:S(2)}, u32[]{:S(2)}) %collective-permute-start.20) | collective-permute-done | bytes 524320 | tf_op jit(solution)/shard_map/ppermute | solution.py:399
  81.2 12.1 %collective-permute-done.21 = f32[512,256]{1,0:T(8,128)S(1)} collective-permute-done((f32[512,256]{1,0:T(8,128)S(1)}, f32[512,256]{1,0:T(8,128)S(1)}, u32[]{:S(2)}, u32[]{:S(2)}) %collective-permute-start.21) | collective-permute-done | bytes 524320 | tf_op jit(solution)/shard_map/ppermute | solution.py:399
  93.4 3.0 %collective-permute-start.23 = (f32[128,256]{1,0:T(8,128)S(1)}, f32[128,256]{1,0:T(8,128)S(1)}, u32[]{:S(2)}, u32[]{:S(2)}) collective-permute-start(f32[128,256]{1,0:T(8,128)S(1)} %get-tuple-element.44), channel_id=1, source_target_pairs={{0,128},{32,160},{64,192},{96,224},{128,0},{160,32},{192,64},{224,... | collective-permute-start | bytes 393224 | tf_op jit(solution)/shard_map/ppermute | solution.py:403
  96.4 3.1 %collective-permute-start.24 = (f32[128,256]{1,0:T(8,128)S(1)}, f32[128,256]{1,0:T(8,128)S(1)}, u32[]{:S(2)}, u32[]{:S(2)}) collective-permute-start(f32[128,256]{1,0:T(8,128)S(1)} %get-tuple-element.46), channel_id=1, source_target_pairs={{0,64},{32,96},{64,128},{96,160},{128,192},{160,224},{192,0},{224,... | collective-permute-start | bytes 393224 | tf_op jit(solution)/shard_map/ppermute | solution.py:403
  99.7 6.3 %listed_values.1.refs_3_ = f32[1056,384]{1,0:T(8,128)S(1)} custom-call(s32[8,128]{1,0:T(8,128)S(1)} %bitcast.37, s32[1024,128]{1,0:T(8,128)S(1)} %broadcast_in_dim.7.rows_ref.refs_4_, f32[32,128]{1,0:T(8,128)S(1)} %bitcast.38, f32[4096,256]{1,0:T(8,128)S(1)} %copy-done), custom_call_target="tpu_custom_call" | custom-call | flops 3600000000 | bytes 18000000 | tf_op jit(solution)/shard_map/listed_values/pallas_call | solution.py:244
  112.9 2.4 %collective-permute-start.28 = (f32[128,256]{1,0:T(8,128)S(1)}, f32[128,256]{1,0:T(8,128)S(1)}, u32[]{:S(2)}, u32[]{:S(2)}) collective-permute-start(f32[128,256]{1,0:T(8,128)S(1)} %collective-permute-done.27.refs_10_), channel_id=1, source_target_pairs={{0,32},{32,0},{64,96},{96,64},{128,160},{160,128},{192,224},{224,1... | collective-permute-start | bytes 393224 | tf_op jit(solution)/shard_map/ppermute | solution.py:405
  115.3 2.4 %collective-permute-start.30 = (f32[128,256]{1,0:T(8,128)S(1)}, f32[128,256]{1,0:T(8,128)S(1)}, u32[]{:S(2)}, u32[]{:S(2)}) collective-permute-start(f32[128,256]{1,0:T(8,128)S(1)} %collective-permute-done.29.refs_11_), channel_id=1, source_target_pairs={{0,32},{32,0},{64,96},{96,64},{128,160},{160,128},{192,224},{224,1... | collective-permute-start | bytes 393224 | tf_op jit(solution)/shard_map/ppermute | solution.py:405
  120.1 7.7 %update.1 = (f32[4096,256]{1,0:T(8,128)}, f32[32,128]{1,0:T(8,128)}) custom-call(s32[24]{0:T(128)S(1)} %pad_add_fusion.1.refs_0_, s32[1024]{0:T(1024)S(1)} %bitcast.35, f32[4096,256]{1,0:T(8,128)} %refs_2_.1, f32[1056,384]{1,0:T(8,128)} %copy-done.1, s32[1024,128]{1,0:T(8,128)S(1)} %broadcast_in_dim.7.rows_ref.refs_4_, ...), custom_call_target="tpu_custom_call" | custom-call | tf_op jit(solution)/shard_map/update/pallas_call | solution.py:315
  (87 shorter events, 28.7 us)
Async XLA Ops:
  0.6 14.8 %collective-permute-start.19 = (s32[1024]{0:T(1024)}, s32[1024]{0:T(1024)S(1)}, u32[]{:S(2)}, u32[]{:S(2)}) collective-permute-start(s32[1024]{0:T(1024)} %bitcast.30), channel_id=1, source_target_pairs={{0,1},{1,2},{2,3},{3,0},{4,5},{5,6},{6,7},{7,4},{8,9},{9,10},{10,1... | collective-permute-start | bytes 12296 | tf_op jit(solution)/shard_map/ppermute | solution.py:360
  2.7 14.5 %collective-permute-start.18 = (s32[1024]{0:T(1024)}, s32[1024]{0:T(1024)S(1)}, u32[]{:S(2)}, u32[]{:S(2)}) collective-permute-start(s32[1024]{0:T(1024)} %bitcast.31), channel_id=1, source_target_pairs={{0,3},{1,0},{2,1},{3,2},{4,7},{5,4},{6,5},{7,6},{8,11},{9,8},{10,9... | collective-permute-start | bytes 12296 | tf_op jit(solution)/shard_map/ppermute | solution.py:360
  4.1 13.2 %collective-permute-start.17 = (s32[1024]{0:T(1024)}, s32[1024]{0:T(1024)S(1)}, u32[]{:S(2)}, u32[]{:S(2)}) collective-permute-start(s32[1024]{0:T(1024)} %bitcast.32), channel_id=1, source_target_pairs={{0,2},{1,3},{2,0},{3,1},{4,6},{5,7},{6,4},{7,5},{8,10},{9,11},{10,... | collective-permute-start | bytes 12296 | tf_op jit(solution)/shard_map/ppermute | solution.py:360
  8.4 12.2 %collective-permute-start = (bf16[256,640]{1,0:T(8,128)(2,1)S(1)}, bf16[256,640]{1,0:T(8,128)(2,1)S(1)}, u32[]{:S(2)}, u32[]{:S(2)}) collective-permute-start(bf16[256,640]{1,0:T(8,128)(2,1)S(1)} %pack.1.refs_1_), channel_id=1, source_target_pairs={{0,4},{1,5},{2,6},{3,7},{4,8},{5,9},{6,10},{7,11},{8,12},{9,13},{1... | collective-permute-start | bytes 983048 | tf_op jit(solution)/shard_map/ppermute | solution.py:382
  10.1 12.6 %collective-permute-start.1 = (bf16[256,640]{1,0:T(8,128)(2,1)S(1)}, bf16[256,640]{1,0:T(8,128)(2,1)S(1)}, u32[]{:S(2)}, u32[]{:S(2)}) collective-permute-start(bf16[256,640]{1,0:T(8,128)(2,1)S(1)} %pack.1.refs_1_), channel_id=1, source_target_pairs={{0,28},{1,29},{2,30},{3,31},{4,0},{5,1},{6,2},{7,3},{8,4},{9,5},{1... | collective-permute-start | bytes 983048 | tf_op jit(solution)/shard_map/ppermute | solution.py:383
  15.4 10.6 %collective-permute-start.2 = (bf16[256,640]{1,0:T(8,128)(2,1)S(1)}, bf16[256,640]{1,0:T(8,128)(2,1)S(1)}, u32[]{:S(2)}, u32[]{:S(2)}) collective-permute-start(bf16[256,640]{1,0:T(8,128)(2,1)S(1)} %pack.1.refs_1_), channel_id=1, source_target_pairs={{0,32},{32,0},{64,96},{96,64},{128,160},{160,128},{192,224},{224,1... | collective-permute-start | bytes 983048 | tf_op jit(solution)/shard_map/ppermute | solution.py:373
  20.6 16.7 %collective-permute-start.3 = (bf16[256,640]{1,0:T(8,128)(2,1)S(1)}, bf16[256,640]{1,0:T(8,128)(2,1)S(1)}, u32[]{:S(2)}, u32[]{:S(2)}) collective-permute-start(bf16[256,640]{1,0:T(8,128)(2,1)S(1)} %collective-permute-done.refs_1_), channel_id=1, source_target_pairs={{0,4},{1,5},{2,6},{3,7},{4,8},{5,9},{6,10},{7,11},{8,12},{9,13},{1... | collective-permute-start | bytes 983048 | tf_op jit(solution)/shard_map/ppermute | solution.py:382
  20.6 16.7 %collective-permute-start.5 = (bf16[256,640]{1,0:T(8,128)(2,1)S(1)}, bf16[256,640]{1,0:T(8,128)(2,1)S(1)}, u32[]{:S(2)}, u32[]{:S(2)}) collective-permute-start(bf16[256,640]{1,0:T(8,128)(2,1)S(1)} %collective-permute-done.refs_1_), channel_id=1, source_target_pairs={{0,32},{32,0},{64,96},{96,64},{128,160},{160,128},{192,224},{224,1... | collective-permute-start | bytes 983048 | tf_op jit(solution)/shard_map/ppermute | solution.py:373
  22.7 10.0 %collective-permute-start.4 = (bf16[256,640]{1,0:T(8,128)(2,1)S(1)}, bf16[256,640]{1,0:T(8,128)(2,1)S(1)}, u32[]{:S(2)}, u32[]{:S(2)}) collective-permute-start(bf16[256,640]{1,0:T(8,128)(2,1)S(1)} %collective-permute-done.1.refs_2_), channel_id=1, source_target_pairs={{0,28},{1,29},{2,30},{3,31},{4,0},{5,1},{6,2},{7,3},{8,4},{9,5},{1... | collective-permute-start | bytes 983048 | tf_op jit(solution)/shard_map/ppermute | solution.py:383
  25.7 11.7 %collective-permute-start.6 = (bf16[256,640]{1,0:T(8,128)(2,1)S(1)}, bf16[256,640]{1,0:T(8,128)(2,1)S(1)}, u32[]{:S(2)}, u32[]{:S(2)}) collective-permute-start(bf16[256,640]{1,0:T(8,128)(2,1)S(1)} %collective-permute-done.1.refs_2_), channel_id=1, source_target_pairs={{0,32},{32,0},{64,96},{96,64},{128,160},{160,128},{192,224},{224,1... | collective-permute-start | bytes 983048 | tf_op jit(solution)/shard_map/ppermute | solution.py:373
  32.7 15.1 %collective-permute-start.8 = (bf16[256,640]{1,0:T(8,128)(2,1)S(1)}, bf16[256,640]{1,0:T(8,128)(2,1)S(1)}, u32[]{:S(2)}, u32[]{:S(2)}) collective-permute-start(bf16[256,640]{1,0:T(8,128)(2,1)S(1)} %collective-permute-done.4.refs_2_), channel_id=1, source_target_pairs={{0,28},{1,29},{2,30},{3,31},{4,0},{5,1},{6,2},{7,3},{8,4},{9,5},{1... | collective-permute-start | bytes 983048 | tf_op jit(solution)/shard_map/ppermute | solution.py:383
  36.1 15.9 %collective-permute-start.10 = (bf16[256,640]{1,0:T(8,128)(2,1)S(1)}, bf16[256,640]{1,0:T(8,128)(2,1)S(1)}, u32[]{:S(2)}, u32[]{:S(2)}) collective-permute-start(bf16[256,640]{1,0:T(8,128)(2,1)S(1)} %collective-permute-done.4.refs_2_), channel_id=1, source_target_pairs={{0,32},{32,0},{64,96},{96,64},{128,160},{160,128},{192,224},{224,1... | collective-permute-start | bytes 983048 | tf_op jit(solution)/shard_map/ppermute | solution.py:373
  37.3 10.5 %collective-permute-start.7 = (bf16[256,640]{1,0:T(8,128)(2,1)S(1)}, bf16[256,640]{1,0:T(8,128)(2,1)S(1)}, u32[]{:S(2)}, u32[]{:S(2)}) collective-permute-start(bf16[256,640]{1,0:T(8,128)(2,1)S(1)} %collective-permute-done.3.refs_1_), channel_id=1, source_target_pairs={{0,4},{1,5},{2,6},{3,7},{4,8},{5,9},{6,10},{7,11},{8,12},{9,13},{1... | collective-permute-start | bytes 983048 | tf_op jit(solution)/shard_map/ppermute | solution.py:382
  37.3 14.8 %collective-permute-start.9 = (bf16[256,640]{1,0:T(8,128)(2,1)S(1)}, bf16[256,640]{1,0:T(8,128)(2,1)S(1)}, u32[]{:S(2)}, u32[]{:S(2)}) collective-permute-start(bf16[256,640]{1,0:T(8,128)(2,1)S(1)} %collective-permute-done.3.refs_1_), channel_id=1, source_target_pairs={{0,32},{32,0},{64,96},{96,64},{128,160},{160,128},{192,224},{224,1... | collective-permute-start | bytes 983048 | tf_op jit(solution)/shard_map/ppermute | solution.py:373
  47.8 7.1 %collective-permute-start.13 = (bf16[128,640]{1,0:T(8,128)(2,1)S(1)}, bf16[128,640]{1,0:T(8,128)(2,1)S(1)}, u32[]{:S(2)}, u32[]{:S(2)}) collective-permute-start(bf16[128,640]{1,0:T(8,128)(2,1)S(1)} %slice.52), channel_id=1, source_target_pairs={{0,4},{1,5},{2,6},{3,7},{4,8},{5,9},{6,10},{7,11},{8,12},{9,13},{1... | collective-permute-start | bytes 491528 | tf_op jit(solution)/shard_map/ppermute | solution.py:386
  47.9 7.8 %collective-permute-start.14 = (bf16[128,640]{1,0:T(8,128)(2,1)S(1)}, bf16[128,640]{1,0:T(8,128)(2,1)S(1)}, u32[]{:S(2)}, u32[]{:S(2)}) collective-permute-start(bf16[128,640]{1,0:T(8,128)(2,1)S(1)} %slice.53), channel_id=1, source_target_pairs={{0,28},{1,29},{2,30},{3,31},{4,0},{5,1},{6,2},{7,3},{8,4},{9,5},{1... | collective-permute-start | bytes 491528 | tf_op jit(solution)/shard_map/ppermute | solution.py:387
  66.5 14.6 %collective-permute-start.20 = (f32[512,256]{1,0:T(8,128)S(1)}, f32[512,256]{1,0:T(8,128)S(1)}, u32[]{:S(2)}, u32[]{:S(2)}) collective-permute-start(f32[512,256]{1,0:T(8,128)S(1)} %bitcast.29), channel_id=1, source_target_pairs={{0,2},{1,3},{2,0},{3,1},{4,6},{5,7},{6,4},{7,5},{8,10},{9,11},{10,... | collective-permute-start | bytes 1572872 | tf_op jit(solution)/shard_map/ppermute | solution.py:399
  68.1 25.1 %collective-permute-start.21 = (f32[512,256]{1,0:T(8,128)S(1)}, f32[512,256]{1,0:T(8,128)S(1)}, u32[]{:S(2)}, u32[]{:S(2)}) collective-permute-start(f32[512,256]{1,0:T(8,128)S(1)} %get-tuple-element.42), channel_id=1, source_target_pairs={{0,1},{1,2},{2,3},{3,0},{4,5},{5,6},{6,7},{7,4},{8,9},{9,10},{10,1... | collective-permute-start | bytes 1572872 | tf_op jit(solution)/shard_map/ppermute | solution.py:399
  68.2 25.0 %collective-permute-start.22 = (f32[512,256]{1,0:T(8,128)S(1)}, f32[512,256]{1,0:T(8,128)S(1)}, u32[]{:S(2)}, u32[]{:S(2)}) collective-permute-start(f32[512,256]{1,0:T(8,128)S(1)} %get-tuple-element.43), channel_id=1, source_target_pairs={{0,3},{1,0},{2,1},{3,2},{4,7},{5,4},{6,5},{7,6},{8,11},{9,8},{10,9... | collective-permute-start | bytes 1572872 | tf_op jit(solution)/shard_map/ppermute | solution.py:399
  93.4 13.8 %collective-permute-start.23 = (f32[128,256]{1,0:T(8,128)S(1)}, f32[128,256]{1,0:T(8,128)S(1)}, u32[]{:S(2)}, u32[]{:S(2)}) collective-permute-start(f32[128,256]{1,0:T(8,128)S(1)} %get-tuple-element.44), channel_id=1, source_target_pairs={{0,128},{32,160},{64,192},{96,224},{128,0},{160,32},{192,64},{224,... | collective-permute-start | bytes 393224 | tf_op jit(solution)/shard_map/ppermute | solution.py:403
  96.4 10.8 %collective-permute-start.24 = (f32[128,256]{1,0:T(8,128)S(1)}, f32[128,256]{1,0:T(8,128)S(1)}, u32[]{:S(2)}, u32[]{:S(2)}) collective-permute-start(f32[128,256]{1,0:T(8,128)S(1)} %get-tuple-element.46), channel_id=1, source_target_pairs={{0,64},{32,96},{64,128},{96,160},{128,192},{160,224},{192,0},{224,... | collective-permute-start | bytes 393224 | tf_op jit(solution)/shard_map/ppermute | solution.py:403
  99.4 7.8 %collective-permute-start.25 = (f32[128,256]{1,0:T(8,128)S(1)}, f32[128,256]{1,0:T(8,128)S(1)}, u32[]{:S(2)}, u32[]{:S(2)}) collective-permute-start(f32[128,256]{1,0:T(8,128)S(1)} %get-tuple-element.45), channel_id=1, source_target_pairs={{0,192},{32,224},{64,0},{96,32},{128,64},{160,96},{192,128},{224,1... | collective-permute-start | bytes 393224 | tf_op jit(solution)/shard_map/ppermute | solution.py:403
  110.6 7.1 %collective-permute-start.31 = (f32[128,256]{1,0:T(8,128)S(1)}, f32[128,256]{1,0:T(8,128)S(1)}, u32[]{:S(2)}, u32[]{:S(2)}) collective-permute-start(f32[128,256]{1,0:T(8,128)S(1)} %fusion.3.refs_9_), channel_id=1, source_target_pairs={{0,64},{32,96},{64,128},{96,160},{128,192},{160,224},{192,0},{224,... | collective-permute-start | bytes 393224 | tf_op jit(solution)/shard_map/ppermute | solution.py:404
  110.8 8.4 %collective-permute-start.26 = (f32[128,256]{1,0:T(8,128)S(1)}, f32[128,256]{1,0:T(8,128)S(1)}, u32[]{:S(2)}, u32[]{:S(2)}) collective-permute-start(f32[128,256]{1,0:T(8,128)S(1)} %fusion.3.refs_9_), channel_id=1, source_target_pairs={{0,32},{32,0},{64,96},{96,64},{128,160},{160,128},{192,224},{224,1... | collective-permute-start | bytes 393224 | tf_op jit(solution)/shard_map/ppermute | solution.py:405
  (14 other events, 116.6 us)

commit v8 on v7

--- a/solution.py
+++ b/solution.py
@@ -164,10 +164,11 @@
     )(z, *packets)
 
 
-def sums_kernel(at_ref, *refs, counts, base, many):
+def sums_kernel(at_ref, *refs, counts, base, many, fresh):
     groups = len(counts)
     metas, xs, keys = refs[0:groups], refs[groups:2 * groups], refs[2 * groups:3 * groups]
-    rows_ref, out_ref, all_ref, k_ref = refs[3 * groups:]
+    rows_ref = refs[3 * groups]
+    out_ref, all_ref, k_ref = refs[-3:]
     for m in range(many):
         column = at_ref[base + m]
         filled = jnp.int32(0)
@@ -191,7 +192,7 @@
             return 0
 
         lax.fori_loop(filled, rounds * 8, blank, 0)
-        out_ref[m] = jnp.zeros((HALF, E), F32)
+        out_ref[m] = jnp.zeros((HALF, E), F32) if fresh else refs[3 * groups + 1][m]
 
         def accumulate(r, _, m=m):
             wide = jnp.concatenate([all_ref[8 * r + j] for j in range(8)], axis=1)
@@ -208,17 +209,17 @@
     return pl.CostEstimate(flops=int(us * 6e8), bytes_accessed=int(us * 3e6), transcendentals=0)
 
 
-def sums(at, base, many, gathered, rows):
+def sums(at, base, many, gathered, rows, old):
     counts = tuple(g[0].shape[0] for g in gathered)
     total = sum(counts)
     return pl.pallas_call(
-        lambda *refs: sums_kernel(*refs, counts=counts, base=base, many=many),
-        in_specs=[SMEM] * (1 + len(counts)) + [VMEM] * (2 * len(counts) + 1),
+        lambda *refs: sums_kernel(*refs, counts=counts, base=base, many=many, fresh=not old),
+        in_specs=[SMEM] * (1 + len(counts)) + [VMEM] * (2 * len(counts) + 1 + len(old)),
         scratch_shapes=[pltpu.VMEM((4 * total, E, LANES), BF16), pltpu.VMEM((4 * total, LANES), I32)],
         out_shape=jax.ShapeDtypeStruct((many, HALF, E), F32),
         cost_estimate=cost(2 * many),
         compiler_params=PARAMS,
-    )(at, *[g[2] for g in gathered], *[g[0] for g in gathered], *[g[1] for g in gathered], rows)
+    )(at, *[g[2] for g in gathered], *[g[0] for g in gathered], *[g[1] for g in gathered], rows, *old)
 
 
 def listed_kernel(list_ref, rows_ref, accum_ref, table_ref, out_ref):
@@ -383,16 +384,18 @@
         down = lax.ppermute(down, "shard", z_pairs(-1))
         gathered.append(gather_of([up, down] + other, 0))
         other = swap([up, down])
-    up = lax.ppermute(up[:E // 2], "shard", z_pairs(1))
-    down = lax.ppermute(down[E // 2:], "shard", z_pairs(-1))
-    gathered.append(gather_of(other + [up, down], 1))
-    gathered.append(gather_of(swap([up, down]), 1))
+    up = lax.ppermute(up, "shard", z_pairs(1))
+    gathered.append(gather_of(other, 0))
+    at = jnp.concatenate([(x + jnp.array(ORDER, I32)) % NX, (NX * z).reshape(1)])
+    most = sums(at, 0, 1, gathered, rows, [])
+    gathered.append(gather_of([up], 0))
+    gathered.append(gather_of(swap([up]), 0))
 
     listed = listed_values(order, all_rows, accum.reshape(32, LANES), table)
-    at = jnp.concatenate([(x + jnp.array(ORDER, I32)) % NX, (NX * z).reshape(1)])
     both = {}
     for base, ks in ((0, (2,)), (1, (1, 3)), (3, (0,))):
-        found = sums(at, base, len(ks), gathered, rows)
+        found = sums(at, base, len(ks), gathered[5:] if base == 0 else gathered, rows,
+                     [most] if base == 0 else [])
         for n, k in enumerate(ks):
             both[k] = found[n]
             if k:

time: 129 us -> 134 us (1.039)
  waiting for transfers between devices: 35.6 us -> 43.2 us
  starting transfers between devices: 49.7 us -> 45.6 us
  Pallas kernels: 39 us -> 40.6 us
    ppermute x3 -> x4, waiting for transfers between devices: 10.7 us -> 18.3 us  [body(): up = lax.ppermute(up, 'shard', z_pairs(1))]
    ppermute x2 -> x0, starting transfers between devices: 2.81 us -> none  [the longest x1 2.73 us: body(): down = lax.ppermute(down[E // 2:], 'shard', z_pairs(-1))]
    pallas_call x3 -> x4, Pallas kernels: 10 us -> 11.2 us  [sums(): pl.pallas_call(lambda *refs: sums_kernel(*refs, counts=counts, base=base,...]
    pallas_call x6 -> x7, Pallas kernels: 12.3 us -> 12.9 us  [gather(): pl.pallas_call(lambda *refs: gather_kernel(*refs, count=count, split=spli...]
    ppermute x9 -> x8, starting transfers between devices: 7.72 us -> 7.28 us  [swap(): return [lax.ppermute(p, 'grp', C_PAIRS) for p in packets]]
  transfers between devices with their start and end apart: 33 -> 31, of which waited for: 6 -> 7; matrix products, arithmetic and copies ran while one was open for 1% -> 1% of each run, Pallas kernels for 18% -> 20%
where the time goes in v8:
time: 134 us; the launch traced here: 133 us
  starting transfers between devices  45.6 us (34%)
  waiting for transfers between devices  43.2 us (32%)
  Pallas kernels  40.6 us (30%)
  local copies, waits for them, and re-layouts  1.82 us (1%)
    ppermute x3, waiting for transfers between devices, body(): both[k] = lax.ppermute(both[k], 'shard', x_pairs(k))  19.4 us
    ppermute x4, waiting for transfers between devices, body(): up = lax.ppermute(up, 'shard', z_pairs(1))  18.3 us
    pallas_call x7, Pallas kernels, gather(): pl.pallas_call(lambda *refs: gather_kernel(*refs, count=count, split=spli...  12.9 us
    pallas_call x4, Pallas kernels, sums(): pl.pallas_call(lambda *refs: sums_kernel(*refs, counts=counts, base=base,...  11.2 us
    ppermute x3, starting transfers between devices, body(): down = lax.ppermute(down, 'shard', z_pairs(-1))  10.4 us
    ppermute x4, starting transfers between devices, body(): other = [lax.ppermute(m, 'grp', C_PAIRS) for m in mine]  8.28 us
    pallas_call x1, Pallas kernels, update(): pl.pallas_call(update_kernel, out_shape=(jax.ShapeDtypeStruct((ROWS_DEV,...  7.67 us
    ppermute x8, starting transfers between devices, swap(): return [lax.ppermute(p, 'grp', C_PAIRS) for p in packets]  7.28 us
  transfers between devices with their start and end apart: 31, of which 7 were waited for; matrix products, arithmetic and copies ran while one was open for 1% of the time, Pallas kernels for 20%

profile of v8, /device:TPU:1, one launch (start us, length us, event | category | flops | bytes accessed | tf_op | source)
XLA Modules:
  0.0 133.0 jit_solution(4428782205285365743)
XLA Ops:
  0.6 2.1 %collective-permute-start.17 = (s32[1024]{0:T(1024)}, s32[1024]{0:T(1024)S(1)}, u32[]{:S(2)}, u32[]{:S(2)}) collective-permute-start(s32[1024]{0:T(1024)} %bitcast.29), channel_id=1, source_target_pairs={{0,1},{1,2},{2,3},{3,0},{4,5},{5,6},{6,7},{7,4},{8,9},{9,10},{10,1... | collective-permute-start | bytes 12296 | tf_op jit(solution)/shard_map/ppermute | solution.py:361
  5.7 2.6 %pack.1.refs_1_ = bf16[256,640]{1,0:T(8,128)(2,1)S(1)} custom-call(s32[32,128]{1,0:T(8,128)} %bitcast.47, s32[32,128]{1,0:T(8,128)} %bitcast.48, bf16[512,256]{1,0:T(8,128)(2,1)} %bitcast.46), custom_call_target="tpu_custom_call" | custom-call | flops 2400000000 | bytes 12000000 | tf_op jit(solution)/shard_map/pack/pallas_call | solution.py:98
  10.1 4.0 %collective-permute-start.1 = (bf16[256,640]{1,0:T(8,128)(2,1)S(1)}, bf16[256,640]{1,0:T(8,128)(2,1)S(1)}, u32[]{:S(2)}, u32[]{:S(2)}) collective-permute-start(bf16[256,640]{1,0:T(8,128)(2,1)S(1)} %pack.1.refs_1_), channel_id=1, source_target_pairs={{0,28},{1,29},{2,30},{3,31},{4,0},{5,1},{6,2},{7,3},{8,4},{9,5},{1... | collective-permute-start | bytes 983048 | tf_op jit(solution)/shard_map/ppermute | solution.py:384
  17.3 3.3 %collective-permute-done.refs_1_ = bf16[256,640]{1,0:T(8,128)(2,1)S(1)} collective-permute-done((bf16[256,640]{1,0:T(8,128)(2,1)S(1)}, bf16[256,640]{1,0:T(8,128)(2,1)S(1)}, u32[]{:S(2)}, u32[]{:S(2)}) %collective-permute-start) | collective-permute-done | bytes 327712 | tf_op jit(solution)/shard_map/ppermute | solution.py:383
  22.7 3.0 %collective-permute-start.4 = (bf16[256,640]{1,0:T(8,128)(2,1)S(1)}, bf16[256,640]{1,0:T(8,128)(2,1)S(1)}, u32[]{:S(2)}, u32[]{:S(2)}) collective-permute-start(bf16[256,640]{1,0:T(8,128)(2,1)S(1)} %collective-permute-done.1.refs_2_), channel_id=1, source_target_pairs={{0,28},{1,29},{2,30},{3,31},{4,0},{5,1},{6,2},{7,3},{8,4},{9,5},{1... | collective-permute-start | bytes 983048 | tf_op jit(solution)/shard_map/ppermute | solution.py:384
  26.0 2.2 %shard_map.87 = (bf16[3,16,256,128]{3,2,1,0:T(8,128)(2,1)S(1)}, s32[3,16,128]{2,1,0:T(8,128)S(1)}, s32[3,8,128]{2,1,0:T(8,128)S(1)}) custom-call(s32[1]{0:T(128)} %bitcast.6.refs_0_, bf16[256,640]{1,0:T(8,128)(2,1)S(1)} %collective-permute-done.refs_1_, bf16[256,640]{1,0:T(8,128)(2,1)S(1)} %collective-permute-done.1.refs_2_, ...), custom_call_target="tpu_custom_call" | custom-call | flops 3000000000 | bytes 15000000 | tf_op jit(solution)/shard_map/pallas_call | solution.py:154
  28.2 4.5 %collective-permute-done.4.refs_2_ = bf16[256,640]{1,0:T(8,128)(2,1)S(1)} collective-permute-done((bf16[256,640]{1,0:T(8,128)(2,1)S(1)}, bf16[256,640]{1,0:T(8,128)(2,1)S(1)}, u32[]{:S(2)}, u32[]{:S(2)}) %collective-permute-start.4) | collective-permute-done | bytes 327712 | tf_op jit(solution)/shard_map/ppermute | solution.py:384
  32.7 3.4 %collective-permute-start.8 = (bf16[256,640]{1,0:T(8,128)(2,1)S(1)}, bf16[256,640]{1,0:T(8,128)(2,1)S(1)}, u32[]{:S(2)}, u32[]{:S(2)}) collective-permute-start(bf16[256,640]{1,0:T(8,128)(2,1)S(1)} %collective-permute-done.4.refs_2_), channel_id=1, source_target_pairs={{0,28},{1,29},{2,30},{3,31},{4,0},{5,1},{6,2},{7,3},{8,4},{9,5},{1... | collective-permute-start | bytes 983048 | tf_op jit(solution)/shard_map/ppermute | solution.py:384
  37.4 3.0 %shard_map.88 = (bf16[4,16,256,128]{3,2,1,0:T(8,128)(2,1)S(1)}, s32[4,16,128]{2,1,0:T(8,128)S(1)}, s32[4,8,128]{2,1,0:T(8,128)S(1)}) custom-call(s32[1]{0:T(128)} %bitcast.6.refs_0_, bf16[256,640]{1,0:T(8,128)(2,1)S(1)} %collective-permute-done.3.refs_1_, bf16[256,640]{1,0:T(8,128)(2,1)S(1)} %collective-permute-done.4.refs_2_, ...), custom_call_target="tpu_custom_call" | custom-call | flops 3600000000 | bytes 18000000 | tf_op jit(solution)/shard_map/pallas_call | solution.py:154
  40.4 7.4 %collective-permute-done.7.refs_1_ = bf16[256,640]{1,0:T(8,128)(2,1)S(1)} collective-permute-done((bf16[256,640]{1,0:T(8,128)(2,1)S(1)}, bf16[256,640]{1,0:T(8,128)(2,1)S(1)}, u32[]{:S(2)}, u32[]{:S(2)}) %collective-permute-start.7) | collective-permute-done | bytes 327712 | tf_op jit(solution)/shard_map/ppermute | solution.py:383
  48.7 2.8 %shard_map.89 = (bf16[4,16,256,128]{3,2,1,0:T(8,128)(2,1)S(1)}, s32[4,16,128]{2,1,0:T(8,128)S(1)}, s32[4,8,128]{2,1,0:T(8,128)S(1)}) custom-call(s32[1]{0:T(128)} %bitcast.6.refs_0_, bf16[256,640]{1,0:T(8,128)(2,1)S(1)} %collective-permute-done.7.refs_1_, bf16[256,640]{1,0:T(8,128)(2,1)S(1)} %collective-permute-done.8.refs_2_, ...), custom_call_target="tpu_custom_call" | custom-call | flops 3600000000 | bytes 18000000 | tf_op jit(solution)/shard_map/pallas_call | solution.py:154
  51.5 7.6 %collective-permute-done.13.refs_1_ = bf16[256,640]{1,0:T(8,128)(2,1)S(1)} collective-permute-done((bf16[256,640]{1,0:T(8,128)(2,1)S(1)}, bf16[256,640]{1,0:T(8,128)(2,1)S(1)}, u32[]{:S(2)}, u32[]{:S(2)}) %collective-permute-start.13) | collective-permute-done | bytes 327712 | tf_op jit(solution)/shard_map/ppermute | solution.py:387
  62.0 2.8 %shard_map.94.refs_8_ = f32[1,512,256]{2,1,0:T(8,128)S(1)} custom-call(s32[5]{0:T(128)S(1)} %pad_add_fusion.2.refs_0_, s32[1,8,128]{2,1,0:T(8,128)S(1)} %get-tuple-element.25.refs_1_, s32[3,8,128]{2,1,0:T(8,128)S(1)} %get-tuple-element.26.refs_2_, s32[4,8,128]{2,1,0:T(8,128)S(1)} %get-tuple-element.27.refs_3_, s32[4,8,128]{2,1,0:T(8,128)S(1)} %get-tuple-element.28.refs_4_, ...), custom_call_target="tpu_custom_call" | custom-call | flops 1200000000 | bytes 6000000 | tf_op jit(solution)/shard_map/pallas_call | solution.py:215
  66.9 4.2 %shard_map.96 = f32[2,512,256]{2,1,0:T(8,128)S(1)} custom-call(s32[5]{0:T(128)S(1)} %pad_add_fusion.2.refs_0_, s32[1,8,128]{2,1,0:T(8,128)S(1)} %get-tuple-element.25.refs_1_, s32[3,8,128]{2,1,0:T(8,128)S(1)} %get-tuple-element.26.refs_2_, s32[4,8,128]{2,1,0:T(8,128)S(1)} %get-tuple-element.27.refs_3_, s32[4,8,128]{2,1,0:T(8,128)S(1)} %get-tuple-element.28.refs_4_, ...), custom_call_target="tpu_custom_call" | custom-call | flops 2400000000 | bytes 12000000 | tf_op jit(solution)/shard_map/pallas_call | solution.py:215
  74.2 2.6 %collective-permute-start.20 = (f32[512,256]{1,0:T(8,128)S(1)}, f32[512,256]{1,0:T(8,128)S(1)}, u32[]{:S(2)}, u32[]{:S(2)}) collective-permute-start(f32[512,256]{1,0:T(8,128)S(1)} %get-tuple-element.49), channel_id=1, source_target_pairs={{0,3},{1,0},{2,1},{3,2},{4,7},{5,4},{6,5},{7,6},{8,11},{9,8},{10,9... | collective-permute-start | bytes 1572872 | tf_op jit(solution)/shard_map/ppermute | solution.py:402
  76.8 2.9 %shard_map.93 = f32[1,512,256]{2,1,0:T(8,128)S(1)} custom-call(s32[5]{0:T(128)S(1)} %pad_add_fusion.2.refs_0_, s32[1,8,128]{2,1,0:T(8,128)S(1)} %get-tuple-element.25.refs_1_, s32[3,8,128]{2,1,0:T(8,128)S(1)} %get-tuple-element.26.refs_2_, s32[4,8,128]{2,1,0:T(8,128)S(1)} %get-tuple-element.27.refs_3_, s32[4,8,128]{2,1,0:T(8,128)S(1)} %get-tuple-element.28.refs_4_, ...), custom_call_target="tpu_custom_call" | custom-call | flops 1200000000 | bytes 6000000 | tf_op jit(solution)/shard_map/pallas_call | solution.py:215
  79.7 7.8 %collective-permute-done.18 = f32[512,256]{1,0:T(8,128)S(1)} collective-permute-done((f32[512,256]{1,0:T(8,128)S(1)}, f32[512,256]{1,0:T(8,128)S(1)}, u32[]{:S(2)}, u32[]{:S(2)}) %collective-permute-start.18) | collective-permute-done | bytes 524320 | tf_op jit(solution)/shard_map/ppermute | solution.py:402
  87.6 11.6 %collective-permute-done.19 = f32[512,256]{1,0:T(8,128)S(1)} collective-permute-done((f32[512,256]{1,0:T(8,128)S(1)}, f32[512,256]{1,0:T(8,128)S(1)}, u32[]{:S(2)}, u32[]{:S(2)}) %collective-permute-start.19) | collective-permute-done | bytes 524320 | tf_op jit(solution)/shard_map/ppermute | solution.py:402
  99.4 3.0 %collective-permute-start.21 = (f32[128,256]{1,0:T(8,128)S(1)}, f32[128,256]{1,0:T(8,128)S(1)}, u32[]{:S(2)}, u32[]{:S(2)}) collective-permute-start(f32[128,256]{1,0:T(8,128)S(1)} %get-tuple-element.50), channel_id=1, source_target_pairs={{0,128},{32,160},{64,192},{96,224},{128,0},{160,32},{192,64},{224,... | collective-permute-start | bytes 393224 | tf_op jit(solution)/shard_map/ppermute | solution.py:406
  102.4 2.2 %collective-permute-start.22 = (f32[128,256]{1,0:T(8,128)S(1)}, f32[128,256]{1,0:T(8,128)S(1)}, u32[]{:S(2)}, u32[]{:S(2)}) collective-permute-start(f32[128,256]{1,0:T(8,128)S(1)} %get-tuple-element.52), channel_id=1, source_target_pairs={{0,64},{32,96},{64,128},{96,160},{128,192},{160,224},{192,0},{224,... | collective-permute-start | bytes 393224 | tf_op jit(solution)/shard_map/ppermute | solution.py:406
  105.3 6.3 %listed_values.1.refs_3_ = f32[1056,384]{1,0:T(8,128)S(1)} custom-call(s32[8,128]{1,0:T(8,128)S(1)} %bitcast.36, s32[1024,128]{1,0:T(8,128)S(1)} %broadcast_in_dim.7.rows_ref.refs_4_, f32[32,128]{1,0:T(8,128)S(1)} %bitcast.38, f32[4096,256]{1,0:T(8,128)S(1)} %copy-done), custom_call_target="tpu_custom_call" | custom-call | flops 3600000000 | bytes 18000000 | tf_op jit(solution)/shard_map/listed_values/pallas_call | solution.py:245
  118.0 2.2 %collective-permute-start.26 = (f32[128,256]{1,0:T(8,128)S(1)}, f32[128,256]{1,0:T(8,128)S(1)}, u32[]{:S(2)}, u32[]{:S(2)}) collective-permute-start(f32[128,256]{1,0:T(8,128)S(1)} %collective-permute-done.25.refs_10_), channel_id=1, source_target_pairs={{0,32},{32,0},{64,96},{96,64},{128,160},{160,128},{192,224},{224,1... | collective-permute-start | bytes 393224 | tf_op jit(solution)/shard_map/ppermute | solution.py:408
  120.2 2.4 %collective-permute-start.28 = (f32[128,256]{1,0:T(8,128)S(1)}, f32[128,256]{1,0:T(8,128)S(1)}, u32[]{:S(2)}, u32[]{:S(2)}) collective-permute-start(f32[128,256]{1,0:T(8,128)S(1)} %collective-permute-done.27.refs_11_), channel_id=1, source_target_pairs={{0,32},{32,0},{64,96},{96,64},{128,160},{160,128},{192,224},{224,1... | collective-permute-start | bytes 393224 | tf_op jit(solution)/shard_map/ppermute | solution.py:408
  125.2 7.7 %update.1 = (f32[4096,256]{1,0:T(8,128)}, f32[32,128]{1,0:T(8,128)}) custom-call(s32[24]{0:T(128)S(1)} %pad_add_fusion.1.refs_0_, s32[1024]{0:T(1024)S(1)} %bitcast.34, f32[4096,256]{1,0:T(8,128)} %refs_2_.1, f32[1056,384]{1,0:T(8,128)} %copy-done.1, s32[1024,128]{1,0:T(8,128)S(1)} %broadcast_in_dim.7.rows_ref.refs_4_, ...), custom_call_target="tpu_custom_call" | custom-call | tf_op jit(solution)/shard_map/update/pallas_call | solution.py:316
  (83 shorter events, 30.2 us)
Async XLA Ops:
  0.6 14.8 %collective-permute-start.17 = (s32[1024]{0:T(1024)}, s32[1024]{0:T(1024)S(1)}, u32[]{:S(2)}, u32[]{:S(2)}) collective-permute-start(s32[1024]{0:T(1024)} %bitcast.29), channel_id=1, source_target_pairs={{0,1},{1,2},{2,3},{3,0},{4,5},{5,6},{6,7},{7,4},{8,9},{9,10},{10,1... | collective-permute-start | bytes 12296 | tf_op jit(solution)/shard_map/ppermute | solution.py:361
  2.7 14.5 %collective-permute-start.16 = (s32[1024]{0:T(1024)}, s32[1024]{0:T(1024)S(1)}, u32[]{:S(2)}, u32[]{:S(2)}) collective-permute-start(s32[1024]{0:T(1024)} %bitcast.30), channel_id=1, source_target_pairs={{0,3},{1,0},{2,1},{3,2},{4,7},{5,4},{6,5},{7,6},{8,11},{9,8},{10,9... | collective-permute-start | bytes 12296 | tf_op jit(solution)/shard_map/ppermute | solution.py:361
  4.1 13.2 %collective-permute-start.15 = (s32[1024]{0:T(1024)}, s32[1024]{0:T(1024)S(1)}, u32[]{:S(2)}, u32[]{:S(2)}) collective-permute-start(s32[1024]{0:T(1024)} %bitcast.31), channel_id=1, source_target_pairs={{0,2},{1,3},{2,0},{3,1},{4,6},{5,7},{6,4},{7,5},{8,10},{9,11},{10,... | collective-permute-start | bytes 12296 | tf_op jit(solution)/shard_map/ppermute | solution.py:361
  8.4 12.2 %collective-permute-start = (bf16[256,640]{1,0:T(8,128)(2,1)S(1)}, bf16[256,640]{1,0:T(8,128)(2,1)S(1)}, u32[]{:S(2)}, u32[]{:S(2)}) collective-permute-start(bf16[256,640]{1,0:T(8,128)(2,1)S(1)} %pack.1.refs_1_), channel_id=1, source_target_pairs={{0,4},{1,5},{2,6},{3,7},{4,8},{5,9},{6,10},{7,11},{8,12},{9,13},{1... | collective-permute-start | bytes 983048 | tf_op jit(solution)/shard_map/ppermute | solution.py:383
  10.1 12.6 %collective-permute-start.1 = (bf16[256,640]{1,0:T(8,128)(2,1)S(1)}, bf16[256,640]{1,0:T(8,128)(2,1)S(1)}, u32[]{:S(2)}, u32[]{:S(2)}) collective-permute-start(bf16[256,640]{1,0:T(8,128)(2,1)S(1)} %pack.1.refs_1_), channel_id=1, source_target_pairs={{0,28},{1,29},{2,30},{3,31},{4,0},{5,1},{6,2},{7,3},{8,4},{9,5},{1... | collective-permute-start | bytes 983048 | tf_op jit(solution)/shard_map/ppermute | solution.py:384
  15.4 10.6 %collective-permute-start.2 = (bf16[256,640]{1,0:T(8,128)(2,1)S(1)}, bf16[256,640]{1,0:T(8,128)(2,1)S(1)}, u32[]{:S(2)}, u32[]{:S(2)}) collective-permute-start(bf16[256,640]{1,0:T(8,128)(2,1)S(1)} %pack.1.refs_1_), channel_id=1, source_target_pairs={{0,32},{32,0},{64,96},{96,64},{128,160},{160,128},{192,224},{224,1... | collective-permute-start | bytes 983048 | tf_op jit(solution)/shard_map/ppermute | solution.py:374
  20.6 16.7 %collective-permute-start.3 = (bf16[256,640]{1,0:T(8,128)(2,1)S(1)}, bf16[256,640]{1,0:T(8,128)(2,1)S(1)}, u32[]{:S(2)}, u32[]{:S(2)}) collective-permute-start(bf16[256,640]{1,0:T(8,128)(2,1)S(1)} %collective-permute-done.refs_1_), channel_id=1, source_target_pairs={{0,4},{1,5},{2,6},{3,7},{4,8},{5,9},{6,10},{7,11},{8,12},{9,13},{1... | collective-permute-start | bytes 983048 | tf_op jit(solution)/shard_map/ppermute | solution.py:383
  20.6 16.7 %collective-permute-start.5 = (bf16[256,640]{1,0:T(8,128)(2,1)S(1)}, bf16[256,640]{1,0:T(8,128)(2,1)S(1)}, u32[]{:S(2)}, u32[]{:S(2)}) collective-permute-start(bf16[256,640]{1,0:T(8,128)(2,1)S(1)} %collective-permute-done.refs_1_), channel_id=1, source_target_pairs={{0,32},{32,0},{64,96},{96,64},{128,160},{160,128},{192,224},{224,1... | collective-permute-start | bytes 983048 | tf_op jit(solution)/shard_map/ppermute | solution.py:374
  22.7 10.0 %collective-permute-start.4 = (bf16[256,640]{1,0:T(8,128)(2,1)S(1)}, bf16[256,640]{1,0:T(8,128)(2,1)S(1)}, u32[]{:S(2)}, u32[]{:S(2)}) collective-permute-start(bf16[256,640]{1,0:T(8,128)(2,1)S(1)} %collective-permute-done.1.refs_2_), channel_id=1, source_target_pairs={{0,28},{1,29},{2,30},{3,31},{4,0},{5,1},{6,2},{7,3},{8,4},{9,5},{1... | collective-permute-start | bytes 983048 | tf_op jit(solution)/shard_map/ppermute | solution.py:384
  25.7 11.7 %collective-permute-start.6 = (bf16[256,640]{1,0:T(8,128)(2,1)S(1)}, bf16[256,640]{1,0:T(8,128)(2,1)S(1)}, u32[]{:S(2)}, u32[]{:S(2)}) collective-permute-start(bf16[256,640]{1,0:T(8,128)(2,1)S(1)} %collective-permute-done.1.refs_2_), channel_id=1, source_target_pairs={{0,32},{32,0},{64,96},{96,64},{128,160},{160,128},{192,224},{224,1... | collective-permute-start | bytes 983048 | tf_op jit(solution)/shard_map/ppermute | solution.py:374
  32.7 15.9 %collective-permute-start.8 = (bf16[256,640]{1,0:T(8,128)(2,1)S(1)}, bf16[256,640]{1,0:T(8,128)(2,1)S(1)}, u32[]{:S(2)}, u32[]{:S(2)}) collective-permute-start(bf16[256,640]{1,0:T(8,128)(2,1)S(1)} %collective-permute-done.4.refs_2_), channel_id=1, source_target_pairs={{0,28},{1,29},{2,30},{3,31},{4,0},{5,1},{6,2},{7,3},{8,4},{9,5},{1... | collective-permute-start | bytes 983048 | tf_op jit(solution)/shard_map/ppermute | solution.py:384
  36.1 12.6 %collective-permute-start.10 = (bf16[256,640]{1,0:T(8,128)(2,1)S(1)}, bf16[256,640]{1,0:T(8,128)(2,1)S(1)}, u32[]{:S(2)}, u32[]{:S(2)}) collective-permute-start(bf16[256,640]{1,0:T(8,128)(2,1)S(1)} %collective-permute-done.4.refs_2_), channel_id=1, source_target_pairs={{0,32},{32,0},{64,96},{96,64},{128,160},{160,128},{192,224},{224,1... | collective-permute-start | bytes 983048 | tf_op jit(solution)/shard_map/ppermute | solution.py:374
  37.3 10.5 %collective-permute-start.7 = (bf16[256,640]{1,0:T(8,128)(2,1)S(1)}, bf16[256,640]{1,0:T(8,128)(2,1)S(1)}, u32[]{:S(2)}, u32[]{:S(2)}) collective-permute-start(bf16[256,640]{1,0:T(8,128)(2,1)S(1)} %collective-permute-done.3.refs_1_), channel_id=1, source_target_pairs={{0,4},{1,5},{2,6},{3,7},{4,8},{5,9},{6,10},{7,11},{8,12},{9,13},{1... | collective-permute-start | bytes 983048 | tf_op jit(solution)/shard_map/ppermute | solution.py:383
  37.3 11.4 %collective-permute-start.9 = (bf16[256,640]{1,0:T(8,128)(2,1)S(1)}, bf16[256,640]{1,0:T(8,128)(2,1)S(1)}, u32[]{:S(2)}, u32[]{:S(2)}) collective-permute-start(bf16[256,640]{1,0:T(8,128)(2,1)S(1)} %collective-permute-done.3.refs_1_), channel_id=1, source_target_pairs={{0,32},{32,0},{64,96},{96,64},{128,160},{160,128},{192,224},{224,1... | collective-permute-start | bytes 983048 | tf_op jit(solution)/shard_map/ppermute | solution.py:374
  47.8 12.2 %collective-permute-start.11 = (bf16[256,640]{1,0:T(8,128)(2,1)S(1)}, bf16[256,640]{1,0:T(8,128)(2,1)S(1)}, u32[]{:S(2)}, u32[]{:S(2)}) collective-permute-start(bf16[256,640]{1,0:T(8,128)(2,1)S(1)} %collective-permute-done.7.refs_1_), channel_id=1, source_target_pairs={{0,32},{32,0},{64,96},{96,64},{128,160},{160,128},{192,224},{224,1... | collective-permute-start | bytes 983048 | tf_op jit(solution)/shard_map/ppermute | solution.py:374
  48.6 10.5 %collective-permute-start.13 = (bf16[256,640]{1,0:T(8,128)(2,1)S(1)}, bf16[256,640]{1,0:T(8,128)(2,1)S(1)}, u32[]{:S(2)}, u32[]{:S(2)}) collective-permute-start(bf16[256,640]{1,0:T(8,128)(2,1)S(1)} %collective-permute-done.7.refs_1_), channel_id=1, source_target_pairs={{0,4},{1,5},{2,6},{3,7},{4,8},{5,9},{6,10},{7,11},{8,12},{9,13},{1... | collective-permute-start | bytes 983048 | tf_op jit(solution)/shard_map/ppermute | solution.py:387
  48.6 11.3 %collective-permute-start.12 = (bf16[256,640]{1,0:T(8,128)(2,1)S(1)}, bf16[256,640]{1,0:T(8,128)(2,1)S(1)}, u32[]{:S(2)}, u32[]{:S(2)}) collective-permute-start(bf16[256,640]{1,0:T(8,128)(2,1)S(1)} %collective-permute-done.8.refs_2_), channel_id=1, source_target_pairs={{0,32},{32,0},{64,96},{96,64},{128,160},{160,128},{192,224},{224,1... | collective-permute-start | bytes 983048 | tf_op jit(solution)/shard_map/ppermute | solution.py:374
  72.5 15.1 %collective-permute-start.18 = (f32[512,256]{1,0:T(8,128)S(1)}, f32[512,256]{1,0:T(8,128)S(1)}, u32[]{:S(2)}, u32[]{:S(2)}) collective-permute-start(f32[512,256]{1,0:T(8,128)S(1)} %bitcast.37), channel_id=1, source_target_pairs={{0,2},{1,3},{2,0},{3,1},{4,6},{5,7},{6,4},{7,5},{8,10},{9,11},{10,... | collective-permute-start | bytes 1572872 | tf_op jit(solution)/shard_map/ppermute | solution.py:402
  74.0 25.1 %collective-permute-start.19 = (f32[512,256]{1,0:T(8,128)S(1)}, f32[512,256]{1,0:T(8,128)S(1)}, u32[]{:S(2)}, u32[]{:S(2)}) collective-permute-start(f32[512,256]{1,0:T(8,128)S(1)} %get-tuple-element.48), channel_id=1, source_target_pairs={{0,1},{1,2},{2,3},{3,0},{4,5},{5,6},{6,7},{7,4},{8,9},{9,10},{10,1... | collective-permute-start | bytes 1572872 | tf_op jit(solution)/shard_map/ppermute | solution.py:402
  74.2 25.0 %collective-permute-start.20 = (f32[512,256]{1,0:T(8,128)S(1)}, f32[512,256]{1,0:T(8,128)S(1)}, u32[]{:S(2)}, u32[]{:S(2)}) collective-permute-start(f32[512,256]{1,0:T(8,128)S(1)} %get-tuple-element.49), channel_id=1, source_target_pairs={{0,3},{1,0},{2,1},{3,2},{4,7},{5,4},{6,5},{7,6},{8,11},{9,8},{10,9... | collective-permute-start | bytes 1572872 | tf_op jit(solution)/shard_map/ppermute | solution.py:402
  99.4 13.4 %collective-permute-start.21 = (f32[128,256]{1,0:T(8,128)S(1)}, f32[128,256]{1,0:T(8,128)S(1)}, u32[]{:S(2)}, u32[]{:S(2)}) collective-permute-start(f32[128,256]{1,0:T(8,128)S(1)} %get-tuple-element.50), channel_id=1, source_target_pairs={{0,128},{32,160},{64,192},{96,224},{128,0},{160,32},{192,64},{224,... | collective-permute-start | bytes 393224 | tf_op jit(solution)/shard_map/ppermute | solution.py:406
  102.4 10.4 %collective-permute-start.22 = (f32[128,256]{1,0:T(8,128)S(1)}, f32[128,256]{1,0:T(8,128)S(1)}, u32[]{:S(2)}, u32[]{:S(2)}) collective-permute-start(f32[128,256]{1,0:T(8,128)S(1)} %get-tuple-element.52), channel_id=1, source_target_pairs={{0,64},{32,96},{64,128},{96,160},{128,192},{160,224},{192,0},{224,... | collective-permute-start | bytes 393224 | tf_op jit(solution)/shard_map/ppermute | solution.py:406
  104.6 8.2 %collective-permute-start.23 = (f32[128,256]{1,0:T(8,128)S(1)}, f32[128,256]{1,0:T(8,128)S(1)}, u32[]{:S(2)}, u32[]{:S(2)}) collective-permute-start(f32[128,256]{1,0:T(8,128)S(1)} %get-tuple-element.51), channel_id=1, source_target_pairs={{0,192},{32,224},{64,0},{96,32},{128,64},{160,96},{192,128},{224,1... | collective-permute-start | bytes 393224 | tf_op jit(solution)/shard_map/ppermute | solution.py:406
  115.9 8.4 %collective-permute-start.24 = (f32[128,256]{1,0:T(8,128)S(1)}, f32[128,256]{1,0:T(8,128)S(1)}, u32[]{:S(2)}, u32[]{:S(2)}) collective-permute-start(f32[128,256]{1,0:T(8,128)S(1)} %fusion.3.refs_9_), channel_id=1, source_target_pairs={{0,32},{32,0},{64,96},{96,64},{128,160},{160,128},{192,224},{224,1... | collective-permute-start | bytes 393224 | tf_op jit(solution)/shard_map/ppermute | solution.py:408
  (12 other events, 115.4 us)

commit v9 on v8

--- a/solution.py
+++ b/solution.py
@@ -110,49 +110,44 @@
     )(*[in_hbm(a) for a in (ids, bags, grads)])
 
 
-def gather_kernel(z_ref, *refs, count, split):
-    packets = refs[0:count + split]
-    x_ref, k_ref, m_ref, all_ref, scalar_ref, sem = refs[count + split:]
+def gather_kernel(z_ref, *refs, counts):
+    groups, total = len(counts), sum(counts)
+    packets = [refs[n].at[i] for n in range(groups) for i in range(counts[n])]
+    x_ref, k_ref, m_ref, all_ref, scalar_ref, sem = refs[groups:]
     copies = []
-    for d in range(count):
-        cut = 128 if split and d == count - 1 else 0
-        tail = packets[-1] if cut else packets[d]
-        side = tail[3 * BLOCKS - cut:3 * BLOCKS + 16 - cut, B_DEV:WIDTH].astype(F32).astype(I32)
+    for d in range(total):
+        side = packets[d][3 * BLOCKS:3 * BLOCKS + 16, B_DEV:WIDTH].astype(F32).astype(I32)
         m_ref[d] = jnp.where(iota((8, LANES), 0) == 0, side[0:8], side[8:16])
         copies.append(pltpu.make_async_copy(m_ref.at[d], scalar_ref.at[d], sem.at[d]))
         copies[d].start()
-    for d in range(count):
-        cut = 128 if split and d == count - 1 else 0
-        tail = packets[-1] if cut else packets[d]
-        low = packets[d][0:2 * BLOCKS, B_DEV:WIDTH].astype(F32).astype(I32)
-        top = tail[2 * BLOCKS - cut:3 * BLOCKS - cut, B_DEV:WIDTH].astype(F32).astype(I32)
-        all_ref[d, 0:BLOCKS] = (low[0:BLOCKS] + (low[BLOCKS:2 * BLOCKS] << 8) + (top << 16)) - 1
+    for d in range(total):
+        pieces = packets[d][0:3 * BLOCKS, B_DEV:WIDTH].astype(F32).astype(I32)
+        all_ref[d, 0:BLOCKS] = (pieces[0:BLOCKS] + (pieces[BLOCKS:2 * BLOCKS] << 8)
+                                + (pieces[2 * BLOCKS:3 * BLOCKS] << 16)) - 1
         all_ref[d, BLOCKS:BLOCKS + 16] = jnp.zeros((16, LANES), I32)
     for copy in copies:
         copy.wait()
-    for d in range(count):
-        parts = packets[d:] if split and d == count - 1 else packets[d:d + 1]
+    for d in range(total):
         first = scalar_ref[d, 0, NX * z_ref[0]]
         last = scalar_ref[d, 0, NX * z_ref[0] + NX - 1] + scalar_ref[d, 1, NX * z_ref[0] + NX - 1]
         k_ref[d] = all_ref[d, pl.ds(first, 16), :] >> 9
 
-        def pair(j, _, d=d, first=first, parts=parts):
+        def pair(j, _, d=d, first=first):
             lines = [all_ref[d, pl.ds(first + 2 * j + i, 1), :] & (B_DEV - 1) for i in range(2)]
             picks = jnp.concatenate([one_hot(line == iota((B_DEV, LANES), 0)) for line in lines], axis=1)
-            rows = E // len(parts)
-            for n, part in enumerate(parts):
-                got = jnp.dot(part[:, 0:B_DEV], picks, preferred_element_type=F32).astype(BF16)
-                for i in range(2):
-                    x_ref[d, 2 * j + i, n * rows:(n + 1) * rows] = got[:, i * LANES:(i + 1) * LANES]
+            got = jnp.dot(packets[d][:, 0:B_DEV], picks, preferred_element_type=F32).astype(BF16)
+            for i in range(2):
+                x_ref[d, 2 * j + i] = got[:, i * LANES:(i + 1) * LANES]
             return 0
 
         lax.fori_loop(0, (last - first + 1) >> 1, pair, 0)
 
 
-def gather(z, packets, split):
-    count = len(packets) - split
+def gather(z, packets):
+    counts = tuple(p.shape[0] for p in packets)
+    count = sum(counts)
     return pl.pallas_call(
-        lambda *refs: gather_kernel(*refs, count=count, split=split),
+        lambda *refs: gather_kernel(*refs, counts=counts),
         out_shape=(jax.ShapeDtypeStruct((count, 16, E, LANES), BF16),
                    jax.ShapeDtypeStruct((count, 16, LANES), I32),
                    jax.ShapeDtypeStruct((count, 8, LANES), I32)),
@@ -254,8 +249,8 @@
 
 def update_kernel(*refs):
     plan_ref, list_ref, table_ref, listed_hbm, rows_ref = refs[0:5]
-    chunks = refs[5:13]
-    table_out, accum_out, new_ref, listed_ref, u_ref, lhs_ref, rhs_ref, load_sem, store_sem = refs[13:]
+    chunks = [refs[5]] + [refs[6].at[n * QUART:(n + 1) * QUART] for n in range(NY - 1)] + list(refs[7:11])
+    table_out, accum_out, new_ref, listed_ref, u_ref, lhs_ref, rhs_ref, load_sem, store_sem = refs[11:]
     tiles = ROWS_DEV // TILE
     listed_load = pltpu.make_async_copy(listed_hbm, listed_ref, load_sem.at[tiles])
     listed_load.start()
@@ -316,7 +311,7 @@
     return pl.pallas_call(
         update_kernel,
         out_shape=(jax.ShapeDtypeStruct((ROWS_DEV, E), F32), jax.ShapeDtypeStruct((32, LANES), F32)),
-        in_specs=[SMEM, SMEM, HBM, HBM] + [VMEM] * 9,
+        in_specs=[SMEM, SMEM, HBM, HBM] + [VMEM] * 7,
         out_specs=(HBM, VMEM),
         scratch_shapes=[pltpu.VMEM((ROWS_DEV, E), F32), pltpu.VMEM((TOUCH + 32, E + LANES), F32),
                         pltpu.VMEM((TOUCH, E), F32),
@@ -328,10 +323,6 @@
     )(plan, natural, in_hbm(table), in_hbm(listed), rows, *chunks)
 
 
-def z_pairs(k):
-    return [(z * NX + x, ((z + k) % NZ) * NX + x) for z in range(NZ) for x in range(NX)]
-
-
 def x_pairs(k):
     return [(z * NX + x, z * NX + (x + k) % NX) for z in range(NZ) for x in range(NX)]
 
@@ -340,6 +331,9 @@
     return [(y * NC + c, ((y + k) % NY) * NC + c) for y in range(NY) for c in range(NC)]
 
 
+HOPS = [((y * NC + c) * NZ * NX + z * NX + x,
+         (y * NC + c) * NZ * NX + (z + 1 - 2 * c) % NZ * NX + x)
+        for y in range(NY) for c in range(NC) for z in range(NZ) for x in range(NX)]
 C_PAIRS = [(y * NC + c, y * NC + 1 - c) for y in range(NY) for c in range(NC)]
 
 
@@ -370,26 +364,33 @@
     packet = pack(row_ids.reshape(32, LANES), bag_ids.reshape(32, LANES),
                   pooled_grad.reshape(B_DEV, E))
 
-    def swap(packets):
-        return [lax.ppermute(p, "grp", C_PAIRS) for p in packets]
-
-    def gather_of(packets, split):
-        return gather(z.reshape(1), packets, split)
-
-    up = down = packet
-    other = swap([packet])
-    gathered = [gather_of([packet], 0)]
-    for _ in range(1, 4):
-        up = lax.ppermute(up, "shard", z_pairs(1))
-        down = lax.ppermute(down, "shard", z_pairs(-1))
-        gathered.append(gather_of([up, down] + other, 0))
-        other = swap([up, down])
-    up = lax.ppermute(up, "shard", z_pairs(1))
-    gathered.append(gather_of(other, 0))
+    def swap(array):
+        return lax.ppermute(array, "grp", C_PAIRS)
+
+    def hop(array):
+        return lax.ppermute(array, ("grp", "shard"), HOPS)
+
+    def gather_of(packets):
+        return gather(z.reshape(1), packets)
+
     at = jnp.concatenate([(x + jnp.array(ORDER, I32)) % NX, (NX * z).reshape(1)])
+    pool = jnp.stack([packet, swap(packet)])
+    one = hop(pool)
+    gathered = [gather_of([pool])]
+    two = hop(one)
+    one_other = swap(one)
+    gathered.append(gather_of([one]))
+    three = hop(two)
+    two_other = swap(two)
+    gathered.append(gather_of([two, one_other]))
+    four = hop(three[0:1])
+    three_other = swap(three)
+    gathered.append(gather_of([three, two_other]))
+    gathered.append(gather_of([three_other]))
     most = sums(at, 0, 1, gathered, rows, [])
-    gathered.append(gather_of([up], 0))
-    gathered.append(gather_of(swap([up]), 0))
+    four_other = swap(four)
+    gathered.append(gather_of([four]))
+    gathered.append(gather_of([four_other]))
 
     listed = listed_values(order, all_rows, accum.reshape(32, LANES), table)
     both = {}
@@ -405,7 +406,7 @@
     for j in (2, 1, 3):
         part = part + lax.ppermute(total[j * QUART:(j + 1) * QUART], "grp", y_pairs(j))
     mine = [part] + [lax.ppermute(part, "grp", y_pairs(-j)) for j in range(1, NY)]
-    other = [lax.ppermute(m, "grp", C_PAIRS) for m in mine]
+    other = [swap(part), swap(jnp.concatenate(mine[1:], axis=0))]
     new_table, new_accum = update(plan, own_list, table, listed, all_rows, other + mine)
     return (new_table, new_accum.reshape(ROWS_DEV))
 

time: 134 us -> 134 us (level)
  waiting for transfers between devices: 43.2 us -> 49.1 us
  starting transfers between devices: 45.6 us -> 40.8 us
    ppermute x3, waiting for transfers between devices: 0.01 us -> 5.78 us  [body(): lax.ppermute(total[j * QUART:(j + 1) * QUART], 'grp', y_pairs(j))]
    ppermute x19 -> x11, starting transfers between devices: 27.7 us -> 23.1 us  [the longest x4 11.8 us: hop(): return lax.ppermute(array, ('grp', 'shard'), HOPS)]
    ppermute x3, starting transfers between devices: 5.1 us -> 2.68 us  [body(): lists[k] = ordered(lax.ppermute(own_list, 'shard', x_pairs(-k)))]
    ppermute x19 -> x11, waiting for transfers between devices: 23.7 us -> 23.2 us  [the longest x4 22 us: hop(): return lax.ppermute(array, ('grp', 'shard'), HOPS)]
  transfers between devices with their start and end apart: 31 -> 23, of which waited for: 7 -> 10; matrix products, arithmetic and copies ran while one was open for 1% -> 1% of each run, Pallas kernels for 20% -> 18%
where the time goes in v9:
time: 134 us
  waiting for transfers between devices  49.1 us (37%)
  starting transfers between devices  40.8 us (30%)
  Pallas kernels  40.6 us (30%)
  local copies, waits for them, and re-layouts  1.86 us (1%)
    ppermute x4, waiting for transfers between devices, hop(): return lax.ppermute(array, ('grp', 'shard'), HOPS)  22 us
    ppermute x3, waiting for transfers between devices, body(): both[k] = lax.ppermute(both[k], 'shard', x_pairs(k))  19.4 us
    pallas_call x7, Pallas kernels, gather(): pl.pallas_call(lambda *refs: gather_kernel(*refs, counts=counts), out_sha...  12.9 us
    ppermute x4, starting transfers between devices, hop(): return lax.ppermute(array, ('grp', 'shard'), HOPS)  11.8 us
    ppermute x7, starting transfers between devices, swap(): return lax.ppermute(array, 'grp', C_PAIRS)  11.3 us
    pallas_call x4, Pallas kernels, sums(): pl.pallas_call(lambda *refs: sums_kernel(*refs, counts=counts, base=base,...  11.2 us
    pallas_call x1, Pallas kernels, update(): pl.pallas_call(update_kernel, out_shape=(jax.ShapeDtypeStruct((ROWS_DEV,...  7.66 us
    ppermute x3, starting transfers between devices, body(): lax.ppermute(total[j * QUART:(j + 1) * QUART], 'grp', y_pairs(j))  6.62 us
  transfers between devices with their start and end apart: 23, of which 10 were waited for; matrix products, arithmetic and copies ran while one was open for 1% of the time, Pallas kernels for 18%

profile of v9, /device:TPU:1, one launch (start us, length us, event | category | flops | bytes accessed | tf_op | source)
XLA Modules:
  0.0 134.3 jit_solution(3489013357132889392)
XLA Ops:
  3.3 3.3 %collective-permute-start = (bf16[256,640]{1,0:T(8,128)(2,1)S(1)}, bf16[256,640]{1,0:T(8,128)(2,1)S(1)}, u32[]{:S(2)}, u32[]{:S(2)}) collective-permute-start(bf16[256,640]{1,0:T(8,128)(2,1)S(1)} %pack.1), channel_id=1, source_target_pairs={{0,32},{32,0},{64,96},{96,64},{128,160},{160,128},{192,224},{224,1... | collective-permute-start | bytes 983048 | tf_op jit(solution)/shard_map/ppermute | solution.py:368
  6.6 2.7 %collective-permute-start.10 = (s32[1024]{0:T(1024)S(1)}, s32[1024]{0:T(1024)S(1)}, u32[]{:S(2)}, u32[]{:S(2)}) collective-permute-start(s32[1024]{0:T(1024)S(1)} %bitcast.33), channel_id=1, source_target_pairs={{0,3},{1,0},{2,1},{3,2},{4,7},{5,4},{6,5},{7,6},{8,11},{9,8},{10,9... | collective-permute-start | bytes 12296 | tf_op jit(solution)/shard_map/ppermute | solution.py:355
  9.3 5.5 %collective-permute-start.1 = (bf16[2,256,640]{2,1,0:T(8,128)(2,1)S(1)}, bf16[2,256,640]{2,1,0:T(8,128)(2,1)S(1)}, u32[]{:S(2)}, u32[]{:S(2)}) collective-permute-start(bf16[2,256,640]{2,1,0:T(8,128)(2,1)S(1)} %pad_maximum_fusion.refs_1_), channel_id=1, source_target_pairs={{0,4},{1,5},{2,6},{3,7},{4,8},{5,9},{6,10},{7,11},{8,12},{9,13},{1... | collective-permute-start | bytes 1966088 | tf_op jit(solution)/shard_map/ppermute | solution.py:371
  14.9 7.4 %collective-permute-done.1.refs_1_ = bf16[2,256,640]{2,1,0:T(8,128)(2,1)S(1)} collective-permute-done((bf16[2,256,640]{2,1,0:T(8,128)(2,1)S(1)}, bf16[2,256,640]{2,1,0:T(8,128)(2,1)S(1)}, u32[]{:S(2)}, u32[]{:S(2)}) %collective-permute-start.1) | collective-permute-done | bytes 655392 | tf_op jit(solution)/shard_map/ppermute | solution.py:371
  22.4 3.1 %collective-permute-start.2 = (bf16[2,256,640]{2,1,0:T(8,128)(2,1)S(1)}, bf16[2,256,640]{2,1,0:T(8,128)(2,1)S(1)}, u32[]{:S(2)}, u32[]{:S(2)}) collective-permute-start(bf16[2,256,640]{2,1,0:T(8,128)(2,1)S(1)} %collective-permute-done.1.refs_1_), channel_id=1, source_target_pairs={{0,4},{1,5},{2,6},{3,7},{4,8},{5,9},{6,10},{7,11},{8,12},{9,13},{1... | collective-permute-start | bytes 1966088 | tf_op jit(solution)/shard_map/ppermute | solution.py:371
  25.6 7.4 %collective-permute-done.2.refs_1_ = bf16[2,256,640]{2,1,0:T(8,128)(2,1)S(1)} collective-permute-done((bf16[2,256,640]{2,1,0:T(8,128)(2,1)S(1)}, bf16[2,256,640]{2,1,0:T(8,128)(2,1)S(1)}, u32[]{:S(2)}, u32[]{:S(2)}) %collective-permute-start.2) | collective-permute-done | bytes 655392 | tf_op jit(solution)/shard_map/ppermute | solution.py:371
  33.0 3.1 %collective-permute-start.4 = (bf16[2,256,640]{2,1,0:T(8,128)(2,1)S(1)}, bf16[2,256,640]{2,1,0:T(8,128)(2,1)S(1)}, u32[]{:S(2)}, u32[]{:S(2)}) collective-permute-start(bf16[2,256,640]{2,1,0:T(8,128)(2,1)S(1)} %collective-permute-done.2.refs_1_), channel_id=1, source_target_pairs={{0,4},{1,5},{2,6},{3,7},{4,8},{5,9},{6,10},{7,11},{8,12},{9,13},{1... | collective-permute-start | bytes 1966088 | tf_op jit(solution)/shard_map/ppermute | solution.py:371
  39.8 3.8 %collective-permute-done.4.refs_1_ = bf16[2,256,640]{2,1,0:T(8,128)(2,1)S(1)} collective-permute-done((bf16[2,256,640]{2,1,0:T(8,128)(2,1)S(1)}, bf16[2,256,640]{2,1,0:T(8,128)(2,1)S(1)}, u32[]{:S(2)}, u32[]{:S(2)}) %collective-permute-start.4) | collective-permute-done | bytes 655392 | tf_op jit(solution)/shard_map/ppermute | solution.py:371
  43.6 4.6 %collective-permute-start.6 = (bf16[2,256,640]{2,1,0:T(8,128)(2,1)S(1)}, bf16[2,256,640]{2,1,0:T(8,128)(2,1)S(1)}, u32[]{:S(2)}, u32[]{:S(2)}) collective-permute-start(bf16[2,256,640]{2,1,0:T(8,128)(2,1)S(1)} %collective-permute-done.4.refs_1_), channel_id=1, source_target_pairs={{0,32},{32,0},{64,96},{96,64},{128,160},{160,128},{192,224},{224,1... | collective-permute-start | bytes 1966088 | tf_op jit(solution)/shard_map/ppermute | solution.py:368
  48.2 2.8 %shard_map.88 = (bf16[4,16,256,128]{3,2,1,0:T(8,128)(2,1)S(1)}, s32[4,16,128]{2,1,0:T(8,128)S(1)}, s32[4,8,128]{2,1,0:T(8,128)S(1)}) custom-call(s32[1]{0:T(128)} %bitcast.6.refs_0_, bf16[2,256,640]{2,1,0:T(8,128)(2,1)S(1)} %collective-permute-done.2.refs_1_, bf16[2,256,640]{2,1,0:T(8,128)(2,1)S(1)} %collective-permute-done.3.refs_2_), custom_call_target="tpu_custom_call" | custom-call | flops 3600000000 | bytes 18000000 | tf_op jit(solution)/shard_map/pallas_call | solution.py:149
  51.1 2.8 %shard_map.89 = (bf16[4,16,256,128]{3,2,1,0:T(8,128)(2,1)S(1)}, s32[4,16,128]{2,1,0:T(8,128)S(1)}, s32[4,8,128]{2,1,0:T(8,128)S(1)}) custom-call(s32[1]{0:T(128)} %bitcast.6.refs_0_, bf16[2,256,640]{2,1,0:T(8,128)(2,1)S(1)} %collective-permute-done.4.refs_1_, bf16[2,256,640]{2,1,0:T(8,128)(2,1)S(1)} %collective-permute-done.5.refs_2_), custom_call_target="tpu_custom_call" | custom-call | flops 3600000000 | bytes 18000000 | tf_op jit(solution)/shard_map/pallas_call | solution.py:149
  53.9 3.4 %collective-permute-done.7.refs_1_ = bf16[1,256,640]{2,1,0:T(8,128)(2,1)S(1)} collective-permute-done((bf16[1,256,640]{2,1,0:T(8,128)(2,1)S(1)}, bf16[1,256,640]{2,1,0:T(8,128)(2,1)S(1)}, u32[]{:S(2)}, u32[]{:S(2)}) %collective-permute-start.7) | collective-permute-done | bytes 327712 | tf_op jit(solution)/shard_map/ppermute | solution.py:371
  62.7 2.8 %shard_map.94.refs_8_ = f32[1,512,256]{2,1,0:T(8,128)S(1)} custom-call(s32[5]{0:T(128)S(1)} %pad_add_fusion.2.refs_0_, s32[2,8,128]{2,1,0:T(8,128)S(1)} %get-tuple-element.25.refs_1_, s32[2,8,128]{2,1,0:T(8,128)S(1)} %get-tuple-element.26.refs_2_, s32[4,8,128]{2,1,0:T(8,128)S(1)} %get-tuple-element.27.refs_3_, s32[4,8,128]{2,1,0:T(8,128)S(1)} %get-tuple-element.28.refs_4_, ...), custom_call_target="tpu_custom_call" | custom-call | flops 1200000000 | bytes 6000000 | tf_op jit(solution)/shard_map/pallas_call | solution.py:210
  66.5 4.2 %shard_map.96 = f32[2,512,256]{2,1,0:T(8,128)S(1)} custom-call(s32[5]{0:T(128)S(1)} %pad_add_fusion.2.refs_0_, s32[2,8,128]{2,1,0:T(8,128)S(1)} %get-tuple-element.25.refs_1_, s32[2,8,128]{2,1,0:T(8,128)S(1)} %get-tuple-element.26.refs_2_, s32[4,8,128]{2,1,0:T(8,128)S(1)} %get-tuple-element.27.refs_3_, s32[4,8,128]{2,1,0:T(8,128)S(1)} %get-tuple-element.28.refs_4_, ...), custom_call_target="tpu_custom_call" | custom-call | flops 2400000000 | bytes 12000000 | tf_op jit(solution)/shard_map/pallas_call | solution.py:210
  76.4 2.9 %shard_map.93 = f32[1,512,256]{2,1,0:T(8,128)S(1)} custom-call(s32[5]{0:T(128)S(1)} %pad_add_fusion.2.refs_0_, s32[2,8,128]{2,1,0:T(8,128)S(1)} %get-tuple-element.25.refs_1_, s32[2,8,128]{2,1,0:T(8,128)S(1)} %get-tuple-element.26.refs_2_, s32[4,8,128]{2,1,0:T(8,128)S(1)} %get-tuple-element.27.refs_3_, s32[4,8,128]{2,1,0:T(8,128)S(1)} %get-tuple-element.28.refs_4_, ...), custom_call_target="tpu_custom_call" | custom-call | flops 1200000000 | bytes 6000000 | tf_op jit(solution)/shard_map/pallas_call | solution.py:210
  79.4 7.8 %collective-permute-done.12 = f32[512,256]{1,0:T(8,128)S(1)} collective-permute-done((f32[512,256]{1,0:T(8,128)S(1)}, f32[512,256]{1,0:T(8,128)S(1)}, u32[]{:S(2)}, u32[]{:S(2)}) %collective-permute-start.12) | collective-permute-done | bytes 524320 | tf_op jit(solution)/shard_map/ppermute | solution.py:403
  87.2 11.6 %collective-permute-done.13 = f32[512,256]{1,0:T(8,128)S(1)} collective-permute-done((f32[512,256]{1,0:T(8,128)S(1)}, f32[512,256]{1,0:T(8,128)S(1)}, u32[]{:S(2)}, u32[]{:S(2)}) %collective-permute-start.13) | collective-permute-done | bytes 524320 | tf_op jit(solution)/shard_map/ppermute | solution.py:403
  98.9 3.0 %collective-permute-start.15 = (f32[128,256]{1,0:T(8,128)S(1)}, f32[128,256]{1,0:T(8,128)S(1)}, u32[]{:S(2)}, u32[]{:S(2)}) collective-permute-start(f32[128,256]{1,0:T(8,128)S(1)} %get-tuple-element.50), channel_id=1, source_target_pairs={{0,128},{32,160},{64,192},{96,224},{128,0},{160,32},{192,64},{224,... | collective-permute-start | bytes 393224 | tf_op jit(solution)/shard_map/ppermute | solution.py:407
  101.9 3.6 %collective-permute-start.16 = (f32[128,256]{1,0:T(8,128)S(1)}, f32[128,256]{1,0:T(8,128)S(1)}, u32[]{:S(2)}, u32[]{:S(2)}) collective-permute-start(f32[128,256]{1,0:T(8,128)S(1)} %get-tuple-element.52), channel_id=1, source_target_pairs={{0,64},{32,96},{64,128},{96,160},{128,192},{160,224},{192,0},{224,... | collective-permute-start | bytes 393224 | tf_op jit(solution)/shard_map/ppermute | solution.py:407
  105.6 2.8 %collective-permute-done.16 = f32[128,256]{1,0:T(8,128)S(1)} collective-permute-done((f32[128,256]{1,0:T(8,128)S(1)}, f32[128,256]{1,0:T(8,128)S(1)}, u32[]{:S(2)}, u32[]{:S(2)}) %collective-permute-start.16) | collective-permute-done | bytes 131104 | tf_op jit(solution)/shard_map/ppermute | solution.py:407
  108.3 3.0 %collective-permute-done.17 = f32[128,256]{1,0:T(8,128)S(1)} collective-permute-done((f32[128,256]{1,0:T(8,128)S(1)}, f32[128,256]{1,0:T(8,128)S(1)}, u32[]{:S(2)}, u32[]{:S(2)}) %collective-permute-start.17) | collective-permute-done | bytes 131104 | tf_op jit(solution)/shard_map/ppermute | solution.py:407
  111.4 3.4 %collective-permute-start.19 = (f32[128,256]{1,0:T(8,128)S(1)}, f32[128,256]{1,0:T(8,128)S(1)}, u32[]{:S(2)}, u32[]{:S(2)}) collective-permute-start(f32[128,256]{1,0:T(8,128)S(1)} %fusion.3.refs_7_), channel_id=1, source_target_pairs={{0,192},{32,224},{64,0},{96,32},{128,64},{160,96},{192,128},{224,1... | collective-permute-start | bytes 393224 | tf_op jit(solution)/shard_map/ppermute | solution.py:408
  115.7 6.3 %listed_values.1.refs_3_ = f32[1056,384]{1,0:T(8,128)S(1)} custom-call(s32[8,128]{1,0:T(8,128)S(1)} %bitcast.39, s32[1024,128]{1,0:T(8,128)S(1)} %broadcast_in_dim.7.rows_ref.refs_4_, f32[32,128]{1,0:T(8,128)S(1)} %bitcast.41, f32[4096,256]{1,0:T(8,128)S(1)} %copy-done), custom_call_target="tpu_custom_call" | custom-call | flops 3600000000 | bytes 18000000 | tf_op jit(solution)/shard_map/listed_values/pallas_call | solution.py:240
  126.5 7.7 %update.1 = (f32[4096,256]{1,0:T(8,128)}, f32[32,128]{1,0:T(8,128)}) custom-call(s32[24]{0:T(128)S(1)} %pad_add_fusion.1.refs_0_, s32[1024]{0:T(1024)S(1)} %bitcast.37, f32[4096,256]{1,0:T(8,128)} %refs_2_.1, f32[1056,384]{1,0:T(8,128)} %copy-done.1, s32[1024,128]{1,0:T(8,128)S(1)} %broadcast_in_dim.7.rows_ref.refs_4_, ...), custom_call_target="tpu_custom_call" | custom-call | tf_op jit(solution)/shard_map/update/pallas_call | solution.py:311
  (70 shorter events, 24.4 us)
Async XLA Ops:
  3.3 6.0 %collective-permute-start = (bf16[256,640]{1,0:T(8,128)(2,1)S(1)}, bf16[256,640]{1,0:T(8,128)(2,1)S(1)}, u32[]{:S(2)}, u32[]{:S(2)}) collective-permute-start(bf16[256,640]{1,0:T(8,128)(2,1)S(1)} %pack.1), channel_id=1, source_target_pairs={{0,32},{32,0},{64,96},{96,64},{128,160},{160,128},{192,224},{224,1... | collective-permute-start | bytes 983048 | tf_op jit(solution)/shard_map/ppermute | solution.py:368
  6.6 18.9 %collective-permute-start.11 = (s32[1024]{0:T(1024)S(1)}, s32[1024]{0:T(1024)S(1)}, u32[]{:S(2)}, u32[]{:S(2)}) collective-permute-start(s32[1024]{0:T(1024)S(1)} %bitcast.32), channel_id=1, source_target_pairs={{0,1},{1,2},{2,3},{3,0},{4,5},{5,6},{6,7},{7,4},{8,9},{9,10},{10,1... | collective-permute-start | bytes 12296 | tf_op jit(solution)/shard_map/ppermute | solution.py:355
  6.6 18.9 %collective-permute-start.10 = (s32[1024]{0:T(1024)S(1)}, s32[1024]{0:T(1024)S(1)}, u32[]{:S(2)}, u32[]{:S(2)}) collective-permute-start(s32[1024]{0:T(1024)S(1)} %bitcast.33), channel_id=1, source_target_pairs={{0,3},{1,0},{2,1},{3,2},{4,7},{5,4},{6,5},{7,6},{8,11},{9,8},{10,9... | collective-permute-start | bytes 12296 | tf_op jit(solution)/shard_map/ppermute | solution.py:355
  9.3 16.3 %collective-permute-start.9 = (s32[1024]{0:T(1024)S(1)}, s32[1024]{0:T(1024)S(1)}, u32[]{:S(2)}, u32[]{:S(2)}) collective-permute-start(s32[1024]{0:T(1024)S(1)} %bitcast.34), channel_id=1, source_target_pairs={{0,2},{1,3},{2,0},{3,1},{4,6},{5,7},{6,4},{7,5},{8,10},{9,11},{10,... | collective-permute-start | bytes 12296 | tf_op jit(solution)/shard_map/ppermute | solution.py:355
  9.3 13.0 %collective-permute-start.1 = (bf16[2,256,640]{2,1,0:T(8,128)(2,1)S(1)}, bf16[2,256,640]{2,1,0:T(8,128)(2,1)S(1)}, u32[]{:S(2)}, u32[]{:S(2)}) collective-permute-start(bf16[2,256,640]{2,1,0:T(8,128)(2,1)S(1)} %pad_maximum_fusion.refs_1_), channel_id=1, source_target_pairs={{0,4},{1,5},{2,6},{3,7},{4,8},{5,9},{6,10},{7,11},{8,12},{9,13},{1... | collective-permute-start | bytes 1966088 | tf_op jit(solution)/shard_map/ppermute | solution.py:371
  22.4 10.6 %collective-permute-start.2 = (bf16[2,256,640]{2,1,0:T(8,128)(2,1)S(1)}, bf16[2,256,640]{2,1,0:T(8,128)(2,1)S(1)}, u32[]{:S(2)}, u32[]{:S(2)}) collective-permute-start(bf16[2,256,640]{2,1,0:T(8,128)(2,1)S(1)} %collective-permute-done.1.refs_1_), channel_id=1, source_target_pairs={{0,4},{1,5},{2,6},{3,7},{4,8},{5,9},{6,10},{7,11},{8,12},{9,13},{1... | collective-permute-start | bytes 1966088 | tf_op jit(solution)/shard_map/ppermute | solution.py:371
  25.5 22.7 %collective-permute-start.3 = (bf16[2,256,640]{2,1,0:T(8,128)(2,1)S(1)}, bf16[2,256,640]{2,1,0:T(8,128)(2,1)S(1)}, u32[]{:S(2)}, u32[]{:S(2)}) collective-permute-start(bf16[2,256,640]{2,1,0:T(8,128)(2,1)S(1)} %collective-permute-done.1.refs_1_), channel_id=1, source_target_pairs={{0,32},{32,0},{64,96},{96,64},{128,160},{160,128},{192,224},{224,1... | collective-permute-start | bytes 1966088 | tf_op jit(solution)/shard_map/ppermute | solution.py:368
  33.0 10.6 %collective-permute-start.4 = (bf16[2,256,640]{2,1,0:T(8,128)(2,1)S(1)}, bf16[2,256,640]{2,1,0:T(8,128)(2,1)S(1)}, u32[]{:S(2)}, u32[]{:S(2)}) collective-permute-start(bf16[2,256,640]{2,1,0:T(8,128)(2,1)S(1)} %collective-permute-done.2.refs_1_), channel_id=1, source_target_pairs={{0,4},{1,5},{2,6},{3,7},{4,8},{5,9},{6,10},{7,11},{8,12},{9,13},{1... | collective-permute-start | bytes 1966088 | tf_op jit(solution)/shard_map/ppermute | solution.py:371
  36.2 14.9 %collective-permute-start.5 = (bf16[2,256,640]{2,1,0:T(8,128)(2,1)S(1)}, bf16[2,256,640]{2,1,0:T(8,128)(2,1)S(1)}, u32[]{:S(2)}, u32[]{:S(2)}) collective-permute-start(bf16[2,256,640]{2,1,0:T(8,128)(2,1)S(1)} %collective-permute-done.2.refs_1_), channel_id=1, source_target_pairs={{0,32},{32,0},{64,96},{96,64},{128,160},{160,128},{192,224},{224,1... | collective-permute-start | bytes 1966088 | tf_op jit(solution)/shard_map/ppermute | solution.py:368
  43.6 16.8 %collective-permute-start.6 = (bf16[2,256,640]{2,1,0:T(8,128)(2,1)S(1)}, bf16[2,256,640]{2,1,0:T(8,128)(2,1)S(1)}, u32[]{:S(2)}, u32[]{:S(2)}) collective-permute-start(bf16[2,256,640]{2,1,0:T(8,128)(2,1)S(1)} %collective-permute-done.4.refs_1_), channel_id=1, source_target_pairs={{0,32},{32,0},{64,96},{96,64},{128,160},{160,128},{192,224},{224,1... | collective-permute-start | bytes 1966088 | tf_op jit(solution)/shard_map/ppermute | solution.py:368
  51.0 6.3 %collective-permute-start.7 = (bf16[1,256,640]{2,1,0:T(8,128)(2,1)S(1)}, bf16[1,256,640]{2,1,0:T(8,128)(2,1)S(1)}, u32[]{:S(2)}, u32[]{:S(2)}) collective-permute-start(bf16[1,256,640]{2,1,0:T(8,128)(2,1)S(1)} %slice.48), channel_id=1, source_target_pairs={{0,4},{1,5},{2,6},{3,7},{4,8},{5,9},{6,10},{7,11},{8,12},{9,13},{1... | collective-permute-start | bytes 983048 | tf_op jit(solution)/shard_map/ppermute | solution.py:371
  57.3 8.1 %collective-permute-start.8 = (bf16[1,256,640]{2,1,0:T(8,128)(2,1)S(1)}, bf16[1,256,640]{2,1,0:T(8,128)(2,1)S(1)}, u32[]{:S(2)}, u32[]{:S(2)}) collective-permute-start(bf16[1,256,640]{2,1,0:T(8,128)(2,1)S(1)} %collective-permute-done.7.refs_1_), channel_id=1, source_target_pairs={{0,32},{32,0},{64,96},{96,64},{128,160},{160,128},{192,224},{224,1... | collective-permute-start | bytes 983048 | tf_op jit(solution)/shard_map/ppermute | solution.py:368
  72.1 15.1 %collective-permute-start.12 = (f32[512,256]{1,0:T(8,128)S(1)}, f32[512,256]{1,0:T(8,128)S(1)}, u32[]{:S(2)}, u32[]{:S(2)}) collective-permute-start(f32[512,256]{1,0:T(8,128)S(1)} %bitcast.40), channel_id=1, source_target_pairs={{0,2},{1,3},{2,0},{3,1},{4,6},{5,7},{6,4},{7,5},{8,10},{9,11},{10,... | collective-permute-start | bytes 1572872 | tf_op jit(solution)/shard_map/ppermute | solution.py:403
  73.7 25.1 %collective-permute-start.13 = (f32[512,256]{1,0:T(8,128)S(1)}, f32[512,256]{1,0:T(8,128)S(1)}, u32[]{:S(2)}, u32[]{:S(2)}) collective-permute-start(f32[512,256]{1,0:T(8,128)S(1)} %get-tuple-element.48), channel_id=1, source_target_pairs={{0,1},{1,2},{2,3},{3,0},{4,5},{5,6},{6,7},{7,4},{8,9},{9,10},{10,1... | collective-permute-start | bytes 1572872 | tf_op jit(solution)/shard_map/ppermute | solution.py:403
  73.8 25.0 %collective-permute-start.14 = (f32[512,256]{1,0:T(8,128)S(1)}, f32[512,256]{1,0:T(8,128)S(1)}, u32[]{:S(2)}, u32[]{:S(2)}) collective-permute-start(f32[512,256]{1,0:T(8,128)S(1)} %get-tuple-element.49), channel_id=1, source_target_pairs={{0,3},{1,0},{2,1},{3,2},{4,7},{5,4},{6,5},{7,6},{8,11},{9,8},{10,9... | collective-permute-start | bytes 1572872 | tf_op jit(solution)/shard_map/ppermute | solution.py:403
  79.3 36.4 %copy-start = (f32[4096,256]{1,0:T(8,128)S(1)}, f32[4096,256]{1,0:T(8,128)}, u32[]{:S(2)}) copy-start(f32[4096,256]{1,0:T(8,128)} %refs_2_.1) | copy-start | bytes 12582916
  98.9 6.6 %collective-permute-start.15 = (f32[128,256]{1,0:T(8,128)S(1)}, f32[128,256]{1,0:T(8,128)S(1)}, u32[]{:S(2)}, u32[]{:S(2)}) collective-permute-start(f32[128,256]{1,0:T(8,128)S(1)} %get-tuple-element.50), channel_id=1, source_target_pairs={{0,128},{32,160},{64,192},{96,224},{128,0},{160,32},{192,64},{224,... | collective-permute-start | bytes 393224 | tf_op jit(solution)/shard_map/ppermute | solution.py:407
  101.9 6.4 %collective-permute-start.16 = (f32[128,256]{1,0:T(8,128)S(1)}, f32[128,256]{1,0:T(8,128)S(1)}, u32[]{:S(2)}, u32[]{:S(2)}) collective-permute-start(f32[128,256]{1,0:T(8,128)S(1)} %get-tuple-element.52), channel_id=1, source_target_pairs={{0,64},{32,96},{64,128},{96,160},{128,192},{160,224},{192,0},{224,... | collective-permute-start | bytes 393224 | tf_op jit(solution)/shard_map/ppermute | solution.py:407
  105.6 5.8 %collective-permute-start.17 = (f32[128,256]{1,0:T(8,128)S(1)}, f32[128,256]{1,0:T(8,128)S(1)}, u32[]{:S(2)}, u32[]{:S(2)}) collective-permute-start(f32[128,256]{1,0:T(8,128)S(1)} %get-tuple-element.51), channel_id=1, source_target_pairs={{0,192},{32,224},{64,0},{96,32},{128,64},{160,96},{192,128},{224,1... | collective-permute-start | bytes 393224 | tf_op jit(solution)/shard_map/ppermute | solution.py:407
  111.4 11.9 %collective-permute-start.19 = (f32[128,256]{1,0:T(8,128)S(1)}, f32[128,256]{1,0:T(8,128)S(1)}, u32[]{:S(2)}, u32[]{:S(2)}) collective-permute-start(f32[128,256]{1,0:T(8,128)S(1)} %fusion.3.refs_7_), channel_id=1, source_target_pairs={{0,192},{32,224},{64,0},{96,32},{128,64},{160,96},{192,128},{224,1... | collective-permute-start | bytes 393224 | tf_op jit(solution)/shard_map/ppermute | solution.py:408
  114.8 8.4 %collective-permute-start.20 = (f32[128,256]{1,0:T(8,128)S(1)}, f32[128,256]{1,0:T(8,128)S(1)}, u32[]{:S(2)}, u32[]{:S(2)}) collective-permute-start(f32[128,256]{1,0:T(8,128)S(1)} %fusion.3.refs_7_), channel_id=1, source_target_pairs={{0,128},{32,160},{64,192},{96,224},{128,0},{160,32},{192,64},{224,... | collective-permute-start | bytes 393224 | tf_op jit(solution)/shard_map/ppermute | solution.py:408
  114.8 9.1 %collective-permute-start.21 = (f32[128,256]{1,0:T(8,128)S(1)}, f32[128,256]{1,0:T(8,128)S(1)}, u32[]{:S(2)}, u32[]{:S(2)}) collective-permute-start(f32[128,256]{1,0:T(8,128)S(1)} %fusion.3.refs_7_), channel_id=1, source_target_pairs={{0,64},{32,96},{64,128},{96,160},{128,192},{160,224},{192,0},{224,... | collective-permute-start | bytes 393224 | tf_op jit(solution)/shard_map/ppermute | solution.py:408
  124.0 2.5 %collective-permute-start.22 = (f32[384,256]{1,0:T(8,128)S(1)}, f32[384,256]{1,0:T(8,128)S(1)}, u32[]{:S(2)}, u32[]{:S(2)}) collective-permute-start(f32[384,256]{1,0:T(8,128)S(1)} %pad_maximum_fusion.1), channel_id=1, source_target_pairs={{0,32},{32,0},{64,96},{96,64},{128,160},{160,128},{192,224},{224,1... | collective-permute-start | bytes 1179656 | tf_op jit(solution)/shard_map/ppermute | solution.py:368
  125.1 1.4 %collective-permute-start.18 = (f32[128,256]{1,0:T(8,128)S(1)}, f32[128,256]{1,0:T(8,128)S(1)}, u32[]{:S(2)}, u32[]{:S(2)}) collective-permute-start(f32[128,256]{1,0:T(8,128)S(1)} %fusion.3.refs_7_), channel_id=1, source_target_pairs={{0,32},{32,0},{64,96},{96,64},{128,160},{160,128},{192,224},{224,1... | collective-permute-start | bytes 393224 | tf_op jit(solution)/shard_map/ppermute | solution.py:368
  (4 other events, 57.7 us)

commit v10 on v8

--- a/solution.py
+++ b/solution.py
@@ -291,16 +291,18 @@
 
     def tile(b, _):
         first, last = plan_ref[b], plan_ref[b + 1]
-        whole = (last - first) >> 3
+        low, high = (first + 7) >> 3, last >> 3
 
         def step(i, _):
+            block = u_ref[pl.ds(pl.multiple_of(i * 8, 8), 8), :]
             for j in range(8):
-                put(first + i * 8 + j)
+                new_ref[pl.ds(list_ref[i * 8 + j], 1), :] = block[j:j + 1, :]
             return 0
 
         load(b).wait()
-        lax.fori_loop(0, whole, step, 0)
-        lax.fori_loop(first + whole * 8, last, lambda n, _: (put(n), 0)[1], 0)
+        lax.fori_loop(first, jnp.minimum(low * 8, last), lambda n, _: (put(n), 0)[1], 0)
+        lax.fori_loop(low, high, step, 0)
+        lax.fori_loop(jnp.maximum(high, low) * 8, last, lambda n, _: (put(n), 0)[1], 0)
         store(b).start()
         return 0
 
@@ -356,9 +358,10 @@
         return lax.dynamic_slice(doubled, (0, y, 0), (NC, NY, QUART)).reshape(TOUCH)
 
     own_list = touched.reshape(TOUCH)
-    lists = {0: ordered(own_list)}
-    for k in range(1, NX):
-        lists[k] = ordered(lax.ppermute(own_list, "shard", x_pairs(-k)))
+    next_list = lax.ppermute(own_list, "shard", x_pairs(-1))
+    far_lists = lax.ppermute(jnp.stack([own_list, next_list]), "shard", x_pairs(-2))
+    lists = {0: ordered(own_list), 1: ordered(next_list),
+             2: ordered(far_lists[0]), 3: ordered(far_lists[1])}
     stacked = jnp.stack([lists[k][HALF:] for k in ORDER])[:, :, None]
     rows = jnp.broadcast_to(stacked, (NX, HALF, LANES))
     all_rows = jnp.broadcast_to(lists[0][:, None], (TOUCH, LANES))

time: 134 us -> 131 us (0.978)
    ppermute x4, waiting for transfers between devices: 18.3 us -> 15.2 us  [body(): up = lax.ppermute(up, 'shard', z_pairs(1))]
    ppermute x3 -> x2, waiting for transfers between devices: 0.01 us -> 2.25 us  [the longest x1 2.24 us: body(): lax.ppermute(jnp.stack([own_list, next_list]), 'shard', x_pairs(-2))]
    ppermute x8, starting transfers between devices: 7.28 us -> 5.88 us  [swap(): return [lax.ppermute(p, 'grp', C_PAIRS) for p in packets]]
    ppermute x3 -> x2, starting transfers between devices: 5.1 us -> 4.32 us  [the longest x1 2.48 us: body(): next_list = lax.ppermute(own_list, 'shard', x_pairs(-1))]
  transfers between devices with their start and end apart: 31 -> 30, of which waited for: 7 -> 8; matrix products, arithmetic and copies ran while one was open for 1% -> 1% of each run, Pallas kernels for 20% -> 18%
where the time goes in v10:
time: 131 us
  starting transfers between devices  45.5 us (35%)
  waiting for transfers between devices  42 us (32%)
  Pallas kernels  39.6 us (30%)
  local copies, waits for them, and re-layouts  1.82 us (1%)
    ppermute x3, waiting for transfers between devices, body(): both[k] = lax.ppermute(both[k], 'shard', x_pairs(k))  19.1 us
    ppermute x4, waiting for transfers between devices, body(): up = lax.ppermute(up, 'shard', z_pairs(1))  15.2 us
    pallas_call x7, Pallas kernels, gather(): pl.pallas_call(lambda *refs: gather_kernel(*refs, count=count, split=spli...  12.7 us
    pallas_call x4, Pallas kernels, sums(): pl.pallas_call(lambda *refs: sums_kernel(*refs, counts=counts, base=base,...  11.2 us
    ppermute x3, starting transfers between devices, body(): down = lax.ppermute(down, 'shard', z_pairs(-1))  10.3 us
    ppermute x4, starting transfers between devices, body(): other = [lax.ppermute(m, 'grp', C_PAIRS) for m in mine]  8.72 us
    pallas_call x1, Pallas kernels, update(): pl.pallas_call(update_kernel, out_shape=(jax.ShapeDtypeStruct((ROWS_DEV,...  6.87 us
    pallas_call x1, Pallas kernels, listed_values(): pl.pallas_call(listed_kernel, out_shape=jax.ShapeDtypeStruct((TOUCH + 32,...  6.32 us
  transfers between devices with their start and end apart: 30, of which 8 were waited for; matrix products, arithmetic and copies ran while one was open for 1% of the time, Pallas kernels for 18%

profile of v10, /device:TPU:1, one launch (start us, length us, event | category | flops | bytes accessed | tf_op | source)
XLA Modules:
  0.0 130.7 jit_solution(1896555244648750945)
XLA Ops:
  0.6 2.6 %pack.1.refs_1_ = bf16[256,640]{1,0:T(8,128)(2,1)S(1)} custom-call(s32[32,128]{1,0:T(8,128)} %bitcast.47, s32[32,128]{1,0:T(8,128)} %bitcast.48, bf16[512,256]{1,0:T(8,128)(2,1)} %bitcast.46), custom_call_target="tpu_custom_call" | custom-call | flops 2400000000 | bytes 12000000 | tf_op jit(solution)/shard_map/pack/pallas_call | solution.py:98
  3.3 2.5 %collective-permute-start = (bf16[256,640]{1,0:T(8,128)(2,1)S(1)}, bf16[256,640]{1,0:T(8,128)(2,1)S(1)}, u32[]{:S(2)}, u32[]{:S(2)}) collective-permute-start(bf16[256,640]{1,0:T(8,128)(2,1)S(1)} %pack.1.refs_1_), channel_id=1, source_target_pairs={{0,4},{1,5},{2,6},{3,7},{4,8},{5,9},{6,10},{7,11},{8,12},{9,13},{1... | collective-permute-start | bytes 983048 | tf_op jit(solution)/shard_map/ppermute | solution.py:386
  5.8 4.0 %collective-permute-start.1 = (bf16[256,640]{1,0:T(8,128)(2,1)S(1)}, bf16[256,640]{1,0:T(8,128)(2,1)S(1)}, u32[]{:S(2)}, u32[]{:S(2)}) collective-permute-start(bf16[256,640]{1,0:T(8,128)(2,1)S(1)} %pack.1.refs_1_), channel_id=1, source_target_pairs={{0,28},{1,29},{2,30},{3,31},{4,0},{5,1},{6,2},{7,3},{8,4},{9,5},{1... | collective-permute-start | bytes 983048 | tf_op jit(solution)/shard_map/ppermute | solution.py:387
  10.8 2.5 %collective-permute-start.15 = (s32[1024]{0:T(1024)S(1)}, s32[1024]{0:T(1024)S(1)}, u32[]{:S(2)}, u32[]{:S(2)}) collective-permute-start(s32[1024]{0:T(1024)S(1)} %bitcast.30), channel_id=1, source_target_pairs={{0,3},{1,0},{2,1},{3,2},{4,7},{5,4},{6,5},{7,6},{8,11},{9,8},{10,9... | collective-permute-start | bytes 12296 | tf_op jit(solution)/shard_map/ppermute | solution.py:361
  16.4 2.2 %collective-permute-done.16 = s32[2,1024]{1,0:T(2,128)S(1)} collective-permute-done((s32[2,1024]{1,0:T(2,128)S(1)}, s32[2,1024]{1,0:T(2,128)S(1)}, u32[]{:S(2)}, u32[]{:S(2)}) %collective-permute-start.16) | collective-permute-done | bytes 8224 | tf_op jit(solution)/shard_map/ppermute | solution.py:362
  20.4 2.9 %collective-permute-start.4 = (bf16[256,640]{1,0:T(8,128)(2,1)S(1)}, bf16[256,640]{1,0:T(8,128)(2,1)S(1)}, u32[]{:S(2)}, u32[]{:S(2)}) collective-permute-start(bf16[256,640]{1,0:T(8,128)(2,1)S(1)} %collective-permute-done.1.refs_2_), channel_id=1, source_target_pairs={{0,28},{1,29},{2,30},{3,31},{4,0},{5,1},{6,2},{7,3},{8,4},{9,5},{1... | collective-permute-start | bytes 983048 | tf_op jit(solution)/shard_map/ppermute | solution.py:387
  25.8 4.5 %collective-permute-done.4.refs_2_ = bf16[256,640]{1,0:T(8,128)(2,1)S(1)} collective-permute-done((bf16[256,640]{1,0:T(8,128)(2,1)S(1)}, bf16[256,640]{1,0:T(8,128)(2,1)S(1)}, u32[]{:S(2)}, u32[]{:S(2)}) %collective-permute-start.4) | collective-permute-done | bytes 327712 | tf_op jit(solution)/shard_map/ppermute | solution.py:387
  30.4 3.4 %collective-permute-start.8 = (bf16[256,640]{1,0:T(8,128)(2,1)S(1)}, bf16[256,640]{1,0:T(8,128)(2,1)S(1)}, u32[]{:S(2)}, u32[]{:S(2)}) collective-permute-start(bf16[256,640]{1,0:T(8,128)(2,1)S(1)} %collective-permute-done.4.refs_2_), channel_id=1, source_target_pairs={{0,28},{1,29},{2,30},{3,31},{4,0},{5,1},{6,2},{7,3},{8,4},{9,5},{1... | collective-permute-start | bytes 983048 | tf_op jit(solution)/shard_map/ppermute | solution.py:387
  35.0 2.8 %shard_map.88 = (bf16[4,16,256,128]{3,2,1,0:T(8,128)(2,1)S(1)}, s32[4,16,128]{2,1,0:T(8,128)S(1)}, s32[4,8,128]{2,1,0:T(8,128)S(1)}) custom-call(s32[1]{0:T(128)} %bitcast.6.refs_0_, bf16[256,640]{1,0:T(8,128)(2,1)S(1)} %collective-permute-done.3.refs_1_, bf16[256,640]{1,0:T(8,128)(2,1)S(1)} %collective-permute-done.4.refs_2_, ...), custom_call_target="tpu_custom_call" | custom-call | flops 3600000000 | bytes 18000000 | tf_op jit(solution)/shard_map/pallas_call | solution.py:154
  37.8 7.6 %collective-permute-done.7.refs_1_ = bf16[256,640]{1,0:T(8,128)(2,1)S(1)} collective-permute-done((bf16[256,640]{1,0:T(8,128)(2,1)S(1)}, bf16[256,640]{1,0:T(8,128)(2,1)S(1)}, u32[]{:S(2)}, u32[]{:S(2)}) %collective-permute-start.7) | collective-permute-done | bytes 327712 | tf_op jit(solution)/shard_map/ppermute | solution.py:386
  46.4 2.8 %shard_map.89 = (bf16[4,16,256,128]{3,2,1,0:T(8,128)(2,1)S(1)}, s32[4,16,128]{2,1,0:T(8,128)S(1)}, s32[4,8,128]{2,1,0:T(8,128)S(1)}) custom-call(s32[1]{0:T(128)} %bitcast.6.refs_0_, bf16[256,640]{1,0:T(8,128)(2,1)S(1)} %collective-permute-done.7.refs_1_, bf16[256,640]{1,0:T(8,128)(2,1)S(1)} %collective-permute-done.8.refs_2_, ...), custom_call_target="tpu_custom_call" | custom-call | flops 3600000000 | bytes 18000000 | tf_op jit(solution)/shard_map/pallas_call | solution.py:154
  49.1 7.6 %collective-permute-done.13.refs_1_ = bf16[256,640]{1,0:T(8,128)(2,1)S(1)} collective-permute-done((bf16[256,640]{1,0:T(8,128)(2,1)S(1)}, bf16[256,640]{1,0:T(8,128)(2,1)S(1)}, u32[]{:S(2)}, u32[]{:S(2)}) %collective-permute-start.13) | collective-permute-done | bytes 327712 | tf_op jit(solution)/shard_map/ppermute | solution.py:390
  59.6 2.8 %shard_map.94.refs_8_ = f32[1,512,256]{2,1,0:T(8,128)S(1)} custom-call(s32[5]{0:T(128)S(1)} %pad_add_fusion.3.refs_0_, s32[1,8,128]{2,1,0:T(8,128)S(1)} %get-tuple-element.25.refs_1_, s32[3,8,128]{2,1,0:T(8,128)S(1)} %get-tuple-element.26.refs_2_, s32[4,8,128]{2,1,0:T(8,128)S(1)} %get-tuple-element.27.refs_3_, s32[4,8,128]{2,1,0:T(8,128)S(1)} %get-tuple-element.28.refs_4_, ...), custom_call_target="tpu_custom_call" | custom-call | flops 1200000000 | bytes 6000000 | tf_op jit(solution)/shard_map/pallas_call | solution.py:215
  64.6 4.2 %shard_map.96 = f32[2,512,256]{2,1,0:T(8,128)S(1)} custom-call(s32[5]{0:T(128)S(1)} %pad_add_fusion.3.refs_0_, s32[1,8,128]{2,1,0:T(8,128)S(1)} %get-tuple-element.25.refs_1_, s32[3,8,128]{2,1,0:T(8,128)S(1)} %get-tuple-element.26.refs_2_, s32[4,8,128]{2,1,0:T(8,128)S(1)} %get-tuple-element.27.refs_3_, s32[4,8,128]{2,1,0:T(8,128)S(1)} %get-tuple-element.28.refs_4_, ...), custom_call_target="tpu_custom_call" | custom-call | flops 2400000000 | bytes 12000000 | tf_op jit(solution)/shard_map/pallas_call | solution.py:215
  70.1 2.4 %collective-permute-start.17 = (f32[512,256]{1,0:T(8,128)S(1)}, f32[512,256]{1,0:T(8,128)S(1)}, u32[]{:S(2)}, u32[]{:S(2)}) collective-permute-start(f32[512,256]{1,0:T(8,128)S(1)} %bitcast.36), channel_id=1, source_target_pairs={{0,2},{1,3},{2,0},{3,1},{4,6},{5,7},{6,4},{7,5},{8,10},{9,11},{10,... | collective-permute-start | bytes 1572872 | tf_op jit(solution)/shard_map/ppermute | solution.py:405
  75.3 2.9 %shard_map.93 = f32[1,512,256]{2,1,0:T(8,128)S(1)} custom-call(s32[5]{0:T(128)S(1)} %pad_add_fusion.3.refs_0_, s32[1,8,128]{2,1,0:T(8,128)S(1)} %get-tuple-element.25.refs_1_, s32[3,8,128]{2,1,0:T(8,128)S(1)} %get-tuple-element.26.refs_2_, s32[4,8,128]{2,1,0:T(8,128)S(1)} %get-tuple-element.27.refs_3_, s32[4,8,128]{2,1,0:T(8,128)S(1)} %get-tuple-element.28.refs_4_, ...), custom_call_target="tpu_custom_call" | custom-call | flops 1200000000 | bytes 6000000 | tf_op jit(solution)/shard_map/pallas_call | solution.py:215
  78.2 7.0 %collective-permute-done.17 = f32[512,256]{1,0:T(8,128)S(1)} collective-permute-done((f32[512,256]{1,0:T(8,128)S(1)}, f32[512,256]{1,0:T(8,128)S(1)}, u32[]{:S(2)}, u32[]{:S(2)}) %collective-permute-start.17) | collective-permute-done | bytes 524320 | tf_op jit(solution)/shard_map/ppermute | solution.py:405
  85.2 11.6 %collective-permute-done.18 = f32[512,256]{1,0:T(8,128)S(1)} collective-permute-done((f32[512,256]{1,0:T(8,128)S(1)}, f32[512,256]{1,0:T(8,128)S(1)}, u32[]{:S(2)}, u32[]{:S(2)}) %collective-permute-start.18) | collective-permute-done | bytes 524320 | tf_op jit(solution)/shard_map/ppermute | solution.py:405
  97.4 3.0 %collective-permute-start.20 = (f32[128,256]{1,0:T(8,128)S(1)}, f32[128,256]{1,0:T(8,128)S(1)}, u32[]{:S(2)}, u32[]{:S(2)}) collective-permute-start(f32[128,256]{1,0:T(8,128)S(1)} %get-tuple-element.50), channel_id=1, source_target_pairs={{0,128},{32,160},{64,192},{96,224},{128,0},{160,32},{192,64},{224,... | collective-permute-start | bytes 393224 | tf_op jit(solution)/shard_map/ppermute | solution.py:409
  103.3 6.3 %listed_values.1.refs_3_ = f32[1056,384]{1,0:T(8,128)S(1)} custom-call(s32[8,128]{1,0:T(8,128)S(1)} %bitcast.35, s32[1024,128]{1,0:T(8,128)S(1)} %broadcast_in_dim.7.rows_ref.refs_4_, f32[32,128]{1,0:T(8,128)S(1)} %bitcast.37, f32[4096,256]{1,0:T(8,128)S(1)} %copy-done), custom_call_target="tpu_custom_call" | custom-call | flops 3600000000 | bytes 18000000 | tf_op jit(solution)/shard_map/listed_values/pallas_call | solution.py:245
  111.5 2.3 %collective-permute-start.26 = (f32[128,256]{1,0:T(8,128)S(1)}, f32[128,256]{1,0:T(8,128)S(1)}, u32[]{:S(2)}, u32[]{:S(2)}) collective-permute-start(f32[128,256]{1,0:T(8,128)S(1)} %fusion.3.refs_9_), channel_id=1, source_target_pairs={{0,128},{32,160},{64,192},{96,224},{128,0},{160,32},{192,64},{224,... | collective-permute-start | bytes 393224 | tf_op jit(solution)/shard_map/ppermute | solution.py:410
  114.0 2.8 %collective-permute-start.23 = (f32[128,256]{1,0:T(8,128)S(1)}, f32[128,256]{1,0:T(8,128)S(1)}, u32[]{:S(2)}, u32[]{:S(2)}) collective-permute-start(f32[128,256]{1,0:T(8,128)S(1)} %fusion.3.refs_9_), channel_id=1, source_target_pairs={{0,32},{32,0},{64,96},{96,64},{128,160},{160,128},{192,224},{224,1... | collective-permute-start | bytes 393224 | tf_op jit(solution)/shard_map/ppermute | solution.py:411
  118.5 2.3 %collective-permute-start.27 = (f32[128,256]{1,0:T(8,128)S(1)}, f32[128,256]{1,0:T(8,128)S(1)}, u32[]{:S(2)}, u32[]{:S(2)}) collective-permute-start(f32[128,256]{1,0:T(8,128)S(1)} %collective-permute-done.26.refs_11_), channel_id=1, source_target_pairs={{0,32},{32,0},{64,96},{96,64},{128,160},{160,128},{192,224},{224,1... | collective-permute-start | bytes 393224 | tf_op jit(solution)/shard_map/ppermute | solution.py:411
  123.7 6.9 %update.1 = (f32[4096,256]{1,0:T(8,128)}, f32[32,128]{1,0:T(8,128)}) custom-call(s32[24]{0:T(128)S(1)} %pad_add_fusion.2.refs_0_, s32[1024]{0:T(1024)S(1)} %bitcast.33, f32[4096,256]{1,0:T(8,128)} %refs_2_.1, f32[1056,384]{1,0:T(8,128)} %copy-done.1, s32[1024,128]{1,0:T(8,128)S(1)} %broadcast_in_dim.7.rows_ref.refs_4_, ...), custom_call_target="tpu_custom_call" | custom-call | tf_op jit(solution)/shard_map/update/pallas_call | solution.py:318
  (83 shorter events, 29.8 us)
Async XLA Ops:
  3.3 15.5 %collective-permute-start = (bf16[256,640]{1,0:T(8,128)(2,1)S(1)}, bf16[256,640]{1,0:T(8,128)(2,1)S(1)}, u32[]{:S(2)}, u32[]{:S(2)}) collective-permute-start(bf16[256,640]{1,0:T(8,128)(2,1)S(1)} %pack.1.refs_1_), channel_id=1, source_target_pairs={{0,4},{1,5},{2,6},{3,7},{4,8},{5,9},{6,10},{7,11},{8,12},{9,13},{1... | collective-permute-start | bytes 983048 | tf_op jit(solution)/shard_map/ppermute | solution.py:386
  5.8 14.6 %collective-permute-start.1 = (bf16[256,640]{1,0:T(8,128)(2,1)S(1)}, bf16[256,640]{1,0:T(8,128)(2,1)S(1)}, u32[]{:S(2)}, u32[]{:S(2)}) collective-permute-start(bf16[256,640]{1,0:T(8,128)(2,1)S(1)} %pack.1.refs_1_), channel_id=1, source_target_pairs={{0,28},{1,29},{2,30},{3,31},{4,0},{5,1},{6,2},{7,3},{8,4},{9,5},{1... | collective-permute-start | bytes 983048 | tf_op jit(solution)/shard_map/ppermute | solution.py:387
  9.9 13.8 %collective-permute-start.2 = (bf16[256,640]{1,0:T(8,128)(2,1)S(1)}, bf16[256,640]{1,0:T(8,128)(2,1)S(1)}, u32[]{:S(2)}, u32[]{:S(2)}) collective-permute-start(bf16[256,640]{1,0:T(8,128)(2,1)S(1)} %pack.1.refs_1_), channel_id=1, source_target_pairs={{0,32},{32,0},{64,96},{96,64},{128,160},{160,128},{192,224},{224,1... | collective-permute-start | bytes 983048 | tf_op jit(solution)/shard_map/ppermute | solution.py:377
  18.8 16.2 %collective-permute-start.3 = (bf16[256,640]{1,0:T(8,128)(2,1)S(1)}, bf16[256,640]{1,0:T(8,128)(2,1)S(1)}, u32[]{:S(2)}, u32[]{:S(2)}) collective-permute-start(bf16[256,640]{1,0:T(8,128)(2,1)S(1)} %collective-permute-done.refs_1_), channel_id=1, source_target_pairs={{0,4},{1,5},{2,6},{3,7},{4,8},{5,9},{6,10},{7,11},{8,12},{9,13},{1... | collective-permute-start | bytes 983048 | tf_op jit(solution)/shard_map/ppermute | solution.py:386
  18.9 16.1 %collective-permute-start.5 = (bf16[256,640]{1,0:T(8,128)(2,1)S(1)}, bf16[256,640]{1,0:T(8,128)(2,1)S(1)}, u32[]{:S(2)}, u32[]{:S(2)}) collective-permute-start(bf16[256,640]{1,0:T(8,128)(2,1)S(1)} %collective-permute-done.refs_1_), channel_id=1, source_target_pairs={{0,32},{32,0},{64,96},{96,64},{128,160},{160,128},{192,224},{224,1... | collective-permute-start | bytes 983048 | tf_op jit(solution)/shard_map/ppermute | solution.py:377
  20.4 9.9 %collective-permute-start.4 = (bf16[256,640]{1,0:T(8,128)(2,1)S(1)}, bf16[256,640]{1,0:T(8,128)(2,1)S(1)}, u32[]{:S(2)}, u32[]{:S(2)}) collective-permute-start(bf16[256,640]{1,0:T(8,128)(2,1)S(1)} %collective-permute-done.1.refs_2_), channel_id=1, source_target_pairs={{0,28},{1,29},{2,30},{3,31},{4,0},{5,1},{6,2},{7,3},{8,4},{9,5},{1... | collective-permute-start | bytes 983048 | tf_op jit(solution)/shard_map/ppermute | solution.py:387
  23.3 11.7 %collective-permute-start.6 = (bf16[256,640]{1,0:T(8,128)(2,1)S(1)}, bf16[256,640]{1,0:T(8,128)(2,1)S(1)}, u32[]{:S(2)}, u32[]{:S(2)}) collective-permute-start(bf16[256,640]{1,0:T(8,128)(2,1)S(1)} %collective-permute-done.1.refs_2_), channel_id=1, source_target_pairs={{0,32},{32,0},{64,96},{96,64},{128,160},{160,128},{192,224},{224,1... | collective-permute-start | bytes 983048 | tf_op jit(solution)/shard_map/ppermute | solution.py:377
  30.4 15.9 %collective-permute-start.8 = (bf16[256,640]{1,0:T(8,128)(2,1)S(1)}, bf16[256,640]{1,0:T(8,128)(2,1)S(1)}, u32[]{:S(2)}, u32[]{:S(2)}) collective-permute-start(bf16[256,640]{1,0:T(8,128)(2,1)S(1)} %collective-permute-done.4.refs_2_), channel_id=1, source_target_pairs={{0,28},{1,29},{2,30},{3,31},{4,0},{5,1},{6,2},{7,3},{8,4},{9,5},{1... | collective-permute-start | bytes 983048 | tf_op jit(solution)/shard_map/ppermute | solution.py:387
  33.8 12.6 %collective-permute-start.10 = (bf16[256,640]{1,0:T(8,128)(2,1)S(1)}, bf16[256,640]{1,0:T(8,128)(2,1)S(1)}, u32[]{:S(2)}, u32[]{:S(2)}) collective-permute-start(bf16[256,640]{1,0:T(8,128)(2,1)S(1)} %collective-permute-done.4.refs_2_), channel_id=1, source_target_pairs={{0,32},{32,0},{64,96},{96,64},{128,160},{160,128},{192,224},{224,1... | collective-permute-start | bytes 983048 | tf_op jit(solution)/shard_map/ppermute | solution.py:377
  34.9 10.5 %collective-permute-start.7 = (bf16[256,640]{1,0:T(8,128)(2,1)S(1)}, bf16[256,640]{1,0:T(8,128)(2,1)S(1)}, u32[]{:S(2)}, u32[]{:S(2)}) collective-permute-start(bf16[256,640]{1,0:T(8,128)(2,1)S(1)} %collective-permute-done.3.refs_1_), channel_id=1, source_target_pairs={{0,4},{1,5},{2,6},{3,7},{4,8},{5,9},{6,10},{7,11},{8,12},{9,13},{1... | collective-permute-start | bytes 983048 | tf_op jit(solution)/shard_map/ppermute | solution.py:386
  34.9 11.4 %collective-permute-start.9 = (bf16[256,640]{1,0:T(8,128)(2,1)S(1)}, bf16[256,640]{1,0:T(8,128)(2,1)S(1)}, u32[]{:S(2)}, u32[]{:S(2)}) collective-permute-start(bf16[256,640]{1,0:T(8,128)(2,1)S(1)} %collective-permute-done.3.refs_1_), channel_id=1, source_target_pairs={{0,32},{32,0},{64,96},{96,64},{128,160},{160,128},{192,224},{224,1... | collective-permute-start | bytes 983048 | tf_op jit(solution)/shard_map/ppermute | solution.py:377
  45.4 12.2 %collective-permute-start.11 = (bf16[256,640]{1,0:T(8,128)(2,1)S(1)}, bf16[256,640]{1,0:T(8,128)(2,1)S(1)}, u32[]{:S(2)}, u32[]{:S(2)}) collective-permute-start(bf16[256,640]{1,0:T(8,128)(2,1)S(1)} %collective-permute-done.7.refs_1_), channel_id=1, source_target_pairs={{0,32},{32,0},{64,96},{96,64},{128,160},{160,128},{192,224},{224,1... | collective-permute-start | bytes 983048 | tf_op jit(solution)/shard_map/ppermute | solution.py:377
  46.3 10.5 %collective-permute-start.13 = (bf16[256,640]{1,0:T(8,128)(2,1)S(1)}, bf16[256,640]{1,0:T(8,128)(2,1)S(1)}, u32[]{:S(2)}, u32[]{:S(2)}) collective-permute-start(bf16[256,640]{1,0:T(8,128)(2,1)S(1)} %collective-permute-done.7.refs_1_), channel_id=1, source_target_pairs={{0,4},{1,5},{2,6},{3,7},{4,8},{5,9},{6,10},{7,11},{8,12},{9,13},{1... | collective-permute-start | bytes 983048 | tf_op jit(solution)/shard_map/ppermute | solution.py:390
  46.3 11.3 %collective-permute-start.12 = (bf16[256,640]{1,0:T(8,128)(2,1)S(1)}, bf16[256,640]{1,0:T(8,128)(2,1)S(1)}, u32[]{:S(2)}, u32[]{:S(2)}) collective-permute-start(bf16[256,640]{1,0:T(8,128)(2,1)S(1)} %collective-permute-done.8.refs_2_), channel_id=1, source_target_pairs={{0,32},{32,0},{64,96},{96,64},{128,160},{160,128},{192,224},{224,1... | collective-permute-start | bytes 983048 | tf_op jit(solution)/shard_map/ppermute | solution.py:377
  56.7 6.7 %collective-permute-start.14 = (bf16[256,640]{1,0:T(8,128)(2,1)S(1)}, bf16[256,640]{1,0:T(8,128)(2,1)S(1)}, u32[]{:S(2)}, u32[]{:S(2)}) collective-permute-start(bf16[256,640]{1,0:T(8,128)(2,1)S(1)} %collective-permute-done.13.refs_1_), channel_id=1, source_target_pairs={{0,32},{32,0},{64,96},{96,64},{128,160},{160,128},{192,224},{224,1... | collective-permute-start | bytes 983048 | tf_op jit(solution)/shard_map/ppermute | solution.py:377
  70.1 15.1 %collective-permute-start.17 = (f32[512,256]{1,0:T(8,128)S(1)}, f32[512,256]{1,0:T(8,128)S(1)}, u32[]{:S(2)}, u32[]{:S(2)}) collective-permute-start(f32[512,256]{1,0:T(8,128)S(1)} %bitcast.36), channel_id=1, source_target_pairs={{0,2},{1,3},{2,0},{3,1},{4,6},{5,7},{6,4},{7,5},{8,10},{9,11},{10,... | collective-permute-start | bytes 1572872 | tf_op jit(solution)/shard_map/ppermute | solution.py:405
  72.5 24.3 %collective-permute-start.18 = (f32[512,256]{1,0:T(8,128)S(1)}, f32[512,256]{1,0:T(8,128)S(1)}, u32[]{:S(2)}, u32[]{:S(2)}) collective-permute-start(f32[512,256]{1,0:T(8,128)S(1)} %get-tuple-element.48), channel_id=1, source_target_pairs={{0,1},{1,2},{2,3},{3,0},{4,5},{5,6},{6,7},{7,4},{8,9},{9,10},{10,1... | collective-permute-start | bytes 1572872 | tf_op jit(solution)/shard_map/ppermute | solution.py:405
  74.1 23.1 %collective-permute-start.19 = (f32[512,256]{1,0:T(8,128)S(1)}, f32[512,256]{1,0:T(8,128)S(1)}, u32[]{:S(2)}, u32[]{:S(2)}) collective-permute-start(f32[512,256]{1,0:T(8,128)S(1)} %get-tuple-element.49), channel_id=1, source_target_pairs={{0,3},{1,0},{2,1},{3,2},{4,7},{5,4},{6,5},{7,6},{8,11},{9,8},{10,9... | collective-permute-start | bytes 1572872 | tf_op jit(solution)/shard_map/ppermute | solution.py:405
  97.4 13.4 %collective-permute-start.20 = (f32[128,256]{1,0:T(8,128)S(1)}, f32[128,256]{1,0:T(8,128)S(1)}, u32[]{:S(2)}, u32[]{:S(2)}) collective-permute-start(f32[128,256]{1,0:T(8,128)S(1)} %get-tuple-element.50), channel_id=1, source_target_pairs={{0,128},{32,160},{64,192},{96,224},{128,0},{160,32},{192,64},{224,... | collective-permute-start | bytes 393224 | tf_op jit(solution)/shard_map/ppermute | solution.py:409
  100.4 10.4 %collective-permute-start.21 = (f32[128,256]{1,0:T(8,128)S(1)}, f32[128,256]{1,0:T(8,128)S(1)}, u32[]{:S(2)}, u32[]{:S(2)}) collective-permute-start(f32[128,256]{1,0:T(8,128)S(1)} %get-tuple-element.52), channel_id=1, source_target_pairs={{0,64},{32,96},{64,128},{96,160},{128,192},{160,224},{192,0},{224,... | collective-permute-start | bytes 393224 | tf_op jit(solution)/shard_map/ppermute | solution.py:409
  102.4 8.4 %collective-permute-start.22 = (f32[128,256]{1,0:T(8,128)S(1)}, f32[128,256]{1,0:T(8,128)S(1)}, u32[]{:S(2)}, u32[]{:S(2)}) collective-permute-start(f32[128,256]{1,0:T(8,128)S(1)} %get-tuple-element.51), channel_id=1, source_target_pairs={{0,192},{32,224},{64,0},{96,32},{128,64},{160,96},{192,128},{224,1... | collective-permute-start | bytes 393224 | tf_op jit(solution)/shard_map/ppermute | solution.py:409
  111.5 7.0 %collective-permute-start.26 = (f32[128,256]{1,0:T(8,128)S(1)}, f32[128,256]{1,0:T(8,128)S(1)}, u32[]{:S(2)}, u32[]{:S(2)}) collective-permute-start(f32[128,256]{1,0:T(8,128)S(1)} %fusion.3.refs_9_), channel_id=1, source_target_pairs={{0,128},{32,160},{64,192},{96,224},{128,0},{160,32},{192,64},{224,... | collective-permute-start | bytes 393224 | tf_op jit(solution)/shard_map/ppermute | solution.py:410
  113.8 7.0 %collective-permute-start.28 = (f32[128,256]{1,0:T(8,128)S(1)}, f32[128,256]{1,0:T(8,128)S(1)}, u32[]{:S(2)}, u32[]{:S(2)}) collective-permute-start(f32[128,256]{1,0:T(8,128)S(1)} %fusion.3.refs_9_), channel_id=1, source_target_pairs={{0,64},{32,96},{64,128},{96,160},{128,192},{160,224},{192,0},{224,... | collective-permute-start | bytes 393224 | tf_op jit(solution)/shard_map/ppermute | solution.py:410
  114.0 8.8 %collective-permute-start.23 = (f32[128,256]{1,0:T(8,128)S(1)}, f32[128,256]{1,0:T(8,128)S(1)}, u32[]{:S(2)}, u32[]{:S(2)}) collective-permute-start(f32[128,256]{1,0:T(8,128)S(1)} %fusion.3.refs_9_), channel_id=1, source_target_pairs={{0,32},{32,0},{64,96},{96,64},{128,160},{160,128},{192,224},{224,1... | collective-permute-start | bytes 393224 | tf_op jit(solution)/shard_map/ppermute | solution.py:411
  (11 other events, 107.8 us)

commit v11 on v10

--- a/solution.py
+++ b/solution.py
@@ -358,10 +358,9 @@
         return lax.dynamic_slice(doubled, (0, y, 0), (NC, NY, QUART)).reshape(TOUCH)
 
     own_list = touched.reshape(TOUCH)
-    next_list = lax.ppermute(own_list, "shard", x_pairs(-1))
-    far_lists = lax.ppermute(jnp.stack([own_list, next_list]), "shard", x_pairs(-2))
-    lists = {0: ordered(own_list), 1: ordered(next_list),
-             2: ordered(far_lists[0]), 3: ordered(far_lists[1])}
+    lists = {0: ordered(own_list)}
+    for k in range(1, NX):
+        lists[k] = ordered(lax.ppermute(own_list, "shard", x_pairs(-k)))
     stacked = jnp.stack([lists[k][HALF:] for k in ORDER])[:, :, None]
     rows = jnp.broadcast_to(stacked, (NX, HALF, LANES))
     all_rows = jnp.broadcast_to(lists[0][:, None], (TOUCH, LANES))

time: 131 us -> 133 us (1.015)
    ppermute x4, waiting for transfers between devices: 15.2 us -> 18.3 us  [body(): up = lax.ppermute(up, 'shard', z_pairs(1))]
    ppermute x2 -> x3, waiting for transfers between devices: 2.25 us -> 0.01 us  [body(): lists[k] = ordered(lax.ppermute(own_list, 'shard', x_pairs(-k)))]
    ppermute x8, starting transfers between devices: 5.88 us -> 7.28 us  [swap(): return [lax.ppermute(p, 'grp', C_PAIRS) for p in packets]]
    ppermute x2 -> x3, starting transfers between devices: 4.32 us -> 5.1 us  [body(): lists[k] = ordered(lax.ppermute(own_list, 'shard', x_pairs(-k)))]
  transfers between devices with their start and end apart: 30 -> 31, of which waited for: 8 -> 7; matrix products, arithmetic and copies ran while one was open for 1% -> 1% of each run, Pallas kernels for 18% -> 20%
where the time goes in v11:
time: 133 us; the launch traced here: 132 us
  starting transfers between devices  45.6 us (34%)
  waiting for transfers between devices  43.2 us (32%)
  Pallas kernels  39.8 us (30%)
  local copies, waits for them, and re-layouts  1.82 us (1%)
    ppermute x3, waiting for transfers between devices, body(): both[k] = lax.ppermute(both[k], 'shard', x_pairs(k))  19.4 us
    ppermute x4, waiting for transfers between devices, body(): up = lax.ppermute(up, 'shard', z_pairs(1))  18.3 us
    pallas_call x7, Pallas kernels, gather(): pl.pallas_call(lambda *refs: gather_kernel(*refs, count=count, split=spli...  12.9 us
    pallas_call x4, Pallas kernels, sums(): pl.pallas_call(lambda *refs: sums_kernel(*refs, counts=counts, base=base,...  11.2 us
    ppermute x3, starting transfers between devices, body(): down = lax.ppermute(down, 'shard', z_pairs(-1))  10.4 us
    ppermute x4, starting transfers between devices, body(): other = [lax.ppermute(m, 'grp', C_PAIRS) for m in mine]  8.28 us
    ppermute x8, starting transfers between devices, swap(): return [lax.ppermute(p, 'grp', C_PAIRS) for p in packets]  7.28 us
    pallas_call x1, Pallas kernels, update(): pl.pallas_call(update_kernel, out_shape=(jax.ShapeDtypeStruct((ROWS_DEV,...  6.87 us
  transfers between devices with their start and end apart: 31, of which 7 were waited for; matrix products, arithmetic and copies ran while one was open for 1% of the time, Pallas kernels for 20%

profile of v11, /device:TPU:1, one launch (start us, length us, event | category | flops | bytes accessed | tf_op | source)
XLA Modules:
  0.0 132.2 jit_solution(702708956993557983)
XLA Ops:
  0.6 2.1 %collective-permute-start.17 = (s32[1024]{0:T(1024)}, s32[1024]{0:T(1024)S(1)}, u32[]{:S(2)}, u32[]{:S(2)}) collective-permute-start(s32[1024]{0:T(1024)} %bitcast.29), channel_id=1, source_target_pairs={{0,1},{1,2},{2,3},{3,0},{4,5},{5,6},{6,7},{7,4},{8,9},{9,10},{10,1... | collective-permute-start | bytes 12296 | tf_op jit(solution)/shard_map/ppermute | solution.py:363
  5.7 2.6 %pack.1.refs_1_ = bf16[256,640]{1,0:T(8,128)(2,1)S(1)} custom-call(s32[32,128]{1,0:T(8,128)} %bitcast.47, s32[32,128]{1,0:T(8,128)} %bitcast.48, bf16[512,256]{1,0:T(8,128)(2,1)} %bitcast.46), custom_call_target="tpu_custom_call" | custom-call | flops 2400000000 | bytes 12000000 | tf_op jit(solution)/shard_map/pack/pallas_call | solution.py:98
  10.1 4.0 %collective-permute-start.1 = (bf16[256,640]{1,0:T(8,128)(2,1)S(1)}, bf16[256,640]{1,0:T(8,128)(2,1)S(1)}, u32[]{:S(2)}, u32[]{:S(2)}) collective-permute-start(bf16[256,640]{1,0:T(8,128)(2,1)S(1)} %pack.1.refs_1_), channel_id=1, source_target_pairs={{0,28},{1,29},{2,30},{3,31},{4,0},{5,1},{6,2},{7,3},{8,4},{9,5},{1... | collective-permute-start | bytes 983048 | tf_op jit(solution)/shard_map/ppermute | solution.py:386
  17.3 3.3 %collective-permute-done.refs_1_ = bf16[256,640]{1,0:T(8,128)(2,1)S(1)} collective-permute-done((bf16[256,640]{1,0:T(8,128)(2,1)S(1)}, bf16[256,640]{1,0:T(8,128)(2,1)S(1)}, u32[]{:S(2)}, u32[]{:S(2)}) %collective-permute-start) | collective-permute-done | bytes 327712 | tf_op jit(solution)/shard_map/ppermute | solution.py:385
  22.7 3.0 %collective-permute-start.4 = (bf16[256,640]{1,0:T(8,128)(2,1)S(1)}, bf16[256,640]{1,0:T(8,128)(2,1)S(1)}, u32[]{:S(2)}, u32[]{:S(2)}) collective-permute-start(bf16[256,640]{1,0:T(8,128)(2,1)S(1)} %collective-permute-done.1.refs_2_), channel_id=1, source_target_pairs={{0,28},{1,29},{2,30},{3,31},{4,0},{5,1},{6,2},{7,3},{8,4},{9,5},{1... | collective-permute-start | bytes 983048 | tf_op jit(solution)/shard_map/ppermute | solution.py:386
  26.0 2.2 %shard_map.87 = (bf16[3,16,256,128]{3,2,1,0:T(8,128)(2,1)S(1)}, s32[3,16,128]{2,1,0:T(8,128)S(1)}, s32[3,8,128]{2,1,0:T(8,128)S(1)}) custom-call(s32[1]{0:T(128)} %bitcast.6.refs_0_, bf16[256,640]{1,0:T(8,128)(2,1)S(1)} %collective-permute-done.refs_1_, bf16[256,640]{1,0:T(8,128)(2,1)S(1)} %collective-permute-done.1.refs_2_, ...), custom_call_target="tpu_custom_call" | custom-call | flops 3000000000 | bytes 15000000 | tf_op jit(solution)/shard_map/pallas_call | solution.py:154
  28.2 4.5 %collective-permute-done.4.refs_2_ = bf16[256,640]{1,0:T(8,128)(2,1)S(1)} collective-permute-done((bf16[256,640]{1,0:T(8,128)(2,1)S(1)}, bf16[256,640]{1,0:T(8,128)(2,1)S(1)}, u32[]{:S(2)}, u32[]{:S(2)}) %collective-permute-start.4) | collective-permute-done | bytes 327712 | tf_op jit(solution)/shard_map/ppermute | solution.py:386
  32.7 3.4 %collective-permute-start.8 = (bf16[256,640]{1,0:T(8,128)(2,1)S(1)}, bf16[256,640]{1,0:T(8,128)(2,1)S(1)}, u32[]{:S(2)}, u32[]{:S(2)}) collective-permute-start(bf16[256,640]{1,0:T(8,128)(2,1)S(1)} %collective-permute-done.4.refs_2_), channel_id=1, source_target_pairs={{0,28},{1,29},{2,30},{3,31},{4,0},{5,1},{6,2},{7,3},{8,4},{9,5},{1... | collective-permute-start | bytes 983048 | tf_op jit(solution)/shard_map/ppermute | solution.py:386
  37.4 3.0 %shard_map.88 = (bf16[4,16,256,128]{3,2,1,0:T(8,128)(2,1)S(1)}, s32[4,16,128]{2,1,0:T(8,128)S(1)}, s32[4,8,128]{2,1,0:T(8,128)S(1)}) custom-call(s32[1]{0:T(128)} %bitcast.6.refs_0_, bf16[256,640]{1,0:T(8,128)(2,1)S(1)} %collective-permute-done.3.refs_1_, bf16[256,640]{1,0:T(8,128)(2,1)S(1)} %collective-permute-done.4.refs_2_, ...), custom_call_target="tpu_custom_call" | custom-call | flops 3600000000 | bytes 18000000 | tf_op jit(solution)/shard_map/pallas_call | solution.py:154
  40.4 7.4 %collective-permute-done.7.refs_1_ = bf16[256,640]{1,0:T(8,128)(2,1)S(1)} collective-permute-done((bf16[256,640]{1,0:T(8,128)(2,1)S(1)}, bf16[256,640]{1,0:T(8,128)(2,1)S(1)}, u32[]{:S(2)}, u32[]{:S(2)}) %collective-permute-start.7) | collective-permute-done | bytes 327712 | tf_op jit(solution)/shard_map/ppermute | solution.py:385
  48.7 2.8 %shard_map.89 = (bf16[4,16,256,128]{3,2,1,0:T(8,128)(2,1)S(1)}, s32[4,16,128]{2,1,0:T(8,128)S(1)}, s32[4,8,128]{2,1,0:T(8,128)S(1)}) custom-call(s32[1]{0:T(128)} %bitcast.6.refs_0_, bf16[256,640]{1,0:T(8,128)(2,1)S(1)} %collective-permute-done.7.refs_1_, bf16[256,640]{1,0:T(8,128)(2,1)S(1)} %collective-permute-done.8.refs_2_, ...), custom_call_target="tpu_custom_call" | custom-call | flops 3600000000 | bytes 18000000 | tf_op jit(solution)/shard_map/pallas_call | solution.py:154
  51.5 7.6 %collective-permute-done.13.refs_1_ = bf16[256,640]{1,0:T(8,128)(2,1)S(1)} collective-permute-done((bf16[256,640]{1,0:T(8,128)(2,1)S(1)}, bf16[256,640]{1,0:T(8,128)(2,1)S(1)}, u32[]{:S(2)}, u32[]{:S(2)}) %collective-permute-start.13) | collective-permute-done | bytes 327712 | tf_op jit(solution)/shard_map/ppermute | solution.py:389
  62.0 2.8 %shard_map.94.refs_8_ = f32[1,512,256]{2,1,0:T(8,128)S(1)} custom-call(s32[5]{0:T(128)S(1)} %pad_add_fusion.2.refs_0_, s32[1,8,128]{2,1,0:T(8,128)S(1)} %get-tuple-element.25.refs_1_, s32[3,8,128]{2,1,0:T(8,128)S(1)} %get-tuple-element.26.refs_2_, s32[4,8,128]{2,1,0:T(8,128)S(1)} %get-tuple-element.27.refs_3_, s32[4,8,128]{2,1,0:T(8,128)S(1)} %get-tuple-element.28.refs_4_, ...), custom_call_target="tpu_custom_call" | custom-call | flops 1200000000 | bytes 6000000 | tf_op jit(solution)/shard_map/pallas_call | solution.py:215
  66.9 4.2 %shard_map.96 = f32[2,512,256]{2,1,0:T(8,128)S(1)} custom-call(s32[5]{0:T(128)S(1)} %pad_add_fusion.2.refs_0_, s32[1,8,128]{2,1,0:T(8,128)S(1)} %get-tuple-element.25.refs_1_, s32[3,8,128]{2,1,0:T(8,128)S(1)} %get-tuple-element.26.refs_2_, s32[4,8,128]{2,1,0:T(8,128)S(1)} %get-tuple-element.27.refs_3_, s32[4,8,128]{2,1,0:T(8,128)S(1)} %get-tuple-element.28.refs_4_, ...), custom_call_target="tpu_custom_call" | custom-call | flops 2400000000 | bytes 12000000 | tf_op jit(solution)/shard_map/pallas_call | solution.py:215
  74.2 2.6 %collective-permute-start.20 = (f32[512,256]{1,0:T(8,128)S(1)}, f32[512,256]{1,0:T(8,128)S(1)}, u32[]{:S(2)}, u32[]{:S(2)}) collective-permute-start(f32[512,256]{1,0:T(8,128)S(1)} %get-tuple-element.49), channel_id=1, source_target_pairs={{0,3},{1,0},{2,1},{3,2},{4,7},{5,4},{6,5},{7,6},{8,11},{9,8},{10,9... | collective-permute-start | bytes 1572872 | tf_op jit(solution)/shard_map/ppermute | solution.py:404
  76.8 2.9 %shard_map.93 = f32[1,512,256]{2,1,0:T(8,128)S(1)} custom-call(s32[5]{0:T(128)S(1)} %pad_add_fusion.2.refs_0_, s32[1,8,128]{2,1,0:T(8,128)S(1)} %get-tuple-element.25.refs_1_, s32[3,8,128]{2,1,0:T(8,128)S(1)} %get-tuple-element.26.refs_2_, s32[4,8,128]{2,1,0:T(8,128)S(1)} %get-tuple-element.27.refs_3_, s32[4,8,128]{2,1,0:T(8,128)S(1)} %get-tuple-element.28.refs_4_, ...), custom_call_target="tpu_custom_call" | custom-call | flops 1200000000 | bytes 6000000 | tf_op jit(solution)/shard_map/pallas_call | solution.py:215
  79.7 7.8 %collective-permute-done.18 = f32[512,256]{1,0:T(8,128)S(1)} collective-permute-done((f32[512,256]{1,0:T(8,128)S(1)}, f32[512,256]{1,0:T(8,128)S(1)}, u32[]{:S(2)}, u32[]{:S(2)}) %collective-permute-start.18) | collective-permute-done | bytes 524320 | tf_op jit(solution)/shard_map/ppermute | solution.py:404
  87.6 11.6 %collective-permute-done.19 = f32[512,256]{1,0:T(8,128)S(1)} collective-permute-done((f32[512,256]{1,0:T(8,128)S(1)}, f32[512,256]{1,0:T(8,128)S(1)}, u32[]{:S(2)}, u32[]{:S(2)}) %collective-permute-start.19) | collective-permute-done | bytes 524320 | tf_op jit(solution)/shard_map/ppermute | solution.py:404
  99.4 3.0 %collective-permute-start.21 = (f32[128,256]{1,0:T(8,128)S(1)}, f32[128,256]{1,0:T(8,128)S(1)}, u32[]{:S(2)}, u32[]{:S(2)}) collective-permute-start(f32[128,256]{1,0:T(8,128)S(1)} %get-tuple-element.50), channel_id=1, source_target_pairs={{0,128},{32,160},{64,192},{96,224},{128,0},{160,32},{192,64},{224,... | collective-permute-start | bytes 393224 | tf_op jit(solution)/shard_map/ppermute | solution.py:408
  102.4 2.2 %collective-permute-start.22 = (f32[128,256]{1,0:T(8,128)S(1)}, f32[128,256]{1,0:T(8,128)S(1)}, u32[]{:S(2)}, u32[]{:S(2)}) collective-permute-start(f32[128,256]{1,0:T(8,128)S(1)} %get-tuple-element.52), channel_id=1, source_target_pairs={{0,64},{32,96},{64,128},{96,160},{128,192},{160,224},{192,0},{224,... | collective-permute-start | bytes 393224 | tf_op jit(solution)/shard_map/ppermute | solution.py:408
  105.3 6.3 %listed_values.1.refs_3_ = f32[1056,384]{1,0:T(8,128)S(1)} custom-call(s32[8,128]{1,0:T(8,128)S(1)} %bitcast.36, s32[1024,128]{1,0:T(8,128)S(1)} %broadcast_in_dim.7.rows_ref.refs_4_, f32[32,128]{1,0:T(8,128)S(1)} %bitcast.38, f32[4096,256]{1,0:T(8,128)S(1)} %copy-done), custom_call_target="tpu_custom_call" | custom-call | flops 3600000000 | bytes 18000000 | tf_op jit(solution)/shard_map/listed_values/pallas_call | solution.py:245
  118.0 2.2 %collective-permute-start.26 = (f32[128,256]{1,0:T(8,128)S(1)}, f32[128,256]{1,0:T(8,128)S(1)}, u32[]{:S(2)}, u32[]{:S(2)}) collective-permute-start(f32[128,256]{1,0:T(8,128)S(1)} %collective-permute-done.25.refs_10_), channel_id=1, source_target_pairs={{0,32},{32,0},{64,96},{96,64},{128,160},{160,128},{192,224},{224,1... | collective-permute-start | bytes 393224 | tf_op jit(solution)/shard_map/ppermute | solution.py:410
  120.2 2.4 %collective-permute-start.28 = (f32[128,256]{1,0:T(8,128)S(1)}, f32[128,256]{1,0:T(8,128)S(1)}, u32[]{:S(2)}, u32[]{:S(2)}) collective-permute-start(f32[128,256]{1,0:T(8,128)S(1)} %collective-permute-done.27.refs_11_), channel_id=1, source_target_pairs={{0,32},{32,0},{64,96},{96,64},{128,160},{160,128},{192,224},{224,1... | collective-permute-start | bytes 393224 | tf_op jit(solution)/shard_map/ppermute | solution.py:410
  125.2 6.9 %update.1 = (f32[4096,256]{1,0:T(8,128)}, f32[32,128]{1,0:T(8,128)}) custom-call(s32[24]{0:T(128)S(1)} %pad_add_fusion.1.refs_0_, s32[1024]{0:T(1024)S(1)} %bitcast.34, f32[4096,256]{1,0:T(8,128)} %refs_2_.1, f32[1056,384]{1,0:T(8,128)} %copy-done.1, s32[1024,128]{1,0:T(8,128)S(1)} %broadcast_in_dim.7.rows_ref.refs_4_, ...), custom_call_target="tpu_custom_call" | custom-call | tf_op jit(solution)/shard_map/update/pallas_call | solution.py:318
  (83 shorter events, 30.2 us)
Async XLA Ops:
  0.6 14.8 %collective-permute-start.17 = (s32[1024]{0:T(1024)}, s32[1024]{0:T(1024)S(1)}, u32[]{:S(2)}, u32[]{:S(2)}) collective-permute-start(s32[1024]{0:T(1024)} %bitcast.29), channel_id=1, source_target_pairs={{0,1},{1,2},{2,3},{3,0},{4,5},{5,6},{6,7},{7,4},{8,9},{9,10},{10,1... | collective-permute-start | bytes 12296 | tf_op jit(solution)/shard_map/ppermute | solution.py:363
  2.7 14.5 %collective-permute-start.16 = (s32[1024]{0:T(1024)}, s32[1024]{0:T(1024)S(1)}, u32[]{:S(2)}, u32[]{:S(2)}) collective-permute-start(s32[1024]{0:T(1024)} %bitcast.30), channel_id=1, source_target_pairs={{0,3},{1,0},{2,1},{3,2},{4,7},{5,4},{6,5},{7,6},{8,11},{9,8},{10,9... | collective-permute-start | bytes 12296 | tf_op jit(solution)/shard_map/ppermute | solution.py:363
  4.1 13.2 %collective-permute-start.15 = (s32[1024]{0:T(1024)}, s32[1024]{0:T(1024)S(1)}, u32[]{:S(2)}, u32[]{:S(2)}) collective-permute-start(s32[1024]{0:T(1024)} %bitcast.31), channel_id=1, source_target_pairs={{0,2},{1,3},{2,0},{3,1},{4,6},{5,7},{6,4},{7,5},{8,10},{9,11},{10,... | collective-permute-start | bytes 12296 | tf_op jit(solution)/shard_map/ppermute | solution.py:363
  8.4 12.2 %collective-permute-start = (bf16[256,640]{1,0:T(8,128)(2,1)S(1)}, bf16[256,640]{1,0:T(8,128)(2,1)S(1)}, u32[]{:S(2)}, u32[]{:S(2)}) collective-permute-start(bf16[256,640]{1,0:T(8,128)(2,1)S(1)} %pack.1.refs_1_), channel_id=1, source_target_pairs={{0,4},{1,5},{2,6},{3,7},{4,8},{5,9},{6,10},{7,11},{8,12},{9,13},{1... | collective-permute-start | bytes 983048 | tf_op jit(solution)/shard_map/ppermute | solution.py:385
  10.1 12.6 %collective-permute-start.1 = (bf16[256,640]{1,0:T(8,128)(2,1)S(1)}, bf16[256,640]{1,0:T(8,128)(2,1)S(1)}, u32[]{:S(2)}, u32[]{:S(2)}) collective-permute-start(bf16[256,640]{1,0:T(8,128)(2,1)S(1)} %pack.1.refs_1_), channel_id=1, source_target_pairs={{0,28},{1,29},{2,30},{3,31},{4,0},{5,1},{6,2},{7,3},{8,4},{9,5},{1... | collective-permute-start | bytes 983048 | tf_op jit(solution)/shard_map/ppermute | solution.py:386
  15.4 10.6 %collective-permute-start.2 = (bf16[256,640]{1,0:T(8,128)(2,1)S(1)}, bf16[256,640]{1,0:T(8,128)(2,1)S(1)}, u32[]{:S(2)}, u32[]{:S(2)}) collective-permute-start(bf16[256,640]{1,0:T(8,128)(2,1)S(1)} %pack.1.refs_1_), channel_id=1, source_target_pairs={{0,32},{32,0},{64,96},{96,64},{128,160},{160,128},{192,224},{224,1... | collective-permute-start | bytes 983048 | tf_op jit(solution)/shard_map/ppermute | solution.py:376
  20.6 16.7 %collective-permute-start.3 = (bf16[256,640]{1,0:T(8,128)(2,1)S(1)}, bf16[256,640]{1,0:T(8,128)(2,1)S(1)}, u32[]{:S(2)}, u32[]{:S(2)}) collective-permute-start(bf16[256,640]{1,0:T(8,128)(2,1)S(1)} %collective-permute-done.refs_1_), channel_id=1, source_target_pairs={{0,4},{1,5},{2,6},{3,7},{4,8},{5,9},{6,10},{7,11},{8,12},{9,13},{1... | collective-permute-start | bytes 983048 | tf_op jit(solution)/shard_map/ppermute | solution.py:385
  20.6 16.7 %collective-permute-start.5 = (bf16[256,640]{1,0:T(8,128)(2,1)S(1)}, bf16[256,640]{1,0:T(8,128)(2,1)S(1)}, u32[]{:S(2)}, u32[]{:S(2)}) collective-permute-start(bf16[256,640]{1,0:T(8,128)(2,1)S(1)} %collective-permute-done.refs_1_), channel_id=1, source_target_pairs={{0,32},{32,0},{64,96},{96,64},{128,160},{160,128},{192,224},{224,1... | collective-permute-start | bytes 983048 | tf_op jit(solution)/shard_map/ppermute | solution.py:376
  22.7 10.0 %collective-permute-start.4 = (bf16[256,640]{1,0:T(8,128)(2,1)S(1)}, bf16[256,640]{1,0:T(8,128)(2,1)S(1)}, u32[]{:S(2)}, u32[]{:S(2)}) collective-permute-start(bf16[256,640]{1,0:T(8,128)(2,1)S(1)} %collective-permute-done.1.refs_2_), channel_id=1, source_target_pairs={{0,28},{1,29},{2,30},{3,31},{4,0},{5,1},{6,2},{7,3},{8,4},{9,5},{1... | collective-permute-start | bytes 983048 | tf_op jit(solution)/shard_map/ppermute | solution.py:386
  25.7 11.7 %collective-permute-start.6 = (bf16[256,640]{1,0:T(8,128)(2,1)S(1)}, bf16[256,640]{1,0:T(8,128)(2,1)S(1)}, u32[]{:S(2)}, u32[]{:S(2)}) collective-permute-start(bf16[256,640]{1,0:T(8,128)(2,1)S(1)} %collective-permute-done.1.refs_2_), channel_id=1, source_target_pairs={{0,32},{32,0},{64,96},{96,64},{128,160},{160,128},{192,224},{224,1... | collective-permute-start | bytes 983048 | tf_op jit(solution)/shard_map/ppermute | solution.py:376
  32.7 15.9 %collective-permute-start.8 = (bf16[256,640]{1,0:T(8,128)(2,1)S(1)}, bf16[256,640]{1,0:T(8,128)(2,1)S(1)}, u32[]{:S(2)}, u32[]{:S(2)}) collective-permute-start(bf16[256,640]{1,0:T(8,128)(2,1)S(1)} %collective-permute-done.4.refs_2_), channel_id=1, source_target_pairs={{0,28},{1,29},{2,30},{3,31},{4,0},{5,1},{6,2},{7,3},{8,4},{9,5},{1... | collective-permute-start | bytes 983048 | tf_op jit(solution)/shard_map/ppermute | solution.py:386
  36.1 12.6 %collective-permute-start.10 = (bf16[256,640]{1,0:T(8,128)(2,1)S(1)}, bf16[256,640]{1,0:T(8,128)(2,1)S(1)}, u32[]{:S(2)}, u32[]{:S(2)}) collective-permute-start(bf16[256,640]{1,0:T(8,128)(2,1)S(1)} %collective-permute-done.4.refs_2_), channel_id=1, source_target_pairs={{0,32},{32,0},{64,96},{96,64},{128,160},{160,128},{192,224},{224,1... | collective-permute-start | bytes 983048 | tf_op jit(solution)/shard_map/ppermute | solution.py:376
  37.3 10.5 %collective-permute-start.7 = (bf16[256,640]{1,0:T(8,128)(2,1)S(1)}, bf16[256,640]{1,0:T(8,128)(2,1)S(1)}, u32[]{:S(2)}, u32[]{:S(2)}) collective-permute-start(bf16[256,640]{1,0:T(8,128)(2,1)S(1)} %collective-permute-done.3.refs_1_), channel_id=1, source_target_pairs={{0,4},{1,5},{2,6},{3,7},{4,8},{5,9},{6,10},{7,11},{8,12},{9,13},{1... | collective-permute-start | bytes 983048 | tf_op jit(solution)/shard_map/ppermute | solution.py:385
  37.3 11.4 %collective-permute-start.9 = (bf16[256,640]{1,0:T(8,128)(2,1)S(1)}, bf16[256,640]{1,0:T(8,128)(2,1)S(1)}, u32[]{:S(2)}, u32[]{:S(2)}) collective-permute-start(bf16[256,640]{1,0:T(8,128)(2,1)S(1)} %collective-permute-done.3.refs_1_), channel_id=1, source_target_pairs={{0,32},{32,0},{64,96},{96,64},{128,160},{160,128},{192,224},{224,1... | collective-permute-start | bytes 983048 | tf_op jit(solution)/shard_map/ppermute | solution.py:376
  47.8 12.2 %collective-permute-start.11 = (bf16[256,640]{1,0:T(8,128)(2,1)S(1)}, bf16[256,640]{1,0:T(8,128)(2,1)S(1)}, u32[]{:S(2)}, u32[]{:S(2)}) collective-permute-start(bf16[256,640]{1,0:T(8,128)(2,1)S(1)} %collective-permute-done.7.refs_1_), channel_id=1, source_target_pairs={{0,32},{32,0},{64,96},{96,64},{128,160},{160,128},{192,224},{224,1... | collective-permute-start | bytes 983048 | tf_op jit(solution)/shard_map/ppermute | solution.py:376
  48.6 10.5 %collective-permute-start.13 = (bf16[256,640]{1,0:T(8,128)(2,1)S(1)}, bf16[256,640]{1,0:T(8,128)(2,1)S(1)}, u32[]{:S(2)}, u32[]{:S(2)}) collective-permute-start(bf16[256,640]{1,0:T(8,128)(2,1)S(1)} %collective-permute-done.7.refs_1_), channel_id=1, source_target_pairs={{0,4},{1,5},{2,6},{3,7},{4,8},{5,9},{6,10},{7,11},{8,12},{9,13},{1... | collective-permute-start | bytes 983048 | tf_op jit(solution)/shard_map/ppermute | solution.py:389
  48.6 11.3 %collective-permute-start.12 = (bf16[256,640]{1,0:T(8,128)(2,1)S(1)}, bf16[256,640]{1,0:T(8,128)(2,1)S(1)}, u32[]{:S(2)}, u32[]{:S(2)}) collective-permute-start(bf16[256,640]{1,0:T(8,128)(2,1)S(1)} %collective-permute-done.8.refs_2_), channel_id=1, source_target_pairs={{0,32},{32,0},{64,96},{96,64},{128,160},{160,128},{192,224},{224,1... | collective-permute-start | bytes 983048 | tf_op jit(solution)/shard_map/ppermute | solution.py:376
  72.5 15.1 %collective-permute-start.18 = (f32[512,256]{1,0:T(8,128)S(1)}, f32[512,256]{1,0:T(8,128)S(1)}, u32[]{:S(2)}, u32[]{:S(2)}) collective-permute-start(f32[512,256]{1,0:T(8,128)S(1)} %bitcast.37), channel_id=1, source_target_pairs={{0,2},{1,3},{2,0},{3,1},{4,6},{5,7},{6,4},{7,5},{8,10},{9,11},{10,... | collective-permute-start | bytes 1572872 | tf_op jit(solution)/shard_map/ppermute | solution.py:404
  74.0 25.1 %collective-permute-start.19 = (f32[512,256]{1,0:T(8,128)S(1)}, f32[512,256]{1,0:T(8,128)S(1)}, u32[]{:S(2)}, u32[]{:S(2)}) collective-permute-start(f32[512,256]{1,0:T(8,128)S(1)} %get-tuple-element.48), channel_id=1, source_target_pairs={{0,1},{1,2},{2,3},{3,0},{4,5},{5,6},{6,7},{7,4},{8,9},{9,10},{10,1... | collective-permute-start | bytes 1572872 | tf_op jit(solution)/shard_map/ppermute | solution.py:404
  74.2 25.0 %collective-permute-start.20 = (f32[512,256]{1,0:T(8,128)S(1)}, f32[512,256]{1,0:T(8,128)S(1)}, u32[]{:S(2)}, u32[]{:S(2)}) collective-permute-start(f32[512,256]{1,0:T(8,128)S(1)} %get-tuple-element.49), channel_id=1, source_target_pairs={{0,3},{1,0},{2,1},{3,2},{4,7},{5,4},{6,5},{7,6},{8,11},{9,8},{10,9... | collective-permute-start | bytes 1572872 | tf_op jit(solution)/shard_map/ppermute | solution.py:404
  99.4 13.4 %collective-permute-start.21 = (f32[128,256]{1,0:T(8,128)S(1)}, f32[128,256]{1,0:T(8,128)S(1)}, u32[]{:S(2)}, u32[]{:S(2)}) collective-permute-start(f32[128,256]{1,0:T(8,128)S(1)} %get-tuple-element.50), channel_id=1, source_target_pairs={{0,128},{32,160},{64,192},{96,224},{128,0},{160,32},{192,64},{224,... | collective-permute-start | bytes 393224 | tf_op jit(solution)/shard_map/ppermute | solution.py:408
  102.4 10.4 %collective-permute-start.22 = (f32[128,256]{1,0:T(8,128)S(1)}, f32[128,256]{1,0:T(8,128)S(1)}, u32[]{:S(2)}, u32[]{:S(2)}) collective-permute-start(f32[128,256]{1,0:T(8,128)S(1)} %get-tuple-element.52), channel_id=1, source_target_pairs={{0,64},{32,96},{64,128},{96,160},{128,192},{160,224},{192,0},{224,... | collective-permute-start | bytes 393224 | tf_op jit(solution)/shard_map/ppermute | solution.py:408
  104.6 8.2 %collective-permute-start.23 = (f32[128,256]{1,0:T(8,128)S(1)}, f32[128,256]{1,0:T(8,128)S(1)}, u32[]{:S(2)}, u32[]{:S(2)}) collective-permute-start(f32[128,256]{1,0:T(8,128)S(1)} %get-tuple-element.51), channel_id=1, source_target_pairs={{0,192},{32,224},{64,0},{96,32},{128,64},{160,96},{192,128},{224,1... | collective-permute-start | bytes 393224 | tf_op jit(solution)/shard_map/ppermute | solution.py:408
  115.9 8.4 %collective-permute-start.24 = (f32[128,256]{1,0:T(8,128)S(1)}, f32[128,256]{1,0:T(8,128)S(1)}, u32[]{:S(2)}, u32[]{:S(2)}) collective-permute-start(f32[128,256]{1,0:T(8,128)S(1)} %fusion.3.refs_9_), channel_id=1, source_target_pairs={{0,32},{32,0},{64,96},{96,64},{128,160},{160,128},{192,224},{224,1... | collective-permute-start | bytes 393224 | tf_op jit(solution)/shard_map/ppermute | solution.py:410
  (12 other events, 115.4 us)
